TPU v7x, 32 devices: a whole 2x2x4 slice. The times are simulated.
32 devices in a mesh: groups: 2 (over y), wide: 8 (over z, x), narrow: 2 (over core).
Axes of the slice: x: 2, y: 2, z: 4, core: 2. Of those that a mesh axis runs over, the one named last changes fastest.
Arguments:
- features: bfloat16 [1024, 128, 128], P(('groups', 'wide'), 'narrow'), parts along dimension 0, may hold values from -6 to 6
- cotangent: bfloat16 [1024, 128, 128], P(('groups', 'wide'), 'narrow'), parts along dimension 0, may hold values from -6 to 6
- down_weight: bfloat16 [3, 3, 128, 128], replicated, may hold values from -0.1875 to 0.1875
- down_bias: float32 [128], replicated, may hold values from -3 to 3
- up_weight: bfloat16 [3, 3, 128, 128], replicated, may hold values from -0.1875 to 0.1875
Outputs:
- feature_grad: bfloat16 [1024, 128, 128], P(('groups', 'wide'), 'narrow'), parts along dimension 0
- down_grad: float32 [6, 3, 128, 128], P('groups'), parts along dimension 0
- up_grad: float32 [6, 3, 128, 128], P('groups'), parts along dimension 0
- bias_grad: float32 [256], P('groups'), parts along dimension 0
There are 2 independent parts, one for each index of `groups`. A program takes and returns all parts, laid end to end along the dimension named above; an argument that names none is the same for every part. Nothing has to cross between parts.
All inputs are finite; a program needn't handle non-finite values.
Results may differ from a plain program's by a relative error of at most 0.0055.
Values may be sent and summed in bfloat16 or wider, within the bound.
No kernel may reach another device: no remote copies, remote signals or barrier semaphores. Data moves between devices by JAX's collectives and lax.ppermute only.
A program may use at most 64 MiB of HBM per device.

v0:
```python
import jax
import jax.numpy as jnp
from jax import lax
from jax.sharding import PartitionSpec as P


def passed_along(value, axis, steps):
    count = lax.axis_size(axis)
    first, last = (max(0, -steps), min(count, count - steps))
    return lax.ppermute(value, axis, [(source, source + steps) for source in range(first, last)])


def phase_patches(tile, top_row, left_col, half_rows, half_cols, channels):
    quads = tile.reshape(half_rows, 2, half_cols, 2 * channels)
    even_rows = quads[:, 0]
    odd_rows = quads[:, 1]
    upper_rows = jnp.concatenate(
        [top_row.reshape(1, half_cols, 2 * channels), odd_rows[:-1]], axis=0
    )
    row_sets = [upper_rows, even_rows, odd_rows]
    column_ext = jnp.concatenate([left_col, jnp.zeros((1, channels), left_col.dtype)], axis=0)
    column_ext = column_ext.reshape(half_rows + 1, 2, channels)
    rim_sets = [column_ext[:half_rows, 0], column_ext[:half_rows, 1], column_ext[1:, 0]]
    left_sets = [
        jnp.concatenate([rim_sets[index][:, None], row_sets[index][:, :-1, channels:]], axis=1)
        for index in range(3)
    ]
    joined = jnp.concatenate(row_sets + left_sets, axis=2)
    return joined.reshape(half_rows * half_cols, 9 * channels)


def arrange(kernel, channels):
    paired = kernel[:, 1:3].reshape(6 * channels, channels)
    single = kernel[:, 0].reshape(3 * channels, channels)
    return jnp.concatenate([paired, single], axis=0)


def restore(slots, channels):
    slots = slots.reshape(9, channels, channels)
    paired = slots[:6].reshape(3, 2, channels, channels)
    single = slots[6:].reshape(3, 1, channels, channels)
    return jnp.concatenate([single, paired], axis=1)


def shards(features, cotangent, down_weight, down_bias, up_weight):
    tile_rows, tile_cols, channels = features.shape
    half_rows = tile_rows // 2
    half_cols = tile_cols // 2
    edge_rows = jnp.stack([features[-1], cotangent[-1]], axis=0)
    from_above = passed_along(edge_rows, "wide", 1)
    feat_column = jnp.concatenate([from_above[0, -1:], features[:, -1]], axis=0)
    cot_column = jnp.concatenate([from_above[1, -1:], cotangent[:, -1]], axis=0)
    edge_cols = jnp.stack([feat_column, cot_column], axis=0)
    from_left = passed_along(edge_cols, "narrow", 1)
    feat_patch = phase_patches(
        features, from_above[0], from_left[0], half_rows, half_cols, channels
    )
    cot_patch = phase_patches(
        cotangent, from_above[1], from_left[1], half_rows, half_cols, channels
    )
    down_mat = arrange(down_weight, channels)
    up_mat = arrange(up_weight.transpose(0, 1, 3, 2), channels)
    pre_act = jnp.dot(feat_patch, down_mat, preferred_element_type=jnp.float32) + down_bias
    activated = jax.nn.silu(pre_act).astype(jnp.bfloat16)
    act_grad = jnp.dot(cot_patch, up_mat, preferred_element_type=jnp.float32)
    sigm = jax.nn.sigmoid(pre_act)
    pre_grad = (act_grad * sigm * (1.0 + pre_act * (1.0 - sigm))).astype(jnp.bfloat16)
    up_slots = lax.dot_general(
        activated, cot_patch, (((0,), (0,)), ((), ())), preferred_element_type=jnp.float32
    )
    raw_up = restore(up_slots.reshape(channels, 9, channels).transpose(1, 0, 2), channels)
    down_slots = lax.dot_general(
        feat_patch, pre_grad, (((0,), (0,)), ((), ())), preferred_element_type=jnp.float32
    )
    raw_down = restore(down_slots, channels)
    raw_bias = jnp.sum(pre_grad.astype(jnp.float32), axis=0)
    down_trans = down_weight.transpose(3, 0, 1, 2).reshape(channels, 9 * channels)
    terms = jnp.dot(pre_grad, down_trans, preferred_element_type=jnp.float32)
    terms = terms.reshape(half_rows, half_cols, 3, 3 * channels)
    from_right = passed_along(terms[:, 0, :, :channels].astype(jnp.bfloat16), "narrow", -1).astype(
        jnp.float32
    )
    next_cols = jnp.concatenate([terms[:, 1:, :, :channels], from_right[:, None]], axis=1)
    combined = jnp.concatenate(
        [terms[..., channels : 2 * channels], terms[..., 2 * channels :] + next_cols], axis=3
    )
    from_below = passed_along(combined[0:1, :, 0].astype(jnp.bfloat16), "wide", -1).astype(
        jnp.float32
    )
    upper_next = jnp.concatenate([combined[1:, :, 0], from_below], axis=0)
    even_out = combined[:, :, 1]
    odd_out = combined[:, :, 2] + upper_next
    interior = jnp.stack([even_out, odd_out], axis=1).reshape(tile_rows, tile_cols, channels)
    feature_grad = (cotangent.astype(jnp.float32) + interior).astype(jnp.bfloat16)
    clip_level = 0.5 * jnp.sqrt(jnp.float32(18 * channels * channels + channels))
    kernel_size = 9 * channels * channels
    stacked = jnp.concatenate([raw_down.reshape(-1), raw_up.reshape(-1)], axis=0)
    pair_half = lax.psum_scatter(stacked, "narrow", scatter_dimension=0, tiled=True)
    half_total, bias_part = lax.psum((pair_half, raw_bias), "wide")
    square_part, total_bias = lax.psum((jnp.sum(half_total * half_total), bias_part), "narrow")
    square_sum = square_part + jnp.sum(total_bias * total_bias)
    factor = jnp.minimum(1.0, clip_level / jnp.sqrt(square_sum))
    gathered = lax.all_gather(half_total * factor, "narrow", axis=0, tiled=True)
    down_grad = gathered[:kernel_size].reshape(3, 3, channels, channels)
    up_grad = gathered[kernel_size:].reshape(3, 3, channels, channels)
    return (feature_grad, down_grad, up_grad, total_bias * factor)


def solution(mesh):
    return jax.shard_map(
        shards,
        mesh=mesh,
        in_specs=(
            P(("groups", "wide"), "narrow", None),
            P(("groups", "wide"), "narrow", None),
            P(),
            P(),
            P(),
        ),
        out_specs=(
            P(("groups", "wide"), "narrow", None),
            P("groups", None, None, None),
            P("groups", None, None, None),
            P("groups"),
        ),
        check_vma=False,
    )
```

profile of v0, /device:TPU:0, one launch (start us, length us, event | category | flops | bytes accessed | tf_op | source)
XLA Modules:
  0.0 178.2 jit_solution(11205446657348065485)
XLA Ops:
  8.7 4.9 %collective-permute-start = (bf16[2,64,128]{2,1,0:T(8,128)(2,1)S(1)}, bf16[2,64,128]{2,1,0:T(8,128)(2,1)S(1)}, u32[]{:S(2)}, u32[]{:S(2)}) collective-permute-start(bf16[2,64,128]{2,1,0:T(8,128)(2,1)S(1)} %pad_maximum_fusion.14), channel_id=1, source_target_pairs={{0,2},{2,4},{4,6},{6,8},{8,10},{10,12},{12,14},{1,3},{3,5},{5,7},{... | collective-permute-start | bytes 98312 | tf_op jit(solution)/shard_map/ppermute | solution.py:10
  13.6 1.4 reshape.154
  15.5 1.4 slice_bitcast_fusion.7
  16.9 1.4 slice_bitcast_fusion.9
  23.0 1.7 slice.233
  28.6 1.6 collective-permute-start.1
  32.8 1.3 copy-done.5
  34.5 1.2 pad_maximum_fusion.8
  42.4 3.1 %copy.59 = bf16[1152,1024]{1,0:T(8,128)(2,1)S(1)} copy(bf16[1152,1024]{0,1:T(8,128)(2,1)} %bitcast.119) | data formatting | bytes 4718592 | tf_op jit(solution)/shard_map/dot_general | solution.py:68
  48.8 2.1 %copy-done = f32[32,32,3,384]{3,1,2,0:T(8,128)} copy-done((f32[32,32,3,384]{3,1,2,0:T(8,128)}, f32[32,32,3,384]{3,1,2,0:T(8,128)S(1)}, u32[]{:S(2)}) %copy-start) | copy-done | bytes 4718616
  51.0 1.3 collective-permute-start.2
  53.6 3.1 %slice.250 = f32[32,31,3,128]{3,1,2,0:T(8,128)} slice(f32[32,32,3,384]{3,1,2,0:T(8,128)} %copy-done), slice={[0:32], [1:32], [0:3], [0:128]} | slice | bytes 3047424 | tf_op jit(solution)/shard_map/slice | solution.py:83
  56.7 19.5 %psum.30 = f32[128]{0:T(128)S(1)} all-reduce(f32[128]{0:T(128)S(1)} %get-tuple-element.30), channel_id=1, replica_groups=mesh['groups'=2,'wide'=8,'narrow'=2] {'wide'}, use_global_device_ids=true, to_apply=%region_5.6 | all-reduce | flops 128 | bytes 1024 | tf_op jit(solution)/shard_map/psum | solution.py:99
  76.3 1.9 %dynamic-slice.1 = f32[147456]{0:T(1024)} dynamic-slice(f32[294912]{0:T(1024)} %all-reduce.9.cloned.1.call-done, u32[]{:T(128)S(6)} %multiply.2), dynamic_slice_sizes={147456} | dynamic-slice | bytes 1179652
  78.3 3.0 %slice_add_fusion = (f32[32,32,3,128]{3,1,2,0:T(8,128)S(1)}, f32[32,32,3,128]{3,1,2,0:T(8,128)S(1)}) fusion(f32[32,32,3,384]{3,1,2,0:T(8,128)} %copy-done, f32[32,1,3,128]{3,1,2,0:T(1,128)S(1)} %copy.53, f32[32,31,3,128]{3,1,2,0:T(8,128)} %slice.250), kind=kLoop, calls=%fused_computation.8 | loop fusion | flops 786432 | bytes 7864320 | tf_op jit(solution)/shard_map/add | solution.py:85
  82.4 66.6 %all-reduce.7.cloned.1.call-done = f32[147456]{0:T(1024)} async-done(((f32[147456]{0:T(1024)}), f32[147456]{0:T(1024)}) %all-reduce.7.cloned.1.call-update) | async-done | bytes 589840 | tf_op jit(solution)/shard_map/psum | solution.py:99
  148.9 1.8 %multiply_reduce_fusion = f32[]{:T(128)} fusion(f32[147456]{0:T(1024)} %all-reduce.7.cloned.1.call-done), kind=kLoop, calls=%fused_computation.28 | loop fusion | flops 294911 | bytes 589828 | tf_op jit(solution)/shard_map/reduce_sum | solution.py:100
  150.8 1.3 collective-permute-start.3
  152.1 3.1 %all-reduce.3 = (f32[]{:T(128)}, f32[128]{0:T(128)S(1)}) all-reduce(f32[]{:T(128)} %multiply_reduce_fusion, f32[128]{0:T(128)S(1)} %psum.30), channel_id=1, replica_groups=mesh['groups'=2,'wide'=8,'narrow'=2] {'narrow'}, use_global_device_ids=true, to_apply=%region_3.4 | all-reduce | flops 129 | bytes 1032 | tf_op jit(solution)/shard_map/psum | solution.py:100
  157.1 1.9 %broadcast_multiply_fusion = f32[147456]{0:T(1024)} fusion(f32[147456]{0:T(1024)} %all-reduce.7.cloned.1.call-done, f32[]{:T(128)S(6)} %min.3), kind=kLoop, calls=%fused_computation.42 | loop fusion | flops 147456 | bytes 1179652 | tf_op jit(solution)/shard_map/mul | solution.py:103
  160.8 1.4 reshape.158
  162.5 2.9 %add_convert_fusion = bf16[64,64,128]{2,1,0:T(8,128)(2,1)} fusion(f32[64,64,128]{2,1,0:T(8,128)} %reshape.158, bf16[64,64,128]{2,1,0:T(8,128)(2,1)S(1)} %copy-done.2), kind=kLoop, calls=%fused_computation.7 | loop fusion | flops 1572864 | bytes 4194304 | tf_op jit(solution)/shard_map/convert_element_type | solution.py:94
  165.9 3.5 %all-gather.2.cloned.1.call-done = f32[294912]{0:T(1024)} async-done(((f32[147456]{0:T(1024)}), f32[294912]{0:T(1024)}) %all-gather.2.cloned.1.call-update) | async-done | bytes 1179664 | tf_op jit(solution)/shard_map/all_gather | solution.py:103
  169.4 2.3 %fusion.23 = (f32[147456]{0:T(1024)}, f32[147456]{0:T(1024)}) fusion(f32[294912]{0:T(1024)} %all-gather.2.cloned.1.call-done), kind=kLoop, calls=%fused_computation.91 | loop fusion | bytes 2359296 | tf_op jit(solution)/shard_map/slice | solution.py:105
  (135 shorter events, 28.0 us)
Async XLA Ops:
  7.2 7.9 %copy-start.1 = (bf16[64,64,128]{2,1,0:T(8,128)(2,1)S(1)}, bf16[64,64,128]{2,1,0:T(8,128)(2,1)}, u32[]{:S(2)}) copy-start(bf16[64,64,128]{2,1,0:T(8,128)(2,1)} %param.6) | copy-start | bytes 3145732
  7.2 69.2 %all-reduce.9.cloned.1.call-start = ((), (), s32[]{:S(2)}) async-start(), calls=%async_computation.2 | async-start | bytes 2359296
  8.7 18.2 %collective-permute-start = (bf16[2,64,128]{2,1,0:T(8,128)(2,1)S(1)}, bf16[2,64,128]{2,1,0:T(8,128)(2,1)S(1)}, u32[]{:S(2)}, u32[]{:S(2)}) collective-permute-start(bf16[2,64,128]{2,1,0:T(8,128)(2,1)S(1)} %pad_maximum_fusion.14), channel_id=1, source_target_pairs={{0,2},{2,4},{4,6},{6,8},{8,10},{10,12},{12,14},{1,3},{3,5},{5,7},{... | collective-permute-start | bytes 98312 | tf_op jit(solution)/shard_map/ppermute | solution.py:10
  18.4 7.0 %copy-start.13 = (bf16[32,32,256]{2,1,0:T(8,128)(2,1)S(1)}, bf16[32,32,256]{2,1,0:T(8,128)(2,1)}, u32[]{:S(2)}) copy-start(bf16[32,32,256]{2,1,0:T(8,128)(2,1)} %get-tuple-element.10) | copy-start | bytes 1572868
  18.4 7.8 %copy-start.12 = (bf16[32,32,256]{2,1,0:T(8,128)(2,1)S(1)}, bf16[32,32,256]{2,1,0:T(8,128)(2,1)}, u32[]{:S(2)}) copy-start(bf16[32,32,256]{2,1,0:T(8,128)(2,1)} %get-tuple-element.11) | copy-start | bytes 1572868
  18.4 6.2 %copy-start.14 = (bf16[32,32,256]{2,1,0:T(8,128)(2,1)S(1)}, bf16[32,32,256]{2,1,0:T(8,128)(2,1)}, u32[]{:S(2)}) copy-start(bf16[32,32,256]{2,1,0:T(8,128)(2,1)} %get-tuple-element.15) | copy-start | bytes 1572868
  28.5 1.8 %copy-start.8 = (bf16[32,32,256]{2,1,0:T(8,128)(2,1)S(1)}, bf16[32,32,256]{2,1,0:T(8,128)(2,1)}, u32[]{:S(2)}) copy-start(bf16[32,32,256]{2,1,0:T(8,128)(2,1)} %pad_maximum_fusion.3) | copy-start | bytes 1572868
  28.6 5.5 %collective-permute-start.1 = (bf16[2,65,128]{2,1,0:T(8,128)(2,1)S(1)}, bf16[2,65,128]{2,1,0:T(8,128)(2,1)S(1)}, u32[]{:S(2)}, u32[]{:S(2)}) collective-permute-start(bf16[2,65,128]{2,1,0:T(8,128)(2,1)S(1)} %pad_maximum_fusion.12), channel_id=1, source_target_pairs={{0,1},{2,3},{4,5},{6,7},{8,9},{10,11},{12,13},{14,15},{16,17},{18,... | collective-permute-start | bytes 99848 | tf_op jit(solution)/shard_map/ppermute | solution.py:10
  30.3 2.4 %copy-start.10 = (bf16[32,1,32,256]{3,2,1,0:T(8,128)(2,1)S(1)}, bf16[32,1,32,256]{3,2,1,0:T(8,128)(2,1)}, u32[]{:S(2)}) copy-start(bf16[32,1,32,256]{3,2,1,0:T(8,128)(2,1)} %get-tuple-element.13) | copy-start | bytes 1572868
  30.3 2.4 %copy-start.9 = (bf16[32,1,32,256]{3,2,1,0:T(8,128)(2,1)S(1)}, bf16[32,1,32,256]{3,2,1,0:T(8,128)(2,1)}, u32[]{:S(2)}) copy-start(bf16[32,1,32,256]{3,2,1,0:T(8,128)(2,1)} %get-tuple-element.12) | copy-start | bytes 1572868
  31.5 2.7 %copy-start.17 = (bf16[32,31,128]{2,1,0:T(8,128)(2,1)S(1)}, bf16[32,31,128]{2,1,0:T(8,128)(2,1)}, u32[]{:S(2)}) copy-start(bf16[32,31,128]{2,1,0:T(8,128)(2,1)} %fusion.15) | copy-start | bytes 761860
  32.7 1.4 copy-start.5
  34.2 4.8 %copy-start.6 = (bf16[1024,1152]{1,0:T(8,128)(2,1)S(1)}, bf16[1024,1152]{1,0:T(8,128)(2,1)}, u32[]{:S(2)}) copy-start(bf16[1024,1152]{1,0:T(8,128)(2,1)} %copy-done.5) | copy-start | bytes 7077892
  35.7 3.7 %slice-start.2 = ((bf16[3,3,128,128]{3,2,1,0:T(8,128)(2,1)}), bf16[3,1,128,128]{3,2,1,0:T(8,128)(2,1)S(1)}, s32[]{:S(2)}) async-start(bf16[3,3,128,128]{3,2,1,0:T(8,128)(2,1)} %param.7), calls=%async_computation.5 | async-start | bytes 196608 | tf_op jit(solution)/shard_map/slice | solution.py:34
  35.7 3.7 %slice-start.3 = ((bf16[3,3,128,128]{3,2,1,0:T(8,128)(2,1)}), bf16[3,2,128,128]{3,2,1,0:T(8,128)(2,1)S(1)}, s32[]{:S(2)}) async-start(bf16[3,3,128,128]{3,2,1,0:T(8,128)(2,1)} %param.7), calls=%async_computation.6 | async-start | bytes 393216 | tf_op jit(solution)/shard_map/slice | solution.py:33
  35.7 3.7 %copy-start.20 = (f32[128]{0:T(128)S(1)}, f32[128]{0:T(128)}, u32[]{:S(2)}) copy-start(f32[128]{0:T(128)} %param.8) | copy-start | bytes 1540
  42.4 3.1 %copy-start.4 = (f32[1152,128]{1,0:T(8,128)}, f32[1152,128]{1,0:T(8,128)S(1)}, u32[]{:S(2)}) copy-start(f32[1152,128]{1,0:T(8,128)S(1)} %fusion.28) | copy-start | bytes 1769476
  47.9 101.0 %all-reduce.7.cloned.1.call-start = ((), (), s32[]{:S(2)}) async-start(), calls=%async_computation | async-start | bytes 1179648 | tf_op jit(solution)/shard_map/psum | solution.py:99
  48.0 4.3 %copy-start.21 = (u32[32]{0:T(128)S(1)}, u32[32]{0:T(128)}, u32[]{:S(2)}) copy-start(u32[32]{0:T(128)} %constant.17) | copy-start | bytes 388
  48.8 2.1 %copy-start = (f32[32,32,3,384]{3,1,2,0:T(8,128)}, f32[32,32,3,384]{3,1,2,0:T(8,128)S(1)}, u32[]{:S(2)}) copy-start(f32[32,32,3,384]{3,1,2,0:T(8,128)S(1)} %fusion.27) | copy-start | bytes 14155780
  51.0 25.2 %collective-permute-start.2 = (bf16[32,3,128]{2,0,1:T(8,128)(2,1)S(1)}, bf16[32,3,128]{2,0,1:T(8,128)(2,1)S(1)}, u32[]{:S(2)}, u32[]{:S(2)}) collective-permute-start(bf16[32,3,128]{2,0,1:T(8,128)(2,1)S(1)} %bitcast.148), channel_id=1, source_target_pairs={{1,0},{3,2},{5,4},{7,6},{9,8},{11,10},{13,12},{15,14},{17,16},{19,... | collective-permute-start | bytes 73736 | tf_op jit(solution)/shard_map/ppermute | solution.py:10
  78.3 91.1 %all-gather.2.cloned.1.call-start = ((), (), s32[]{:S(2)}) async-start(), calls=%async_computation.1 | async-start | bytes 1769472 | tf_op jit(solution)/shard_map/all_gather | solution.py:103
  150.8 8.4 %collective-permute-start.3 = (bf16[1,32,256]{2,1,0:T(8,128)(2,1)S(1)}, bf16[1,32,256]{2,1,0:T(8,128)(2,1)S(1)}, u32[]{:S(2)}, u32[]{:S(2)}) collective-permute-start(bf16[1,32,256]{2,1,0:T(8,128)(2,1)S(1)} %fusion.19), channel_id=1, source_target_pairs={{2,0},{4,2},{6,4},{8,6},{10,8},{12,10},{14,12},{3,1},{5,3},{7,5},{... | collective-permute-start | bytes 49160 | tf_op jit(solution)/shard_map/ppermute | solution.py:10
  160.8 1.7 copy-start.2
  (9 other events, 10.6 us)
Sparse Core Ops, SparseCore 0:
  48.1 19.9 all-reduce.8
  78.4 70.4 all-reduce.6
  159.2 10.1 all-gather.1
where the time goes:
time: 179 us; the launch traced here: 178 us
  waiting for transfers between devices  70.1 us (39%)
  local copies, waits for them, and re-layouts  36.1 us (20%)
  blocking collectives  22.6 us (13%)
  other arithmetic  19.8 us (11%)
  between operations  16.5 us (9%)
  starting transfers between devices  9.15 us (5%)
  matrix products  4 us (2%)
    psum x1, waiting for transfers between devices, shards(): half_total, bias_part = lax.psum((pair_half, raw_bias), 'wide')  66.6 us
    psum x1, blocking collectives, shards(): half_total, bias_part = lax.psum((pair_half, raw_bias), 'wide')  19.5 us
    unnamed x59, local copies, waits for them, and re-layouts  11.7 us
    ppermute x4, starting transfers between devices, passed_along(): lax.ppermute(value, axis, [(source, source + steps) for source in range(f...  9.03 us
    concatenate x6, other arithmetic, phase_patches(): jnp.concatenate([rim_sets[index][:, None], row_sets[index][:, :-1, channe...  4.61 us
    slice x4, local copies, waits for them, and re-layouts, phase_patches(): row_sets[index][:, :-1, channels:]  3.93 us
  transfers between devices with their start and end apart: 7, of which 2 were waited for; matrix products, arithmetic and copies ran while one was open for 18% of the time, Pallas kernels for 0%

commit v1 on v0

v1 whole, which is shorter than its diff:
```python
import functools

import jax
import jax.numpy as jnp
from jax import lax
from jax.experimental import pallas as pl
from jax.experimental.pallas import tpu as pltpu
from jax.sharding import PartitionSpec as P

F32 = jnp.float32
BF16 = jnp.bfloat16
VM = pl.BlockSpec(memory_space=pltpu.VMEM)
ANY = pl.BlockSpec(memory_space=pl.ANY)
SIDE = 16


def call(body, out_shape, scratch=(), in_specs=None, n_in=0, flops=0, nbytes=0, name=None):
    return pl.pallas_call(
        body,
        out_shape=out_shape,
        in_specs=in_specs if in_specs is not None else [VM] * n_in,
        out_specs=jax.tree.map(lambda _: VM, out_shape),
        scratch_shapes=list(scratch),
        name=name,
        cost_estimate=pl.CostEstimate(flops=flops, transcendentals=0, bytes_accessed=nbytes),
    )


def sds(shape, dtype):
    return jax.ShapeDtypeStruct(shape, dtype)


def edge_body(feat, cot, rows, cols, strip, wide_strip, sems):
    tile_rows, tile_cols, _ = feat.shape
    copies = []
    for which, ref in enumerate((feat, cot)):
        copies.append(
            pltpu.make_async_copy(ref.at[tile_rows - 1], rows.at[which], sems.at[2 * which])
        )
        copies.append(
            pltpu.make_async_copy(
                ref.at[:, pl.ds(tile_cols - 16, 16), :], strip.at[which], sems.at[2 * which + 1]
            )
        )
    for copy in copies:
        copy.start()
    for copy in copies:
        copy.wait()
    for which in range(2):
        wide_strip[...] = strip[which].astype(F32).reshape(wide_strip.shape)
        cols[which] = wide_strip[pl.ds(15, tile_rows, stride=16), :].astype(BF16)


def phase_body(tile, out, wide):
    rows, cols, channels = tile.shape
    wide[:, 0:8, :] = jnp.zeros((rows, 8, channels), F32)
    wide[:, 8:, :] = tile[...].astype(F32)
    for col_off in range(3):
        out[col_off] = wide[:, pl.ds(7 + col_off, cols // 2, stride=2), :].astype(BF16)


def fill_patches(phases, top, left, patch, line, column):
    _, rows, half_cols, channels = phases.shape
    half_rows = rows // 2
    line[0:8, :] = jnp.broadcast_to(left[0:1, :].astype(F32), (8, channels))
    line[8:, :] = top[...].astype(F32)
    column[...] = left[...].astype(F32)
    first = lax.broadcasted_iota(jnp.int32, (half_rows, half_cols, channels), 1) == 0
    paired = phases.reshape(3, half_rows, 2, half_cols, channels)
    for col_off in range(3):
        lanes = [pl.ds((3 * row_off + col_off) * channels, channels) for row_off in range(3)]
        even = paired[col_off, :, 0].astype(F32) if col_off == 0 else paired[col_off, :, 0]
        odd = paired[col_off, :, 1].astype(F32) if col_off == 0 else paired[col_off, :, 1]
        if col_off == 0:
            rim = [
                column[pl.ds(off, half_rows, stride=2), :].reshape(half_rows, 1, channels)
                for off in (1, 2)
            ]
            even = jnp.where(first, rim[0], even).astype(BF16)
            odd = jnp.where(first, rim[1], odd).astype(BF16)
        patch[:, :, lanes[1]] = even
        patch[:, :, lanes[2]] = odd
        patch[1:, :, lanes[0]] = odd[:-1]
        patch[0, :, lanes[0]] = line[pl.ds(7 + col_off, half_cols, stride=2), :].astype(BF16)


def main_body(
    feat_phases, cot_phases, top, left, down_weight, down_bias, up_weight,
    grads, first_row, first_col, mine, other, bias_part,
    feat_patch, cot_patch, up_mat, act, wide_grads, line, column,
):
    _, rows, half_cols, channels = feat_phases.shape
    half_rows = rows // 2
    pixels = half_rows * half_cols
    taps = 9 * channels
    fill_patches(feat_phases, top.at[0], left.at[0], feat_patch, line, column)
    fill_patches(cot_phases, top.at[1], left.at[1], cot_patch, line, column)
    for tap in range(9):
        up_mat[:, pl.ds(tap * channels, channels)] = up_weight[tap // 3, tap % 3]
    down_mat = down_weight[...].reshape(taps, channels)
    bias_row = down_bias[...].reshape(1, channels)
    step = 8
    for start in range(0, half_rows, step):
        span = pl.ds(start * half_cols, step * half_cols)
        feat_rows = feat_patch[start : start + step].reshape(step * half_cols, taps)
        cot_rows = cot_patch[start : start + step].reshape(step * half_cols, taps)
        pre = jnp.dot(feat_rows, down_mat, preferred_element_type=F32) + bias_row
        act_grad = lax.dot_general(
            cot_rows, up_mat[...], (((1,), (1,)), ((), ())), preferred_element_type=F32
        )
        sigm = 1.0 / (1.0 + jnp.exp(-pre))
        act[span, :] = (pre * sigm).astype(BF16)
        pre_grad = (act_grad * sigm * (1.0 + pre * (1.0 - sigm))).astype(BF16)
        grads[span, :] = pre_grad
        wide_grads[span, :] = pre_grad.astype(F32)
    first_row[...] = grads[0:half_cols, :]
    first_col[...] = wide_grads[pl.ds(0, half_rows, stride=half_cols), :].astype(BF16)
    raw_bias = jnp.sum(wide_grads[...], axis=0, keepdims=True)
    coarse = raw_bias.astype(BF16)
    fine = (raw_bias - coarse.astype(F32)).astype(BF16)
    bias_part[...] = jnp.broadcast_to(coarse.astype(F32) + fine.astype(F32), bias_part.shape)
    put_side(other, taps, coarse, fine)
    raw_up = lax.dot_general(
        act[...], cot_patch[...].reshape(pixels, taps), (((0,), (0,)), ((), ())),
        preferred_element_type=F32,
    )
    raw_down = lax.dot_general(
        feat_patch[...].reshape(pixels, taps), grads[...], (((0,), (0,)), ((), ())),
        preferred_element_type=F32,
    )
    core = lax.axis_index("narrow")

    @pl.when(core == 0)
    def _():
        mine[...] = raw_down
        for tap in range(9):
            span = pl.ds(tap * channels, channels)
            other[span, :] = raw_up[:, tap * channels : (tap + 1) * channels].astype(BF16)

    @pl.when(core != 0)
    def _():
        other[0:taps, :] = raw_down.astype(BF16)
        for tap in range(9):
            span = pl.ds(tap * channels, channels)
            mine[span, :] = raw_up[:, tap * channels : (tap + 1) * channels]


def put_side(out, at, coarse, fine):
    channels = out.shape[1]
    row = lax.broadcasted_iota(jnp.int32, (SIDE, channels), 0)
    block = jnp.where(row == 0, coarse.astype(F32), jnp.where(row == 1, fine.astype(F32), 0.0))
    out[at : at + SIDE, :] = block.astype(BF16)


def take_side(ref, at):
    block = ref[at : at + SIDE, :].astype(F32)
    return block[0:1] + block[1:2]


def bit_of(position):
    low, high = position
    at = lax.axis_index("wide")
    shift = jnp.where(lax.axis_index("narrow") == 0, low, high)
    return lax.rem(lax.shift_right_logical(at, shift.astype(at.dtype)), 2)


def joined_bias(bias_in, got, size, out, sent, at):
    total = bias_in[0:1, :] + take_side(got, size)
    coarse = total.astype(BF16)
    fine = (total - coarse.astype(F32)).astype(BF16)
    out[...] = jnp.broadcast_to(coarse.astype(F32) + fine.astype(F32), out.shape)
    if sent is not None:
        put_side(sent, at, coarse, fine)


def halve_body(position, held, got, bias_in, keep, send, bias_out):
    size = held.shape[0]
    half = size // 2
    bit = bit_of(position)
    near = pl.ds(pl.multiple_of(bit * half, 16), half)
    away = pl.ds(pl.multiple_of((1 - bit) * half, 16), half)
    send[0:half, :] = (held[away, :] + got[away, :].astype(F32)).astype(BF16)
    keep[...] = held[near, :] + got[near, :].astype(F32)
    joined_bias(bias_in, got, size, bias_out, send, half)


def whole_body(held, got, bias_in, send, bias_out):
    size = got.shape[0] - SIDE
    send[0:size, :] = (held[0:size, :].astype(F32) + got[0:size, :].astype(F32)).astype(BF16)
    joined_bias(bias_in, got, size, bias_out, send, size)


def last_body(held, got, bias_in, total, bias_out):
    size = got.shape[0] - SIDE
    total[...] = (held[0:size, :].astype(F32) + got[0:size, :].astype(F32)).astype(BF16)
    joined_bias(bias_in, got, size, bias_out, None, 0)


def place_body(position, held, got, out):
    size = held.shape[0]
    bit = bit_of(position)
    out[pl.ds(pl.multiple_of(bit * size, 16), size), :] = held[...]
    out[pl.ds(pl.multiple_of((1 - bit) * size, 16), size), :] = got[...]


def final_body(held, got, bias_in, down, up, bias_out):
    channels = held.shape[1]
    core = lax.axis_index("narrow")
    squares = jnp.zeros((channels, channels), F32)
    for ref in (held, got):
        part = jnp.zeros((channels, channels), F32)
        for tap in range(9):
            block = ref[tap * channels : (tap + 1) * channels, :].astype(F32)
            part = part + block * block
        squares = squares + part
    bias = bias_in[0:1, :]
    total = jnp.sum(jnp.sum(squares, axis=0, keepdims=True) + bias * bias, axis=1, keepdims=True)
    clip_level = 0.5 * float(18 * channels * channels + channels) ** 0.5
    factor = jnp.minimum(1.0, clip_level / jnp.sqrt(total))
    factor = jnp.broadcast_to(factor, (1, channels))
    bias_out[...] = bias * factor

    def write(down_ref, up_ref):
        for tap in range(9):
            rows = slice(tap * channels, (tap + 1) * channels)
            down[tap] = down_ref[rows, :].astype(F32) * factor
            up[tap] = up_ref[rows, :].astype(F32) * factor

    @pl.when(core == 0)
    def _():
        write(held, got)

    @pl.when(core != 0)
    def _():
        write(got, held)


def feature_body(grads, right, below, cot, down_weight, out, wide, pairs, near_mat, low_mat, woven):
    tile_rows, tile_cols, channels = cot.shape
    half_rows, half_cols = tile_rows // 2, tile_cols // 2
    wide[0:half_rows, 0:half_cols, :] = grads[...].astype(F32).reshape(
        half_rows, half_cols, channels
    )
    last = lax.broadcasted_iota(jnp.int32, (half_rows, 8, channels), 1) == 0
    rim = right[...].astype(F32).reshape(half_rows, 1, channels)
    wide[0:half_rows, half_cols:, :] = jnp.where(last, rim, 0.0)
    low = below[...].astype(F32)
    wide[half_rows, :, :] = low
    pairs[:, :, 0:channels] = wide[:, 0:half_cols, :].astype(BF16)
    pairs[:, :, channels:] = wide[:, 1 : half_cols + 1, :].astype(BF16)
    zero = jnp.zeros((channels, channels), BF16)
    blocks = [(1, 1, None), (1, 2, 0), (2, 1, None), (2, 2, 0)]
    for at, (row_off, here, next_off) in enumerate(blocks):
        rows = slice(at * channels, (at + 1) * channels)
        near_mat[rows, 0:channels] = down_weight[row_off, here]
        near_mat[rows, channels:] = zero if next_off is None else down_weight[row_off, next_off]
    for at, (here, next_off) in enumerate([(1, None), (2, 0)]):
        rows = slice(at * channels, (at + 1) * channels)
        low_mat[rows, 0:channels] = down_weight[0, here]
        low_mat[rows, channels:] = zero if next_off is None else down_weight[0, next_off]
    step = 8
    dims = (((1,), (1,)), ((), ()))
    for start in range(0, half_rows, step):
        count = step * half_cols
        here = pairs[start : start + step].reshape(count, 2 * channels)
        under = pairs[start + 1 : start + 1 + step].reshape(count, 2 * channels)
        near = lax.dot_general(here, near_mat[...], dims, preferred_element_type=F32)
        far = lax.dot_general(under, low_mat[...], dims, preferred_element_type=F32)
        shape = (step, half_cols, channels)
        for row_par in range(2):
            for col_par in range(2):
                lanes = slice((2 * row_par + col_par) * channels, (2 * row_par + col_par + 1) * channels)
                value = near[:, lanes]
                if row_par:
                    value = value + far[:, col_par * channels : (col_par + 1) * channels]
                woven[:, row_par, pl.ds(col_par, half_cols, stride=2), :] = value.reshape(shape)
        span = slice(2 * start, 2 * (start + step))
        total = cot[span].astype(F32) + woven[...].reshape(2 * step, tile_cols, channels)
        out[span] = total.astype(BF16)


def passed_along(value, axis, steps):
    count = lax.axis_size(axis)
    first, last = (max(0, -steps), min(count, count - steps))
    return lax.ppermute(value, axis, [(source, source + steps) for source in range(first, last)])


def traded(value, position):
    count, cores = lax.axis_size("wide"), lax.axis_size("narrow")
    pairs = []
    for at in range(count):
        for core in range(cores):
            mate = at ^ (1 << position[0 if core == 0 else 1])
            pairs.append((at * cores + core, mate * cores + core))
    return lax.ppermute(value, ("wide", "narrow"), pairs)


def shards(features, cotangent, down_weight, down_bias, up_weight):
    tile_rows, tile_cols, channels = features.shape
    half_rows, half_cols = tile_rows // 2, tile_cols // 2
    pixels = half_rows * half_cols
    taps = 9 * channels
    rows, cols = call(
        edge_body,
        (sds((2, tile_cols, channels), BF16), sds((2, tile_rows, channels), BF16)),
        scratch=[
            pltpu.VMEM((2, tile_rows, 16, channels), BF16),
            pltpu.VMEM((tile_rows * 16, channels), F32),
            pltpu.SemaphoreType.DMA((4,)),
        ],
        in_specs=[ANY, ANY],
        nbytes=1 << 19,
        name="edges",
    )(features, cotangent)
    from_above = passed_along(rows, "wide", 1)
    phases = call(
        phase_body,
        sds((3, tile_rows, half_cols, channels), BF16),
        scratch=[pltpu.VMEM((tile_rows, tile_cols + 8, channels), F32)],
        n_in=1,
        flops=1 << 28,
        nbytes=3 << 20,
        name="phases",
    )
    feat_phases = phases(features)
    cot_phases = phases(cotangent)
    cols = jnp.concatenate(
        [from_above[:, -1:], cols, jnp.zeros((2, 7, channels), BF16)], axis=1
    )
    from_left = passed_along(cols, "narrow", 1)
    grads, first_row, first_col, mine, other, bias_sum = call(
        main_body,
        (
            sds((pixels, channels), BF16),
            sds((half_cols, channels), BF16),
            sds((half_rows, channels), BF16),
            sds((taps, channels), F32),
            sds((taps + SIDE, channels), BF16),
            sds((8, channels), F32),
        ),
        scratch=[
            pltpu.VMEM((half_rows, half_cols, taps), BF16),
            pltpu.VMEM((half_rows, half_cols, taps), BF16),
            pltpu.VMEM((channels, taps), BF16),
            pltpu.VMEM((pixels, channels), BF16),
            pltpu.VMEM((pixels, channels), F32),
            pltpu.VMEM((tile_cols + 8, channels), F32),
            pltpu.VMEM((tile_rows + 8, channels), F32),
        ],
        n_in=7,
        flops=8 * pixels * taps * channels,
        nbytes=6 << 20,
        name="main",
    )(feat_phases, cot_phases, from_above, from_left, down_weight, down_bias, up_weight)

    got = lax.ppermute(other, "narrow", [(0, 1), (1, 0)])

    from_right = passed_along(first_col, "narrow", -1)
    low_row = jnp.concatenate(
        [first_row, from_right[:1], jnp.zeros((7, channels), BF16)], axis=0
    )
    from_below = passed_along(low_row, "wide", -1)
    feature_grad = call(
        feature_body,
        sds((tile_rows, tile_cols, channels), BF16),
        scratch=[
            pltpu.VMEM((half_rows + 1, half_cols + 8, channels), F32),
            pltpu.VMEM((half_rows + 1, half_cols, 2 * channels), BF16),
            pltpu.VMEM((4 * channels, 2 * channels), BF16),
            pltpu.VMEM((2 * channels, 2 * channels), BF16),
            pltpu.VMEM((8, 2, tile_cols, channels), F32),
        ],
        n_in=5,
        flops=2 * pixels * 6 * 2 * channels * channels,
        nbytes=3 << 20,
        name="feature",
    )(grads, from_right, from_below, cotangent, down_weight)

    count = lax.axis_size("wide")
    bits = count.bit_length() - 1
    order = [(bit, bit) for bit in range(bits)]
    if bits > 1:
        order[0], order[1] = (0, 1), (1, 0)
    halvings = min(bits - 1, 3)
    held = mine
    for step in range(halvings):
        half = held.shape[0] // 2
        held, send, bias_sum = call(
            functools.partial(halve_body, order[step]),
            (sds((half, channels), F32), sds((half + SIDE, channels), BF16), sds((8, channels), F32)),
            n_in=3,
            nbytes=held.size * 4,
            name="halve",
        )(held, got, bias_sum)
        got = traded(send, order[step])
    for step in range(halvings, bits):
        size = held.shape[0] if step == halvings else held.shape[0] - SIDE
        send, bias_sum = call(
            whole_body,
            (sds((size + SIDE, channels), BF16), sds((8, channels), F32)),
            n_in=3,
            nbytes=held.size * 4,
            name="whole",
        )(held, got, bias_sum)
        got = traded(send, order[step])
        held = send
    size = got.shape[0] - SIDE
    block, bias_sum = call(
        last_body,
        (sds((size, channels), BF16), sds((8, channels), F32)),
        n_in=3,
        nbytes=size * channels * 4,
        name="last",
    )(held, got, bias_sum)
    for step in reversed(range(halvings)):
        got = traded(block, order[step])
        block = call(
            functools.partial(place_body, order[step]),
            sds((2 * block.shape[0], channels), BF16),
            n_in=2,
            nbytes=block.size * 4,
            name="place",
        )(block, got)
    got = lax.ppermute(block, "narrow", [(0, 1), (1, 0)])
    down, up, bias_grad = call(
        final_body,
        (
            sds((9, channels, channels), F32),
            sds((9, channels, channels), F32),
            sds((1, channels), F32),
        ),
        n_in=3,
        nbytes=12 * taps * channels,
        name="final",
    )(block, got, bias_sum)
    shape = (3, 3, channels, channels)
    return (feature_grad, down.reshape(shape), up.reshape(shape), bias_grad.reshape(channels))


def solution(mesh):
    return jax.shard_map(
        shards,
        mesh=mesh,
        in_specs=(
            P(("groups", "wide"), "narrow", None),
            P(("groups", "wide"), "narrow", None),
            P(),
            P(),
            P(),
        ),
        out_specs=(
            P(("groups", "wide"), "narrow", None),
            P("groups", None, None, None),
            P("groups", None, None, None),
            P("groups"),
        ),
        check_vma=False,
    )
```

time: 179 us -> 82.1 us (0.46)
  waiting for transfers between devices: 70.1 us -> 25.2 us
  local copies, waits for them, and re-layouts: 36.1 us -> 6.03 us
  Pallas kernels: 0 us -> 28.7 us
  blocking collectives: 22.6 us -> 0 us
  other arithmetic: 19.8 us -> 0.92 us
  between operations: 16.5 us -> 0.73 us
  starting transfers between devices: 9.15 us -> 19.9 us
  matrix products: 4 us -> 0 us
    psum x1 -> x0, waiting for transfers between devices: 66.6 us -> none  [shards(): half_total, bias_part = lax.psum((pair_half, raw_bias), 'wide')]
    pallas_call x0 -> x12, Pallas kernels: none -> 28.7 us  [the longest x1 5.73 us: shards(): call(main_body, (sds((pixels, channels), BF16), sds((half_cols, channels)...]
    psum x2 -> x0, blocking collectives: 22.6 us -> none  [the longest x1 19.5 us: shards(): half_total, bias_part = lax.psum((pair_half, raw_bias), 'wide')]
    ppermute x0 -> x7, waiting for transfers between devices: none -> 17.4 us  [the longest x5 15.6 us: traded(): return lax.ppermute(value, ('wide', 'narrow'), pairs)]
    slice x28 -> x2, local copies, waits for them, and re-layouts: 14.7 us -> 0.01 us  [the longest x1 0.01 us: shards(): from_above[:, -1:]]
    ppermute x0 -> x7, starting transfers between devices: none -> 11.2 us  [the longest x5 11.1 us: traded(): return lax.ppermute(value, ('wide', 'narrow'), pairs)]
    ppermute x4, waiting for transfers between devices: 0.01 us -> 7.77 us  [passed_along(): lax.ppermute(value, axis, [(source, source + steps) for source in range(f...]
    concatenate x15 -> x2, other arithmetic: 7.61 us -> 0.92 us  [the longest x1 0.85 us: shards(): jnp.concatenate([from_above[:, -1:], cols, jnp.zeros((2, 7, channels), BF...]
  transfers between devices with their start and end apart: 7 -> 11, of which waited for: 2 -> 9; matrix products, arithmetic and copies ran while one was open for 18% -> 0% of each run, Pallas kernels for 0% -> 11%
where the time goes in v1:
time: 82.1 us; the launch traced here: 81.5 us
  Pallas kernels  28.7 us (35%)
  waiting for transfers between devices  25.2 us (31%)
  starting transfers between devices  19.9 us (24%)
  local copies, waits for them, and re-layouts  6.03 us (7%)
  other arithmetic  0.92 us (1%)
    ppermute x5, waiting for transfers between devices, traded(): return lax.ppermute(value, ('wide', 'narrow'), pairs)  15.6 us
    ppermute x5, starting transfers between devices, traded(): return lax.ppermute(value, ('wide', 'narrow'), pairs)  11.1 us
    ppermute x4, starting transfers between devices, passed_along(): lax.ppermute(value, axis, [(source, source + steps) for source in range(f...  8.73 us
    ppermute x4, waiting for transfers between devices, passed_along(): lax.ppermute(value, axis, [(source, source + steps) for source in range(f...  7.77 us
    unnamed x26, local copies, waits for them, and re-layouts  5.87 us
    pallas_call x1, Pallas kernels, shards(): call(main_body, (sds((pixels, channels), BF16), sds((half_cols, channels)...  5.73 us
    pallas_call x2, Pallas kernels, shards(): call(functools.partial(halve_body, order[step]), (sds((half, channels), F...  3.75 us
    pallas_call x2, Pallas kernels, shards(): call(functools.partial(place_body, order[step]), sds((2 * block.shape[0],...  3.32 us
  transfers between devices with their start and end apart: 11, of which 9 were waited for; matrix products, arithmetic and copies ran while one was open for 0% of the time, Pallas kernels for 11%

profile of v1, /device:TPU:0, one launch (start us, length us, event | category | flops | bytes accessed | tf_op | source)
XLA Modules:
  0.0 81.5 jit_solution(10427767100908294499)
XLA Ops:
  0.6 1.8 %edges.1 = (bf16[2,64,128]{2,1,0:T(8,128)(2,1)}, bf16[2,64,128]{2,1,0:T(8,128)(2,1)}) custom-call(bf16[64,64,128]{2,1,0:T(8,128)(2,1)} %feat.1, bf16[64,64,128]{2,1,0:T(8,128)(2,1)} %cot.3), custom_call_target="tpu_custom_call" | custom-call | bytes 524288 | tf_op jit(solution)/shard_map/edges/pallas_call | solution.py:303
  2.4 4.9 %collective-permute-start = (bf16[2,64,128]{2,1,0:T(8,128)(2,1)}, bf16[2,64,128]{2,1,0:T(8,128)(2,1)S(1)}, u32[]{:S(2)}, u32[]{:S(2)}) collective-permute-start(bf16[2,64,128]{2,1,0:T(8,128)(2,1)} %get-tuple-element.25), channel_id=1, source_target_pairs={{0,2},{2,4},{4,6},{6,8},{8,10},{10,12},{12,14},{1,3},{3,5},{5,7},{... | collective-permute-start | bytes 98312 | tf_op jit(solution)/shard_map/ppermute | solution.py:285
  7.4 1.8 %collective-permute-done.top = bf16[2,64,128]{2,1,0:T(8,128)(2,1)S(1)} collective-permute-done((bf16[2,64,128]{2,1,0:T(8,128)(2,1)}, bf16[2,64,128]{2,1,0:T(8,128)(2,1)S(1)}, u32[]{:S(2)}, u32[]{:S(2)}) %collective-permute-start) | collective-permute-done | bytes 32800 | tf_op jit(solution)/shard_map/ppermute | solution.py:285
  11.4 2.8 %phases.2.feat_phases = bf16[3,64,32,128]{3,2,1,0:T(8,128)(2,1)} custom-call(bf16[64,64,128]{2,1,0:T(8,128)(2,1)} %feat.1), custom_call_target="tpu_custom_call" | custom-call | flops 268435456 | bytes 3145728 | tf_op jit(solution)/shard_map/phases/pallas_call | solution.py:325
  14.1 2.7 %phases.3.cot_phases = bf16[3,64,32,128]{3,2,1,0:T(8,128)(2,1)} custom-call(bf16[64,64,128]{2,1,0:T(8,128)(2,1)} %cot.3), custom_call_target="tpu_custom_call" | custom-call | flops 268435456 | bytes 3145728 | tf_op jit(solution)/shard_map/phases/pallas_call | solution.py:326
  17.5 5.7 %main.1 = (bf16[1024,128]{1,0:T(8,128)(2,1)}, bf16[32,128]{1,0:T(8,128)(2,1)}, bf16[32,128]{1,0:T(8,128)(2,1)}, f32[1152,128]{1,0:T(8,128)}, bf16[1168,128]{1,0:T(8,128)(2,1)}, /*index=5*/f32[8,128]{1,0:T(8,128)}) custom-call(bf16[3,64,32,128]{3,2,1,0:T(8,128)(2,1)} %phases.2.feat_phases, bf16[3,64,32,128]{3,2,1,0:T(8,128)(2,1)} %phases.3.cot_phases, ...), custom_call_target="tpu_custom_call" | custom-call | flops 1207959552 | bytes 6291456 | tf_op jit(solution)/shard_map/main/pallas_call | solution.py:331
  23.3 1.8 %collective-permute-done.4.got = bf16[1168,128]{1,0:T(8,128)(2,1)S(1)} collective-permute-done((bf16[1168,128]{1,0:T(8,128)(2,1)}, bf16[1168,128]{1,0:T(8,128)(2,1)S(1)}, u32[]{:S(2)}, u32[]{:S(2)}) %collective-permute-start.4) | collective-permute-done | bytes 299040 | tf_op jit(solution)/shard_map/ppermute | solution.py:356
  25.8 2.0 %halve.2 = (f32[576,128]{1,0:T(8,128)}, bf16[592,128]{1,0:T(8,128)(2,1)}, f32[8,128]{1,0:T(8,128)}) custom-call(f32[1152,128]{1,0:T(8,128)} %get-tuple-element.30.held, bf16[1168,128]{1,0:T(8,128)(2,1)} %copy-done, f32[8,128]{1,0:T(8,128)} %get-tuple-element.32.bias_in), custom_call_target="tpu_custom_call" | custom-call | bytes 589824 | tf_op jit(solution)/shard_map/halve/pallas_call | solution.py:388
  27.8 2.2 %collective-permute-start.5 = (bf16[592,128]{1,0:T(8,128)(2,1)}, bf16[592,128]{1,0:T(8,128)(2,1)S(1)}, u32[]{:S(2)}, u32[]{:S(2)}) collective-permute-start(bf16[592,128]{1,0:T(8,128)(2,1)} %get-tuple-element.34), channel_id=1, source_target_pairs={{0,2},{1,5},{2,0},{3,7},{4,6},{5,1},{6,4},{7,3},{8,10},{9,13},{10,... | collective-permute-start | bytes 454664 | tf_op jit(solution)/shard_map/ppermute | solution.py:295
  30.0 3.4 %collective-permute-done.5.got = bf16[592,128]{1,0:T(8,128)(2,1)S(1)} collective-permute-done((bf16[592,128]{1,0:T(8,128)(2,1)}, bf16[592,128]{1,0:T(8,128)(2,1)S(1)}, u32[]{:S(2)}, u32[]{:S(2)}) %collective-permute-start.5) | collective-permute-done | bytes 151584 | tf_op jit(solution)/shard_map/ppermute | solution.py:295
  34.0 1.8 %halve.3 = (f32[288,128]{1,0:T(8,128)}, bf16[304,128]{1,0:T(8,128)(2,1)}, f32[8,128]{1,0:T(8,128)}) custom-call(f32[576,128]{1,0:T(8,128)} %get-tuple-element.33.held, bf16[592,128]{1,0:T(8,128)(2,1)} %copy-done.2, f32[8,128]{1,0:T(8,128)} %get-tuple-element.35.bias_in), custom_call_target="tpu_custom_call" | custom-call | bytes 294912 | tf_op jit(solution)/shard_map/halve/pallas_call | solution.py:388
  35.8 3.0 %collective-permute-start.6 = (bf16[304,128]{1,0:T(8,128)(2,1)}, bf16[304,128]{1,0:T(8,128)(2,1)S(1)}, u32[]{:S(2)}, u32[]{:S(2)}) collective-permute-start(bf16[304,128]{1,0:T(8,128)(2,1)} %get-tuple-element.37), channel_id=1, source_target_pairs={{0,4},{1,3},{2,6},{3,1},{4,0},{5,7},{6,2},{7,5},{8,12},{9,11},{10,... | collective-permute-start | bytes 233480 | tf_op jit(solution)/shard_map/ppermute | solution.py:295
  38.8 2.6 %collective-permute-done.6.got = bf16[304,128]{1,0:T(8,128)(2,1)S(1)} collective-permute-done((bf16[304,128]{1,0:T(8,128)(2,1)}, bf16[304,128]{1,0:T(8,128)(2,1)S(1)}, u32[]{:S(2)}, u32[]{:S(2)}) %collective-permute-start.6) | collective-permute-done | bytes 77856 | tf_op jit(solution)/shard_map/ppermute | solution.py:295
  42.0 1.6 %whole.1 = (bf16[304,128]{1,0:T(8,128)(2,1)}, f32[8,128]{1,0:T(8,128)}) custom-call(f32[288,128]{1,0:T(8,128)} %get-tuple-element.36.held, bf16[304,128]{1,0:T(8,128)(2,1)} %copy-done.4, f32[8,128]{1,0:T(8,128)} %get-tuple-element.38.bias_in), custom_call_target="tpu_custom_call" | custom-call | bytes 147456 | tf_op jit(solution)/shard_map/whole/pallas_call | solution.py:398
  43.6 3.0 %collective-permute-start.7 = (bf16[304,128]{1,0:T(8,128)(2,1)}, bf16[304,128]{1,0:T(8,128)(2,1)S(1)}, u32[]{:S(2)}, u32[]{:S(2)}) collective-permute-start(bf16[304,128]{1,0:T(8,128)(2,1)} %get-tuple-element.39.held), channel_id=1, source_target_pairs={{0,8},{1,9},{2,10},{3,11},{4,12},{5,13},{6,14},{7,15},{8,0},{9,1},... | collective-permute-start | bytes 233480 | tf_op jit(solution)/shard_map/ppermute | solution.py:295
  46.7 2.6 %collective-permute-done.7.got = bf16[304,128]{1,0:T(8,128)(2,1)S(1)} collective-permute-done((bf16[304,128]{1,0:T(8,128)(2,1)}, bf16[304,128]{1,0:T(8,128)(2,1)S(1)}, u32[]{:S(2)}, u32[]{:S(2)}) %collective-permute-start.7) | collective-permute-done | bytes 77856 | tf_op jit(solution)/shard_map/ppermute | solution.py:295
  51.4 1.9 %collective-permute-start.8 = (bf16[288,128]{1,0:T(8,128)(2,1)}, bf16[288,128]{1,0:T(8,128)(2,1)S(1)}, u32[]{:S(2)}, u32[]{:S(2)}) collective-permute-start(bf16[288,128]{1,0:T(8,128)(2,1)} %get-tuple-element.41.held), channel_id=1, source_target_pairs={{0,4},{1,3},{2,6},{3,1},{4,0},{5,7},{6,2},{7,5},{8,12},{9,11},{10,... | collective-permute-start | bytes 221192 | tf_op jit(solution)/shard_map/ppermute | solution.py:295
  53.4 2.6 %collective-permute-done.8.got = bf16[288,128]{1,0:T(8,128)(2,1)S(1)} collective-permute-done((bf16[288,128]{1,0:T(8,128)(2,1)}, bf16[288,128]{1,0:T(8,128)(2,1)S(1)}, u32[]{:S(2)}, u32[]{:S(2)}) %collective-permute-start.8) | collective-permute-done | bytes 73760 | tf_op jit(solution)/shard_map/ppermute | solution.py:295
  59.2 4.4 %collective-permute-done.9.got = bf16[576,128]{1,0:T(8,128)(2,1)S(1)} collective-permute-done((bf16[576,128]{1,0:T(8,128)(2,1)}, bf16[576,128]{1,0:T(8,128)(2,1)S(1)}, u32[]{:S(2)}, u32[]{:S(2)}) %collective-permute-start.9) | collective-permute-done | bytes 147488 | tf_op jit(solution)/shard_map/ppermute | solution.py:295
  64.3 1.7 %place.3.held = bf16[1152,128]{1,0:T(8,128)(2,1)} custom-call(bf16[576,128]{1,0:T(8,128)(2,1)} %place.2.held, bf16[576,128]{1,0:T(8,128)(2,1)} %copy-done.3), custom_call_target="tpu_custom_call" | custom-call | bytes 294912 | tf_op jit(solution)/shard_map/place/pallas_call | solution.py:417
  67.4 1.7 %collective-permute-done.2.right = bf16[32,128]{1,0:T(8,128)(2,1)S(1)} collective-permute-done((bf16[32,128]{1,0:T(8,128)(2,1)S(1)}, bf16[32,128]{1,0:T(8,128)(2,1)S(1)}, u32[]{:S(2)}, u32[]{:S(2)}) %collective-permute-start.2) | collective-permute-done | bytes 8224 | tf_op jit(solution)/shard_map/ppermute | solution.py:285
  70.4 4.3 %collective-permute-done.3.below = bf16[40,128]{1,0:T(8,128)(2,1)S(1)} collective-permute-done((bf16[40,128]{1,0:T(8,128)(2,1)S(1)}, bf16[40,128]{1,0:T(8,128)(2,1)S(1)}, u32[]{:S(2)}, u32[]{:S(2)}) %collective-permute-start.3) | collective-permute-done | bytes 10272 | tf_op jit(solution)/shard_map/ppermute | solution.py:285
  75.3 3.2 %feature.1 = bf16[64,64,128]{2,1,0:T(8,128)(2,1)} custom-call(bf16[1024,128]{1,0:T(8,128)(2,1)} %get-tuple-element.27.grads, bf16[32,128]{1,0:T(8,128)(2,1)} %copy-done.8, bf16[40,128]{1,0:T(8,128)(2,1)} %copy-done.7, bf16[64,64,128]{2,1,0:T(8,128)(2,1)} %cot.3, bf16[3,3,128,128]{3,2,1,0:T(8,128)(2,1)} %down_weight.3), custom_call_target="tpu_custom_call" | custom-call | flops 402653184 | bytes 3145728 | tf_op jit(solution)/shard_map/feature/pallas_call | solution.py:363
  79.2 2.3 %final.1 = (f32[9,128,128]{2,1,0:T(8,128)}, f32[9,128,128]{2,1,0:T(8,128)}, f32[1,128]{1,0:T(1,128)}) custom-call(bf16[1152,128]{1,0:T(8,128)(2,1)} %place.3.held, bf16[1152,128]{1,0:T(8,128)(2,1)} %copy-done.1, f32[8,128]{1,0:T(8,128)} %get-tuple-element.42.bias_in), custom_call_target="tpu_custom_call" | custom-call | bytes 1769472 | tf_op jit(solution)/shard_map/final/pallas_call | solution.py:425
  (43 shorter events, 15.0 us)
Async XLA Ops:
  2.4 6.8 %collective-permute-start = (bf16[2,64,128]{2,1,0:T(8,128)(2,1)}, bf16[2,64,128]{2,1,0:T(8,128)(2,1)S(1)}, u32[]{:S(2)}, u32[]{:S(2)}) collective-permute-start(bf16[2,64,128]{2,1,0:T(8,128)(2,1)} %get-tuple-element.25), channel_id=1, source_target_pairs={{0,2},{2,4},{4,6},{6,8},{8,10},{10,12},{12,14},{1,3},{3,5},{5,7},{... | collective-permute-start | bytes 98312 | tf_op jit(solution)/shard_map/ppermute | solution.py:285
  9.2 7.6 %copy-start.10 = (bf16[2,64,128]{2,1,0:T(8,128)(2,1)}, bf16[2,64,128]{2,1,0:T(8,128)(2,1)S(1)}, u32[]{:S(2)}) copy-start(bf16[2,64,128]{2,1,0:T(8,128)(2,1)S(1)} %collective-permute-done.top) | copy-start | bytes 98308
  10.1 6.8 %collective-permute-start.1 = (bf16[2,72,128]{2,1,0:T(8,128)(2,1)S(1)}, bf16[2,72,128]{2,1,0:T(8,128)(2,1)S(1)}, u32[]{:S(2)}, u32[]{:S(2)}) collective-permute-start(bf16[2,72,128]{2,1,0:T(8,128)(2,1)S(1)} %maximum_maximum_fusion), channel_id=1, source_target_pairs={{0,1},{2,3},{4,5},{6,7},{8,9},{10,11},{12,13},{14,15},{16,17},{18,... | collective-permute-start | bytes 110600 | tf_op jit(solution)/shard_map/ppermute | solution.py:285
  16.8 0.6 copy-start.11
  23.2 42.8 %copy-start.12 = (bf16[32,128]{1,0:T(8,128)(2,1)S(1)}, bf16[32,128]{1,0:T(8,128)(2,1)}, u32[]{:S(2)}) copy-start(bf16[32,128]{1,0:T(8,128)(2,1)} %get-tuple-element.28) | copy-start | bytes 24580
  23.2 45.9 %copy-start.9 = (bf16[32,128]{1,0:T(8,128)(2,1)S(1)}, bf16[32,128]{1,0:T(8,128)(2,1)}, u32[]{:S(2)}) copy-start(bf16[32,128]{1,0:T(8,128)(2,1)} %get-tuple-element.29) | copy-start | bytes 24580
  23.2 1.9 %collective-permute-start.4 = (bf16[1168,128]{1,0:T(8,128)(2,1)}, bf16[1168,128]{1,0:T(8,128)(2,1)S(1)}, u32[]{:S(2)}, u32[]{:S(2)}) collective-permute-start(bf16[1168,128]{1,0:T(8,128)(2,1)} %get-tuple-element.31), channel_id=1, source_target_pairs={{0,1},{1,0},{2,3},{3,2},{4,5},{5,4},{6,7},{7,6},{8,9},{9,8},{10,11... | collective-permute-start | bytes 897032 | tf_op jit(solution)/shard_map/ppermute | solution.py:356
  25.1 0.7 copy-start
  27.8 5.6 %collective-permute-start.5 = (bf16[592,128]{1,0:T(8,128)(2,1)}, bf16[592,128]{1,0:T(8,128)(2,1)S(1)}, u32[]{:S(2)}, u32[]{:S(2)}) collective-permute-start(bf16[592,128]{1,0:T(8,128)(2,1)} %get-tuple-element.34), channel_id=1, source_target_pairs={{0,2},{1,5},{2,0},{3,7},{4,6},{5,1},{6,4},{7,3},{8,10},{9,13},{10,... | collective-permute-start | bytes 454664 | tf_op jit(solution)/shard_map/ppermute | solution.py:295
  33.3 0.7 copy-start.2
  35.8 5.6 %collective-permute-start.6 = (bf16[304,128]{1,0:T(8,128)(2,1)}, bf16[304,128]{1,0:T(8,128)(2,1)S(1)}, u32[]{:S(2)}, u32[]{:S(2)}) collective-permute-start(bf16[304,128]{1,0:T(8,128)(2,1)} %get-tuple-element.37), channel_id=1, source_target_pairs={{0,4},{1,3},{2,6},{3,1},{4,0},{5,7},{6,2},{7,5},{8,12},{9,11},{10,... | collective-permute-start | bytes 233480 | tf_op jit(solution)/shard_map/ppermute | solution.py:295
  41.4 0.6 copy-start.4
  43.6 5.6 %collective-permute-start.7 = (bf16[304,128]{1,0:T(8,128)(2,1)}, bf16[304,128]{1,0:T(8,128)(2,1)S(1)}, u32[]{:S(2)}, u32[]{:S(2)}) collective-permute-start(bf16[304,128]{1,0:T(8,128)(2,1)} %get-tuple-element.39.held), channel_id=1, source_target_pairs={{0,8},{1,9},{2,10},{3,11},{4,12},{5,13},{6,14},{7,15},{8,0},{9,1},... | collective-permute-start | bytes 233480 | tf_op jit(solution)/shard_map/ppermute | solution.py:295
  49.2 0.6 copy-start.5
  51.4 4.6 %collective-permute-start.8 = (bf16[288,128]{1,0:T(8,128)(2,1)}, bf16[288,128]{1,0:T(8,128)(2,1)S(1)}, u32[]{:S(2)}, u32[]{:S(2)}) collective-permute-start(bf16[288,128]{1,0:T(8,128)(2,1)} %get-tuple-element.41.held), channel_id=1, source_target_pairs={{0,4},{1,3},{2,6},{3,1},{4,0},{5,7},{6,2},{7,5},{8,12},{9,11},{10,... | collective-permute-start | bytes 221192 | tf_op jit(solution)/shard_map/ppermute | solution.py:295
  56.0 0.6 copy-start.6
  58.2 5.4 %collective-permute-start.9 = (bf16[576,128]{1,0:T(8,128)(2,1)}, bf16[576,128]{1,0:T(8,128)(2,1)S(1)}, u32[]{:S(2)}, u32[]{:S(2)}) collective-permute-start(bf16[576,128]{1,0:T(8,128)(2,1)} %place.2.held), channel_id=1, source_target_pairs={{0,2},{1,5},{2,0},{3,7},{4,6},{5,1},{6,4},{7,3},{8,10},{9,13},{10,... | collective-permute-start | bytes 442376 | tf_op jit(solution)/shard_map/ppermute | solution.py:295
  63.6 0.7 copy-start.3
  66.0 12.5 %collective-permute-start.10 = (bf16[1152,128]{1,0:T(8,128)(2,1)}, bf16[1152,128]{1,0:T(8,128)(2,1)S(1)}, u32[]{:S(2)}, u32[]{:S(2)}) collective-permute-start(bf16[1152,128]{1,0:T(8,128)(2,1)} %place.3.held), channel_id=1, source_target_pairs={{0,1},{1,0},{2,3},{3,2},{4,5},{5,4},{6,7},{7,6},{8,9},{9,8},{10,11... | collective-permute-start | bytes 884744 | tf_op jit(solution)/shard_map/ppermute | solution.py:424
  66.0 3.1 %collective-permute-start.2 = (bf16[32,128]{1,0:T(8,128)(2,1)S(1)}, bf16[32,128]{1,0:T(8,128)(2,1)S(1)}, u32[]{:S(2)}, u32[]{:S(2)}) collective-permute-start(bf16[32,128]{1,0:T(8,128)(2,1)S(1)} %copy-done.12), channel_id=1, source_target_pairs={{1,0},{3,2},{5,4},{7,6},{9,8},{11,10},{13,12},{15,14},{17,16},{19,... | collective-permute-start | bytes 24584 | tf_op jit(solution)/shard_map/ppermute | solution.py:285
  69.0 5.6 %copy-start.8 = (bf16[32,128]{1,0:T(8,128)(2,1)}, bf16[32,128]{1,0:T(8,128)(2,1)S(1)}, u32[]{:S(2)}) copy-start(bf16[32,128]{1,0:T(8,128)(2,1)S(1)} %collective-permute-done.2.right) | copy-start | bytes 24580
  69.1 5.6 %collective-permute-start.3 = (bf16[40,128]{1,0:T(8,128)(2,1)S(1)}, bf16[40,128]{1,0:T(8,128)(2,1)S(1)}, u32[]{:S(2)}, u32[]{:S(2)}) collective-permute-start(bf16[40,128]{1,0:T(8,128)(2,1)S(1)} %maximum_maximum_fusion.1), channel_id=1, source_target_pairs={{2,0},{4,2},{6,4},{8,6},{10,8},{12,10},{14,12},{3,1},{5,3},{7,5},{... | collective-permute-start | bytes 30728 | tf_op jit(solution)/shard_map/ppermute | solution.py:285
  74.7 0.6 copy-start.7
  78.4 0.7 copy-start.1

commit v2 on v1

--- a/solution.py
+++ b/solution.py
@@ -14,16 +14,32 @@
 SIDE = 16
 
 
-def call(body, out_shape, scratch=(), in_specs=None, n_in=0, flops=0, nbytes=0, name=None):
-    return pl.pallas_call(
+def call(body, out_shape, scratch=(), in_specs=None, n_in=0, flops=0, nbytes=0, name=None, near=(), far=(), room=4):
+    kernel = pl.pallas_call(
         body,
         out_shape=out_shape,
         in_specs=in_specs if in_specs is not None else [VM] * n_in,
         out_specs=jax.tree.map(lambda _: VM, out_shape),
         scratch_shapes=list(scratch),
         name=name,
+        compiler_params=pltpu.CompilerParams(vmem_limit_bytes=room << 20),
         cost_estimate=pl.CostEstimate(flops=flops, transcendentals=0, bytes_accessed=nbytes),
     )
+
+    def run(*args):
+        placed = [
+            pltpu.with_memory_space_constraint(arg, pltpu.VMEM if at in near else pltpu.HBM)
+            if at in near or at in far
+            else arg
+            for at, arg in enumerate(args)
+        ]
+        return kernel(*placed)
+
+    return run
+
+
+def vm(shape, dtype):
+    return pltpu.VMEM(shape, dtype)
 
 
 def sds(shape, dtype):
@@ -302,7 +318,7 @@
     taps = 9 * channels
     rows, cols = call(
         edge_body,
-        (sds((2, tile_cols, channels), BF16), sds((2, tile_rows, channels), BF16)),
+        (vm((2, tile_cols, channels), BF16), vm((2, tile_rows, channels), BF16)),
         scratch=[
             pltpu.VMEM((2, tile_rows, 16, channels), BF16),
             pltpu.VMEM((tile_rows * 16, channels), F32),
@@ -311,18 +327,22 @@
         in_specs=[ANY, ANY],
         nbytes=1 << 19,
         name="edges",
+        far=(0, 1),
+        room=8,
     )(features, cotangent)
     from_above = passed_along(rows, "wide", 1)
     phases = call(
         phase_body,
-        sds((3, tile_rows, half_cols, channels), BF16),
+        vm((3, tile_rows, half_cols, channels), BF16),
         scratch=[pltpu.VMEM((tile_rows, tile_cols + 8, channels), F32)],
         n_in=1,
         flops=1 << 28,
         nbytes=3 << 20,
         name="phases",
+        room=16,
     )
     feat_phases = phases(features)
+    from_above, feat_phases = lax.optimization_barrier((from_above, feat_phases))
     cot_phases = phases(cotangent)
     cols = jnp.concatenate(
         [from_above[:, -1:], cols, jnp.zeros((2, 7, channels), BF16)], axis=1
@@ -331,12 +351,12 @@
     grads, first_row, first_col, mine, other, bias_sum = call(
         main_body,
         (
-            sds((pixels, channels), BF16),
-            sds((half_cols, channels), BF16),
-            sds((half_rows, channels), BF16),
-            sds((taps, channels), F32),
-            sds((taps + SIDE, channels), BF16),
-            sds((8, channels), F32),
+            vm((pixels, channels), BF16),
+            vm((half_cols, channels), BF16),
+            vm((half_rows, channels), BF16),
+            vm((taps, channels), F32),
+            vm((taps + SIDE, channels), BF16),
+            vm((8, channels), F32),
         ),
         scratch=[
             pltpu.VMEM((half_rows, half_cols, taps), BF16),
@@ -351,15 +371,38 @@
         flops=8 * pixels * taps * channels,
         nbytes=6 << 20,
         name="main",
+        room=32,
+        near=(0, 1, 2, 3),
     )(feat_phases, cot_phases, from_above, from_left, down_weight, down_bias, up_weight)
 
     got = lax.ppermute(other, "narrow", [(0, 1), (1, 0)])
 
     from_right = passed_along(first_col, "narrow", -1)
+    got, from_right = lax.optimization_barrier((got, from_right))
     low_row = jnp.concatenate(
         [first_row, from_right[:1], jnp.zeros((7, channels), BF16)], axis=0
     )
     from_below = passed_along(low_row, "wide", -1)
+    count = lax.axis_size("wide")
+    bits = count.bit_length() - 1
+    order = [(bit, bit) for bit in range(bits)]
+    if bits > 1:
+        order[0], order[1] = (0, 1), (1, 0)
+    halvings = min(bits - 1, 3)
+    held = mine
+    for step in range(halvings):
+        half = held.shape[0] // 2
+        held, send, bias_sum = call(
+            functools.partial(halve_body, order[step]),
+            (vm((half, channels), F32), vm((half + SIDE, channels), BF16), vm((8, channels), F32)),
+            n_in=3,
+            nbytes=held.size * 4,
+            name="halve",
+            near=(0, 1, 2),
+        )(held, got, bias_sum)
+        got = traded(send, order[step])
+        if step == 0:
+            got, from_below = lax.optimization_barrier((got, from_below))
     feature_grad = call(
         feature_body,
         sds((tile_rows, tile_cols, channels), BF16),
@@ -374,52 +417,41 @@
         flops=2 * pixels * 6 * 2 * channels * channels,
         nbytes=3 << 20,
         name="feature",
+        room=16,
+        near=(0, 1, 2),
     )(grads, from_right, from_below, cotangent, down_weight)
-
-    count = lax.axis_size("wide")
-    bits = count.bit_length() - 1
-    order = [(bit, bit) for bit in range(bits)]
-    if bits > 1:
-        order[0], order[1] = (0, 1), (1, 0)
-    halvings = min(bits - 1, 3)
-    held = mine
-    for step in range(halvings):
-        half = held.shape[0] // 2
-        held, send, bias_sum = call(
-            functools.partial(halve_body, order[step]),
-            (sds((half, channels), F32), sds((half + SIDE, channels), BF16), sds((8, channels), F32)),
-            n_in=3,
-            nbytes=held.size * 4,
-            name="halve",
-        )(held, got, bias_sum)
-        got = traded(send, order[step])
     for step in range(halvings, bits):
         size = held.shape[0] if step == halvings else held.shape[0] - SIDE
         send, bias_sum = call(
             whole_body,
-            (sds((size + SIDE, channels), BF16), sds((8, channels), F32)),
+            (vm((size + SIDE, channels), BF16), vm((8, channels), F32)),
             n_in=3,
             nbytes=held.size * 4,
             name="whole",
+            near=(0, 1, 2),
         )(held, got, bias_sum)
         got = traded(send, order[step])
+        if step == bits - 1:
+            got, feature_grad = lax.optimization_barrier((got, feature_grad))
         held = send
     size = got.shape[0] - SIDE
     block, bias_sum = call(
         last_body,
-        (sds((size, channels), BF16), sds((8, channels), F32)),
+        (vm((size, channels), BF16), vm((8, channels), F32)),
         n_in=3,
         nbytes=size * channels * 4,
         name="last",
+            near=(0, 1, 2),
     )(held, got, bias_sum)
     for step in reversed(range(halvings)):
         got = traded(block, order[step])
         block = call(
             functools.partial(place_body, order[step]),
-            sds((2 * block.shape[0], channels), BF16),
+            vm((2 * block.shape[0], channels), BF16),
             n_in=2,
             nbytes=block.size * 4,
             name="place",
+            near=(0, 1),
         )(block, got)
     got = lax.ppermute(block, "narrow", [(0, 1), (1, 0)])
     down, up, bias_grad = call(
@@ -432,6 +464,8 @@
         n_in=3,
         nbytes=12 * taps * channels,
         name="final",
+            room=8,
+            near=(0, 1, 2),
     )(block, got, bias_sum)
     shape = (3, 3, channels, channels)
     return (feature_grad, down.reshape(shape), up.reshape(shape), bias_grad.reshape(channels))

time: 82.1 us -> 48.6 us (0.59)
  Pallas kernels: 28.7 us -> 7.94 us
  waiting for transfers between devices: 25.2 us -> 18.8 us
  local copies, waits for them, and re-layouts: 6.03 us -> 0.19 us
    pallas_call x12, Pallas kernels: 28.7 us -> 7.94 us  [run(): return kernel(*placed)]
    ppermute x5, waiting for transfers between devices: 15.6 us -> 9.67 us  [traded(): return lax.ppermute(value, ('wide', 'narrow'), pairs)]
    unnamed x26 -> x10, local copies, waits for them, and re-layouts: 5.87 us -> 0.03 us
    ppermute x1, waiting for transfers between devices: 1.79 us -> 0.01 us  [shards(): got = lax.ppermute(other, 'narrow', [(0, 1), (1, 0)])]
    ppermute x1, waiting for transfers between devices: 0.01 us -> 1.57 us  [shards(): got = lax.ppermute(block, 'narrow', [(0, 1), (1, 0)])]
  transfers between devices with their start and end apart: 11 -> 11, of which waited for: 9 -> 9; matrix products, arithmetic and copies ran while one was open for 0% -> 0% of each run, Pallas kernels for 11% -> 5%
where the time goes in v2:
time: 48.6 us; the launch traced here: 48.4 us
  starting transfers between devices  20.5 us (42%)
  waiting for transfers between devices  18.8 us (39%)
  Pallas kernels  7.94 us (16%)
  between operations  0.78 us (2%)
    ppermute x5, starting transfers between devices, traded(): return lax.ppermute(value, ('wide', 'narrow'), pairs)  11.1 us
    ppermute x5, waiting for transfers between devices, traded(): return lax.ppermute(value, ('wide', 'narrow'), pairs)  9.67 us
    ppermute x4, starting transfers between devices, passed_along(): lax.ppermute(value, axis, [(source, source + steps) for source in range(f...  8.86 us
    pallas_call x12, Pallas kernels, run(): return kernel(*placed)  7.94 us
    ppermute x4, waiting for transfers between devices, passed_along(): lax.ppermute(value, axis, [(source, source + steps) for source in range(f...  7.56 us
    ppermute x1, waiting for transfers between devices, shards(): got = lax.ppermute(block, 'narrow', [(0, 1), (1, 0)])  1.57 us
  transfers between devices with their start and end apart: 11, of which 9 were waited for; matrix products, arithmetic and copies ran while one was open for 0% of the time, Pallas kernels for 5%

profile of v2, /device:TPU:0, one launch (start us, length us, event | category | flops | bytes accessed | tf_op | source)
XLA Modules:
  0.0 48.4 jit_solution(1687690686472469253)
XLA Ops:
  0.6 1.3 %edges.1 = (bf16[2,64,128]{2,1,0:T(8,128)(2,1)S(1)}, bf16[2,64,128]{2,1,0:T(8,128)(2,1)S(1)}) custom-call(bf16[64,64,128]{2,1,0:T(8,128)(2,1)} %tile.2, bf16[64,64,128]{2,1,0:T(8,128)(2,1)} %cot.3), custom_call_target="tpu_custom_call" | custom-call | bytes 524288 | tf_op jit(solution)/shard_map/edges/pallas_call | solution.py:36
  1.9 5.0 %collective-permute-start = (bf16[2,64,128]{2,1,0:T(8,128)(2,1)S(1)}, bf16[2,64,128]{2,1,0:T(8,128)(2,1)S(1)}, u32[]{:S(2)}, u32[]{:S(2)}) collective-permute-start(bf16[2,64,128]{2,1,0:T(8,128)(2,1)S(1)} %get-tuple-element.33), channel_id=1, source_target_pairs={{0,2},{2,4},{4,6},{6,8},{8,10},{10,12},{12,14},{1,3},{3,5},{5,7},{... | collective-permute-start | bytes 98312 | tf_op jit(solution)/shard_map/ppermute | solution.py:301
  7.4 1.1 %collective-permute-done.top = bf16[2,64,128]{2,1,0:T(8,128)(2,1)S(1)} collective-permute-done((bf16[2,64,128]{2,1,0:T(8,128)(2,1)S(1)}, bf16[2,64,128]{2,1,0:T(8,128)(2,1)S(1)}, u32[]{:S(2)}, u32[]{:S(2)}) %collective-permute-start) | collective-permute-done | bytes 32800 | tf_op jit(solution)/shard_map/ppermute | solution.py:301
  8.6 1.3 %collective-permute-start.1 = (bf16[2,72,128]{2,1,0:T(8,128)(2,1)S(1)}, bf16[2,72,128]{2,1,0:T(8,128)(2,1)S(1)}, u32[]{:S(2)}, u32[]{:S(2)}) collective-permute-start(bf16[2,72,128]{2,1,0:T(8,128)(2,1)S(1)} %maximum_maximum_fusion), channel_id=1, source_target_pairs={{0,1},{2,3},{4,5},{6,7},{8,9},{10,11},{12,13},{14,15},{16,17},{18,... | collective-permute-start | bytes 110600 | tf_op jit(solution)/shard_map/ppermute | solution.py:301
  9.9 0.3 phases.3.cot_phases
  10.3 0.5 %collective-permute-done.1.left = bf16[2,72,128]{2,1,0:T(8,128)(2,1)S(1)} collective-permute-done((bf16[2,72,128]{2,1,0:T(8,128)(2,1)S(1)}, bf16[2,72,128]{2,1,0:T(8,128)(2,1)S(1)}, u32[]{:S(2)}, u32[]{:S(2)}) %collective-permute-start.1) | collective-permute-done | bytes 36896 | tf_op jit(solution)/shard_map/ppermute | solution.py:301
  10.8 2.7 %main.1 = (bf16[1024,128]{1,0:T(8,128)(2,1)S(1)}, bf16[32,128]{1,0:T(8,128)(2,1)S(1)}, bf16[32,128]{1,0:T(8,128)(2,1)S(1)}, f32[1152,128]{1,0:T(8,128)S(1)}, bf1...) custom-call(bf16[3,64,32,128]{3,2,1,0:T(8,128)(2,1)S(1)} %phases.2.feat_phases, ...), custom_call_target="tpu_custom_call" | custom-call | flops 1207959552 | bytes 6291456 | tf_op jit(solution)/shard_map/main/pallas_call | solution.py:36
  13.5 0.4 collective-permute-start.2
  13.9 1.3 %collective-permute-start.3 = (bf16[32,128]{1,0:T(8,128)(2,1)S(1)}, bf16[32,128]{1,0:T(8,128)(2,1)S(1)}, u32[]{:S(2)}, u32[]{:S(2)}) collective-permute-start(bf16[32,128]{1,0:T(8,128)(2,1)S(1)} %get-tuple-element.39), channel_id=1, source_target_pairs={{1,0},{3,2},{5,4},{7,6},{9,8},{11,10},{13,12},{15,14},{17,16},{19,... | collective-permute-start | bytes 24584 | tf_op jit(solution)/shard_map/ppermute | solution.py:301
  15.3 1.7 %collective-permute-done.3.right = bf16[32,128]{1,0:T(8,128)(2,1)S(1)} collective-permute-done((bf16[32,128]{1,0:T(8,128)(2,1)S(1)}, bf16[32,128]{1,0:T(8,128)(2,1)S(1)}, u32[]{:S(2)}, u32[]{:S(2)}) %collective-permute-start.3) | collective-permute-done | bytes 8224 | tf_op jit(solution)/shard_map/ppermute | solution.py:301
  17.0 2.4 %collective-permute-start.4 = (bf16[592,128]{1,0:T(8,128)(2,1)S(1)}, bf16[592,128]{1,0:T(8,128)(2,1)S(1)}, u32[]{:S(2)}, u32[]{:S(2)}) collective-permute-start(bf16[592,128]{1,0:T(8,128)(2,1)S(1)} %get-tuple-element.43), channel_id=1, source_target_pairs={{0,2},{1,5},{2,0},{3,7},{4,6},{5,1},{6,4},{7,3},{8,10},{9,13},{10,... | collective-permute-start | bytes 454664 | tf_op jit(solution)/shard_map/ppermute | solution.py:311
  19.5 1.3 %collective-permute-start.5 = (bf16[40,128]{1,0:T(8,128)(2,1)S(1)}, bf16[40,128]{1,0:T(8,128)(2,1)S(1)}, u32[]{:S(2)}, u32[]{:S(2)}) collective-permute-start(bf16[40,128]{1,0:T(8,128)(2,1)S(1)} %maximum_maximum_fusion.1), channel_id=1, source_target_pairs={{2,0},{4,2},{6,4},{8,6},{10,8},{12,10},{14,12},{3,1},{5,3},{7,5},{... | collective-permute-start | bytes 30728 | tf_op jit(solution)/shard_map/ppermute | solution.py:301
  20.8 4.3 %collective-permute-done.5.below = bf16[40,128]{1,0:T(8,128)(2,1)S(1)} collective-permute-done((bf16[40,128]{1,0:T(8,128)(2,1)S(1)}, bf16[40,128]{1,0:T(8,128)(2,1)S(1)}, u32[]{:S(2)}, u32[]{:S(2)}) %collective-permute-start.5) | collective-permute-done | bytes 10272 | tf_op jit(solution)/shard_map/ppermute | solution.py:301
  25.1 1.6 %collective-permute-start.6 = (bf16[304,128]{1,0:T(8,128)(2,1)S(1)}, bf16[304,128]{1,0:T(8,128)(2,1)S(1)}, u32[]{:S(2)}, u32[]{:S(2)}) collective-permute-start(bf16[304,128]{1,0:T(8,128)(2,1)S(1)} %get-tuple-element.49), channel_id=1, source_target_pairs={{0,4},{1,3},{2,6},{3,1},{4,0},{5,7},{6,2},{7,5},{8,12},{9,11},{10,... | collective-permute-start | bytes 233480 | tf_op jit(solution)/shard_map/ppermute | solution.py:311
  26.8 2.8 %collective-permute-done.6.got = bf16[304,128]{1,0:T(8,128)(2,1)S(1)} collective-permute-done((bf16[304,128]{1,0:T(8,128)(2,1)S(1)}, bf16[304,128]{1,0:T(8,128)(2,1)S(1)}, u32[]{:S(2)}, u32[]{:S(2)}) %collective-permute-start.6) | collective-permute-done | bytes 77856 | tf_op jit(solution)/shard_map/ppermute | solution.py:311
  29.6 2.7 %collective-permute-start.7 = (bf16[304,128]{1,0:T(8,128)(2,1)S(1)}, bf16[304,128]{1,0:T(8,128)(2,1)S(1)}, u32[]{:S(2)}, u32[]{:S(2)}) collective-permute-start(bf16[304,128]{1,0:T(8,128)(2,1)S(1)} %get-tuple-element.51.held), channel_id=1, source_target_pairs={{0,8},{1,9},{2,10},{3,11},{4,12},{5,13},{6,14},{7,15},{8,0},{9,1},... | collective-permute-start | bytes 233480 | tf_op jit(solution)/shard_map/ppermute | solution.py:311
  32.3 1.8 %feature.1 = bf16[64,64,128]{2,1,0:T(8,128)(2,1)} custom-call(bf16[1024,128]{1,0:T(8,128)(2,1)S(1)} %get-tuple-element.52.grads, bf16[32,128]{1,0:T(8,128)(2,1)S(1)} %collective-permute-done.3.right, bf16[40,128]{1,0:T(8,128)(2,1)S(1)} %collective-permute-done.5.below, bf16[64,64,128]{2,1,0:T(8,128)(2,1)S(1)} %copy-done, bf16[3,3,128,128]{3,2,1,0:T(8,128)(2,1)S(1)} %copy-done.2), custom_call_target="tpu_custom_call" | custom-call | flops 402653184 | bytes 3145728 | tf_op jit(solution)/shard_map/feature/pallas_call | solution.py:36
  34.1 0.9 %collective-permute-done.7.got = bf16[304,128]{1,0:T(8,128)(2,1)S(1)} collective-permute-done((bf16[304,128]{1,0:T(8,128)(2,1)S(1)}, bf16[304,128]{1,0:T(8,128)(2,1)S(1)}, u32[]{:S(2)}, u32[]{:S(2)}) %collective-permute-start.7) | collective-permute-done | bytes 77856 | tf_op jit(solution)/shard_map/ppermute | solution.py:311
  35.0 1.6 %collective-permute-start.8 = (bf16[288,128]{1,0:T(8,128)(2,1)S(1)}, bf16[288,128]{1,0:T(8,128)(2,1)S(1)}, u32[]{:S(2)}, u32[]{:S(2)}) collective-permute-start(bf16[288,128]{1,0:T(8,128)(2,1)S(1)} %get-tuple-element.57.held), channel_id=1, source_target_pairs={{0,4},{1,3},{2,6},{3,1},{4,0},{5,7},{6,2},{7,5},{8,12},{9,11},{10,... | collective-permute-start | bytes 221192 | tf_op jit(solution)/shard_map/ppermute | solution.py:311
  36.6 2.8 %collective-permute-done.8.got = bf16[288,128]{1,0:T(8,128)(2,1)S(1)} collective-permute-done((bf16[288,128]{1,0:T(8,128)(2,1)S(1)}, bf16[288,128]{1,0:T(8,128)(2,1)S(1)}, u32[]{:S(2)}, u32[]{:S(2)}) %collective-permute-start.8) | collective-permute-done | bytes 73760 | tf_op jit(solution)/shard_map/ppermute | solution.py:311
  39.4 2.8 %collective-permute-start.9 = (bf16[576,128]{1,0:T(8,128)(2,1)S(1)}, bf16[576,128]{1,0:T(8,128)(2,1)S(1)}, u32[]{:S(2)}, u32[]{:S(2)}) collective-permute-start(bf16[576,128]{1,0:T(8,128)(2,1)S(1)} %place.2.held), channel_id=1, source_target_pairs={{0,2},{1,5},{2,0},{3,7},{4,6},{5,1},{6,4},{7,3},{8,10},{9,13},{10,... | collective-permute-start | bytes 442376 | tf_op jit(solution)/shard_map/ppermute | solution.py:311
  42.3 3.1 %collective-permute-done.9.got = bf16[576,128]{1,0:T(8,128)(2,1)S(1)} collective-permute-done((bf16[576,128]{1,0:T(8,128)(2,1)S(1)}, bf16[576,128]{1,0:T(8,128)(2,1)S(1)}, u32[]{:S(2)}, u32[]{:S(2)}) %collective-permute-start.9) | collective-permute-done | bytes 147488 | tf_op jit(solution)/shard_map/ppermute | solution.py:311
  45.5 1.6 %collective-permute-done.10.got = bf16[1152,128]{1,0:T(8,128)(2,1)S(1)} collective-permute-done((bf16[1152,128]{1,0:T(8,128)(2,1)S(1)}, bf16[1152,128]{1,0:T(8,128)(2,1)S(1)}, u32[]{:S(2)}, u32[]{:S(2)}) %collective-permute-start.10) | collective-permute-done | bytes 294944 | tf_op jit(solution)/shard_map/ppermute | solution.py:456
  47.1 1.3 %final.1 = (f32[9,128,128]{2,1,0:T(8,128)}, f32[9,128,128]{2,1,0:T(8,128)}, f32[1,128]{1,0:T(1,128)}) custom-call(bf16[1152,128]{1,0:T(8,128)(2,1)S(1)} %place.3.held, bf16[1152,128]{1,0:T(8,128)(2,1)S(1)} %collective-permute-done.10.got, f32[8,128]{1,0:T(8,128)S(1)} %get-tuple-element.58.bias_in), custom_call_target="tpu_custom_call" | custom-call | bytes 1769472 | tf_op jit(solution)/shard_map/final/pallas_call | solution.py:36
  (27 shorter events, 1.0 us)
Async XLA Ops:
  0.6 6.4 %copy-start.1 = (bf16[64,64,128]{2,1,0:T(8,128)(2,1)S(1)}, bf16[64,64,128]{2,1,0:T(8,128)(2,1)}, u32[]{:S(2)}) copy-start(bf16[64,64,128]{2,1,0:T(8,128)(2,1)} %tile.2) | copy-start | bytes 3145732
  1.9 8.0 %copy-start = (bf16[64,64,128]{2,1,0:T(8,128)(2,1)S(1)}, bf16[64,64,128]{2,1,0:T(8,128)(2,1)}, u32[]{:S(2)}) copy-start(bf16[64,64,128]{2,1,0:T(8,128)(2,1)} %cot.3) | copy-start | bytes 3145732
  1.9 6.6 %collective-permute-start = (bf16[2,64,128]{2,1,0:T(8,128)(2,1)S(1)}, bf16[2,64,128]{2,1,0:T(8,128)(2,1)S(1)}, u32[]{:S(2)}, u32[]{:S(2)}) collective-permute-start(bf16[2,64,128]{2,1,0:T(8,128)(2,1)S(1)} %get-tuple-element.33), channel_id=1, source_target_pairs={{0,2},{2,4},{4,6},{6,8},{8,10},{10,12},{12,14},{1,3},{3,5},{5,7},{... | collective-permute-start | bytes 98312 | tf_op jit(solution)/shard_map/ppermute | solution.py:301
  7.4 3.4 %copy-start.2 = (bf16[3,3,128,128]{3,2,1,0:T(8,128)(2,1)S(1)}, bf16[3,3,128,128]{3,2,1,0:T(8,128)(2,1)}, u32[]{:S(2)}) copy-start(bf16[3,3,128,128]{3,2,1,0:T(8,128)(2,1)} %down_weight.3) | copy-start | bytes 884740
  7.4 3.4 %copy-start.3 = (bf16[3,3,128,128]{3,2,1,0:T(8,128)(2,1)S(1)}, bf16[3,3,128,128]{3,2,1,0:T(8,128)(2,1)}, u32[]{:S(2)}) copy-start(bf16[3,3,128,128]{3,2,1,0:T(8,128)(2,1)} %up_weight.1) | copy-start | bytes 884740
  7.4 3.4 %copy-start.4 = (f32[128]{0:T(128)S(1)}, f32[128]{0:T(128)}, u32[]{:S(2)}) copy-start(f32[128]{0:T(128)} %down_bias.1) | copy-start | bytes 1540
  8.6 2.1 %collective-permute-start.1 = (bf16[2,72,128]{2,1,0:T(8,128)(2,1)S(1)}, bf16[2,72,128]{2,1,0:T(8,128)(2,1)S(1)}, u32[]{:S(2)}, u32[]{:S(2)}) collective-permute-start(bf16[2,72,128]{2,1,0:T(8,128)(2,1)S(1)} %maximum_maximum_fusion), channel_id=1, source_target_pairs={{0,1},{2,3},{4,5},{6,7},{8,9},{10,11},{12,13},{14,15},{16,17},{18,... | collective-permute-start | bytes 110600 | tf_op jit(solution)/shard_map/ppermute | solution.py:301
  13.5 3.5 %collective-permute-start.2 = (bf16[1168,128]{1,0:T(8,128)(2,1)S(1)}, bf16[1168,128]{1,0:T(8,128)(2,1)S(1)}, u32[]{:S(2)}, u32[]{:S(2)}) collective-permute-start(bf16[1168,128]{1,0:T(8,128)(2,1)S(1)} %get-tuple-element.38), channel_id=1, source_target_pairs={{0,1},{1,0},{2,3},{3,2},{4,5},{5,4},{6,7},{7,6},{8,9},{9,8},{10,11... | collective-permute-start | bytes 897032 | tf_op jit(solution)/shard_map/ppermute | solution.py:378
  13.9 3.1 %collective-permute-start.3 = (bf16[32,128]{1,0:T(8,128)(2,1)S(1)}, bf16[32,128]{1,0:T(8,128)(2,1)S(1)}, u32[]{:S(2)}, u32[]{:S(2)}) collective-permute-start(bf16[32,128]{1,0:T(8,128)(2,1)S(1)} %get-tuple-element.39), channel_id=1, source_target_pairs={{1,0},{3,2},{5,4},{7,6},{9,8},{11,10},{13,12},{15,14},{17,16},{19,... | collective-permute-start | bytes 24584 | tf_op jit(solution)/shard_map/ppermute | solution.py:301
  17.0 8.0 %collective-permute-start.4 = (bf16[592,128]{1,0:T(8,128)(2,1)S(1)}, bf16[592,128]{1,0:T(8,128)(2,1)S(1)}, u32[]{:S(2)}, u32[]{:S(2)}) collective-permute-start(bf16[592,128]{1,0:T(8,128)(2,1)S(1)} %get-tuple-element.43), channel_id=1, source_target_pairs={{0,2},{1,5},{2,0},{3,7},{4,6},{5,1},{6,4},{7,3},{8,10},{9,13},{10,... | collective-permute-start | bytes 454664 | tf_op jit(solution)/shard_map/ppermute | solution.py:311
  19.5 5.6 %collective-permute-start.5 = (bf16[40,128]{1,0:T(8,128)(2,1)S(1)}, bf16[40,128]{1,0:T(8,128)(2,1)S(1)}, u32[]{:S(2)}, u32[]{:S(2)}) collective-permute-start(bf16[40,128]{1,0:T(8,128)(2,1)S(1)} %maximum_maximum_fusion.1), channel_id=1, source_target_pairs={{2,0},{4,2},{6,4},{8,6},{10,8},{12,10},{14,12},{3,1},{5,3},{7,5},{... | collective-permute-start | bytes 30728 | tf_op jit(solution)/shard_map/ppermute | solution.py:301
  25.1 4.5 %collective-permute-start.6 = (bf16[304,128]{1,0:T(8,128)(2,1)S(1)}, bf16[304,128]{1,0:T(8,128)(2,1)S(1)}, u32[]{:S(2)}, u32[]{:S(2)}) collective-permute-start(bf16[304,128]{1,0:T(8,128)(2,1)S(1)} %get-tuple-element.49), channel_id=1, source_target_pairs={{0,4},{1,3},{2,6},{3,1},{4,0},{5,7},{6,2},{7,5},{8,12},{9,11},{10,... | collective-permute-start | bytes 233480 | tf_op jit(solution)/shard_map/ppermute | solution.py:311
  29.6 5.4 %collective-permute-start.7 = (bf16[304,128]{1,0:T(8,128)(2,1)S(1)}, bf16[304,128]{1,0:T(8,128)(2,1)S(1)}, u32[]{:S(2)}, u32[]{:S(2)}) collective-permute-start(bf16[304,128]{1,0:T(8,128)(2,1)S(1)} %get-tuple-element.51.held), channel_id=1, source_target_pairs={{0,8},{1,9},{2,10},{3,11},{4,12},{5,13},{6,14},{7,15},{8,0},{9,1},... | collective-permute-start | bytes 233480 | tf_op jit(solution)/shard_map/ppermute | solution.py:311
  35.0 4.4 %collective-permute-start.8 = (bf16[288,128]{1,0:T(8,128)(2,1)S(1)}, bf16[288,128]{1,0:T(8,128)(2,1)S(1)}, u32[]{:S(2)}, u32[]{:S(2)}) collective-permute-start(bf16[288,128]{1,0:T(8,128)(2,1)S(1)} %get-tuple-element.57.held), channel_id=1, source_target_pairs={{0,4},{1,3},{2,6},{3,1},{4,0},{5,7},{6,2},{7,5},{8,12},{9,11},{10,... | collective-permute-start | bytes 221192 | tf_op jit(solution)/shard_map/ppermute | solution.py:311
  39.4 6.0 %collective-permute-start.9 = (bf16[576,128]{1,0:T(8,128)(2,1)S(1)}, bf16[576,128]{1,0:T(8,128)(2,1)S(1)}, u32[]{:S(2)}, u32[]{:S(2)}) collective-permute-start(bf16[576,128]{1,0:T(8,128)(2,1)S(1)} %place.2.held), channel_id=1, source_target_pairs={{0,2},{1,5},{2,0},{3,7},{4,6},{5,1},{6,4},{7,3},{8,10},{9,13},{10,... | collective-permute-start | bytes 442376 | tf_op jit(solution)/shard_map/ppermute | solution.py:311
  45.5 1.6 %collective-permute-start.10 = (bf16[1152,128]{1,0:T(8,128)(2,1)S(1)}, bf16[1152,128]{1,0:T(8,128)(2,1)S(1)}, u32[]{:S(2)}, u32[]{:S(2)}) collective-permute-start(bf16[1152,128]{1,0:T(8,128)(2,1)S(1)} %place.3.held), channel_id=1, source_target_pairs={{0,1},{1,0},{2,3},{3,2},{4,5},{5,4},{6,7},{7,6},{8,9},{9,8},{10,11... | collective-permute-start | bytes 884744 | tf_op jit(solution)/shard_map/ppermute | solution.py:456

commit v3 on v2

--- a/solution.py
+++ b/solution.py
@@ -46,7 +46,7 @@
     return jax.ShapeDtypeStruct(shape, dtype)
 
 
-def edge_body(feat, cot, rows, cols, strip, wide_strip, sems):
+def edge_body(feat, cot, rows, cols, corner, strip, wide_strip, sems):
     tile_rows, tile_cols, _ = feat.shape
     copies = []
     for which, ref in enumerate((feat, cot)):
@@ -65,6 +65,7 @@
     for which in range(2):
         wide_strip[...] = strip[which].astype(F32).reshape(wide_strip.shape)
         cols[which] = wide_strip[pl.ds(15, tile_rows, stride=16), :].astype(BF16)
+        corner[which] = wide_strip[tile_rows * 16 - 8 :, :].astype(BF16)
 
 
 def phase_body(tile, out, wide):
@@ -75,12 +76,18 @@
         out[col_off] = wide[:, pl.ds(7 + col_off, cols // 2, stride=2), :].astype(BF16)
 
 
-def fill_patches(phases, top, left, patch, line, column):
+def if_any(there, value):
+    return jnp.where(there, value, jnp.zeros_like(value))
+
+
+def fill_patches(phases, top, left, corner, patch, line, column):
     _, rows, half_cols, channels = phases.shape
     half_rows = rows // 2
-    line[0:8, :] = jnp.broadcast_to(left[0:1, :].astype(F32), (8, channels))
-    line[8:, :] = top[...].astype(F32)
-    column[...] = left[...].astype(F32)
+    above = lax.axis_index("wide") > 0
+    aside = lax.axis_index("narrow") > 0
+    line[0:8, :] = if_any(above & aside, corner[...].astype(F32))
+    line[8:, :] = if_any(above, top[...].astype(F32))
+    column[...] = if_any(aside, left[...].astype(F32))
     first = lax.broadcasted_iota(jnp.int32, (half_rows, half_cols, channels), 1) == 0
     paired = phases.reshape(3, half_rows, 2, half_cols, channels)
     for col_off in range(3):
@@ -90,7 +97,7 @@
         if col_off == 0:
             rim = [
                 column[pl.ds(off, half_rows, stride=2), :].reshape(half_rows, 1, channels)
-                for off in (1, 2)
+                for off in (0, 1)
             ]
             even = jnp.where(first, rim[0], even).astype(BF16)
             odd = jnp.where(first, rim[1], odd).astype(BF16)
@@ -101,7 +108,7 @@
 
 
 def main_body(
-    feat_phases, cot_phases, top, left, down_weight, down_bias, up_weight,
+    feat_phases, cot_phases, top, left, corner, down_weight, down_bias, up_weight,
     grads, first_row, first_col, mine, other, bias_part,
     feat_patch, cot_patch, up_mat, act, wide_grads, line, column,
 ):
@@ -109,8 +116,8 @@
     half_rows = rows // 2
     pixels = half_rows * half_cols
     taps = 9 * channels
-    fill_patches(feat_phases, top.at[0], left.at[0], feat_patch, line, column)
-    fill_patches(cot_phases, top.at[1], left.at[1], cot_patch, line, column)
+    fill_patches(feat_phases, top.at[0], left.at[0], corner.at[0], feat_patch, line, column)
+    fill_patches(cot_phases, top.at[1], left.at[1], corner.at[1], cot_patch, line, column)
     for tap in range(9):
         up_mat[:, pl.ds(tap * channels, channels)] = up_weight[tap // 3, tap % 3]
     down_mat = down_weight[...].reshape(taps, channels)
@@ -174,10 +181,7 @@
 
 
 def bit_of(position):
-    low, high = position
-    at = lax.axis_index("wide")
-    shift = jnp.where(lax.axis_index("narrow") == 0, low, high)
-    return lax.rem(lax.shift_right_logical(at, shift.astype(at.dtype)), 2)
+    return lax.rem(lax.shift_right_logical(lax.axis_index("wide"), jnp.int32(position)), 2)
 
 
 def joined_bias(bias_in, got, size, out, sent, at):
@@ -189,34 +193,54 @@
         put_side(sent, at, coarse, fine)
 
 
-def halve_body(position, held, got, bias_in, keep, send, bias_out):
-    size = held.shape[0]
+def split(position, held, got, base, size, keep, send):
     half = size // 2
     bit = bit_of(position)
-    near = pl.ds(pl.multiple_of(bit * half, 16), half)
-    away = pl.ds(pl.multiple_of((1 - bit) * half, 16), half)
+    near = pl.ds(pl.multiple_of(base + bit * half, 16), half)
+    away = pl.ds(pl.multiple_of(base + (1 - bit) * half, 16), half)
     send[0:half, :] = (held[away, :] + got[away, :].astype(F32)).astype(BF16)
     keep[...] = held[near, :] + got[near, :].astype(F32)
-    joined_bias(bias_in, got, size, bias_out, send, half)
-
-
-def whole_body(held, got, bias_in, send, bias_out):
-    size = got.shape[0] - SIDE
+
+
+def first_body(positions, held, got, bias_in, keep_a, send_a, keep_b, send_b, bias_out):
+    size = held.shape[0] // 2
+    split(positions[0], held, got, 0, size, keep_a, send_a)
+    split(positions[1], held, got, size, size, keep_b, send_b)
+    joined_bias(bias_in, got, 2 * size, bias_out, send_a, size // 2)
+
+
+def halve_body(position, held, got, *rest):
+    size = held.shape[0]
+    if len(rest) == 4:
+        bias_in, keep, send, bias_out = rest
+        joined_bias(bias_in, got, size, bias_out, send, size // 2)
+    else:
+        keep, send = rest
+    split(position, held, got, 0, size, keep, send)
+
+
+def whole_body(size, held, got, *rest):
+    send = rest[-2] if len(rest) == 3 else rest[-1]
     send[0:size, :] = (held[0:size, :].astype(F32) + got[0:size, :].astype(F32)).astype(BF16)
-    joined_bias(bias_in, got, size, bias_out, send, size)
-
-
-def last_body(held, got, bias_in, total, bias_out):
-    size = got.shape[0] - SIDE
-    total[...] = (held[0:size, :].astype(F32) + got[0:size, :].astype(F32)).astype(BF16)
-    joined_bias(bias_in, got, size, bias_out, None, 0)
+    if len(rest) == 3:
+        bias_in, _, bias_out = rest
+        joined_bias(bias_in, got, size, bias_out, send if send.shape[0] > size else None, size)
 
 
 def place_body(position, held, got, out):
+    place(position, held, got, out, 0)
+
+
+def place(position, held, got, out, base):
     size = held.shape[0]
     bit = bit_of(position)
-    out[pl.ds(pl.multiple_of(bit * size, 16), size), :] = held[...]
-    out[pl.ds(pl.multiple_of((1 - bit) * size, 16), size), :] = got[...]
+    out[pl.ds(pl.multiple_of(base + bit * size, 16), size), :] = held[...]
+    out[pl.ds(pl.multiple_of(base + (1 - bit) * size, 16), size), :] = got[...]
+
+
+def both_body(positions, held_a, got_a, held_b, got_b, out):
+    place(positions[0], held_a, got_a, out, 0)
+    place(positions[1], held_b, got_b, out, 2 * held_a.shape[0])
 
 
 def final_body(held, got, bias_in, down, up, bias_out):
@@ -258,10 +282,12 @@
         half_rows, half_cols, channels
     )
     last = lax.broadcasted_iota(jnp.int32, (half_rows, 8, channels), 1) == 0
-    rim = right[...].astype(F32).reshape(half_rows, 1, channels)
+    aside = lax.axis_index("narrow") < lax.axis_size("narrow") - 1
+    under = lax.axis_index("wide") < lax.axis_size("wide") - 1
+    rim = if_any(aside, right[...].astype(F32)).reshape(half_rows, 1, channels)
     wide[0:half_rows, half_cols:, :] = jnp.where(last, rim, 0.0)
-    low = below[...].astype(F32)
-    wide[half_rows, :, :] = low
+    wide[half_rows, 0:half_cols, :] = if_any(under, below[0:half_cols, :].astype(F32))
+    wide[half_rows, half_cols:, :] = if_any(under & aside, below[half_cols:, :].astype(F32))
     pairs[:, :, 0:channels] = wide[:, 0:half_cols, :].astype(BF16)
     pairs[:, :, channels:] = wide[:, 1 : half_cols + 1, :].astype(BF16)
     zero = jnp.zeros((channels, channels), BF16)
@@ -279,9 +305,9 @@
     for start in range(0, half_rows, step):
         count = step * half_cols
         here = pairs[start : start + step].reshape(count, 2 * channels)
-        under = pairs[start + 1 : start + 1 + step].reshape(count, 2 * channels)
+        lower = pairs[start + 1 : start + 1 + step].reshape(count, 2 * channels)
         near = lax.dot_general(here, near_mat[...], dims, preferred_element_type=F32)
-        far = lax.dot_general(under, low_mat[...], dims, preferred_element_type=F32)
+        far = lax.dot_general(lower, low_mat[...], dims, preferred_element_type=F32)
         shape = (step, half_cols, channels)
         for row_par in range(2):
             for col_par in range(2):
@@ -295,20 +321,24 @@
         out[span] = total.astype(BF16)
 
 
-def passed_along(value, axis, steps):
+def turned(value, axis, steps):
     count = lax.axis_size(axis)
-    first, last = (max(0, -steps), min(count, count - steps))
-    return lax.ppermute(value, axis, [(source, source + steps) for source in range(first, last)])
+    return lax.ppermute(value, axis, [(at, (at + steps) % count) for at in range(count)])
+
+
+def turned_both(value):
+    count, cores = lax.axis_size("wide"), lax.axis_size("narrow")
+    pairs = [
+        (at * cores + core, (at + 1) % count * cores + (core + 1) % cores)
+        for at in range(count)
+        for core in range(cores)
+    ]
+    return lax.ppermute(value, ("wide", "narrow"), pairs)
 
 
 def traded(value, position):
-    count, cores = lax.axis_size("wide"), lax.axis_size("narrow")
-    pairs = []
-    for at in range(count):
-        for core in range(cores):
-            mate = at ^ (1 << position[0 if core == 0 else 1])
-            pairs.append((at * cores + core, mate * cores + core))
-    return lax.ppermute(value, ("wide", "narrow"), pairs)
+    count = lax.axis_size("wide")
+    return lax.ppermute(value, "wide", [(at, at ^ (1 << position)) for at in range(count)])
 
 
 def shards(features, cotangent, down_weight, down_bias, up_weight):
@@ -316,9 +346,13 @@
     half_rows, half_cols = tile_rows // 2, tile_cols // 2
     pixels = half_rows * half_cols
     taps = 9 * channels
-    rows, cols = call(
+    rows, cols, corner = call(
         edge_body,
-        (vm((2, tile_cols, channels), BF16), vm((2, tile_rows, channels), BF16)),
+        (
+            vm((2, tile_cols, channels), BF16),
+            vm((2, tile_rows, channels), BF16),
+            vm((2, 8, channels), BF16),
+        ),
         scratch=[
             pltpu.VMEM((2, tile_rows, 16, channels), BF16),
             pltpu.VMEM((tile_rows * 16, channels), F32),
@@ -330,7 +364,9 @@
         far=(0, 1),
         room=8,
     )(features, cotangent)
-    from_above = passed_along(rows, "wide", 1)
+    from_above = turned(rows, "wide", 1)
+    from_corner = turned_both(corner)
+    from_left = turned(cols, "narrow", 1)
     phases = call(
         phase_body,
         vm((3, tile_rows, half_cols, channels), BF16),
@@ -342,12 +378,10 @@
         room=16,
     )
     feat_phases = phases(features)
-    from_above, feat_phases = lax.optimization_barrier((from_above, feat_phases))
     cot_phases = phases(cotangent)
-    cols = jnp.concatenate(
-        [from_above[:, -1:], cols, jnp.zeros((2, 7, channels), BF16)], axis=1
-    )
-    from_left = passed_along(cols, "narrow", 1)
+    from_above, from_corner, from_left, feat_phases, cot_phases = lax.optimization_barrier(
+        (from_above, from_corner, from_left, feat_phases, cot_phases)
+    )
     grads, first_row, first_col, mine, other, bias_sum = call(
         main_body,
         (
@@ -365,44 +399,63 @@
             pltpu.VMEM((pixels, channels), BF16),
             pltpu.VMEM((pixels, channels), F32),
             pltpu.VMEM((tile_cols + 8, channels), F32),
-            pltpu.VMEM((tile_rows + 8, channels), F32),
+            pltpu.VMEM((tile_rows, channels), F32),
         ],
-        n_in=7,
+        n_in=8,
         flops=8 * pixels * taps * channels,
         nbytes=6 << 20,
         name="main",
+        near=(0, 1, 2, 3, 4),
         room=32,
-        near=(0, 1, 2, 3),
-    )(feat_phases, cot_phases, from_above, from_left, down_weight, down_bias, up_weight)
-
-    got = lax.ppermute(other, "narrow", [(0, 1), (1, 0)])
-
-    from_right = passed_along(first_col, "narrow", -1)
+    )(
+        feat_phases, cot_phases, from_above, from_left, from_corner,
+        down_weight, down_bias, up_weight,
+    )
+
+    got = turned(other, "narrow", 1)
+    from_right = turned(first_col, "narrow", -1)
     got, from_right = lax.optimization_barrier((got, from_right))
-    low_row = jnp.concatenate(
-        [first_row, from_right[:1], jnp.zeros((7, channels), BF16)], axis=0
-    )
-    from_below = passed_along(low_row, "wide", -1)
-    count = lax.axis_size("wide")
-    bits = count.bit_length() - 1
-    order = [(bit, bit) for bit in range(bits)]
-    if bits > 1:
-        order[0], order[1] = (0, 1), (1, 0)
-    halvings = min(bits - 1, 3)
-    held = mine
-    for step in range(halvings):
-        half = held.shape[0] // 2
-        held, send, bias_sum = call(
-            functools.partial(halve_body, order[step]),
+    from_below = turned(jnp.concatenate([first_row, from_right[:8]], axis=0), "wide", -1)
+
+    bits = lax.axis_size("wide").bit_length() - 1
+    order_a = list(range(bits))
+    order_b = order_a[1::-1] + order_a[2:]
+    halvings = 1 if bits <= 3 else 2
+    half = taps // 4
+    held_a, send_a, held_b, send_b, bias_sum = call(
+        functools.partial(first_body, (order_a[0], order_b[0])),
+        (
+            vm((half, channels), F32),
+            vm((half + SIDE, channels), BF16),
+            vm((half, channels), F32),
+            vm((half, channels), BF16),
+            vm((8, channels), F32),
+        ),
+        n_in=3,
+        nbytes=taps * channels * 6,
+        name="first",
+        near=(0, 1, 2),
+    )(mine, got, bias_sum)
+    got_a = traded(send_a, order_a[0])
+    got_b = traded(send_b, order_b[0])
+    for step in range(1, halvings):
+        half //= 2
+        held_a, send_a, bias_sum = call(
+            functools.partial(halve_body, order_a[step]),
             (vm((half, channels), F32), vm((half + SIDE, channels), BF16), vm((8, channels), F32)),
             n_in=3,
-            nbytes=held.size * 4,
             name="halve",
             near=(0, 1, 2),
-        )(held, got, bias_sum)
-        got = traded(send, order[step])
-        if step == 0:
-            got, from_below = lax.optimization_barrier((got, from_below))
+        )(held_a, got_a, bias_sum)
+        held_b, send_b = call(
+            functools.partial(halve_body, order_b[step]),
+            (vm((half, channels), F32), vm((half, channels), BF16)),
+            n_in=2,
+            name="halve",
+            near=(0, 1),
+        )(held_b, got_b)
+        got_a = traded(send_a, order_a[step])
+        got_b = traded(send_b, order_b[step])
     feature_grad = call(
         feature_body,
         sds((tile_rows, tile_cols, channels), BF16),
@@ -417,43 +470,62 @@
         flops=2 * pixels * 6 * 2 * channels * channels,
         nbytes=3 << 20,
         name="feature",
+        near=(0, 1, 2),
         room=16,
-        near=(0, 1, 2),
     )(grads, from_right, from_below, cotangent, down_weight)
-    for step in range(halvings, bits):
-        size = held.shape[0] if step == halvings else held.shape[0] - SIDE
-        send, bias_sum = call(
-            whole_body,
-            (vm((size + SIDE, channels), BF16), vm((8, channels), F32)),
+    for step in range(halvings, bits + 1):
+        side = SIDE if step < bits else 0
+        held_a, bias_sum = call(
+            functools.partial(whole_body, half),
+            (vm((half + side, channels), BF16), vm((8, channels), F32)),
             n_in=3,
-            nbytes=held.size * 4,
+            nbytes=half * channels * 8,
             name="whole",
             near=(0, 1, 2),
-        )(held, got, bias_sum)
-        got = traded(send, order[step])
-        if step == bits - 1:
-            got, feature_grad = lax.optimization_barrier((got, feature_grad))
-        held = send
-    size = got.shape[0] - SIDE
-    block, bias_sum = call(
-        last_body,
-        (vm((size, channels), BF16), vm((8, channels), F32)),
-        n_in=3,
-        nbytes=size * channels * 4,
-        name="last",
-            near=(0, 1, 2),
-    )(held, got, bias_sum)
+        )(held_a, got_a, bias_sum)
+        held_b = call(
+            functools.partial(whole_body, half),
+            vm((half, channels), BF16),
+            n_in=2,
+            nbytes=half * channels * 8,
+            name="whole",
+            near=(0, 1),
+        )(held_b, got_b)
+        if step < bits:
+            got_a = traded(held_a, order_a[step])
+            got_b = traded(held_b, order_b[step])
+            if step == halvings:
+                got_a, from_below = lax.optimization_barrier((got_a, from_below))
+            if step == bits - 1:
+                got_a, feature_grad = lax.optimization_barrier((got_a, feature_grad))
     for step in reversed(range(halvings)):
-        got = traded(block, order[step])
-        block = call(
-            functools.partial(place_body, order[step]),
-            vm((2 * block.shape[0], channels), BF16),
-            n_in=2,
-            nbytes=block.size * 4,
-            name="place",
-            near=(0, 1),
-        )(block, got)
-    got = lax.ppermute(block, "narrow", [(0, 1), (1, 0)])
+        got_a = traded(held_a, order_a[step])
+        got_b = traded(held_b, order_b[step])
+        if step:
+            half *= 2
+            held_a = call(
+                functools.partial(place_body, order_a[step]),
+                vm((half, channels), BF16),
+                n_in=2,
+                name="place",
+                near=(0, 1),
+            )(held_a, got_a)
+            held_b = call(
+                functools.partial(place_body, order_b[step]),
+                vm((half, channels), BF16),
+                n_in=2,
+                name="place",
+                near=(0, 1),
+            )(held_b, got_b)
+    block = call(
+        functools.partial(both_body, (order_a[0], order_b[0])),
+        vm((taps, channels), BF16),
+        n_in=4,
+        nbytes=taps * channels * 4,
+        name="both",
+        near=(0, 1, 2, 3),
+    )(held_a, got_a, held_b, got_b)
+    got = turned(block, "narrow", 1)
     down, up, bias_grad = call(
         final_body,
         (
@@ -464,8 +536,8 @@
         n_in=3,
         nbytes=12 * taps * channels,
         name="final",
-            room=8,
-            near=(0, 1, 2),
+        near=(0, 1, 2),
+        room=8,
     )(block, got, bias_sum)
     shape = (3, 3, channels, channels)
     return (feature_grad, down.reshape(shape), up.reshape(shape), bias_grad.reshape(channels))

time: 48.6 us -> 43.3 us (0.89)
  starting transfers between devices: 20.5 us -> 16.2 us
  waiting for transfers between devices: 18.8 us -> 18.1 us
    ppermute x11 -> x15, starting transfers between devices: 20.5 us -> 16.2 us  [the longest x8 8.84 us: traded(): lax.ppermute(value, 'wide', [(at, at ^ 1 << position) for at in range(cou...]
    ppermute x11 -> x15, waiting for transfers between devices: 18.8 us -> 18.1 us  [the longest x8 10.1 us: traded(): lax.ppermute(value, 'wide', [(at, at ^ 1 << position) for at in range(cou...]
    pallas_call x12 -> x14, Pallas kernels: 7.94 us -> 7.97 us  [run(): return kernel(*placed)]
  transfers between devices with their start and end apart: 11 -> 15, of which waited for: 9 -> 10; matrix products, arithmetic and copies ran while one was open for 0% -> 0% of each run, Pallas kernels for 5% -> 6%
where the time goes in v3:
time: 43.3 us; the launch traced here: 43.1 us
  waiting for transfers between devices  18.1 us (42%)
  starting transfers between devices  16.2 us (37%)
  Pallas kernels  7.97 us (18%)
  between operations  0.82 us (2%)
    ppermute x8, waiting for transfers between devices, traded(): lax.ppermute(value, 'wide', [(at, at ^ 1 << position) for at in range(cou...  10.1 us
    ppermute x8, starting transfers between devices, traded(): lax.ppermute(value, 'wide', [(at, at ^ 1 << position) for at in range(cou...  8.84 us
    pallas_call x14, Pallas kernels, run(): return kernel(*placed)  7.97 us
    ppermute x6, waiting for transfers between devices, turned(): lax.ppermute(value, axis, [(at, (at + steps) % count) for at in range(cou...  6.41 us
    ppermute x6, starting transfers between devices, turned(): lax.ppermute(value, axis, [(at, (at + steps) % count) for at in range(cou...  4.9 us
    ppermute x1, starting transfers between devices, turned_both(): return lax.ppermute(value, ('wide', 'narrow'), pairs)  2.46 us
    ppermute x1, waiting for transfers between devices, turned_both(): return lax.ppermute(value, ('wide', 'narrow'), pairs)  1.64 us
  transfers between devices with their start and end apart: 15, of which 10 were waited for; matrix products, arithmetic and copies ran while one was open for 0% of the time, Pallas kernels for 6%

profile of v3, /device:TPU:0, one launch (start us, length us, event | category | flops | bytes accessed | tf_op | source)
XLA Modules:
  0.0 43.1 jit_solution(2416155534247429535)
XLA Ops:
  0.6 1.3 %edges.1 = (bf16[2,64,128]{2,1,0:T(8,128)(2,1)S(1)}, bf16[2,64,128]{2,1,0:T(8,128)(2,1)S(1)}, bf16[2,8,128]{2,1,0:T(8,128)(2,1)S(1)}) custom-call(bf16[64,64,128]{2,1,0:T(8,128)(2,1)} %tile.2, bf16[64,64,128]{2,1,0:T(8,128)(2,1)} %cot.3), custom_call_target="tpu_custom_call" | custom-call | bytes 524288 | tf_op jit(solution)/shard_map/edges/pallas_call | solution.py:36
  1.9 2.5 %collective-permute-start.1 = (bf16[2,8,128]{2,1,0:T(8,128)(2,1)S(1)}, bf16[2,8,128]{2,1,0:T(8,128)(2,1)S(1)}, u32[]{:S(2)}, u32[]{:S(2)}) collective-permute-start(bf16[2,8,128]{2,1,0:T(8,128)(2,1)S(1)} %get-tuple-element.38), channel_id=1, source_target_pairs={{0,3},{1,2},{2,5},{3,4},{4,7},{5,6},{6,9},{7,8},{8,11},{9,10},{10,... | collective-permute-start | bytes 12296 | tf_op jit(solution)/shard_map/ppermute | solution.py:336
  4.4 1.5 %collective-permute-start = (bf16[2,64,128]{2,1,0:T(8,128)(2,1)S(1)}, bf16[2,64,128]{2,1,0:T(8,128)(2,1)S(1)}, u32[]{:S(2)}, u32[]{:S(2)}) collective-permute-start(bf16[2,64,128]{2,1,0:T(8,128)(2,1)S(1)} %get-tuple-element.37), channel_id=1, source_target_pairs={{0,2},{2,4},{4,6},{6,8},{8,10},{10,12},{12,14},{14,0},{1,3},{3,5},... | collective-permute-start | bytes 98312 | tf_op jit(solution)/shard_map/ppermute | solution.py:326
  5.9 0.4 collective-permute-start.2
  7.1 1.6 %collective-permute-done.1.corner = bf16[2,8,128]{2,1,0:T(8,128)(2,1)S(1)} collective-permute-done((bf16[2,8,128]{2,1,0:T(8,128)(2,1)S(1)}, bf16[2,8,128]{2,1,0:T(8,128)(2,1)S(1)}, u32[]{:S(2)}, u32[]{:S(2)}) %collective-permute-start.1) | collective-permute-done | bytes 4128 | tf_op jit(solution)/shard_map/ppermute | solution.py:336
  8.7 2.3 %collective-permute-done.top = bf16[2,64,128]{2,1,0:T(8,128)(2,1)S(1)} collective-permute-done((bf16[2,64,128]{2,1,0:T(8,128)(2,1)S(1)}, bf16[2,64,128]{2,1,0:T(8,128)(2,1)S(1)}, u32[]{:S(2)}, u32[]{:S(2)}) %collective-permute-start) | collective-permute-done | bytes 32800 | tf_op jit(solution)/shard_map/ppermute | solution.py:326
  11.1 2.7 %main.1 = (bf16[1024,128]{1,0:T(8,128)(2,1)S(1)}, bf16[32,128]{1,0:T(8,128)(2,1)S(1)}, bf16[32,128]{1,0:T(8,128)(2,1)S(1)}, f32[1152,128]{1,0:T(8,128)S(1)}, bf1...) custom-call(bf16[3,64,32,128]{3,2,1,0:T(8,128)(2,1)S(1)} %phases.2.feat_phases, ...), custom_call_target="tpu_custom_call" | custom-call | flops 1207959552 | bytes 6291456 | tf_op jit(solution)/shard_map/main/pallas_call | solution.py:36
  13.9 0.5 %collective-permute-start.4 = (bf16[32,128]{1,0:T(8,128)(2,1)S(1)}, bf16[32,128]{1,0:T(8,128)(2,1)S(1)}, u32[]{:S(2)}, u32[]{:S(2)}) collective-permute-start(bf16[32,128]{1,0:T(8,128)(2,1)S(1)} %get-tuple-element.47), channel_id=1, source_target_pairs={{0,1},{1,0},{2,3},{3,2},{4,5},{5,4},{6,7},{7,6},{8,9},{9,8},{10,11... | collective-permute-start | bytes 24584 | tf_op jit(solution)/shard_map/ppermute | solution.py:326
  14.4 1.1 %collective-permute-done.4.right = bf16[32,128]{1,0:T(8,128)(2,1)S(1)} collective-permute-done((bf16[32,128]{1,0:T(8,128)(2,1)S(1)}, bf16[32,128]{1,0:T(8,128)(2,1)S(1)}, u32[]{:S(2)}, u32[]{:S(2)}) %collective-permute-start.4) | collective-permute-done | bytes 8224 | tf_op jit(solution)/shard_map/ppermute | solution.py:326
  15.6 0.4 collective-permute-start.10
  16.0 4.0 %collective-permute-done.10.got = bf16[288,128]{1,0:T(8,128)(2,1)S(1)} collective-permute-done((bf16[288,128]{1,0:T(8,128)(2,1)S(1)}, bf16[288,128]{1,0:T(8,128)(2,1)S(1)}, u32[]{:S(2)}, u32[]{:S(2)}) %collective-permute-start.10) | collective-permute-done | bytes 73760 | tf_op jit(solution)/shard_map/ppermute | solution.py:341
  20.1 2.0 %collective-permute-start.11 = (bf16[288,128]{1,0:T(8,128)(2,1)S(1)}, bf16[288,128]{1,0:T(8,128)(2,1)S(1)}, u32[]{:S(2)}, u32[]{:S(2)}) collective-permute-start(bf16[288,128]{1,0:T(8,128)(2,1)S(1)} %whole.9.held), channel_id=1, source_target_pairs={{0,2},{2,0},{4,6},{6,4},{8,10},{10,8},{12,14},{14,12},{1,3},{3,1},... | collective-permute-start | bytes 221192 | tf_op jit(solution)/shard_map/ppermute | solution.py:341
  22.2 2.3 %collective-permute-start.7 = (bf16[40,128]{1,0:T(8,128)(2,1)S(1)}, bf16[40,128]{1,0:T(8,128)(2,1)S(1)}, u32[]{:S(2)}, u32[]{:S(2)}) collective-permute-start(bf16[40,128]{1,0:T(8,128)(2,1)S(1)} %pad_maximum_fusion), channel_id=1, source_target_pairs={{0,14},{2,0},{4,2},{6,4},{8,6},{10,8},{12,10},{14,12},{1,15},{3,1}... | collective-permute-start | bytes 30728 | tf_op jit(solution)/shard_map/ppermute | solution.py:326
  24.5 1.4 %collective-permute-done.7.below = bf16[40,128]{1,0:T(8,128)(2,1)S(1)} collective-permute-done((bf16[40,128]{1,0:T(8,128)(2,1)S(1)}, bf16[40,128]{1,0:T(8,128)(2,1)S(1)}, u32[]{:S(2)}, u32[]{:S(2)}) %collective-permute-start.7) | collective-permute-done | bytes 10272 | tf_op jit(solution)/shard_map/ppermute | solution.py:326
  25.9 0.6 %collective-permute-done.6.got = bf16[304,128]{1,0:T(8,128)(2,1)S(1)} collective-permute-done((bf16[304,128]{1,0:T(8,128)(2,1)S(1)}, bf16[304,128]{1,0:T(8,128)(2,1)S(1)}, u32[]{:S(2)}, u32[]{:S(2)}) %collective-permute-start.6) | collective-permute-done | bytes 77856 | tf_op jit(solution)/shard_map/ppermute | solution.py:341
  26.6 1.7 %collective-permute-start.8 = (bf16[304,128]{1,0:T(8,128)(2,1)S(1)}, bf16[304,128]{1,0:T(8,128)(2,1)S(1)}, u32[]{:S(2)}, u32[]{:S(2)}) collective-permute-start(bf16[304,128]{1,0:T(8,128)(2,1)S(1)} %get-tuple-element.58.held), channel_id=1, source_target_pairs={{0,8},{2,10},{4,12},{6,14},{8,0},{10,2},{12,4},{14,6},{1,9},{3,11}... | collective-permute-start | bytes 233480 | tf_op jit(solution)/shard_map/ppermute | solution.py:341
  28.3 1.3 %collective-permute-start.12 = (bf16[288,128]{1,0:T(8,128)(2,1)S(1)}, bf16[288,128]{1,0:T(8,128)(2,1)S(1)}, u32[]{:S(2)}, u32[]{:S(2)}) collective-permute-start(bf16[288,128]{1,0:T(8,128)(2,1)S(1)} %whole.10.held), channel_id=1, source_target_pairs={{0,8},{2,10},{4,12},{6,14},{8,0},{10,2},{12,4},{14,6},{1,9},{3,11}... | collective-permute-start | bytes 221192 | tf_op jit(solution)/shard_map/ppermute | solution.py:341
  29.7 1.8 %feature.1 = bf16[64,64,128]{2,1,0:T(8,128)(2,1)} custom-call(bf16[1024,128]{1,0:T(8,128)(2,1)S(1)} %get-tuple-element.59.grads, bf16[32,128]{1,0:T(8,128)(2,1)S(1)} %collective-permute-done.4.right, bf16[40,128]{1,0:T(8,128)(2,1)S(1)} %collective-permute-done.7.below, bf16[64,64,128]{2,1,0:T(8,128)(2,1)S(1)} %copy-done, bf16[3,3,128,128]{3,2,1,0:T(8,128)(2,1)S(1)} %copy-done.2), custom_call_target="tpu_custom_call" | custom-call | flops 402653184 | bytes 3145728 | tf_op jit(solution)/shard_map/feature/pallas_call | solution.py:36
  31.5 3.1 %collective-permute-done.12.got = bf16[288,128]{1,0:T(8,128)(2,1)S(1)} collective-permute-done((bf16[288,128]{1,0:T(8,128)(2,1)S(1)}, bf16[288,128]{1,0:T(8,128)(2,1)S(1)}, u32[]{:S(2)}, u32[]{:S(2)}) %collective-permute-start.12) | collective-permute-done | bytes 73760 | tf_op jit(solution)/shard_map/ppermute | solution.py:341
  34.7 3.2 %collective-permute-start.9 = (bf16[288,128]{1,0:T(8,128)(2,1)S(1)}, bf16[288,128]{1,0:T(8,128)(2,1)S(1)}, u32[]{:S(2)}, u32[]{:S(2)}) collective-permute-start(bf16[288,128]{1,0:T(8,128)(2,1)S(1)} %get-tuple-element.63.held_a), channel_id=1, source_target_pairs={{0,2},{2,0},{4,6},{6,4},{8,10},{10,8},{12,14},{14,12},{1,3},{3,1},... | collective-permute-start | bytes 221192 | tf_op jit(solution)/shard_map/ppermute | solution.py:341
  37.9 1.1 %collective-permute-done.13.got_b = bf16[288,128]{1,0:T(8,128)(2,1)S(1)} collective-permute-done((bf16[288,128]{1,0:T(8,128)(2,1)S(1)}, bf16[288,128]{1,0:T(8,128)(2,1)S(1)}, u32[]{:S(2)}, u32[]{:S(2)}) %collective-permute-start.13) | collective-permute-done | bytes 73760 | tf_op jit(solution)/shard_map/ppermute | solution.py:341
  39.0 1.2 %collective-permute-done.9.got_a = bf16[288,128]{1,0:T(8,128)(2,1)S(1)} collective-permute-done((bf16[288,128]{1,0:T(8,128)(2,1)S(1)}, bf16[288,128]{1,0:T(8,128)(2,1)S(1)}, u32[]{:S(2)}, u32[]{:S(2)}) %collective-permute-start.9) | collective-permute-done | bytes 73760 | tf_op jit(solution)/shard_map/ppermute | solution.py:341
  40.3 1.6 %collective-permute-done.14.got = bf16[1152,128]{1,0:T(8,128)(2,1)S(1)} collective-permute-done((bf16[1152,128]{1,0:T(8,128)(2,1)S(1)}, bf16[1152,128]{1,0:T(8,128)(2,1)S(1)}, u32[]{:S(2)}, u32[]{:S(2)}) %collective-permute-start.14) | collective-permute-done | bytes 294944 | tf_op jit(solution)/shard_map/ppermute | solution.py:326
  41.9 1.3 %final.1 = (f32[9,128,128]{2,1,0:T(8,128)}, f32[9,128,128]{2,1,0:T(8,128)}, f32[1,128]{1,0:T(1,128)}) custom-call(bf16[1152,128]{1,0:T(8,128)(2,1)S(1)} %both.1.held, bf16[1152,128]{1,0:T(8,128)(2,1)S(1)} %collective-permute-done.14.got, f32[8,128]{1,0:T(8,128)S(1)} %get-tuple-element.66.bias_in), custom_call_target="tpu_custom_call" | custom-call | bytes 1769472 | tf_op jit(solution)/shard_map/final/pallas_call | solution.py:36
  (32 shorter events, 1.3 us)
Async XLA Ops:
  0.6 5.7 %copy-start.1 = (bf16[64,64,128]{2,1,0:T(8,128)(2,1)S(1)}, bf16[64,64,128]{2,1,0:T(8,128)(2,1)}, u32[]{:S(2)}) copy-start(bf16[64,64,128]{2,1,0:T(8,128)(2,1)} %tile.2) | copy-start | bytes 3145732
  1.9 4.8 %copy-start = (bf16[64,64,128]{2,1,0:T(8,128)(2,1)S(1)}, bf16[64,64,128]{2,1,0:T(8,128)(2,1)}, u32[]{:S(2)}) copy-start(bf16[64,64,128]{2,1,0:T(8,128)(2,1)} %cot.3) | copy-start | bytes 3145732
  1.9 6.8 %collective-permute-start.1 = (bf16[2,8,128]{2,1,0:T(8,128)(2,1)S(1)}, bf16[2,8,128]{2,1,0:T(8,128)(2,1)S(1)}, u32[]{:S(2)}, u32[]{:S(2)}) collective-permute-start(bf16[2,8,128]{2,1,0:T(8,128)(2,1)S(1)} %get-tuple-element.38), channel_id=1, source_target_pairs={{0,3},{1,2},{2,5},{3,4},{4,7},{5,6},{6,9},{7,8},{8,11},{9,10},{10,... | collective-permute-start | bytes 12296 | tf_op jit(solution)/shard_map/ppermute | solution.py:336
  4.4 6.7 %collective-permute-start = (bf16[2,64,128]{2,1,0:T(8,128)(2,1)S(1)}, bf16[2,64,128]{2,1,0:T(8,128)(2,1)S(1)}, u32[]{:S(2)}, u32[]{:S(2)}) collective-permute-start(bf16[2,64,128]{2,1,0:T(8,128)(2,1)S(1)} %get-tuple-element.37), channel_id=1, source_target_pairs={{0,2},{2,4},{4,6},{6,8},{8,10},{10,12},{12,14},{14,0},{1,3},{3,5},... | collective-permute-start | bytes 98312 | tf_op jit(solution)/shard_map/ppermute | solution.py:326
  5.9 5.1 %collective-permute-start.2 = (bf16[2,64,128]{2,1,0:T(8,128)(2,1)S(1)}, bf16[2,64,128]{2,1,0:T(8,128)(2,1)S(1)}, u32[]{:S(2)}, u32[]{:S(2)}) collective-permute-start(bf16[2,64,128]{2,1,0:T(8,128)(2,1)S(1)} %get-tuple-element.39), channel_id=1, source_target_pairs={{0,1},{1,0},{2,3},{3,2},{4,5},{5,4},{6,7},{7,6},{8,9},{9,8},{10,11... | collective-permute-start | bytes 98312 | tf_op jit(solution)/shard_map/ppermute | solution.py:326
  6.7 4.4 %copy-start.2 = (bf16[3,3,128,128]{3,2,1,0:T(8,128)(2,1)S(1)}, bf16[3,3,128,128]{3,2,1,0:T(8,128)(2,1)}, u32[]{:S(2)}) copy-start(bf16[3,3,128,128]{3,2,1,0:T(8,128)(2,1)} %down_weight.3) | copy-start | bytes 884740
  6.7 4.4 %copy-start.3 = (bf16[3,3,128,128]{3,2,1,0:T(8,128)(2,1)S(1)}, bf16[3,3,128,128]{3,2,1,0:T(8,128)(2,1)}, u32[]{:S(2)}) copy-start(bf16[3,3,128,128]{3,2,1,0:T(8,128)(2,1)} %up_weight.1) | copy-start | bytes 884740
  6.7 4.4 %copy-start.4 = (f32[128]{0:T(128)S(1)}, f32[128]{0:T(128)}, u32[]{:S(2)}) copy-start(f32[128]{0:T(128)} %down_bias.1) | copy-start | bytes 1540
  13.8 1.7 %collective-permute-start.3 = (bf16[1168,128]{1,0:T(8,128)(2,1)S(1)}, bf16[1168,128]{1,0:T(8,128)(2,1)S(1)}, u32[]{:S(2)}, u32[]{:S(2)}) collective-permute-start(bf16[1168,128]{1,0:T(8,128)(2,1)S(1)} %get-tuple-element.46), channel_id=1, source_target_pairs={{0,1},{1,0},{2,3},{3,2},{4,5},{5,4},{6,7},{7,6},{8,9},{9,8},{10,11... | collective-permute-start | bytes 897032 | tf_op jit(solution)/shard_map/ppermute | solution.py:326
  13.9 1.6 %collective-permute-start.4 = (bf16[32,128]{1,0:T(8,128)(2,1)S(1)}, bf16[32,128]{1,0:T(8,128)(2,1)S(1)}, u32[]{:S(2)}, u32[]{:S(2)}) collective-permute-start(bf16[32,128]{1,0:T(8,128)(2,1)S(1)} %get-tuple-element.47), channel_id=1, source_target_pairs={{0,1},{1,0},{2,3},{3,2},{4,5},{5,4},{6,7},{7,6},{8,9},{9,8},{10,11... | collective-permute-start | bytes 24584 | tf_op jit(solution)/shard_map/ppermute | solution.py:326
  15.5 6.5 %collective-permute-start.5 = (bf16[304,128]{1,0:T(8,128)(2,1)S(1)}, bf16[304,128]{1,0:T(8,128)(2,1)S(1)}, u32[]{:S(2)}, u32[]{:S(2)}) collective-permute-start(bf16[304,128]{1,0:T(8,128)(2,1)S(1)} %get-tuple-element.51), channel_id=1, source_target_pairs={{0,2},{2,0},{4,6},{6,4},{8,10},{10,8},{12,14},{14,12},{1,3},{3,1},... | collective-permute-start | bytes 233480 | tf_op jit(solution)/shard_map/ppermute | solution.py:341
  15.6 4.4 %collective-permute-start.10 = (bf16[288,128]{1,0:T(8,128)(2,1)S(1)}, bf16[288,128]{1,0:T(8,128)(2,1)S(1)}, u32[]{:S(2)}, u32[]{:S(2)}) collective-permute-start(bf16[288,128]{1,0:T(8,128)(2,1)S(1)} %get-tuple-element.65), channel_id=1, source_target_pairs={{0,4},{2,6},{4,0},{6,2},{8,12},{10,14},{12,8},{14,10},{1,5},{3,7},... | collective-permute-start | bytes 221192 | tf_op jit(solution)/shard_map/ppermute | solution.py:341
  20.1 8.3 %collective-permute-start.11 = (bf16[288,128]{1,0:T(8,128)(2,1)S(1)}, bf16[288,128]{1,0:T(8,128)(2,1)S(1)}, u32[]{:S(2)}, u32[]{:S(2)}) collective-permute-start(bf16[288,128]{1,0:T(8,128)(2,1)S(1)} %whole.9.held), channel_id=1, source_target_pairs={{0,2},{2,0},{4,6},{6,4},{8,10},{10,8},{12,14},{14,12},{1,3},{3,1},... | collective-permute-start | bytes 221192 | tf_op jit(solution)/shard_map/ppermute | solution.py:341
  22.1 4.5 %collective-permute-start.6 = (bf16[304,128]{1,0:T(8,128)(2,1)S(1)}, bf16[304,128]{1,0:T(8,128)(2,1)S(1)}, u32[]{:S(2)}, u32[]{:S(2)}) collective-permute-start(bf16[304,128]{1,0:T(8,128)(2,1)S(1)} %get-tuple-element.53.held), channel_id=1, source_target_pairs={{0,4},{2,6},{4,0},{6,2},{8,12},{10,14},{12,8},{14,10},{1,5},{3,7},... | collective-permute-start | bytes 233480 | tf_op jit(solution)/shard_map/ppermute | solution.py:341
  22.2 3.7 %collective-permute-start.7 = (bf16[40,128]{1,0:T(8,128)(2,1)S(1)}, bf16[40,128]{1,0:T(8,128)(2,1)S(1)}, u32[]{:S(2)}, u32[]{:S(2)}) collective-permute-start(bf16[40,128]{1,0:T(8,128)(2,1)S(1)} %pad_maximum_fusion), channel_id=1, source_target_pairs={{0,14},{2,0},{4,2},{6,4},{8,6},{10,8},{12,10},{14,12},{1,15},{3,1}... | collective-permute-start | bytes 30728 | tf_op jit(solution)/shard_map/ppermute | solution.py:326
  26.6 8.1 %collective-permute-start.8 = (bf16[304,128]{1,0:T(8,128)(2,1)S(1)}, bf16[304,128]{1,0:T(8,128)(2,1)S(1)}, u32[]{:S(2)}, u32[]{:S(2)}) collective-permute-start(bf16[304,128]{1,0:T(8,128)(2,1)S(1)} %get-tuple-element.58.held), channel_id=1, source_target_pairs={{0,8},{2,10},{4,12},{6,14},{8,0},{10,2},{12,4},{14,6},{1,9},{3,11}... | collective-permute-start | bytes 233480 | tf_op jit(solution)/shard_map/ppermute | solution.py:341
  28.3 6.2 %collective-permute-start.12 = (bf16[288,128]{1,0:T(8,128)(2,1)S(1)}, bf16[288,128]{1,0:T(8,128)(2,1)S(1)}, u32[]{:S(2)}, u32[]{:S(2)}) collective-permute-start(bf16[288,128]{1,0:T(8,128)(2,1)S(1)} %whole.10.held), channel_id=1, source_target_pairs={{0,8},{2,10},{4,12},{6,14},{8,0},{10,2},{12,4},{14,6},{1,9},{3,11}... | collective-permute-start | bytes 221192 | tf_op jit(solution)/shard_map/ppermute | solution.py:341
  34.6 4.4 %collective-permute-start.13 = (bf16[288,128]{1,0:T(8,128)(2,1)S(1)}, bf16[288,128]{1,0:T(8,128)(2,1)S(1)}, u32[]{:S(2)}, u32[]{:S(2)}) collective-permute-start(bf16[288,128]{1,0:T(8,128)(2,1)S(1)} %whole.11.held_b), channel_id=1, source_target_pairs={{0,4},{2,6},{4,0},{6,2},{8,12},{10,14},{12,8},{14,10},{1,5},{3,7},... | collective-permute-start | bytes 221192 | tf_op jit(solution)/shard_map/ppermute | solution.py:341
  34.7 5.5 %collective-permute-start.9 = (bf16[288,128]{1,0:T(8,128)(2,1)S(1)}, bf16[288,128]{1,0:T(8,128)(2,1)S(1)}, u32[]{:S(2)}, u32[]{:S(2)}) collective-permute-start(bf16[288,128]{1,0:T(8,128)(2,1)S(1)} %get-tuple-element.63.held_a), channel_id=1, source_target_pairs={{0,2},{2,0},{4,6},{6,4},{8,10},{10,8},{12,14},{14,12},{1,3},{3,1},... | collective-permute-start | bytes 221192 | tf_op jit(solution)/shard_map/ppermute | solution.py:341
  40.2 1.6 %collective-permute-start.14 = (bf16[1152,128]{1,0:T(8,128)(2,1)S(1)}, bf16[1152,128]{1,0:T(8,128)(2,1)S(1)}, u32[]{:S(2)}, u32[]{:S(2)}) collective-permute-start(bf16[1152,128]{1,0:T(8,128)(2,1)S(1)} %both.1.held), channel_id=1, source_target_pairs={{0,1},{1,0},{2,3},{3,2},{4,5},{5,4},{6,7},{7,6},{8,9},{9,8},{10,11... | collective-permute-start | bytes 884744 | tf_op jit(solution)/shard_map/ppermute | solution.py:326

commit v4 on v3

--- a/solution.py
+++ b/solution.py
@@ -68,104 +68,160 @@
         corner[which] = wide_strip[tile_rows * 16 - 8 :, :].astype(BF16)
 
 
-def phase_body(tile, out, wide):
-    rows, cols, channels = tile.shape
-    wide[:, 0:8, :] = jnp.zeros((rows, 8, channels), F32)
-    wide[:, 8:, :] = tile[...].astype(F32)
-    for col_off in range(3):
-        out[col_off] = wide[:, pl.ds(7 + col_off, cols // 2, stride=2), :].astype(BF16)
-
-
 def if_any(there, value):
     return jnp.where(there, value, jnp.zeros_like(value))
 
 
-def fill_patches(phases, top, left, corner, patch, line, column):
-    _, rows, half_cols, channels = phases.shape
-    half_rows = rows // 2
-    above = lax.axis_index("wide") > 0
-    aside = lax.axis_index("narrow") > 0
-    line[0:8, :] = if_any(above & aside, corner[...].astype(F32))
-    line[8:, :] = if_any(above, top[...].astype(F32))
-    column[...] = if_any(aside, left[...].astype(F32))
-    first = lax.broadcasted_iota(jnp.int32, (half_rows, half_cols, channels), 1) == 0
-    paired = phases.reshape(3, half_rows, 2, half_cols, channels)
+def own_patches(tile, wide, strip, patch, firsts):
+    rows, cols, channels = tile.shape
+    half_rows, half_cols = rows // 2, cols // 2
+    wide[:, :, 0:8, :] = jnp.zeros((half_rows, 2, 8, channels), F32)
+    wide[:, :, 8:, :] = tile[...].astype(F32).reshape(half_rows, 2, cols, channels)
     for col_off in range(3):
         lanes = [pl.ds((3 * row_off + col_off) * channels, channels) for row_off in range(3)]
-        even = paired[col_off, :, 0].astype(F32) if col_off == 0 else paired[col_off, :, 0]
-        odd = paired[col_off, :, 1].astype(F32) if col_off == 0 else paired[col_off, :, 1]
-        if col_off == 0:
-            rim = [
-                column[pl.ds(off, half_rows, stride=2), :].reshape(half_rows, 1, channels)
-                for off in (0, 1)
-            ]
-            even = jnp.where(first, rim[0], even).astype(BF16)
-            odd = jnp.where(first, rim[1], odd).astype(BF16)
-        patch[:, :, lanes[1]] = even
+        taken = pl.ds(7 + col_off, half_cols, stride=2)
+        patch[:, :, lanes[1]] = wide[:, 0, taken, :].astype(BF16)
+        odd = wide[:, 1, taken, :].astype(BF16)
         patch[:, :, lanes[2]] = odd
         patch[1:, :, lanes[0]] = odd[:-1]
-        patch[0, :, lanes[0]] = line[pl.ds(7 + col_off, half_cols, stride=2), :].astype(BF16)
-
-
-def main_body(
-    feat_phases, cot_phases, top, left, corner, down_weight, down_bias, up_weight,
-    grads, first_row, first_col, mine, other, bias_part,
-    feat_patch, cot_patch, up_mat, act, wide_grads, line, column,
+        patch[0, :, lanes[0]] = jnp.zeros((half_cols, channels), BF16)
+    strip[...] = tile[:, 0:16, :].astype(F32).reshape(strip.shape)
+    for col in range(2):
+        firsts[col] = strip[pl.ds(col, rows, stride=16), :].astype(BF16)
+
+
+def pointwise(pre, act_grad):
+    sigm = 1.0 / (1.0 + jnp.exp(-pre))
+    return pre * sigm, act_grad * sigm * (1.0 + pre * (1.0 - sigm))
+
+
+def interior_body(
+    feat, cot, down_weight, down_bias, up_weight,
+    grads, raw_up, raw_down, raw_bias, feat_row, cot_row, feat_firsts, cot_firsts, up_mat,
+    feat_patch, cot_patch, act, wide, strip,
 ):
-    _, rows, half_cols, channels = feat_phases.shape
-    half_rows = rows // 2
+    rows, cols, channels = feat.shape
+    half_rows, half_cols = rows // 2, cols // 2
     pixels = half_rows * half_cols
     taps = 9 * channels
-    fill_patches(feat_phases, top.at[0], left.at[0], corner.at[0], feat_patch, line, column)
-    fill_patches(cot_phases, top.at[1], left.at[1], corner.at[1], cot_patch, line, column)
+    own_patches(feat, wide, strip, feat_patch, feat_firsts)
+    own_patches(cot, wide, strip, cot_patch, cot_firsts)
+    feat_row[...] = feat_patch[0]
+    cot_row[...] = cot_patch[0]
     for tap in range(9):
         up_mat[:, pl.ds(tap * channels, channels)] = up_weight[tap // 3, tap % 3]
     down_mat = down_weight[...].reshape(taps, channels)
     bias_row = down_bias[...].reshape(1, channels)
     step = 8
+    count = step * half_cols
+    total = jnp.zeros((1, channels), F32)
+    at = lax.broadcasted_iota(jnp.int32, (count, channels), 0)
     for start in range(0, half_rows, step):
-        span = pl.ds(start * half_cols, step * half_cols)
-        feat_rows = feat_patch[start : start + step].reshape(step * half_cols, taps)
-        cot_rows = cot_patch[start : start + step].reshape(step * half_cols, taps)
+        span = pl.ds(start * half_cols, count)
+        feat_rows = feat_patch[start : start + step].reshape(count, taps)
+        cot_rows = cot_patch[start : start + step].reshape(count, taps)
         pre = jnp.dot(feat_rows, down_mat, preferred_element_type=F32) + bias_row
         act_grad = lax.dot_general(
             cot_rows, up_mat[...], (((1,), (1,)), ((), ())), preferred_element_type=F32
         )
-        sigm = 1.0 / (1.0 + jnp.exp(-pre))
-        act[span, :] = (pre * sigm).astype(BF16)
-        pre_grad = (act_grad * sigm * (1.0 + pre * (1.0 - sigm))).astype(BF16)
-        grads[span, :] = pre_grad
-        wide_grads[span, :] = pre_grad.astype(F32)
-    first_row[...] = grads[0:half_cols, :]
-    first_col[...] = wide_grads[pl.ds(0, half_rows, stride=half_cols), :].astype(BF16)
-    raw_bias = jnp.sum(wide_grads[...], axis=0, keepdims=True)
-    coarse = raw_bias.astype(BF16)
-    fine = (raw_bias - coarse.astype(F32)).astype(BF16)
+        inside = lax.rem(at, half_cols) > 0
+        if start == 0:
+            inside = inside & (at >= half_cols)
+        value, grad = pointwise(pre, act_grad)
+        act[span, :] = if_any(inside, value).astype(BF16)
+        grad = if_any(inside, grad).astype(BF16)
+        grads[span, :] = grad
+        total = total + jnp.sum(grad.astype(F32), axis=0, keepdims=True)
+    raw_bias[...] = jnp.broadcast_to(total, raw_bias.shape)
+    raw_up[...] = lax.dot_general(
+        act[...], cot_patch[...].reshape(pixels, taps), (((0,), (0,)), ((), ())),
+        preferred_element_type=F32,
+    )
+    raw_down[...] = lax.dot_general(
+        feat_patch[...].reshape(pixels, taps), grads[...], (((0,), (0,)), ((), ())),
+        preferred_element_type=F32,
+    )
+
+
+def rim_patches(row_part, firsts, top, left, corner, out, line, column):
+    half_cols, taps = row_part.shape
+    channels = taps // 9
+    half_rows = left.shape[0] // 2
+    above = lax.axis_index("wide") > 0
+    aside = lax.axis_index("narrow") > 0
+    line[0:8, :] = if_any(above & aside, corner[...].astype(F32))
+    line[8:, :] = if_any(above, top[...].astype(F32))
+    column[0, 0:8, :] = line[0:8, :]
+    column[0, 8:, :] = if_any(aside, left[...].astype(F32))
+    for col in range(2):
+        column[1 + col, 0:8, :] = jnp.zeros((8, channels), F32)
+        column[1 + col, 8:, :] = firsts[col].astype(F32)
+    out[0:half_cols, 3 * channels :] = row_part[:, 3 * channels :]
+    first = lax.broadcasted_iota(jnp.int32, (half_cols, channels), 0) == 0
+    for off in range(3):
+        out[0:half_cols, off * channels : (off + 1) * channels] = line[
+            pl.ds(7 + off, half_cols, stride=2), :
+        ].astype(BF16)
+        for col_off in range(3):
+            lanes = slice((3 * off + col_off) * channels, (3 * off + col_off + 1) * channels)
+            out[half_cols:, lanes] = column[
+                col_off, pl.ds(7 + off, half_rows, stride=2), :
+            ].astype(BF16)
+    for off in (1, 2):
+        lanes = slice(3 * off * channels, (3 * off + 1) * channels)
+        rest = row_part[:, lanes].astype(F32)
+        halo = jnp.broadcast_to(column[0, 7 + off : 8 + off, :], rest.shape)
+        out[0:half_cols, lanes] = jnp.where(first, halo, rest).astype(BF16)
+
+
+def rim_body(
+    feat_row, cot_row, feat_firsts, cot_firsts, top, left, corner, raw_up, raw_down, raw_bias,
+    up_mat, down_weight, down_bias,
+    rim_grads, mine, other, bias_part,
+    feat_rim, cot_rim, line, column,
+):
+    half_cols, taps = feat_row.shape
+    channels = taps // 9
+    rim_patches(feat_row, feat_firsts, top.at[0], left.at[0], corner.at[0], feat_rim, line, column)
+    rim_patches(cot_row, cot_firsts, top.at[1], left.at[1], corner.at[1], cot_rim, line, column)
+    pre = jnp.dot(
+        feat_rim[...], down_weight[...].reshape(taps, channels), preferred_element_type=F32
+    ) + down_bias[...].reshape(1, channels)
+    act_grad = lax.dot_general(
+        cot_rim[...], up_mat[...], (((1,), (1,)), ((), ())), preferred_element_type=F32
+    )
+    value, grad = pointwise(pre, act_grad)
+    once = lax.broadcasted_iota(jnp.int32, value.shape, 0) != half_cols
+    act = if_any(once, value).astype(BF16)
+    masked = if_any(once, grad).astype(BF16)
+    full = grad.astype(BF16).astype(F32)
+    rim_grads[...] = jnp.where(once, full, jnp.broadcast_to(full[0:1], full.shape)).astype(BF16)
+    total = raw_bias[0:1, :] + jnp.sum(masked.astype(F32), axis=0, keepdims=True)
+    coarse = total.astype(BF16)
+    fine = (total - coarse.astype(F32)).astype(BF16)
     bias_part[...] = jnp.broadcast_to(coarse.astype(F32) + fine.astype(F32), bias_part.shape)
     put_side(other, taps, coarse, fine)
-    raw_up = lax.dot_general(
-        act[...], cot_patch[...].reshape(pixels, taps), (((0,), (0,)), ((), ())),
-        preferred_element_type=F32,
-    )
-    raw_down = lax.dot_general(
-        feat_patch[...].reshape(pixels, taps), grads[...], (((0,), (0,)), ((), ())),
-        preferred_element_type=F32,
+    more_up = lax.dot_general(
+        act, cot_rim[...], (((0,), (0,)), ((), ())), preferred_element_type=F32
+    )
+    more_down = lax.dot_general(
+        feat_rim[...], masked, (((0,), (0,)), ((), ())), preferred_element_type=F32
     )
     core = lax.axis_index("narrow")
 
     @pl.when(core == 0)
     def _():
-        mine[...] = raw_down
+        mine[...] = raw_down[...] + more_down
         for tap in range(9):
-            span = pl.ds(tap * channels, channels)
-            other[span, :] = raw_up[:, tap * channels : (tap + 1) * channels].astype(BF16)
+            span = slice(tap * channels, (tap + 1) * channels)
+            other[span, :] = (raw_up[:, span] + more_up[:, span]).astype(BF16)
 
     @pl.when(core != 0)
     def _():
-        other[0:taps, :] = raw_down.astype(BF16)
+        other[0:taps, :] = (raw_down[...] + more_down).astype(BF16)
         for tap in range(9):
-            span = pl.ds(tap * channels, channels)
-            mine[span, :] = raw_up[:, tap * channels : (tap + 1) * channels]
+            span = slice(tap * channels, (tap + 1) * channels)
+            mine[span, :] = raw_up[:, span] + more_up[:, span]
 
 
 def put_side(out, at, coarse, fine):
@@ -275,13 +331,16 @@
         write(got, held)
 
 
-def feature_body(grads, right, below, cot, down_weight, out, wide, pairs, near_mat, low_mat, woven):
+def feature_body(grads, rim_grads, right, below, cot, down_weight, out, wide, pairs, near_mat, low_mat, woven):
     tile_rows, tile_cols, channels = cot.shape
     half_rows, half_cols = tile_rows // 2, tile_cols // 2
     wide[0:half_rows, 0:half_cols, :] = grads[...].astype(F32).reshape(
         half_rows, half_cols, channels
     )
     last = lax.broadcasted_iota(jnp.int32, (half_rows, 8, channels), 1) == 0
+    own = rim_grads[half_cols:, :].astype(F32).reshape(half_rows, 1, channels)
+    wide[0:half_rows, 0:8, :] = jnp.where(last, own, wide[0:half_rows, 0:8, :])
+    wide[0, 0:half_cols, :] = rim_grads[0:half_cols, :].astype(F32)
     aside = lax.axis_index("narrow") < lax.axis_size("narrow") - 1
     under = lax.axis_index("wide") < lax.axis_size("wide") - 1
     rim = if_any(aside, right[...].astype(F32)).reshape(half_rows, 1, channels)
@@ -367,55 +426,68 @@
     from_above = turned(rows, "wide", 1)
     from_corner = turned_both(corner)
     from_left = turned(cols, "narrow", 1)
-    phases = call(
-        phase_body,
-        vm((3, tile_rows, half_cols, channels), BF16),
-        scratch=[pltpu.VMEM((tile_rows, tile_cols + 8, channels), F32)],
-        n_in=1,
-        flops=1 << 28,
-        nbytes=3 << 20,
-        name="phases",
+    out_of_interior = (
+        vm((pixels, channels), BF16),
+        vm((channels, taps), F32),
+        vm((taps, channels), F32),
+        vm((8, channels), F32),
+        vm((half_cols, taps), BF16),
+        vm((half_cols, taps), BF16),
+        vm((2, tile_rows, channels), BF16),
+        vm((2, tile_rows, channels), BF16),
+        vm((channels, taps), BF16),
+    )
+    (
+        grads, raw_up, raw_down, raw_bias, feat_row, cot_row, feat_firsts, cot_firsts, up_mat
+    ) = call(
+        interior_body,
+        out_of_interior,
+        scratch=[
+            pltpu.VMEM((half_rows, half_cols, taps), BF16),
+            pltpu.VMEM((half_rows, half_cols, taps), BF16),
+            pltpu.VMEM((pixels, channels), BF16),
+            pltpu.VMEM((half_rows, 2, tile_cols + 8, channels), F32),
+            pltpu.VMEM((tile_rows * 16, channels), F32),
+        ],
+        n_in=5,
+        flops=8 * pixels * taps * channels,
+        nbytes=6 << 20,
+        name="interior",
+        near=(0, 1),
         room=16,
-    )
-    feat_phases = phases(features)
-    cot_phases = phases(cotangent)
-    from_above, from_corner, from_left, feat_phases, cot_phases = lax.optimization_barrier(
-        (from_above, from_corner, from_left, feat_phases, cot_phases)
-    )
-    grads, first_row, first_col, mine, other, bias_sum = call(
-        main_body,
+    )(features, cotangent, down_weight, down_bias, up_weight)
+    from_above, from_corner, from_left, raw_up = lax.optimization_barrier(
+        (from_above, from_corner, from_left, raw_up)
+    )
+    rim_grads, mine, other, bias_sum = call(
+        rim_body,
         (
-            vm((pixels, channels), BF16),
-            vm((half_cols, channels), BF16),
-            vm((half_rows, channels), BF16),
+            vm((half_cols + half_rows, channels), BF16),
             vm((taps, channels), F32),
             vm((taps + SIDE, channels), BF16),
             vm((8, channels), F32),
         ),
         scratch=[
-            pltpu.VMEM((half_rows, half_cols, taps), BF16),
-            pltpu.VMEM((half_rows, half_cols, taps), BF16),
-            pltpu.VMEM((channels, taps), BF16),
-            pltpu.VMEM((pixels, channels), BF16),
-            pltpu.VMEM((pixels, channels), F32),
+            pltpu.VMEM((half_cols + half_rows, taps), BF16),
+            pltpu.VMEM((half_cols + half_rows, taps), BF16),
             pltpu.VMEM((tile_cols + 8, channels), F32),
-            pltpu.VMEM((tile_rows, channels), F32),
+            pltpu.VMEM((3, tile_rows + 8, channels), F32),
         ],
-        n_in=8,
-        flops=8 * pixels * taps * channels,
-        nbytes=6 << 20,
-        name="main",
-        near=(0, 1, 2, 3, 4),
-        room=32,
+        n_in=13,
+        flops=1 << 26,
+        nbytes=3 << 20,
+        name="rim",
+        near=tuple(range(11)),
+        room=16,
     )(
-        feat_phases, cot_phases, from_above, from_left, from_corner,
-        down_weight, down_bias, up_weight,
+        feat_row, cot_row, feat_firsts, cot_firsts, from_above, from_left, from_corner,
+        raw_up, raw_down, raw_bias, up_mat, down_weight, down_bias,
     )
 
     got = turned(other, "narrow", 1)
-    from_right = turned(first_col, "narrow", -1)
+    from_right = turned(rim_grads[half_cols:], "narrow", -1)
     got, from_right = lax.optimization_barrier((got, from_right))
-    from_below = turned(jnp.concatenate([first_row, from_right[:8]], axis=0), "wide", -1)
+    from_below = turned(jnp.concatenate([rim_grads[:half_cols], from_right[:8]], axis=0), "wide", -1)
 
     bits = lax.axis_size("wide").bit_length() - 1
     order_a = list(range(bits))
@@ -466,13 +538,13 @@
             pltpu.VMEM((2 * channels, 2 * channels), BF16),
             pltpu.VMEM((8, 2, tile_cols, channels), F32),
         ],
-        n_in=5,
+        n_in=6,
         flops=2 * pixels * 6 * 2 * channels * channels,
         nbytes=3 << 20,
         name="feature",
-        near=(0, 1, 2),
+        near=(0, 1, 2, 3),
         room=16,
-    )(grads, from_right, from_below, cotangent, down_weight)
+    )(grads, rim_grads, from_right, from_below, cotangent, down_weight)
     for step in range(halvings, bits + 1):
         side = SIDE if step < bits else 0
         held_a, bias_sum = call(
@@ -494,13 +566,13 @@
         if step < bits:
             got_a = traded(held_a, order_a[step])
             got_b = traded(held_b, order_b[step])
-            if step == halvings:
+            if step == bits - 1:
                 got_a, from_below = lax.optimization_barrier((got_a, from_below))
-            if step == bits - 1:
-                got_a, feature_grad = lax.optimization_barrier((got_a, feature_grad))
     for step in reversed(range(halvings)):
         got_a = traded(held_a, order_a[step])
         got_b = traded(held_b, order_b[step])
+        if step == 0:
+            got_a, feature_grad = lax.optimization_barrier((got_a, feature_grad))
         if step:
             half *= 2
             held_a = call(

time: 43.3 us -> 40.7 us (0.940)
  waiting for transfers between devices: 18.1 us -> 10.7 us
  starting transfers between devices: 16.2 us -> 19.3 us
  local copies, waits for them, and re-layouts: 0.03 us -> 1.3 us
  Pallas kernels: 7.97 us -> 8.45 us
    ppermute x8, waiting for transfers between devices: 10.1 us -> 6.26 us  [traded(): lax.ppermute(value, 'wide', [(at, at ^ 1 << position) for at in range(cou...]
    ppermute x8, starting transfers between devices: 8.84 us -> 10.9 us  [traded(): lax.ppermute(value, 'wide', [(at, at ^ 1 << position) for at in range(cou...]
    ppermute x6, waiting for transfers between devices: 6.41 us -> 4.44 us  [turned(): lax.ppermute(value, axis, [(at, (at + steps) % count) for at in range(cou...]
    ppermute x1, waiting for transfers between devices: 1.64 us -> 0.01 us  [turned_both(): return lax.ppermute(value, ('wide', 'narrow'), pairs)]
    unnamed x10 -> x14, local copies, waits for them, and re-layouts: 0.03 us -> 1.25 us
    ppermute x6, starting transfers between devices: 4.9 us -> 5.93 us  [turned(): lax.ppermute(value, axis, [(at, (at + steps) % count) for at in range(cou...]
    pallas_call x14 -> x13, Pallas kernels: 7.97 us -> 8.45 us  [run(): return kernel(*placed)]
  transfers between devices with their start and end apart: 15 -> 15, of which waited for: 10 -> 9; matrix products, arithmetic and copies ran while one was open for 0% -> 0% of each run, Pallas kernels for 6% -> 12%
where the time goes in v4:
time: 40.7 us; the launch traced here: 40.5 us
  starting transfers between devices  19.3 us (47%)
  waiting for transfers between devices  10.7 us (26%)
  Pallas kernels  8.45 us (21%)
  local copies, waits for them, and re-layouts  1.3 us (3%)
  between operations  0.78 us (2%)
    ppermute x8, starting transfers between devices, traded(): lax.ppermute(value, 'wide', [(at, at ^ 1 << position) for at in range(cou...  10.9 us
    pallas_call x13, Pallas kernels, run(): return kernel(*placed)  8.45 us
    ppermute x8, waiting for transfers between devices, traded(): lax.ppermute(value, 'wide', [(at, at ^ 1 << position) for at in range(cou...  6.26 us
    ppermute x6, starting transfers between devices, turned(): lax.ppermute(value, axis, [(at, (at + steps) % count) for at in range(cou...  5.93 us
    ppermute x6, waiting for transfers between devices, turned(): lax.ppermute(value, axis, [(at, (at + steps) % count) for at in range(cou...  4.44 us
    ppermute x1, starting transfers between devices, turned_both(): return lax.ppermute(value, ('wide', 'narrow'), pairs)  2.46 us
    unnamed x14, local copies, waits for them, and re-layouts  1.25 us
  transfers between devices with their start and end apart: 15, of which 9 were waited for; matrix products, arithmetic and copies ran while one was open for 0% of the time, Pallas kernels for 12%

profile of v4, /device:TPU:0, one launch (start us, length us, event | category | flops | bytes accessed | tf_op | source)
XLA Modules:
  0.0 40.5 jit_solution(9429893712338990262)
XLA Ops:
  0.7 1.3 %edges.1 = (bf16[2,64,128]{2,1,0:T(8,128)(2,1)S(1)}, bf16[2,64,128]{2,1,0:T(8,128)(2,1)S(1)}, bf16[2,8,128]{2,1,0:T(8,128)(2,1)S(1)}) custom-call(bf16[64,64,128]{2,1,0:T(8,128)(2,1)} %feat.3, bf16[64,64,128]{2,1,0:T(8,128)(2,1)} %cot.5), custom_call_target="tpu_custom_call" | custom-call | bytes 524288 | tf_op jit(solution)/shard_map/edges/pallas_call | solution.py:36
  2.0 2.5 %collective-permute-start.1 = (bf16[2,8,128]{2,1,0:T(8,128)(2,1)S(1)}, bf16[2,8,128]{2,1,0:T(8,128)(2,1)S(1)}, u32[]{:S(2)}, u32[]{:S(2)}) collective-permute-start(bf16[2,8,128]{2,1,0:T(8,128)(2,1)S(1)} %get-tuple-element.48), channel_id=1, source_target_pairs={{0,3},{1,2},{2,5},{3,4},{4,7},{5,6},{6,9},{7,8},{8,11},{9,10},{10,... | collective-permute-start | bytes 12296 | tf_op jit(solution)/shard_map/ppermute | solution.py:395
  4.4 1.5 %collective-permute-start = (bf16[2,64,128]{2,1,0:T(8,128)(2,1)S(1)}, bf16[2,64,128]{2,1,0:T(8,128)(2,1)S(1)}, u32[]{:S(2)}, u32[]{:S(2)}) collective-permute-start(bf16[2,64,128]{2,1,0:T(8,128)(2,1)S(1)} %get-tuple-element.47), channel_id=1, source_target_pairs={{0,2},{2,4},{4,6},{6,8},{8,10},{10,12},{12,14},{14,0},{1,3},{3,5},... | collective-permute-start | bytes 98312 | tf_op jit(solution)/shard_map/ppermute | solution.py:385
  6.4 1.2 %copy-done.2 = bf16[64,64,128]{2,1,0:T(8,128)(2,1)S(1)} copy-done((bf16[64,64,128]{2,1,0:T(8,128)(2,1)S(1)}, bf16[64,64,128]{2,1,0:T(8,128)(2,1)}, u32[]{:S(2)}) %copy-start.2) | copy-done | bytes 1048600
  7.6 3.1 %interior.1 = (bf16[1024,128]{1,0:T(8,128)(2,1)S(1)}, f32[128,1152]{1,0:T(8,128)S(1)}, f32[1152,128]{1,0:T(8,128)S(1)}, f32[8,128]{1,0:T(8,128)S(1)}, bf16[32,11...) custom-call(bf16[64,64,128]{2,1,0:T(8,128)(2,1)S(1)} %copy-done.2, ...), custom_call_target="tpu_custom_call" | custom-call | flops 1207959552 | bytes 6291456 | tf_op jit(solution)/shard_map/interior/pallas_call | solution.py:36
  11.1 0.8 %rim.1 = (bf16[64,128]{1,0:T(8,128)(2,1)S(1)}, f32[1152,128]{1,0:T(8,128)S(1)}, bf16[1168,128]{1,0:T(8,128)(2,1)S(1)}, f32[8,128]{1,0:T(8,128)S(1)}) custom-call(bf16[32,1152]{1,0:T(8,128)(2,1)S(1)} %get-tuple-element.43.feat_row, bf16[32,1152]{1,0:T(8,128)(2,1)S(1)} %get-tuple-element.44.cot_row, bf16[2,64,128]{2,1,0:T(8,128)(2,1)S(1)} %get-tuple-element.45.feat_firsts, ...), custom_call_target="tpu_custom_call" | custom-call | flops 67108864 | bytes 3145728 | tf_op jit(solution)/shard_map/rim/pallas_call | solution.py:36
  12.5 1.1 %collective-permute-done.4.right = bf16[32,128]{1,0:T(8,128)(2,1)S(1)} collective-permute-done((bf16[32,128]{1,0:T(8,128)(2,1)S(1)}, bf16[32,128]{1,0:T(8,128)(2,1)S(1)}, u32[]{:S(2)}, u32[]{:S(2)}) %collective-permute-start.4) | collective-permute-done | bytes 8224 | tf_op jit(solution)/shard_map/ppermute | solution.py:385
  13.6 1.2 %collective-permute-start.5 = (bf16[304,128]{1,0:T(8,128)(2,1)S(1)}, bf16[304,128]{1,0:T(8,128)(2,1)S(1)}, u32[]{:S(2)}, u32[]{:S(2)}) collective-permute-start(bf16[304,128]{1,0:T(8,128)(2,1)S(1)} %get-tuple-element.64), channel_id=1, source_target_pairs={{0,2},{2,0},{4,6},{6,4},{8,10},{10,8},{12,14},{14,12},{1,3},{3,1},... | collective-permute-start | bytes 233480 | tf_op jit(solution)/shard_map/ppermute | solution.py:400
  14.8 1.6 %collective-permute-start.10 = (bf16[288,128]{1,0:T(8,128)(2,1)S(1)}, bf16[288,128]{1,0:T(8,128)(2,1)S(1)}, u32[]{:S(2)}, u32[]{:S(2)}) collective-permute-start(bf16[288,128]{1,0:T(8,128)(2,1)S(1)} %get-tuple-element.77), channel_id=1, source_target_pairs={{0,4},{2,6},{4,0},{6,2},{8,12},{10,14},{12,8},{14,10},{1,5},{3,7},... | collective-permute-start | bytes 221192 | tf_op jit(solution)/shard_map/ppermute | solution.py:400
  16.4 1.7 %collective-permute-done.5.got = bf16[304,128]{1,0:T(8,128)(2,1)S(1)} collective-permute-done((bf16[304,128]{1,0:T(8,128)(2,1)S(1)}, bf16[304,128]{1,0:T(8,128)(2,1)S(1)}, u32[]{:S(2)}, u32[]{:S(2)}) %collective-permute-start.5) | collective-permute-done | bytes 77856 | tf_op jit(solution)/shard_map/ppermute | solution.py:400
  18.1 1.3 %collective-permute-start.6 = (bf16[304,128]{1,0:T(8,128)(2,1)S(1)}, bf16[304,128]{1,0:T(8,128)(2,1)S(1)}, u32[]{:S(2)}, u32[]{:S(2)}) collective-permute-start(bf16[304,128]{1,0:T(8,128)(2,1)S(1)} %get-tuple-element.66.held), channel_id=1, source_target_pairs={{0,4},{2,6},{4,0},{6,2},{8,12},{10,14},{12,8},{14,10},{1,5},{3,7},... | collective-permute-start | bytes 233480 | tf_op jit(solution)/shard_map/ppermute | solution.py:400
  19.4 1.6 %collective-permute-start.11 = (bf16[288,128]{1,0:T(8,128)(2,1)S(1)}, bf16[288,128]{1,0:T(8,128)(2,1)S(1)}, u32[]{:S(2)}, u32[]{:S(2)}) collective-permute-start(bf16[288,128]{1,0:T(8,128)(2,1)S(1)} %whole.9.held), channel_id=1, source_target_pairs={{0,2},{2,0},{4,6},{6,4},{8,10},{10,8},{12,14},{14,12},{1,3},{3,1},... | collective-permute-start | bytes 221192 | tf_op jit(solution)/shard_map/ppermute | solution.py:400
  21.0 2.9 %collective-permute-done.11.got = bf16[288,128]{1,0:T(8,128)(2,1)S(1)} collective-permute-done((bf16[288,128]{1,0:T(8,128)(2,1)S(1)}, bf16[288,128]{1,0:T(8,128)(2,1)S(1)}, u32[]{:S(2)}, u32[]{:S(2)}) %collective-permute-start.11) | collective-permute-done | bytes 73760 | tf_op jit(solution)/shard_map/ppermute | solution.py:400
  23.8 2.4 %collective-permute-start.12 = (bf16[288,128]{1,0:T(8,128)(2,1)S(1)}, bf16[288,128]{1,0:T(8,128)(2,1)S(1)}, u32[]{:S(2)}, u32[]{:S(2)}) collective-permute-start(bf16[288,128]{1,0:T(8,128)(2,1)S(1)} %whole.10.held), channel_id=1, source_target_pairs={{0,8},{2,10},{4,12},{6,14},{8,0},{10,2},{12,4},{14,6},{1,9},{3,11}... | collective-permute-start | bytes 221192 | tf_op jit(solution)/shard_map/ppermute | solution.py:400
  26.3 0.6 %collective-permute-start.7 = (bf16[304,128]{1,0:T(8,128)(2,1)S(1)}, bf16[304,128]{1,0:T(8,128)(2,1)S(1)}, u32[]{:S(2)}, u32[]{:S(2)}) collective-permute-start(bf16[304,128]{1,0:T(8,128)(2,1)S(1)} %get-tuple-element.68.held), channel_id=1, source_target_pairs={{0,8},{2,10},{4,12},{6,14},{8,0},{10,2},{12,4},{14,6},{1,9},{3,11}... | collective-permute-start | bytes 233480 | tf_op jit(solution)/shard_map/ppermute | solution.py:400
  27.0 3.4 %collective-permute-start.8 = (bf16[40,128]{1,0:T(8,128)(2,1)S(1)}, bf16[40,128]{1,0:T(8,128)(2,1)S(1)}, u32[]{:S(2)}, u32[]{:S(2)}) collective-permute-start(bf16[40,128]{1,0:T(8,128)(2,1)S(1)} %pad_maximum_fusion), channel_id=1, source_target_pairs={{0,14},{2,0},{4,2},{6,4},{8,6},{10,8},{12,10},{14,12},{1,15},{3,1}... | collective-permute-start | bytes 30728 | tf_op jit(solution)/shard_map/ppermute | solution.py:385
  30.4 1.4 %collective-permute-done.8.below = bf16[40,128]{1,0:T(8,128)(2,1)S(1)} collective-permute-done((bf16[40,128]{1,0:T(8,128)(2,1)S(1)}, bf16[40,128]{1,0:T(8,128)(2,1)S(1)}, u32[]{:S(2)}, u32[]{:S(2)}) %collective-permute-start.8) | collective-permute-done | bytes 10272 | tf_op jit(solution)/shard_map/ppermute | solution.py:385
  31.7 0.8 %collective-permute-done.7.got = bf16[304,128]{1,0:T(8,128)(2,1)S(1)} collective-permute-done((bf16[304,128]{1,0:T(8,128)(2,1)S(1)}, bf16[304,128]{1,0:T(8,128)(2,1)S(1)}, u32[]{:S(2)}, u32[]{:S(2)}) %collective-permute-start.7) | collective-permute-done | bytes 77856 | tf_op jit(solution)/shard_map/ppermute | solution.py:400
  32.6 0.6 %collective-permute-start.9 = (bf16[288,128]{1,0:T(8,128)(2,1)S(1)}, bf16[288,128]{1,0:T(8,128)(2,1)S(1)}, u32[]{:S(2)}, u32[]{:S(2)}) collective-permute-start(bf16[288,128]{1,0:T(8,128)(2,1)S(1)} %get-tuple-element.72.held_a), channel_id=1, source_target_pairs={{0,2},{2,0},{4,6},{6,4},{8,10},{10,8},{12,14},{14,12},{1,3},{3,1},... | collective-permute-start | bytes 221192 | tf_op jit(solution)/shard_map/ppermute | solution.py:400
  33.2 1.7 %collective-permute-start.13 = (bf16[288,128]{1,0:T(8,128)(2,1)S(1)}, bf16[288,128]{1,0:T(8,128)(2,1)S(1)}, u32[]{:S(2)}, u32[]{:S(2)}) collective-permute-start(bf16[288,128]{1,0:T(8,128)(2,1)S(1)} %whole.11.held_b), channel_id=1, source_target_pairs={{0,4},{2,6},{4,0},{6,2},{8,12},{10,14},{12,8},{14,10},{1,5},{3,7},... | collective-permute-start | bytes 221192 | tf_op jit(solution)/shard_map/ppermute | solution.py:400
  34.9 1.8 %feature.1 = bf16[64,64,128]{2,1,0:T(8,128)(2,1)} custom-call(bf16[1024,128]{1,0:T(8,128)(2,1)S(1)} %get-tuple-element.73.grads, bf16[64,128]{1,0:T(8,128)(2,1)S(1)} %get-tuple-element.60.rim_grads, bf16[32,128]{1,0:T(8,128)(2,1)S(1)} %copy-done.4, bf16[40,128]{1,0:T(8,128)(2,1)S(1)} %collective-permute-done.8.below, bf16[64,64,128]{2,1,0:T(8,128)(2,1)S(1)} %copy-done, ...), custom_call_target="tpu_custom_call" | custom-call | flops 402653184 | bytes 3145728 | tf_op jit(solution)/shard_map/feature/pallas_call | solution.py:36
  37.0 0.6 %collective-permute-done.13.got_b = bf16[288,128]{1,0:T(8,128)(2,1)S(1)} collective-permute-done((bf16[288,128]{1,0:T(8,128)(2,1)S(1)}, bf16[288,128]{1,0:T(8,128)(2,1)S(1)}, u32[]{:S(2)}, u32[]{:S(2)}) %collective-permute-start.13) | collective-permute-done | bytes 73760 | tf_op jit(solution)/shard_map/ppermute | solution.py:400
  37.7 1.6 %collective-permute-done.14.got = bf16[1152,128]{1,0:T(8,128)(2,1)S(1)} collective-permute-done((bf16[1152,128]{1,0:T(8,128)(2,1)S(1)}, bf16[1152,128]{1,0:T(8,128)(2,1)S(1)}, u32[]{:S(2)}, u32[]{:S(2)}) %collective-permute-start.14) | collective-permute-done | bytes 294944 | tf_op jit(solution)/shard_map/ppermute | solution.py:385
  39.3 1.3 %final.1 = (f32[9,128,128]{2,1,0:T(8,128)}, f32[9,128,128]{2,1,0:T(8,128)}, f32[1,128]{1,0:T(1,128)}) custom-call(bf16[1152,128]{1,0:T(8,128)(2,1)S(1)} %both.1.held, bf16[1152,128]{1,0:T(8,128)(2,1)S(1)} %collective-permute-done.14.got, f32[8,128]{1,0:T(8,128)S(1)} %get-tuple-element.78.bias_in), custom_call_target="tpu_custom_call" | custom-call | bytes 1769472 | tf_op jit(solution)/shard_map/final/pallas_call | solution.py:36
  (37 shorter events, 2.1 us)
Async XLA Ops:
  0.6 5.7 %copy-start = (bf16[64,64,128]{2,1,0:T(8,128)(2,1)S(1)}, bf16[64,64,128]{2,1,0:T(8,128)(2,1)}, u32[]{:S(2)}) copy-start(bf16[64,64,128]{2,1,0:T(8,128)(2,1)} %cot.5) | copy-start | bytes 3145732
  0.6 5.7 %copy-start.1 = (bf16[3,3,128,128]{3,2,1,0:T(8,128)(2,1)S(1)}, bf16[3,3,128,128]{3,2,1,0:T(8,128)(2,1)}, u32[]{:S(2)}) copy-start(bf16[3,3,128,128]{3,2,1,0:T(8,128)(2,1)} %down_weight.5) | copy-start | bytes 884740
  0.7 5.7 %copy-start.6 = (bf16[3,3,128,128]{3,2,1,0:T(8,128)(2,1)S(1)}, bf16[3,3,128,128]{3,2,1,0:T(8,128)(2,1)}, u32[]{:S(2)}) copy-start(bf16[3,3,128,128]{3,2,1,0:T(8,128)(2,1)} %up_weight.1) | copy-start | bytes 884740
  2.0 8.7 %collective-permute-start.1 = (bf16[2,8,128]{2,1,0:T(8,128)(2,1)S(1)}, bf16[2,8,128]{2,1,0:T(8,128)(2,1)S(1)}, u32[]{:S(2)}, u32[]{:S(2)}) collective-permute-start(bf16[2,8,128]{2,1,0:T(8,128)(2,1)S(1)} %get-tuple-element.48), channel_id=1, source_target_pairs={{0,3},{1,2},{2,5},{3,4},{4,7},{5,6},{6,9},{7,8},{8,11},{9,10},{10,... | collective-permute-start | bytes 12296 | tf_op jit(solution)/shard_map/ppermute | solution.py:395
  4.4 2.0 %copy-start.5 = (f32[128]{0:T(128)S(1)}, f32[128]{0:T(128)}, u32[]{:S(2)}) copy-start(f32[128]{0:T(128)} %down_bias.3) | copy-start | bytes 1540
  4.4 6.7 %collective-permute-start = (bf16[2,64,128]{2,1,0:T(8,128)(2,1)S(1)}, bf16[2,64,128]{2,1,0:T(8,128)(2,1)S(1)}, u32[]{:S(2)}, u32[]{:S(2)}) collective-permute-start(bf16[2,64,128]{2,1,0:T(8,128)(2,1)S(1)} %get-tuple-element.47), channel_id=1, source_target_pairs={{0,2},{2,4},{4,6},{6,8},{8,10},{10,12},{12,14},{14,0},{1,3},{3,5},... | collective-permute-start | bytes 98312 | tf_op jit(solution)/shard_map/ppermute | solution.py:385
  6.0 5.1 %collective-permute-start.2 = (bf16[2,64,128]{2,1,0:T(8,128)(2,1)S(1)}, bf16[2,64,128]{2,1,0:T(8,128)(2,1)S(1)}, u32[]{:S(2)}, u32[]{:S(2)}) collective-permute-start(bf16[2,64,128]{2,1,0:T(8,128)(2,1)S(1)} %get-tuple-element.49), channel_id=1, source_target_pairs={{0,1},{1,0},{2,3},{3,2},{4,5},{5,4},{6,7},{7,6},{8,9},{9,8},{10,11... | collective-permute-start | bytes 98312 | tf_op jit(solution)/shard_map/ppermute | solution.py:385
  6.4 1.2 %copy-start.2 = (bf16[64,64,128]{2,1,0:T(8,128)(2,1)S(1)}, bf16[64,64,128]{2,1,0:T(8,128)(2,1)}, u32[]{:S(2)}) copy-start(bf16[64,64,128]{2,1,0:T(8,128)(2,1)} %feat.3) | copy-start | bytes 3145732
  11.9 1.7 %collective-permute-start.3 = (bf16[1168,128]{1,0:T(8,128)(2,1)S(1)}, bf16[1168,128]{1,0:T(8,128)(2,1)S(1)}, u32[]{:S(2)}, u32[]{:S(2)}) collective-permute-start(bf16[1168,128]{1,0:T(8,128)(2,1)S(1)} %get-tuple-element.59), channel_id=1, source_target_pairs={{0,1},{1,0},{2,3},{3,2},{4,5},{5,4},{6,7},{7,6},{8,9},{9,8},{10,11... | collective-permute-start | bytes 897032 | tf_op jit(solution)/shard_map/ppermute | solution.py:385
  12.0 1.6 %collective-permute-start.4 = (bf16[32,128]{1,0:T(8,128)(2,1)S(1)}, bf16[32,128]{1,0:T(8,128)(2,1)S(1)}, u32[]{:S(2)}, u32[]{:S(2)}) collective-permute-start(bf16[32,128]{1,0:T(8,128)(2,1)S(1)} %get-tuple-element.83), channel_id=1, source_target_pairs={{0,1},{1,0},{2,3},{3,2},{4,5},{5,4},{6,7},{7,6},{8,9},{9,8},{10,11... | collective-permute-start | bytes 24584 | tf_op jit(solution)/shard_map/ppermute | solution.py:385
  13.5 7.4 %copy-start.3 = (bf16[32,128]{1,0:T(8,128)(2,1)}, bf16[32,128]{1,0:T(8,128)(2,1)S(1)}, u32[]{:S(2)}) copy-start(bf16[32,128]{1,0:T(8,128)(2,1)S(1)} %collective-permute-done.4.right) | copy-start | bytes 24580
  13.6 4.5 %collective-permute-start.5 = (bf16[304,128]{1,0:T(8,128)(2,1)S(1)}, bf16[304,128]{1,0:T(8,128)(2,1)S(1)}, u32[]{:S(2)}, u32[]{:S(2)}) collective-permute-start(bf16[304,128]{1,0:T(8,128)(2,1)S(1)} %get-tuple-element.64), channel_id=1, source_target_pairs={{0,2},{2,0},{4,6},{6,4},{8,10},{10,8},{12,14},{14,12},{1,3},{3,1},... | collective-permute-start | bytes 233480 | tf_op jit(solution)/shard_map/ppermute | solution.py:400
  14.8 4.6 %collective-permute-start.10 = (bf16[288,128]{1,0:T(8,128)(2,1)S(1)}, bf16[288,128]{1,0:T(8,128)(2,1)S(1)}, u32[]{:S(2)}, u32[]{:S(2)}) collective-permute-start(bf16[288,128]{1,0:T(8,128)(2,1)S(1)} %get-tuple-element.77), channel_id=1, source_target_pairs={{0,4},{2,6},{4,0},{6,2},{8,12},{10,14},{12,8},{14,10},{1,5},{3,7},... | collective-permute-start | bytes 221192 | tf_op jit(solution)/shard_map/ppermute | solution.py:400
  18.1 8.2 %collective-permute-start.6 = (bf16[304,128]{1,0:T(8,128)(2,1)S(1)}, bf16[304,128]{1,0:T(8,128)(2,1)S(1)}, u32[]{:S(2)}, u32[]{:S(2)}) collective-permute-start(bf16[304,128]{1,0:T(8,128)(2,1)S(1)} %get-tuple-element.66.held), channel_id=1, source_target_pairs={{0,4},{2,6},{4,0},{6,2},{8,12},{10,14},{12,8},{14,10},{1,5},{3,7},... | collective-permute-start | bytes 233480 | tf_op jit(solution)/shard_map/ppermute | solution.py:400
  19.4 4.4 %collective-permute-start.11 = (bf16[288,128]{1,0:T(8,128)(2,1)S(1)}, bf16[288,128]{1,0:T(8,128)(2,1)S(1)}, u32[]{:S(2)}, u32[]{:S(2)}) collective-permute-start(bf16[288,128]{1,0:T(8,128)(2,1)S(1)} %whole.9.held), channel_id=1, source_target_pairs={{0,2},{2,0},{4,6},{6,4},{8,10},{10,8},{12,14},{14,12},{1,3},{3,1},... | collective-permute-start | bytes 221192 | tf_op jit(solution)/shard_map/ppermute | solution.py:400
  23.8 9.3 %collective-permute-start.12 = (bf16[288,128]{1,0:T(8,128)(2,1)S(1)}, bf16[288,128]{1,0:T(8,128)(2,1)S(1)}, u32[]{:S(2)}, u32[]{:S(2)}) collective-permute-start(bf16[288,128]{1,0:T(8,128)(2,1)S(1)} %whole.10.held), channel_id=1, source_target_pairs={{0,8},{2,10},{4,12},{6,14},{8,0},{10,2},{12,4},{14,6},{1,9},{3,11}... | collective-permute-start | bytes 221192 | tf_op jit(solution)/shard_map/ppermute | solution.py:400
  26.3 0.7 %slice-start = ((bf16[32,128]{1,0:T(8,128)(2,1)}), bf16[8,128]{1,0:T(8,128)(2,1)S(1)}, s32[]{:S(2)}) async-start(bf16[32,128]{1,0:T(8,128)(2,1)} %copy-done.3), calls=%async_computation | async-start | bytes 4096 | tf_op jit(solution)/shard_map/slice | solution.py:490
  26.3 6.2 %collective-permute-start.7 = (bf16[304,128]{1,0:T(8,128)(2,1)S(1)}, bf16[304,128]{1,0:T(8,128)(2,1)S(1)}, u32[]{:S(2)}, u32[]{:S(2)}) collective-permute-start(bf16[304,128]{1,0:T(8,128)(2,1)S(1)} %get-tuple-element.68.held), channel_id=1, source_target_pairs={{0,8},{2,10},{4,12},{6,14},{8,0},{10,2},{12,4},{14,6},{1,9},{3,11}... | collective-permute-start | bytes 233480 | tf_op jit(solution)/shard_map/ppermute | solution.py:400
  27.0 4.7 %collective-permute-start.8 = (bf16[40,128]{1,0:T(8,128)(2,1)S(1)}, bf16[40,128]{1,0:T(8,128)(2,1)S(1)}, u32[]{:S(2)}, u32[]{:S(2)}) collective-permute-start(bf16[40,128]{1,0:T(8,128)(2,1)S(1)} %pad_maximum_fusion), channel_id=1, source_target_pairs={{0,14},{2,0},{4,2},{6,4},{8,6},{10,8},{12,10},{14,12},{1,15},{3,1}... | collective-permute-start | bytes 30728 | tf_op jit(solution)/shard_map/ppermute | solution.py:385
  32.5 2.3 %copy-start.4 = (bf16[32,128]{1,0:T(8,128)(2,1)S(1)}, bf16[32,128]{1,0:T(8,128)(2,1)}, u32[]{:S(2)}) copy-start(bf16[32,128]{1,0:T(8,128)(2,1)} %copy-done.3) | copy-start | bytes 24580
  32.6 4.4 %collective-permute-start.9 = (bf16[288,128]{1,0:T(8,128)(2,1)S(1)}, bf16[288,128]{1,0:T(8,128)(2,1)S(1)}, u32[]{:S(2)}, u32[]{:S(2)}) collective-permute-start(bf16[288,128]{1,0:T(8,128)(2,1)S(1)} %get-tuple-element.72.held_a), channel_id=1, source_target_pairs={{0,2},{2,0},{4,6},{6,4},{8,10},{10,8},{12,14},{14,12},{1,3},{3,1},... | collective-permute-start | bytes 221192 | tf_op jit(solution)/shard_map/ppermute | solution.py:400
  33.2 4.4 %collective-permute-start.13 = (bf16[288,128]{1,0:T(8,128)(2,1)S(1)}, bf16[288,128]{1,0:T(8,128)(2,1)S(1)}, u32[]{:S(2)}, u32[]{:S(2)}) collective-permute-start(bf16[288,128]{1,0:T(8,128)(2,1)S(1)} %whole.11.held_b), channel_id=1, source_target_pairs={{0,4},{2,6},{4,0},{6,2},{8,12},{10,14},{12,8},{14,10},{1,5},{3,7},... | collective-permute-start | bytes 221192 | tf_op jit(solution)/shard_map/ppermute | solution.py:400
  37.6 1.6 %collective-permute-start.14 = (bf16[1152,128]{1,0:T(8,128)(2,1)S(1)}, bf16[1152,128]{1,0:T(8,128)(2,1)S(1)}, u32[]{:S(2)}, u32[]{:S(2)}) collective-permute-start(bf16[1152,128]{1,0:T(8,128)(2,1)S(1)} %both.1.held), channel_id=1, source_target_pairs={{0,1},{1,0},{2,3},{3,2},{4,5},{5,4},{6,7},{7,6},{8,9},{9,8},{10,11... | collective-permute-start | bytes 884744 | tf_op jit(solution)/shard_map/ppermute | solution.py:385

commit v5 on v4

--- a/solution.py
+++ b/solution.py
@@ -14,12 +14,12 @@
 SIDE = 16
 
 
-def call(body, out_shape, scratch=(), in_specs=None, n_in=0, flops=0, nbytes=0, name=None, near=(), far=(), room=4):
+def call(body, out_shape, scratch=(), in_specs=None, n_in=0, flops=0, nbytes=0, name=None, near=(), far=(), room=4, out_specs=None):
     kernel = pl.pallas_call(
         body,
         out_shape=out_shape,
         in_specs=in_specs if in_specs is not None else [VM] * n_in,
-        out_specs=jax.tree.map(lambda _: VM, out_shape),
+        out_specs=out_specs or jax.tree.map(lambda _: VM, out_shape),
         scratch_shapes=list(scratch),
         name=name,
         compiler_params=pltpu.CompilerParams(vmem_limit_bytes=room << 20),
@@ -46,7 +46,10 @@
     return jax.ShapeDtypeStruct(shape, dtype)
 
 
-def edge_body(feat, cot, rows, cols, corner, strip, wide_strip, sems):
+def edge_body(
+    feat, cot, down, up, bias, feat_near, cot_near, down_near, up_near, bias_near,
+    rows, cols, corner, strip, wide_strip, sems,
+):
     tile_rows, tile_cols, _ = feat.shape
     copies = []
     for which, ref in enumerate((feat, cot)):
@@ -58,7 +61,14 @@
                 ref.at[:, pl.ds(tile_cols - 16, 16), :], strip.at[which], sems.at[2 * which + 1]
             )
         )
-    for copy in copies:
+    bulk = [
+        pltpu.make_async_copy(feat, feat_near, sems.at[4]),
+        pltpu.make_async_copy(cot, cot_near, sems.at[5]),
+        pltpu.make_async_copy(down, down_near, sems.at[6]),
+        pltpu.make_async_copy(up, up_near, sems.at[7]),
+        pltpu.make_async_copy(bias, bias_near, sems.at[8]),
+    ]
+    for copy in copies + bulk:
         copy.start()
     for copy in copies:
         copy.wait()
@@ -66,6 +76,8 @@
         wide_strip[...] = strip[which].astype(F32).reshape(wide_strip.shape)
         cols[which] = wide_strip[pl.ds(15, tile_rows, stride=16), :].astype(BF16)
         corner[which] = wide_strip[tile_rows * 16 - 8 :, :].astype(BF16)
+    for copy in bulk:
+        copy.wait()
 
 
 def if_any(there, value):
@@ -95,10 +107,22 @@
     return pre * sigm, act_grad * sigm * (1.0 + pre * (1.0 - sigm))
 
 
+def taps_of(core_is, patch, values):
+    if core_is:
+        return lax.dot_general(
+            patch, values, (((0,), (0,)), ((), ())), preferred_element_type=F32
+        )
+    channels = values.shape[1]
+    rows = lax.dot_general(values, patch, (((0,), (0,)), ((), ())), preferred_element_type=F32)
+    return jnp.concatenate(
+        [rows[:, tap * channels : (tap + 1) * channels] for tap in range(9)], axis=0
+    )
+
+
 def interior_body(
     feat, cot, down_weight, down_bias, up_weight,
-    grads, raw_up, raw_down, raw_bias, feat_row, cot_row, feat_firsts, cot_firsts, up_mat,
-    feat_patch, cot_patch, act, wide, strip,
+    feat_patch, cot_patch, act, grads, raw_other, raw_bias, feat_firsts, cot_firsts, up_mat,
+    wide, strip,
 ):
     rows, cols, channels = feat.shape
     half_rows, half_cols = rows // 2, cols // 2
@@ -106,8 +130,6 @@
     taps = 9 * channels
     own_patches(feat, wide, strip, feat_patch, feat_firsts)
     own_patches(cot, wide, strip, cot_patch, cot_firsts)
-    feat_row[...] = feat_patch[0]
-    cot_row[...] = cot_patch[0]
     for tap in range(9):
         up_mat[:, pl.ds(tap * channels, channels)] = up_weight[tap // 3, tap % 3]
     down_mat = down_weight[...].reshape(taps, channels)
@@ -133,20 +155,20 @@
         grads[span, :] = grad
         total = total + jnp.sum(grad.astype(F32), axis=0, keepdims=True)
     raw_bias[...] = jnp.broadcast_to(total, raw_bias.shape)
-    raw_up[...] = lax.dot_general(
-        act[...], cot_patch[...].reshape(pixels, taps), (((0,), (0,)), ((), ())),
-        preferred_element_type=F32,
-    )
-    raw_down[...] = lax.dot_general(
-        feat_patch[...].reshape(pixels, taps), grads[...], (((0,), (0,)), ((), ())),
-        preferred_element_type=F32,
-    )
-
-
-def rim_patches(row_part, firsts, top, left, corner, out, line, column):
-    half_cols, taps = row_part.shape
+    core = lax.axis_index("narrow")
+
+    @pl.when(core == 0)
+    def _():
+        raw_other[...] = taps_of(False, cot_patch[...].reshape(pixels, taps), act[...])
+
+    @pl.when(core != 0)
+    def _():
+        raw_other[...] = taps_of(True, feat_patch[...].reshape(pixels, taps), grads[...])
+
+
+def rim_patches(patch, firsts, top, left, corner, out, line, column):
+    half_rows, half_cols, taps = patch.shape
     channels = taps // 9
-    half_rows = left.shape[0] // 2
     above = lax.axis_index("wide") > 0
     aside = lax.axis_index("narrow") > 0
     line[0:8, :] = if_any(above & aside, corner[...].astype(F32))
@@ -156,7 +178,7 @@
     for col in range(2):
         column[1 + col, 0:8, :] = jnp.zeros((8, channels), F32)
         column[1 + col, 8:, :] = firsts[col].astype(F32)
-    out[0:half_cols, 3 * channels :] = row_part[:, 3 * channels :]
+    out[0:half_cols, 3 * channels :] = patch[0, :, 3 * channels :]
     first = lax.broadcasted_iota(jnp.int32, (half_cols, channels), 0) == 0
     for off in range(3):
         out[0:half_cols, off * channels : (off + 1) * channels] = line[
@@ -169,21 +191,24 @@
             ].astype(BF16)
     for off in (1, 2):
         lanes = slice(3 * off * channels, (3 * off + 1) * channels)
-        rest = row_part[:, lanes].astype(F32)
+        rest = patch[0, :, lanes].astype(F32)
         halo = jnp.broadcast_to(column[0, 7 + off : 8 + off, :], rest.shape)
         out[0:half_cols, lanes] = jnp.where(first, halo, rest).astype(BF16)
 
 
 def rim_body(
-    feat_row, cot_row, feat_firsts, cot_firsts, top, left, corner, raw_up, raw_down, raw_bias,
+    feat_patch, cot_patch, feat_firsts, cot_firsts, top, left, corner, raw_other, raw_bias,
     up_mat, down_weight, down_bias,
-    rim_grads, mine, other, bias_part,
-    feat_rim, cot_rim, line, column,
+    rim_grads, feat_rim, cot_rim, rim_act, rim_masked, other_a, other_b, bias_part,
+    line, column,
 ):
-    half_cols, taps = feat_row.shape
+    _, half_cols, taps = feat_patch.shape
     channels = taps // 9
-    rim_patches(feat_row, feat_firsts, top.at[0], left.at[0], corner.at[0], feat_rim, line, column)
-    rim_patches(cot_row, cot_firsts, top.at[1], left.at[1], corner.at[1], cot_rim, line, column)
+    half = taps // 2
+    rim_patches(
+        feat_patch, feat_firsts, top.at[0], left.at[0], corner.at[0], feat_rim, line, column
+    )
+    rim_patches(cot_patch, cot_firsts, top.at[1], left.at[1], corner.at[1], cot_rim, line, column)
     pre = jnp.dot(
         feat_rim[...], down_weight[...].reshape(taps, channels), preferred_element_type=F32
     ) + down_bias[...].reshape(1, channels)
@@ -194,34 +219,51 @@
     once = lax.broadcasted_iota(jnp.int32, value.shape, 0) != half_cols
     act = if_any(once, value).astype(BF16)
     masked = if_any(once, grad).astype(BF16)
+    rim_act[...] = act
+    rim_masked[...] = masked
     full = grad.astype(BF16).astype(F32)
     rim_grads[...] = jnp.where(once, full, jnp.broadcast_to(full[0:1], full.shape)).astype(BF16)
     total = raw_bias[0:1, :] + jnp.sum(masked.astype(F32), axis=0, keepdims=True)
     coarse = total.astype(BF16)
     fine = (total - coarse.astype(F32)).astype(BF16)
     bias_part[...] = jnp.broadcast_to(coarse.astype(F32) + fine.astype(F32), bias_part.shape)
-    put_side(other, taps, coarse, fine)
-    more_up = lax.dot_general(
-        act, cot_rim[...], (((0,), (0,)), ((), ())), preferred_element_type=F32
-    )
-    more_down = lax.dot_general(
-        feat_rim[...], masked, (((0,), (0,)), ((), ())), preferred_element_type=F32
-    )
+    put_side(other_a, half, coarse, fine)
     core = lax.axis_index("narrow")
+
+    def give(more):
+        other_a[0:half, :] = (raw_other[0:half, :] + more[0:half]).astype(BF16)
+        other_b[...] = (raw_other[half:, :] + more[half:]).astype(BF16)
 
     @pl.when(core == 0)
     def _():
-        mine[...] = raw_down[...] + more_down
-        for tap in range(9):
-            span = slice(tap * channels, (tap + 1) * channels)
-            other[span, :] = (raw_up[:, span] + more_up[:, span]).astype(BF16)
+        give(taps_of(False, cot_rim[...], act))
 
     @pl.when(core != 0)
     def _():
-        other[0:taps, :] = (raw_down[...] + more_down).astype(BF16)
-        for tap in range(9):
-            span = slice(tap * channels, (tap + 1) * channels)
-            mine[span, :] = raw_up[:, span] + more_up[:, span]
+        give(taps_of(True, feat_rim[...], masked))
+
+
+def mine_body(
+    feat_patch, cot_patch, act, grads, feat_rim, cot_rim, rim_act, rim_masked, mine_a, mine_b
+):
+    half_rows, half_cols, taps = feat_patch.shape
+    pixels = half_rows * half_cols
+    half = taps // 2
+    core = lax.axis_index("narrow")
+
+    def keep(which, patch, values, rim_patch, rim_values):
+        total = taps_of(which, patch[...].reshape(pixels, taps), values[...])
+        total = total + taps_of(which, rim_patch[...], rim_values[...])
+        mine_a[...] = total[0:half]
+        mine_b[...] = total[half:]
+
+    @pl.when(core == 0)
+    def _():
+        keep(True, feat_patch, grads, feat_rim, rim_masked)
+
+    @pl.when(core != 0)
+    def _():
+        keep(False, cot_patch, act, cot_rim, rim_act)
 
 
 def put_side(out, at, coarse, fine):
@@ -256,13 +298,6 @@
     away = pl.ds(pl.multiple_of(base + (1 - bit) * half, 16), half)
     send[0:half, :] = (held[away, :] + got[away, :].astype(F32)).astype(BF16)
     keep[...] = held[near, :] + got[near, :].astype(F32)
-
-
-def first_body(positions, held, got, bias_in, keep_a, send_a, keep_b, send_b, bias_out):
-    size = held.shape[0] // 2
-    split(positions[0], held, got, 0, size, keep_a, send_a)
-    split(positions[1], held, got, size, size, keep_b, send_b)
-    joined_bias(bias_in, got, 2 * size, bias_out, send_a, size // 2)
 
 
 def halve_body(position, held, got, *rest):
@@ -294,41 +329,49 @@
     out[pl.ds(pl.multiple_of(base + (1 - bit) * size, 16), size), :] = got[...]
 
 
-def both_body(positions, held_a, got_a, held_b, got_b, out):
-    place(positions[0], held_a, got_a, out, 0)
-    place(positions[1], held_b, got_b, out, 2 * held_a.shape[0])
-
-
-def final_body(held, got, bias_in, down, up, bias_out):
-    channels = held.shape[1]
+def final_body(
+    positions, held_a, got_a, held_b, got_b, far_held_a, far_got_a, far_held_b, far_got_b, bias_in,
+    down, up, bias_out, mine, far, sems,
+):
+    channels = held_a.shape[1]
     core = lax.axis_index("narrow")
-    squares = jnp.zeros((channels, channels), F32)
-    for ref in (held, got):
-        part = jnp.zeros((channels, channels), F32)
-        for tap in range(9):
-            block = ref[tap * channels : (tap + 1) * channels, :].astype(F32)
-            part = part + block * block
-        squares = squares + part
+    bit_a, bit_b = bit_of(positions[0]), bit_of(positions[1])
+    def square(ref):
+        block = ref[...].astype(F32).reshape(-1, 8, channels)
+        return jnp.sum(block * block, axis=0)
+
+    def pair(one, two, three, four):
+        return (square(one) + square(two)) + (square(three) + square(four))
+
+    squares = pair(held_a, got_a, held_b, got_b) + pair(
+        far_held_a, far_got_a, far_held_b, far_got_b
+    )
     bias = bias_in[0:1, :]
     total = jnp.sum(jnp.sum(squares, axis=0, keepdims=True) + bias * bias, axis=1, keepdims=True)
     clip_level = 0.5 * float(18 * channels * channels + channels) ** 0.5
     factor = jnp.minimum(1.0, clip_level / jnp.sqrt(total))
     factor = jnp.broadcast_to(factor, (1, channels))
     bias_out[...] = bias * factor
-
-    def write(down_ref, up_ref):
-        for tap in range(9):
-            rows = slice(tap * channels, (tap + 1) * channels)
-            down[tap] = down_ref[rows, :].astype(F32) * factor
-            up[tap] = up_ref[rows, :].astype(F32) * factor
-
-    @pl.when(core == 0)
-    def _():
-        write(held, got)
-
-    @pl.when(core != 0)
-    def _():
-        write(got, held)
+    spots = (bit_a, 1 - bit_a, 2 + bit_b, 3 - bit_b)
+    for at, (near_ref, far_ref) in enumerate(
+        ((held_a, far_held_a), (got_a, far_got_a), (held_b, far_held_b), (got_b, far_got_b))
+    ):
+        mine[at] = near_ref[...].astype(F32) * factor
+        far[at] = far_ref[...].astype(F32) * factor
+
+        @pl.when(core == 0)
+        def _():
+            pltpu.make_async_copy(mine.at[at], down.at[spots[at]], sems.at[at]).start()
+            pltpu.make_async_copy(far.at[at], up.at[spots[at]], sems.at[4 + at]).start()
+
+        @pl.when(core != 0)
+        def _():
+            pltpu.make_async_copy(mine.at[at], up.at[spots[at]], sems.at[at]).start()
+            pltpu.make_async_copy(far.at[at], down.at[spots[at]], sems.at[4 + at]).start()
+
+    for at in range(4):
+        pltpu.make_async_copy(mine.at[at], down.at[spots[at]], sems.at[at]).wait()
+        pltpu.make_async_copy(far.at[at], up.at[spots[at]], sems.at[4 + at]).wait()
 
 
 def feature_body(grads, rim_grads, right, below, cot, down_weight, out, wide, pairs, near_mat, low_mat, woven):
@@ -405,9 +448,14 @@
     half_rows, half_cols = tile_rows // 2, tile_cols // 2
     pixels = half_rows * half_cols
     taps = 9 * channels
-    rows, cols, corner = call(
+    feat_near, cot_near, down_near, up_near, bias_near, rows, cols, corner = call(
         edge_body,
         (
+            vm(features.shape, BF16),
+            vm(features.shape, BF16),
+            vm(down_weight.shape, BF16),
+            vm(up_weight.shape, BF16),
+            vm((1, channels), F32),
             vm((2, tile_cols, channels), BF16),
             vm((2, tile_rows, channels), BF16),
             vm((2, 8, channels), BF16),
@@ -415,107 +463,107 @@
         scratch=[
             pltpu.VMEM((2, tile_rows, 16, channels), BF16),
             pltpu.VMEM((tile_rows * 16, channels), F32),
-            pltpu.SemaphoreType.DMA((4,)),
+            pltpu.SemaphoreType.DMA((9,)),
         ],
-        in_specs=[ANY, ANY],
+        in_specs=[ANY] * 5,
         nbytes=1 << 19,
         name="edges",
-        far=(0, 1),
+        far=(0, 1, 2, 3, 4),
         room=8,
-    )(features, cotangent)
+    )(features, cotangent, down_weight, up_weight, down_bias.reshape(1, channels))
     from_above = turned(rows, "wide", 1)
     from_corner = turned_both(corner)
     from_left = turned(cols, "narrow", 1)
-    out_of_interior = (
-        vm((pixels, channels), BF16),
-        vm((channels, taps), F32),
-        vm((taps, channels), F32),
-        vm((8, channels), F32),
-        vm((half_cols, taps), BF16),
-        vm((half_cols, taps), BF16),
-        vm((2, tile_rows, channels), BF16),
-        vm((2, tile_rows, channels), BF16),
-        vm((channels, taps), BF16),
-    )
+    patches = vm((half_rows, half_cols, taps), BF16)
+    firsts = vm((2, tile_rows, channels), BF16)
     (
-        grads, raw_up, raw_down, raw_bias, feat_row, cot_row, feat_firsts, cot_firsts, up_mat
+        feat_patch, cot_patch, act, grads, raw_other, raw_bias, feat_firsts, cot_firsts, up_mat
     ) = call(
         interior_body,
-        out_of_interior,
+        (
+            patches,
+            patches,
+            vm((pixels, channels), BF16),
+            vm((pixels, channels), BF16),
+            vm((taps, channels), F32),
+            vm((8, channels), F32),
+            firsts,
+            firsts,
+            vm((channels, taps), BF16),
+        ),
         scratch=[
-            pltpu.VMEM((half_rows, half_cols, taps), BF16),
-            pltpu.VMEM((half_rows, half_cols, taps), BF16),
-            pltpu.VMEM((pixels, channels), BF16),
             pltpu.VMEM((half_rows, 2, tile_cols + 8, channels), F32),
             pltpu.VMEM((tile_rows * 16, channels), F32),
         ],
         n_in=5,
-        flops=8 * pixels * taps * channels,
+        flops=6 * pixels * taps * channels,
         nbytes=6 << 20,
         name="interior",
-        near=(0, 1),
-        room=16,
-    )(features, cotangent, down_weight, down_bias, up_weight)
-    from_above, from_corner, from_left, raw_up = lax.optimization_barrier(
-        (from_above, from_corner, from_left, raw_up)
-    )
-    rim_grads, mine, other, bias_sum = call(
+        near=(0, 1, 2, 3, 4),
+        room=12,
+    )(feat_near, cot_near, down_near, bias_near, up_near)
+    from_above, from_corner, from_left, raw_other = lax.optimization_barrier(
+        (from_above, from_corner, from_left, raw_other)
+    )
+    pieces = half_cols + half_rows
+    rim_grads, feat_rim, cot_rim, rim_act, rim_masked, other_a, other_b, bias_sum = call(
         rim_body,
         (
-            vm((half_cols + half_rows, channels), BF16),
-            vm((taps, channels), F32),
-            vm((taps + SIDE, channels), BF16),
+            vm((pieces, channels), BF16),
+            vm((pieces, taps), BF16),
+            vm((pieces, taps), BF16),
+            vm((pieces, channels), BF16),
+            vm((pieces, channels), BF16),
+            vm((taps // 2 + SIDE, channels), BF16),
+            vm((taps // 2, channels), BF16),
             vm((8, channels), F32),
         ),
         scratch=[
-            pltpu.VMEM((half_cols + half_rows, taps), BF16),
-            pltpu.VMEM((half_cols + half_rows, taps), BF16),
             pltpu.VMEM((tile_cols + 8, channels), F32),
             pltpu.VMEM((3, tile_rows + 8, channels), F32),
         ],
-        n_in=13,
+        n_in=12,
         flops=1 << 26,
         nbytes=3 << 20,
         name="rim",
-        near=tuple(range(11)),
-        room=16,
+        near=tuple(range(12)),
+        room=8,
     )(
-        feat_row, cot_row, feat_firsts, cot_firsts, from_above, from_left, from_corner,
-        raw_up, raw_down, raw_bias, up_mat, down_weight, down_bias,
-    )
-
-    got = turned(other, "narrow", 1)
+        feat_patch, cot_patch, feat_firsts, cot_firsts, from_above, from_left, from_corner,
+        raw_other, raw_bias, up_mat, down_near, bias_near,
+    )
+    got_a = turned(other_a, "narrow", 1)
+    got_b = turned(other_b, "narrow", 1)
+    mine_a, mine_b = call(
+        mine_body,
+        (vm((taps // 2, channels), F32), vm((taps // 2, channels), F32)),
+        n_in=8,
+        flops=2 * pixels * taps * channels,
+        nbytes=3 << 20,
+        name="mine",
+        near=tuple(range(8)),
+        room=12,
+    )(feat_patch, cot_patch, act, grads, feat_rim, cot_rim, rim_act, rim_masked)
     from_right = turned(rim_grads[half_cols:], "narrow", -1)
-    got, from_right = lax.optimization_barrier((got, from_right))
-    from_below = turned(jnp.concatenate([rim_grads[:half_cols], from_right[:8]], axis=0), "wide", -1)
+    got_a, mine_a, mine_b = lax.optimization_barrier((got_a, mine_a, mine_b))
+    got_b, from_right = lax.optimization_barrier((got_b, from_right))
+    from_below = turned(
+        jnp.concatenate([rim_grads[:half_cols], from_right[:8]], axis=0), "wide", -1
+    )
 
     bits = lax.axis_size("wide").bit_length() - 1
     order_a = list(range(bits))
     order_b = order_a[1::-1] + order_a[2:]
     halvings = 1 if bits <= 3 else 2
-    half = taps // 4
-    held_a, send_a, held_b, send_b, bias_sum = call(
-        functools.partial(first_body, (order_a[0], order_b[0])),
-        (
-            vm((half, channels), F32),
-            vm((half + SIDE, channels), BF16),
-            vm((half, channels), F32),
-            vm((half, channels), BF16),
-            vm((8, channels), F32),
-        ),
-        n_in=3,
-        nbytes=taps * channels * 6,
-        name="first",
-        near=(0, 1, 2),
-    )(mine, got, bias_sum)
-    got_a = traded(send_a, order_a[0])
-    got_b = traded(send_b, order_b[0])
-    for step in range(1, halvings):
+    half = taps // 2
+    held_a, held_b = mine_a, mine_b
+    for step in range(halvings):
         half //= 2
         held_a, send_a, bias_sum = call(
             functools.partial(halve_body, order_a[step]),
             (vm((half, channels), F32), vm((half + SIDE, channels), BF16), vm((8, channels), F32)),
             n_in=3,
+            nbytes=half * channels * 12,
             name="halve",
             near=(0, 1, 2),
         )(held_a, got_a, bias_sum)
@@ -523,6 +571,7 @@
             functools.partial(halve_body, order_b[step]),
             (vm((half, channels), F32), vm((half, channels), BF16)),
             n_in=2,
+            nbytes=half * channels * 12,
             name="halve",
             near=(0, 1),
         )(held_b, got_b)
@@ -542,9 +591,9 @@
         flops=2 * pixels * 6 * 2 * channels * channels,
         nbytes=3 << 20,
         name="feature",
-        near=(0, 1, 2, 3),
+        near=(0, 1, 2, 3, 4, 5),
         room=16,
-    )(grads, rim_grads, from_right, from_below, cotangent, down_weight)
+    )(grads, rim_grads, from_right, from_below, cot_near, down_near)
     for step in range(halvings, bits + 1):
         side = SIDE if step < bits else 0
         held_a, bias_sum = call(
@@ -566,13 +615,13 @@
         if step < bits:
             got_a = traded(held_a, order_a[step])
             got_b = traded(held_b, order_b[step])
+            if step == halvings:
+                got_b, from_below = lax.optimization_barrier((got_b, from_below))
             if step == bits - 1:
-                got_a, from_below = lax.optimization_barrier((got_a, from_below))
+                got_b, feature_grad = lax.optimization_barrier((got_b, feature_grad))
     for step in reversed(range(halvings)):
         got_a = traded(held_a, order_a[step])
         got_b = traded(held_b, order_b[step])
-        if step == 0:
-            got_a, feature_grad = lax.optimization_barrier((got_a, feature_grad))
         if step:
             half *= 2
             held_a = call(
@@ -589,28 +638,28 @@
                 name="place",
                 near=(0, 1),
             )(held_b, got_b)
-    block = call(
-        functools.partial(both_body, (order_a[0], order_b[0])),
-        vm((taps, channels), BF16),
-        n_in=4,
-        nbytes=taps * channels * 4,
-        name="both",
-        near=(0, 1, 2, 3),
-    )(held_a, got_a, held_b, got_b)
-    got = turned(block, "narrow", 1)
+    blocks = (held_a, got_a, held_b, got_b)
+    far_blocks = [turned(block, "narrow", 1) for block in blocks]
+    size = taps // 4
     down, up, bias_grad = call(
-        final_body,
+        functools.partial(final_body, (order_a[0], order_b[0])),
         (
-            sds((9, channels, channels), F32),
-            sds((9, channels, channels), F32),
+            sds((4, size, channels), F32),
+            sds((4, size, channels), F32),
             sds((1, channels), F32),
         ),
-        n_in=3,
+        scratch=[
+            pltpu.VMEM((4, size, channels), F32),
+            pltpu.VMEM((4, size, channels), F32),
+            pltpu.SemaphoreType.DMA((8,)),
+        ],
+        n_in=9,
         nbytes=12 * taps * channels,
         name="final",
-        near=(0, 1, 2),
+        near=tuple(range(9)),
         room=8,
-    )(block, got, bias_sum)
+        out_specs=(ANY, ANY, VM),
+    )(*blocks, *far_blocks, bias_sum)
     shape = (3, 3, channels, channels)
     return (feature_grad, down.reshape(shape), up.reshape(shape), bias_grad.reshape(channels))
 

time: 40.7 us -> 41.1 us (level)
  waiting for transfers between devices: 10.7 us -> 13.3 us
  starting transfers between devices: 19.3 us -> 16.9 us
  Pallas kernels: 8.45 us -> 9.95 us
  local copies, waits for them, and re-layouts: 1.3 us -> 0.01 us
    ppermute x8, waiting for transfers between devices: 6.26 us -> 9.93 us  [traded(): lax.ppermute(value, 'wide', [(at, at ^ 1 << position) for at in range(cou...]
    ppermute x8, starting transfers between devices: 10.9 us -> 8.13 us  [traded(): lax.ppermute(value, 'wide', [(at, at ^ 1 << position) for at in range(cou...]
    pallas_call x13 -> x14, Pallas kernels: 8.45 us -> 9.95 us  [run(): return kernel(*placed)]
    unnamed x14 -> x0, local copies, waits for them, and re-layouts: 1.25 us -> none
    ppermute x6 -> x10, waiting for transfers between devices: 4.44 us -> 3.36 us  [turned(): lax.ppermute(value, axis, [(at, (at + steps) % count) for at in range(cou...]
    ppermute x6 -> x10, starting transfers between devices: 5.93 us -> 6.31 us  [turned(): lax.ppermute(value, axis, [(at, (at + steps) % count) for at in range(cou...]
  transfers between devices with their start and end apart: 15 -> 19, of which waited for: 9 -> 9; matrix products, arithmetic and copies ran while one was open for 0% -> 0% of each run, Pallas kernels for 12% -> 14%
where the time goes in v5:
time: 41.1 us; the launch traced here: 40.9 us
  starting transfers between devices  16.9 us (41%)
  waiting for transfers between devices  13.3 us (32%)
  Pallas kernels  9.95 us (24%)
  between operations  0.74 us (2%)
    pallas_call x14, Pallas kernels, run(): return kernel(*placed)  9.95 us
    ppermute x8, waiting for transfers between devices, traded(): lax.ppermute(value, 'wide', [(at, at ^ 1 << position) for at in range(cou...  9.93 us
    ppermute x8, starting transfers between devices, traded(): lax.ppermute(value, 'wide', [(at, at ^ 1 << position) for at in range(cou...  8.13 us
    ppermute x10, starting transfers between devices, turned(): lax.ppermute(value, axis, [(at, (at + steps) % count) for at in range(cou...  6.31 us
    ppermute x10, waiting for transfers between devices, turned(): lax.ppermute(value, axis, [(at, (at + steps) % count) for at in range(cou...  3.36 us
    ppermute x1, starting transfers between devices, turned_both(): return lax.ppermute(value, ('wide', 'narrow'), pairs)  2.46 us
  transfers between devices with their start and end apart: 19, of which 9 were waited for; matrix products, arithmetic and copies ran while one was open for 0% of the time, Pallas kernels for 14%

profile of v5, /device:TPU:0, one launch (start us, length us, event | category | flops | bytes accessed | tf_op | source)
XLA Modules:
  0.0 40.9 jit_solution(452271037821104605)
XLA Ops:
  0.6 2.0 %edges.1 = (bf16[64,64,128]{2,1,0:T(8,128)(2,1)S(1)}, bf16[64,64,128]{2,1,0:T(8,128)(2,1)S(1)}, bf16[3,3,128,128]{3,2,1,0:T(8,128)(2,1)S(1)}, bf16[3,3,128,128]{...) custom-call(bf16[64,64,128]{2,1,0:T(8,128)(2,1)} %feat.1, ...), custom_call_target="tpu_custom_call" | custom-call | bytes 524288 | tf_op jit(solution)/shard_map/edges/pallas_call | solution.py:36
  2.6 2.5 %collective-permute-start.1 = (bf16[2,8,128]{2,1,0:T(8,128)(2,1)S(1)}, bf16[2,8,128]{2,1,0:T(8,128)(2,1)S(1)}, u32[]{:S(2)}, u32[]{:S(2)}) collective-permute-start(bf16[2,8,128]{2,1,0:T(8,128)(2,1)S(1)} %get-tuple-element.67), channel_id=1, source_target_pairs={{0,3},{1,2},{2,5},{3,4},{4,7},{5,6},{6,9},{7,8},{8,11},{9,10},{10,... | collective-permute-start | bytes 12296 | tf_op jit(solution)/shard_map/ppermute | solution.py:438
  5.1 1.5 %collective-permute-start = (bf16[2,64,128]{2,1,0:T(8,128)(2,1)S(1)}, bf16[2,64,128]{2,1,0:T(8,128)(2,1)S(1)}, u32[]{:S(2)}, u32[]{:S(2)}) collective-permute-start(bf16[2,64,128]{2,1,0:T(8,128)(2,1)S(1)} %get-tuple-element.66), channel_id=1, source_target_pairs={{0,2},{2,4},{4,6},{6,8},{8,10},{10,12},{12,14},{14,0},{1,3},{3,5},... | collective-permute-start | bytes 98312 | tf_op jit(solution)/shard_map/ppermute | solution.py:428
  7.0 2.7 %interior.1 = (bf16[32,32,1152]{2,1,0:T(8,128)(2,1)S(1)}, bf16[32,32,1152]{2,1,0:T(8,128)(2,1)S(1)}, bf16[1024,128]{1,0:T(8,128)(2,1)S(1)}, bf16[1024,128]{1,0:T...) custom-call(bf16[64,64,128]{2,1,0:T(8,128)(2,1)S(1)} %get-tuple-elem, ...), custom_call_target="tpu_custom_call" | custom-call | flops 905969664 | bytes 6291456 | tf_op jit(solution)/shard_map/interior/pallas_call | solution.py:36
  9.7 2.0 %collective-permute-done.top = bf16[2,64,128]{2,1,0:T(8,128)(2,1)S(1)} collective-permute-done((bf16[2,64,128]{2,1,0:T(8,128)(2,1)S(1)}, bf16[2,64,128]{2,1,0:T(8,128)(2,1)S(1)}, u32[]{:S(2)}, u32[]{:S(2)}) %collective-permute-start) | collective-permute-done | bytes 32800 | tf_op jit(solution)/shard_map/ppermute | solution.py:428
  11.7 0.5 %rim.1 = (bf16[64,128]{1,0:T(8,128)(2,1)S(1)}, bf16[64,1152]{1,0:T(8,128)(2,1)S(1)}, bf16[64,1152]{1,0:T(8,128)(2,1)S(1)}, bf16[64,128]{1,0:T(8,128)(2,1)S(1)}, ...) custom-call(bf16[32,32,1152]{2,1,0:T(8,128)(2,1)S(1)} %get-tuple-ele, ...), custom_call_target="tpu_custom_call" | custom-call | flops 67108864 | bytes 3145728 | tf_op jit(solution)/shard_map/rim/pallas_call | solution.py:36
  12.9 0.9 %mine.1 = (f32[576,128]{1,0:T(8,128)S(1)}, f32[576,128]{1,0:T(8,128)S(1)}) custom-call(bf16[32,32,1152]{2,1,0:T(8,128)(2,1)S(1)} %get-tuple-element.62.feat_patch, bf16[32,32,1152]{2,1,0:T(8,128)(2,1)S(1)} %get-tuple-element.63.cot_patch, bf16[1024,128]{1,0:T(8,128)(2,1)S(1)} %get-tuple-element.77.act, bf16[1024,128]{1,0:T(8,128)(2,1)S(1)} %get-tuple-element.78.grads, ...), custom_call_target="tpu_custom_call" | custom-call | flops 301989888 | bytes 3145728 | tf_op jit(solution)/shard_map/mine/pallas_call | solution.py:36
  14.1 1.4 %collective-permute-start.6 = (bf16[288,128]{1,0:T(8,128)(2,1)S(1)}, bf16[288,128]{1,0:T(8,128)(2,1)S(1)}, u32[]{:S(2)}, u32[]{:S(2)}) collective-permute-start(bf16[288,128]{1,0:T(8,128)(2,1)S(1)} %get-tuple-element.90), channel_id=1, source_target_pairs={{0,4},{2,6},{4,0},{6,2},{8,12},{10,14},{12,8},{14,10},{1,5},{3,7},... | collective-permute-start | bytes 221192 | tf_op jit(solution)/shard_map/ppermute | solution.py:443
  15.6 3.1 %collective-permute-done.6.got = bf16[288,128]{1,0:T(8,128)(2,1)S(1)} collective-permute-done((bf16[288,128]{1,0:T(8,128)(2,1)S(1)}, bf16[288,128]{1,0:T(8,128)(2,1)S(1)}, u32[]{:S(2)}, u32[]{:S(2)}) %collective-permute-start.6) | collective-permute-done | bytes 73760 | tf_op jit(solution)/shard_map/ppermute | solution.py:443
  18.7 1.9 %collective-permute-start.7 = (bf16[288,128]{1,0:T(8,128)(2,1)S(1)}, bf16[288,128]{1,0:T(8,128)(2,1)S(1)}, u32[]{:S(2)}, u32[]{:S(2)}) collective-permute-start(bf16[288,128]{1,0:T(8,128)(2,1)S(1)} %whole.6.held), channel_id=1, source_target_pairs={{0,2},{2,0},{4,6},{6,4},{8,10},{10,8},{12,14},{14,12},{1,3},{3,1},... | collective-permute-start | bytes 221192 | tf_op jit(solution)/shard_map/ppermute | solution.py:443
  20.9 3.2 %collective-permute-start.8 = (bf16[40,128]{1,0:T(8,128)(2,1)S(1)}, bf16[40,128]{1,0:T(8,128)(2,1)S(1)}, u32[]{:S(2)}, u32[]{:S(2)}) collective-permute-start(bf16[40,128]{1,0:T(8,128)(2,1)S(1)} %pad_maximum_fusion), channel_id=1, source_target_pairs={{0,14},{2,0},{4,2},{6,4},{8,6},{10,8},{12,10},{14,12},{1,15},{3,1}... | collective-permute-start | bytes 30728 | tf_op jit(solution)/shard_map/ppermute | solution.py:428
  24.1 1.1 %collective-permute-done.11.got = bf16[304,128]{1,0:T(8,128)(2,1)S(1)} collective-permute-done((bf16[304,128]{1,0:T(8,128)(2,1)S(1)}, bf16[304,128]{1,0:T(8,128)(2,1)S(1)}, u32[]{:S(2)}, u32[]{:S(2)}) %collective-permute-start.11) | collective-permute-done | bytes 77856 | tf_op jit(solution)/shard_map/ppermute | solution.py:443
  25.2 1.0 %collective-permute-start.12 = (bf16[304,128]{1,0:T(8,128)(2,1)S(1)}, bf16[304,128]{1,0:T(8,128)(2,1)S(1)}, u32[]{:S(2)}, u32[]{:S(2)}) collective-permute-start(bf16[304,128]{1,0:T(8,128)(2,1)S(1)} %get-tuple-element.102.held), channel_id=1, source_target_pairs={{0,8},{2,10},{4,12},{6,14},{8,0},{10,2},{12,4},{14,6},{1,9},{3,11}... | collective-permute-start | bytes 233480 | tf_op jit(solution)/shard_map/ppermute | solution.py:443
  26.2 2.0 %collective-permute-start.9 = (bf16[288,128]{1,0:T(8,128)(2,1)S(1)}, bf16[288,128]{1,0:T(8,128)(2,1)S(1)}, u32[]{:S(2)}, u32[]{:S(2)}) collective-permute-start(bf16[288,128]{1,0:T(8,128)(2,1)S(1)} %whole.7.held), channel_id=1, source_target_pairs={{0,8},{2,10},{4,12},{6,14},{8,0},{10,2},{12,4},{14,6},{1,9},{3,11}... | collective-permute-start | bytes 221192 | tf_op jit(solution)/shard_map/ppermute | solution.py:443
  28.2 1.8 %feature.1 = bf16[64,64,128]{2,1,0:T(8,128)(2,1)} custom-call(bf16[1024,128]{1,0:T(8,128)(2,1)S(1)} %get-tuple-element.78.grads, bf16[64,128]{1,0:T(8,128)(2,1)S(1)} %get-tuple-element.87.rim_grads, bf16[32,128]{1,0:T(8,128)(2,1)S(1)} %collective-permute-done.5.right, bf16[40,128]{1,0:T(8,128)(2,1)S(1)} %collective-permute-done.8.below, ...), custom_call_target="tpu_custom_call" | custom-call | flops 402653184 | bytes 3145728 | tf_op jit(solution)/shard_map/feature/pallas_call | solution.py:36
  30.0 2.8 %collective-permute-done.9.got = bf16[288,128]{1,0:T(8,128)(2,1)S(1)} collective-permute-done((bf16[288,128]{1,0:T(8,128)(2,1)S(1)}, bf16[288,128]{1,0:T(8,128)(2,1)S(1)}, u32[]{:S(2)}, u32[]{:S(2)}) %collective-permute-start.9) | collective-permute-done | bytes 73760 | tf_op jit(solution)/shard_map/ppermute | solution.py:443
  32.8 0.6 %collective-permute-start.14 = (bf16[288,128]{1,0:T(8,128)(2,1)S(1)}, bf16[288,128]{1,0:T(8,128)(2,1)S(1)}, u32[]{:S(2)}, u32[]{:S(2)}) collective-permute-start(bf16[288,128]{1,0:T(8,128)(2,1)S(1)} %whole.11.held_b), channel_id=1, source_target_pairs={{0,4},{2,6},{4,0},{6,2},{8,12},{10,14},{12,8},{14,10},{1,5},{3,7},... | collective-permute-start | bytes 221192 | tf_op jit(solution)/shard_map/ppermute | solution.py:443
  33.4 0.9 %collective-permute-start.13 = (bf16[288,128]{1,0:T(8,128)(2,1)S(1)}, bf16[288,128]{1,0:T(8,128)(2,1)S(1)}, u32[]{:S(2)}, u32[]{:S(2)}) collective-permute-start(bf16[288,128]{1,0:T(8,128)(2,1)S(1)} %get-tuple-element.104.held_a), channel_id=1, source_target_pairs={{0,2},{2,0},{4,6},{6,4},{8,10},{10,8},{12,14},{14,12},{1,3},{3,1},... | collective-permute-start | bytes 221192 | tf_op jit(solution)/shard_map/ppermute | solution.py:443
  34.3 0.5 %collective-permute-start.15 = (bf16[288,128]{1,0:T(8,128)(2,1)S(1)}, bf16[288,128]{1,0:T(8,128)(2,1)S(1)}, u32[]{:S(2)}, u32[]{:S(2)}) collective-permute-start(bf16[288,128]{1,0:T(8,128)(2,1)S(1)} %get-tuple-element.104.held_a), channel_id=1, source_target_pairs={{0,1},{1,0},{2,3},{3,2},{4,5},{5,4},{6,7},{7,6},{8,9},{9,8},{10,11... | collective-permute-start | bytes 221192 | tf_op jit(solution)/shard_map/ppermute | solution.py:428
  34.8 2.4 %collective-permute-done.14.got_b = bf16[288,128]{1,0:T(8,128)(2,1)S(1)} collective-permute-done((bf16[288,128]{1,0:T(8,128)(2,1)S(1)}, bf16[288,128]{1,0:T(8,128)(2,1)S(1)}, u32[]{:S(2)}, u32[]{:S(2)}) %collective-permute-start.14) | collective-permute-done | bytes 73760 | tf_op jit(solution)/shard_map/ppermute | solution.py:443
  37.2 0.6 %collective-permute-done.13.got_a = bf16[288,128]{1,0:T(8,128)(2,1)S(1)} collective-permute-done((bf16[288,128]{1,0:T(8,128)(2,1)S(1)}, bf16[288,128]{1,0:T(8,128)(2,1)S(1)}, u32[]{:S(2)}, u32[]{:S(2)}) %collective-permute-start.13) | collective-permute-done | bytes 73760 | tf_op jit(solution)/shard_map/ppermute | solution.py:443
  37.8 0.7 %collective-permute-done.18.far_got_b = bf16[288,128]{1,0:T(8,128)(2,1)S(1)} collective-permute-done((bf16[288,128]{1,0:T(8,128)(2,1)S(1)}, bf16[288,128]{1,0:T(8,128)(2,1)S(1)}, u32[]{:S(2)}, u32[]{:S(2)}) %collective-permute-start.18) | collective-permute-done | bytes 73760 | tf_op jit(solution)/shard_map/ppermute | solution.py:428
  38.5 0.6 %collective-permute-done.16.far_got_a = bf16[288,128]{1,0:T(8,128)(2,1)S(1)} collective-permute-done((bf16[288,128]{1,0:T(8,128)(2,1)S(1)}, bf16[288,128]{1,0:T(8,128)(2,1)S(1)}, u32[]{:S(2)}, u32[]{:S(2)}) %collective-permute-start.16) | collective-permute-done | bytes 73760 | tf_op jit(solution)/shard_map/ppermute | solution.py:428
  39.1 1.8 %final.1 = (f32[4,288,128]{2,1,0:T(8,128)}, f32[4,288,128]{2,1,0:T(8,128)}, f32[1,128]{1,0:T(1,128)}) custom-call(bf16[288,128]{1,0:T(8,128)(2,1)S(1)} %get-tuple-element.104.held_a, bf16[288,128]{1,0:T(8,128)(2,1)S(1)} %collective-permute-done.13.got_a, bf16[288,128]{1,0:T(8,128)(2,1)S(1)} %whole.11.held_b, ...), custom_call_target="tpu_custom_call" | custom-call | bytes 1769472 | tf_op jit(solution)/shard_map/final/pallas_call | solution.py:36
  (31 shorter events, 1.7 us)
Async XLA Ops:
  2.6 7.1 %collective-permute-start.1 = (bf16[2,8,128]{2,1,0:T(8,128)(2,1)S(1)}, bf16[2,8,128]{2,1,0:T(8,128)(2,1)S(1)}, u32[]{:S(2)}, u32[]{:S(2)}) collective-permute-start(bf16[2,8,128]{2,1,0:T(8,128)(2,1)S(1)} %get-tuple-element.67), channel_id=1, source_target_pairs={{0,3},{1,2},{2,5},{3,4},{4,7},{5,6},{6,9},{7,8},{8,11},{9,10},{10,... | collective-permute-start | bytes 12296 | tf_op jit(solution)/shard_map/ppermute | solution.py:438
  5.1 6.7 %collective-permute-start = (bf16[2,64,128]{2,1,0:T(8,128)(2,1)S(1)}, bf16[2,64,128]{2,1,0:T(8,128)(2,1)S(1)}, u32[]{:S(2)}, u32[]{:S(2)}) collective-permute-start(bf16[2,64,128]{2,1,0:T(8,128)(2,1)S(1)} %get-tuple-element.66), channel_id=1, source_target_pairs={{0,2},{2,4},{4,6},{6,8},{8,10},{10,12},{12,14},{14,0},{1,3},{3,5},... | collective-permute-start | bytes 98312 | tf_op jit(solution)/shard_map/ppermute | solution.py:428
  6.6 5.1 %collective-permute-start.2 = (bf16[2,64,128]{2,1,0:T(8,128)(2,1)S(1)}, bf16[2,64,128]{2,1,0:T(8,128)(2,1)S(1)}, u32[]{:S(2)}, u32[]{:S(2)}) collective-permute-start(bf16[2,64,128]{2,1,0:T(8,128)(2,1)S(1)} %get-tuple-element.68), channel_id=1, source_target_pairs={{0,1},{1,0},{2,3},{3,2},{4,5},{5,4},{6,7},{7,6},{8,9},{9,8},{10,11... | collective-permute-start | bytes 98312 | tf_op jit(solution)/shard_map/ppermute | solution.py:428
  12.3 1.8 %collective-permute-start.4 = (bf16[576,128]{1,0:T(8,128)(2,1)S(1)}, bf16[576,128]{1,0:T(8,128)(2,1)S(1)}, u32[]{:S(2)}, u32[]{:S(2)}) collective-permute-start(bf16[576,128]{1,0:T(8,128)(2,1)S(1)} %get-tuple-element.86), channel_id=1, source_target_pairs={{0,1},{1,0},{2,3},{3,2},{4,5},{5,4},{6,7},{7,6},{8,9},{9,8},{10,11... | collective-permute-start | bytes 442376 | tf_op jit(solution)/shard_map/ppermute | solution.py:428
  12.4 1.6 %collective-permute-start.3 = (bf16[592,128]{1,0:T(8,128)(2,1)S(1)}, bf16[592,128]{1,0:T(8,128)(2,1)S(1)}, u32[]{:S(2)}, u32[]{:S(2)}) collective-permute-start(bf16[592,128]{1,0:T(8,128)(2,1)S(1)} %get-tuple-element.76), channel_id=1, source_target_pairs={{0,1},{1,0},{2,3},{3,2},{4,5},{5,4},{6,7},{7,6},{8,9},{9,8},{10,11... | collective-permute-start | bytes 454664 | tf_op jit(solution)/shard_map/ppermute | solution.py:428
  12.9 1.2 %collective-permute-start.5 = (bf16[32,128]{1,0:T(8,128)(2,1)S(1)}, bf16[32,128]{1,0:T(8,128)(2,1)S(1)}, u32[]{:S(2)}, u32[]{:S(2)}) collective-permute-start(bf16[32,128]{1,0:T(8,128)(2,1)S(1)} %get-tuple-element.111), channel_id=1, source_target_pairs={{0,1},{1,0},{2,3},{3,2},{4,5},{5,4},{6,7},{7,6},{8,9},{9,8},{10,11... | collective-permute-start | bytes 24584 | tf_op jit(solution)/shard_map/ppermute | solution.py:428
  14.0 6.6 %collective-permute-start.10 = (bf16[304,128]{1,0:T(8,128)(2,1)S(1)}, bf16[304,128]{1,0:T(8,128)(2,1)S(1)}, u32[]{:S(2)}, u32[]{:S(2)}) collective-permute-start(bf16[304,128]{1,0:T(8,128)(2,1)S(1)} %get-tuple-element.98), channel_id=1, source_target_pairs={{0,2},{2,0},{4,6},{6,4},{8,10},{10,8},{12,14},{14,12},{1,3},{3,1},... | collective-permute-start | bytes 233480 | tf_op jit(solution)/shard_map/ppermute | solution.py:443
  14.1 4.5 %collective-permute-start.6 = (bf16[288,128]{1,0:T(8,128)(2,1)S(1)}, bf16[288,128]{1,0:T(8,128)(2,1)S(1)}, u32[]{:S(2)}, u32[]{:S(2)}) collective-permute-start(bf16[288,128]{1,0:T(8,128)(2,1)S(1)} %get-tuple-element.90), channel_id=1, source_target_pairs={{0,4},{2,6},{4,0},{6,2},{8,12},{10,14},{12,8},{14,10},{1,5},{3,7},... | collective-permute-start | bytes 221192 | tf_op jit(solution)/shard_map/ppermute | solution.py:443
  18.7 7.5 %collective-permute-start.7 = (bf16[288,128]{1,0:T(8,128)(2,1)S(1)}, bf16[288,128]{1,0:T(8,128)(2,1)S(1)}, u32[]{:S(2)}, u32[]{:S(2)}) collective-permute-start(bf16[288,128]{1,0:T(8,128)(2,1)S(1)} %whole.6.held), channel_id=1, source_target_pairs={{0,2},{2,0},{4,6},{6,4},{8,10},{10,8},{12,14},{14,12},{1,3},{3,1},... | collective-permute-start | bytes 221192 | tf_op jit(solution)/shard_map/ppermute | solution.py:443
  20.7 4.5 %collective-permute-start.11 = (bf16[304,128]{1,0:T(8,128)(2,1)S(1)}, bf16[304,128]{1,0:T(8,128)(2,1)S(1)}, u32[]{:S(2)}, u32[]{:S(2)}) collective-permute-start(bf16[304,128]{1,0:T(8,128)(2,1)S(1)} %get-tuple-element.100.held), channel_id=1, source_target_pairs={{0,4},{2,6},{4,0},{6,2},{8,12},{10,14},{12,8},{14,10},{1,5},{3,7},... | collective-permute-start | bytes 233480 | tf_op jit(solution)/shard_map/ppermute | solution.py:443
  20.9 5.3 %collective-permute-start.8 = (bf16[40,128]{1,0:T(8,128)(2,1)S(1)}, bf16[40,128]{1,0:T(8,128)(2,1)S(1)}, u32[]{:S(2)}, u32[]{:S(2)}) collective-permute-start(bf16[40,128]{1,0:T(8,128)(2,1)S(1)} %pad_maximum_fusion), channel_id=1, source_target_pairs={{0,14},{2,0},{4,2},{6,4},{8,6},{10,8},{12,10},{14,12},{1,15},{3,1}... | collective-permute-start | bytes 30728 | tf_op jit(solution)/shard_map/ppermute | solution.py:428
  25.2 8.2 %collective-permute-start.12 = (bf16[304,128]{1,0:T(8,128)(2,1)S(1)}, bf16[304,128]{1,0:T(8,128)(2,1)S(1)}, u32[]{:S(2)}, u32[]{:S(2)}) collective-permute-start(bf16[304,128]{1,0:T(8,128)(2,1)S(1)} %get-tuple-element.102.held), channel_id=1, source_target_pairs={{0,8},{2,10},{4,12},{6,14},{8,0},{10,2},{12,4},{14,6},{1,9},{3,11}... | collective-permute-start | bytes 233480 | tf_op jit(solution)/shard_map/ppermute | solution.py:443
  26.2 6.6 %collective-permute-start.9 = (bf16[288,128]{1,0:T(8,128)(2,1)S(1)}, bf16[288,128]{1,0:T(8,128)(2,1)S(1)}, u32[]{:S(2)}, u32[]{:S(2)}) collective-permute-start(bf16[288,128]{1,0:T(8,128)(2,1)S(1)} %whole.7.held), channel_id=1, source_target_pairs={{0,8},{2,10},{4,12},{6,14},{8,0},{10,2},{12,4},{14,6},{1,9},{3,11}... | collective-permute-start | bytes 221192 | tf_op jit(solution)/shard_map/ppermute | solution.py:443
  32.8 4.4 %collective-permute-start.14 = (bf16[288,128]{1,0:T(8,128)(2,1)S(1)}, bf16[288,128]{1,0:T(8,128)(2,1)S(1)}, u32[]{:S(2)}, u32[]{:S(2)}) collective-permute-start(bf16[288,128]{1,0:T(8,128)(2,1)S(1)} %whole.11.held_b), channel_id=1, source_target_pairs={{0,4},{2,6},{4,0},{6,2},{8,12},{10,14},{12,8},{14,10},{1,5},{3,7},... | collective-permute-start | bytes 221192 | tf_op jit(solution)/shard_map/ppermute | solution.py:443
  33.4 4.4 %collective-permute-start.13 = (bf16[288,128]{1,0:T(8,128)(2,1)S(1)}, bf16[288,128]{1,0:T(8,128)(2,1)S(1)}, u32[]{:S(2)}, u32[]{:S(2)}) collective-permute-start(bf16[288,128]{1,0:T(8,128)(2,1)S(1)} %get-tuple-element.104.held_a), channel_id=1, source_target_pairs={{0,2},{2,0},{4,6},{6,4},{8,10},{10,8},{12,14},{14,12},{1,3},{3,1},... | collective-permute-start | bytes 221192 | tf_op jit(solution)/shard_map/ppermute | solution.py:443
  34.3 3.5 %collective-permute-start.17 = (bf16[288,128]{1,0:T(8,128)(2,1)S(1)}, bf16[288,128]{1,0:T(8,128)(2,1)S(1)}, u32[]{:S(2)}, u32[]{:S(2)}) collective-permute-start(bf16[288,128]{1,0:T(8,128)(2,1)S(1)} %whole.11.held_b), channel_id=1, source_target_pairs={{0,1},{1,0},{2,3},{3,2},{4,5},{5,4},{6,7},{7,6},{8,9},{9,8},{10,11... | collective-permute-start | bytes 221192 | tf_op jit(solution)/shard_map/ppermute | solution.py:428
  34.3 3.5 %collective-permute-start.15 = (bf16[288,128]{1,0:T(8,128)(2,1)S(1)}, bf16[288,128]{1,0:T(8,128)(2,1)S(1)}, u32[]{:S(2)}, u32[]{:S(2)}) collective-permute-start(bf16[288,128]{1,0:T(8,128)(2,1)S(1)} %get-tuple-element.104.held_a), channel_id=1, source_target_pairs={{0,1},{1,0},{2,3},{3,2},{4,5},{5,4},{6,7},{7,6},{8,9},{9,8},{10,11... | collective-permute-start | bytes 221192 | tf_op jit(solution)/shard_map/ppermute | solution.py:428
  37.2 1.3 %collective-permute-start.18 = (bf16[288,128]{1,0:T(8,128)(2,1)S(1)}, bf16[288,128]{1,0:T(8,128)(2,1)S(1)}, u32[]{:S(2)}, u32[]{:S(2)}) collective-permute-start(bf16[288,128]{1,0:T(8,128)(2,1)S(1)} %collective-permute-done.14.got_b), channel_id=1, source_target_pairs={{0,1},{1,0},{2,3},{3,2},{4,5},{5,4},{6,7},{7,6},{8,9},{9,8},{10,11... | collective-permute-start | bytes 221192 | tf_op jit(solution)/shard_map/ppermute | solution.py:428
  37.8 1.3 %collective-permute-start.16 = (bf16[288,128]{1,0:T(8,128)(2,1)S(1)}, bf16[288,128]{1,0:T(8,128)(2,1)S(1)}, u32[]{:S(2)}, u32[]{:S(2)}) collective-permute-start(bf16[288,128]{1,0:T(8,128)(2,1)S(1)} %collective-permute-done.13.got_a), channel_id=1, source_target_pairs={{0,1},{1,0},{2,3},{3,2},{4,5},{5,4},{6,7},{7,6},{8,9},{9,8},{10,11... | collective-permute-start | bytes 221192 | tf_op jit(solution)/shard_map/ppermute | solution.py:428

commit v6 on v5

--- a/solution.py
+++ b/solution.py
@@ -46,10 +46,7 @@
     return jax.ShapeDtypeStruct(shape, dtype)
 
 
-def edge_body(
-    feat, cot, down, up, bias, feat_near, cot_near, down_near, up_near, bias_near,
-    rows, cols, corner, strip, wide_strip, sems,
-):
+def edge_body(feat, cot, feat_near, rows, cols, corner, strip, wide_strip, sems):
     tile_rows, tile_cols, _ = feat.shape
     copies = []
     for which, ref in enumerate((feat, cot)):
@@ -61,13 +58,7 @@
                 ref.at[:, pl.ds(tile_cols - 16, 16), :], strip.at[which], sems.at[2 * which + 1]
             )
         )
-    bulk = [
-        pltpu.make_async_copy(feat, feat_near, sems.at[4]),
-        pltpu.make_async_copy(cot, cot_near, sems.at[5]),
-        pltpu.make_async_copy(down, down_near, sems.at[6]),
-        pltpu.make_async_copy(up, up_near, sems.at[7]),
-        pltpu.make_async_copy(bias, bias_near, sems.at[8]),
-    ]
+    bulk = [pltpu.make_async_copy(feat, feat_near, sems.at[4])]
     for copy in copies + bulk:
         copy.start()
     for copy in copies:
@@ -120,18 +111,32 @@
 
 
 def interior_body(
-    feat, cot, down_weight, down_bias, up_weight,
+    feat, far_cot, far_down, far_bias, far_up,
     feat_patch, cot_patch, act, grads, raw_other, raw_bias, feat_firsts, cot_firsts, up_mat,
-    wide, strip,
+    wide, strip, cot, down_weight, down_bias, sems,
 ):
     rows, cols, channels = feat.shape
     half_rows, half_cols = rows // 2, cols // 2
     pixels = half_rows * half_cols
     taps = 9 * channels
+    copies = [
+        pltpu.make_async_copy(far_cot, cot, sems.at[9]),
+        pltpu.make_async_copy(far_down, down_weight, sems.at[10]),
+        pltpu.make_async_copy(far_bias, down_bias, sems.at[11]),
+    ] + [
+        pltpu.make_async_copy(
+            far_up.at[tap // 3, tap % 3], up_mat.at[:, pl.ds(tap * channels, channels)],
+            sems.at[tap],
+        )
+        for tap in range(9)
+    ]
+    for copy in copies:
+        copy.start()
     own_patches(feat, wide, strip, feat_patch, feat_firsts)
+    copies[0].wait()
     own_patches(cot, wide, strip, cot_patch, cot_firsts)
-    for tap in range(9):
-        up_mat[:, pl.ds(tap * channels, channels)] = up_weight[tap // 3, tap % 3]
+    for copy in copies[1:]:
+        copy.wait()
     down_mat = down_weight[...].reshape(taps, channels)
     bias_row = down_bias[...].reshape(1, channels)
     step = 8
@@ -331,7 +336,7 @@
 
 def final_body(
     positions, held_a, got_a, held_b, got_b, far_held_a, far_got_a, far_held_b, far_got_b, bias_in,
-    down, up, bias_out, mine, far, sems,
+    down, up, bias_out,
 ):
     channels = held_a.shape[1]
     core = lax.axis_index("narrow")
@@ -356,22 +361,18 @@
     for at, (near_ref, far_ref) in enumerate(
         ((held_a, far_held_a), (got_a, far_got_a), (held_b, far_held_b), (got_b, far_got_b))
     ):
-        mine[at] = near_ref[...].astype(F32) * factor
-        far[at] = far_ref[...].astype(F32) * factor
+        near_block = near_ref[...].astype(F32) * factor
+        far_block = far_ref[...].astype(F32) * factor
 
         @pl.when(core == 0)
         def _():
-            pltpu.make_async_copy(mine.at[at], down.at[spots[at]], sems.at[at]).start()
-            pltpu.make_async_copy(far.at[at], up.at[spots[at]], sems.at[4 + at]).start()
+            down[spots[at]] = near_block
+            up[spots[at]] = far_block
 
         @pl.when(core != 0)
         def _():
-            pltpu.make_async_copy(mine.at[at], up.at[spots[at]], sems.at[at]).start()
-            pltpu.make_async_copy(far.at[at], down.at[spots[at]], sems.at[4 + at]).start()
-
-    for at in range(4):
-        pltpu.make_async_copy(mine.at[at], down.at[spots[at]], sems.at[at]).wait()
-        pltpu.make_async_copy(far.at[at], up.at[spots[at]], sems.at[4 + at]).wait()
+            up[spots[at]] = near_block
+            down[spots[at]] = far_block
 
 
 def feature_body(grads, rim_grads, right, below, cot, down_weight, out, wide, pairs, near_mat, low_mat, woven):
@@ -448,14 +449,10 @@
     half_rows, half_cols = tile_rows // 2, tile_cols // 2
     pixels = half_rows * half_cols
     taps = 9 * channels
-    feat_near, cot_near, down_near, up_near, bias_near, rows, cols, corner = call(
+    feat_near, rows, cols, corner = call(
         edge_body,
         (
             vm(features.shape, BF16),
-            vm(features.shape, BF16),
-            vm(down_weight.shape, BF16),
-            vm(up_weight.shape, BF16),
-            vm((1, channels), F32),
             vm((2, tile_cols, channels), BF16),
             vm((2, tile_rows, channels), BF16),
             vm((2, 8, channels), BF16),
@@ -463,14 +460,14 @@
         scratch=[
             pltpu.VMEM((2, tile_rows, 16, channels), BF16),
             pltpu.VMEM((tile_rows * 16, channels), F32),
-            pltpu.SemaphoreType.DMA((9,)),
+            pltpu.SemaphoreType.DMA((5,)),
         ],
-        in_specs=[ANY] * 5,
+        in_specs=[ANY] * 2,
         nbytes=1 << 19,
         name="edges",
-        far=(0, 1, 2, 3, 4),
+        far=(0, 1),
         room=8,
-    )(features, cotangent, down_weight, up_weight, down_bias.reshape(1, channels))
+    )(features, cotangent)
     from_above = turned(rows, "wide", 1)
     from_corner = turned_both(corner)
     from_left = turned(cols, "narrow", 1)
@@ -494,14 +491,19 @@
         scratch=[
             pltpu.VMEM((half_rows, 2, tile_cols + 8, channels), F32),
             pltpu.VMEM((tile_rows * 16, channels), F32),
+            pltpu.VMEM(features.shape, BF16),
+            pltpu.VMEM(down_weight.shape, BF16),
+            pltpu.VMEM((1, channels), F32),
+            pltpu.SemaphoreType.DMA((12,)),
         ],
-        n_in=5,
+        in_specs=[VM, ANY, ANY, ANY, ANY],
         flops=6 * pixels * taps * channels,
         nbytes=6 << 20,
         name="interior",
-        near=(0, 1, 2, 3, 4),
+        near=(0,),
+        far=(1, 2, 3, 4),
         room=12,
-    )(feat_near, cot_near, down_near, bias_near, up_near)
+    )(feat_near, cotangent, down_weight, down_bias.reshape(1, channels), up_weight)
     from_above, from_corner, from_left, raw_other = lax.optimization_barrier(
         (from_above, from_corner, from_left, raw_other)
     )
@@ -526,11 +528,11 @@
         flops=1 << 26,
         nbytes=3 << 20,
         name="rim",
-        near=tuple(range(12)),
+        near=tuple(range(10)),
         room=8,
     )(
         feat_patch, cot_patch, feat_firsts, cot_firsts, from_above, from_left, from_corner,
-        raw_other, raw_bias, up_mat, down_near, bias_near,
+        raw_other, raw_bias, up_mat, down_weight, down_bias,
     )
     got_a = turned(other_a, "narrow", 1)
     got_b = turned(other_b, "narrow", 1)
@@ -591,9 +593,9 @@
         flops=2 * pixels * 6 * 2 * channels * channels,
         nbytes=3 << 20,
         name="feature",
-        near=(0, 1, 2, 3, 4, 5),
+        near=(0, 1, 2, 3),
         room=16,
-    )(grads, rim_grads, from_right, from_below, cot_near, down_near)
+    )(grads, rim_grads, from_right, from_below, cotangent, down_weight)
     for step in range(halvings, bits + 1):
         side = SIDE if step < bits else 0
         held_a, bias_sum = call(
@@ -648,17 +650,11 @@
             sds((4, size, channels), F32),
             sds((1, channels), F32),
         ),
-        scratch=[
-            pltpu.VMEM((4, size, channels), F32),
-            pltpu.VMEM((4, size, channels), F32),
-            pltpu.SemaphoreType.DMA((8,)),
-        ],
         n_in=9,
         nbytes=12 * taps * channels,
         name="final",
         near=tuple(range(9)),
         room=8,
-        out_specs=(ANY, ANY, VM),
     )(*blocks, *far_blocks, bias_sum)
     shape = (3, 3, channels, channels)
     return (feature_grad, down.reshape(shape), up.reshape(shape), bias_grad.reshape(channels))

time: 41.1 us -> 40.6 us (0.988)
  waiting for transfers between devices: 13.3 us -> 10.1 us
  starting transfers between devices: 16.9 us -> 19.3 us
    ppermute x8, starting transfers between devices: 8.13 us -> 9.95 us  [traded(): lax.ppermute(value, 'wide', [(at, at ^ 1 << position) for at in range(cou...]
    ppermute x8, waiting for transfers between devices: 9.93 us -> 8.31 us  [traded(): lax.ppermute(value, 'wide', [(at, at ^ 1 << position) for at in range(cou...]
    ppermute x10, waiting for transfers between devices: 3.36 us -> 1.83 us  [turned(): lax.ppermute(value, axis, [(at, (at + steps) % count) for at in range(cou...]
    ppermute x10, starting transfers between devices: 6.31 us -> 6.9 us  [turned(): lax.ppermute(value, axis, [(at, (at + steps) % count) for at in range(cou...]
  transfers between devices with their start and end apart: 19 -> 19, of which waited for: 9 -> 8; matrix products, arithmetic and copies ran while one was open for 0% -> 0% of each run, Pallas kernels for 14% -> 17%
where the time goes in v6:
time: 40.6 us; the launch traced here: 40.4 us
  starting transfers between devices  19.3 us (48%)
  Pallas kernels  10.2 us (25%)
  waiting for transfers between devices  10.1 us (25%)
  between operations  0.76 us (2%)
    pallas_call x14, Pallas kernels, run(): return kernel(*placed)  10.2 us
    ppermute x8, starting transfers between devices, traded(): lax.ppermute(value, 'wide', [(at, at ^ 1 << position) for at in range(cou...  9.95 us
    ppermute x8, waiting for transfers between devices, traded(): lax.ppermute(value, 'wide', [(at, at ^ 1 << position) for at in range(cou...  8.31 us
    ppermute x10, starting transfers between devices, turned(): lax.ppermute(value, axis, [(at, (at + steps) % count) for at in range(cou...  6.9 us
    ppermute x1, starting transfers between devices, turned_both(): return lax.ppermute(value, ('wide', 'narrow'), pairs)  2.46 us
    ppermute x10, waiting for transfers between devices, turned(): lax.ppermute(value, axis, [(at, (at + steps) % count) for at in range(cou...  1.83 us
  transfers between devices with their start and end apart: 19, of which 8 were waited for; matrix products, arithmetic and copies ran while one was open for 0% of the time, Pallas kernels for 17%

profile of v6, /device:TPU:0, one launch (start us, length us, event | category | flops | bytes accessed | tf_op | source)
XLA Modules:
  0.0 40.4 jit_solution(16454961841235232578)
XLA Ops:
  0.7 1.5 %edges.1 = (bf16[64,64,128]{2,1,0:T(8,128)(2,1)S(1)}, bf16[2,64,128]{2,1,0:T(8,128)(2,1)S(1)}, bf16[2,64,128]{2,1,0:T(8,128)(2,1)S(1)}, bf16[2,8,128]{2,1,0:T(8,128)(2,1)S(1)}) custom-call(bf16[64,64,128]{2,1,0:T(8,128)(2,1)} %feat.1, bf16[64,64,128]{2,1,0:T(8,128)(2,1)} %cot.3), custom_call_target="tpu_custom_call" | custom-call | bytes 524288 | tf_op jit(solution)/shard_map/edges/pallas_call | solution.py:36
  2.2 2.5 %collective-permute-start.1 = (bf16[2,8,128]{2,1,0:T(8,128)(2,1)S(1)}, bf16[2,8,128]{2,1,0:T(8,128)(2,1)S(1)}, u32[]{:S(2)}, u32[]{:S(2)}) collective-permute-start(bf16[2,8,128]{2,1,0:T(8,128)(2,1)S(1)} %get-tuple-element.59), channel_id=1, source_target_pairs={{0,3},{1,2},{2,5},{3,4},{4,7},{5,6},{6,9},{7,8},{8,11},{9,10},{10,... | collective-permute-start | bytes 12296 | tf_op jit(solution)/shard_map/ppermute | solution.py:439
  4.6 1.5 %collective-permute-start = (bf16[2,64,128]{2,1,0:T(8,128)(2,1)S(1)}, bf16[2,64,128]{2,1,0:T(8,128)(2,1)S(1)}, u32[]{:S(2)}, u32[]{:S(2)}) collective-permute-start(bf16[2,64,128]{2,1,0:T(8,128)(2,1)S(1)} %get-tuple-element.58), channel_id=1, source_target_pairs={{0,2},{2,4},{4,6},{6,8},{8,10},{10,12},{12,14},{14,0},{1,3},{3,5},... | collective-permute-start | bytes 98312 | tf_op jit(solution)/shard_map/ppermute | solution.py:429
  6.2 0.4 collective-permute-start.2
  6.6 3.9 %interior.1 = (bf16[32,32,1152]{2,1,0:T(8,128)(2,1)S(1)}, bf16[32,32,1152]{2,1,0:T(8,128)(2,1)S(1)}, bf16[1024,128]{1,0:T(8,128)(2,1)S(1)}, bf16[1024,128]{1,0:T...) custom-call(bf16[64,64,128]{2,1,0:T(8,128)(2,1)S(1)} %get-tuple-elem, ...), custom_call_target="tpu_custom_call" | custom-call | flops 905969664 | bytes 6291456 | tf_op jit(solution)/shard_map/interior/pallas_call | solution.py:36
  10.5 0.8 %collective-permute-done.top = bf16[2,64,128]{2,1,0:T(8,128)(2,1)S(1)} collective-permute-done((bf16[2,64,128]{2,1,0:T(8,128)(2,1)S(1)}, bf16[2,64,128]{2,1,0:T(8,128)(2,1)S(1)}, u32[]{:S(2)}, u32[]{:S(2)}) %collective-permute-start) | collective-permute-done | bytes 32800 | tf_op jit(solution)/shard_map/ppermute | solution.py:429
  11.3 0.6 %rim.1 = (bf16[64,128]{1,0:T(8,128)(2,1)S(1)}, bf16[64,1152]{1,0:T(8,128)(2,1)S(1)}, bf16[64,1152]{1,0:T(8,128)(2,1)S(1)}, bf16[64,128]{1,0:T(8,128)(2,1)S(1)}, ...) custom-call(bf16[32,32,1152]{2,1,0:T(8,128)(2,1)S(1)} %get-tuple-ele, ...), custom_call_target="tpu_custom_call" | custom-call | flops 67108864 | bytes 3145728 | tf_op jit(solution)/shard_map/rim/pallas_call | solution.py:36
  12.0 0.5 %collective-permute-start.3 = (bf16[592,128]{1,0:T(8,128)(2,1)S(1)}, bf16[592,128]{1,0:T(8,128)(2,1)S(1)}, u32[]{:S(2)}, u32[]{:S(2)}) collective-permute-start(bf16[592,128]{1,0:T(8,128)(2,1)S(1)} %get-tuple-element.68), channel_id=1, source_target_pairs={{0,1},{1,0},{2,3},{3,2},{4,5},{5,4},{6,7},{7,6},{8,9},{9,8},{10,11... | collective-permute-start | bytes 454664 | tf_op jit(solution)/shard_map/ppermute | solution.py:429
  12.5 0.9 %mine.1 = (f32[576,128]{1,0:T(8,128)S(1)}, f32[576,128]{1,0:T(8,128)S(1)}) custom-call(bf16[32,32,1152]{2,1,0:T(8,128)(2,1)S(1)} %get-tuple-element.54.feat_patch, bf16[32,32,1152]{2,1,0:T(8,128)(2,1)S(1)} %get-tuple-element.55.cot_patch, bf16[1024,128]{1,0:T(8,128)(2,1)S(1)} %get-tuple-element.69.act, bf16[1024,128]{1,0:T(8,128)(2,1)S(1)} %get-tuple-element.70.grads, ...), custom_call_target="tpu_custom_call" | custom-call | flops 301989888 | bytes 3145728 | tf_op jit(solution)/shard_map/mine/pallas_call | solution.py:36
  13.6 1.1 %collective-permute-start.10 = (bf16[304,128]{1,0:T(8,128)(2,1)S(1)}, bf16[304,128]{1,0:T(8,128)(2,1)S(1)}, u32[]{:S(2)}, u32[]{:S(2)}) collective-permute-start(bf16[304,128]{1,0:T(8,128)(2,1)S(1)} %get-tuple-element.90), channel_id=1, source_target_pairs={{0,2},{2,0},{4,6},{6,4},{8,10},{10,8},{12,14},{14,12},{1,3},{3,1},... | collective-permute-start | bytes 233480 | tf_op jit(solution)/shard_map/ppermute | solution.py:444
  14.7 1.6 %collective-permute-start.6 = (bf16[288,128]{1,0:T(8,128)(2,1)S(1)}, bf16[288,128]{1,0:T(8,128)(2,1)S(1)}, u32[]{:S(2)}, u32[]{:S(2)}) collective-permute-start(bf16[288,128]{1,0:T(8,128)(2,1)S(1)} %get-tuple-element.82), channel_id=1, source_target_pairs={{0,4},{2,6},{4,0},{6,2},{8,12},{10,14},{12,8},{14,10},{1,5},{3,7},... | collective-permute-start | bytes 221192 | tf_op jit(solution)/shard_map/ppermute | solution.py:444
  16.4 2.8 %collective-permute-done.6.got = bf16[288,128]{1,0:T(8,128)(2,1)S(1)} collective-permute-done((bf16[288,128]{1,0:T(8,128)(2,1)S(1)}, bf16[288,128]{1,0:T(8,128)(2,1)S(1)}, u32[]{:S(2)}, u32[]{:S(2)}) %collective-permute-start.6) | collective-permute-done | bytes 73760 | tf_op jit(solution)/shard_map/ppermute | solution.py:444
  19.2 1.1 %collective-permute-start.7 = (bf16[288,128]{1,0:T(8,128)(2,1)S(1)}, bf16[288,128]{1,0:T(8,128)(2,1)S(1)}, u32[]{:S(2)}, u32[]{:S(2)}) collective-permute-start(bf16[288,128]{1,0:T(8,128)(2,1)S(1)} %whole.6.held), channel_id=1, source_target_pairs={{0,2},{2,0},{4,6},{6,4},{8,10},{10,8},{12,14},{14,12},{1,3},{3,1},... | collective-permute-start | bytes 221192 | tf_op jit(solution)/shard_map/ppermute | solution.py:444
  20.2 1.2 %collective-permute-start.11 = (bf16[304,128]{1,0:T(8,128)(2,1)S(1)}, bf16[304,128]{1,0:T(8,128)(2,1)S(1)}, u32[]{:S(2)}, u32[]{:S(2)}) collective-permute-start(bf16[304,128]{1,0:T(8,128)(2,1)S(1)} %get-tuple-element.92.held), channel_id=1, source_target_pairs={{0,4},{2,6},{4,0},{6,2},{8,12},{10,14},{12,8},{14,10},{1,5},{3,7},... | collective-permute-start | bytes 233480 | tf_op jit(solution)/shard_map/ppermute | solution.py:444
  21.4 3.4 %collective-permute-start.8 = (bf16[40,128]{1,0:T(8,128)(2,1)S(1)}, bf16[40,128]{1,0:T(8,128)(2,1)S(1)}, u32[]{:S(2)}, u32[]{:S(2)}) collective-permute-start(bf16[40,128]{1,0:T(8,128)(2,1)S(1)} %pad_maximum_fusion), channel_id=1, source_target_pairs={{0,14},{2,0},{4,2},{6,4},{8,6},{10,8},{12,10},{14,12},{1,15},{3,1}... | collective-permute-start | bytes 30728 | tf_op jit(solution)/shard_map/ppermute | solution.py:429
  24.9 2.1 %collective-permute-start.12 = (bf16[304,128]{1,0:T(8,128)(2,1)S(1)}, bf16[304,128]{1,0:T(8,128)(2,1)S(1)}, u32[]{:S(2)}, u32[]{:S(2)}) collective-permute-start(bf16[304,128]{1,0:T(8,128)(2,1)S(1)} %get-tuple-element.94.held), channel_id=1, source_target_pairs={{0,8},{2,10},{4,12},{6,14},{8,0},{10,2},{12,4},{14,6},{1,9},{3,11}... | collective-permute-start | bytes 233480 | tf_op jit(solution)/shard_map/ppermute | solution.py:444
  27.0 1.0 %collective-permute-start.9 = (bf16[288,128]{1,0:T(8,128)(2,1)S(1)}, bf16[288,128]{1,0:T(8,128)(2,1)S(1)}, u32[]{:S(2)}, u32[]{:S(2)}) collective-permute-start(bf16[288,128]{1,0:T(8,128)(2,1)S(1)} %whole.7.held), channel_id=1, source_target_pairs={{0,8},{2,10},{4,12},{6,14},{8,0},{10,2},{12,4},{14,6},{1,9},{3,11}... | collective-permute-start | bytes 221192 | tf_op jit(solution)/shard_map/ppermute | solution.py:444
  28.0 1.8 %feature.1 = bf16[64,64,128]{2,1,0:T(8,128)(2,1)} custom-call(bf16[1024,128]{1,0:T(8,128)(2,1)S(1)} %get-tuple-element.70.grads, bf16[64,128]{1,0:T(8,128)(2,1)S(1)} %get-tuple-element.79.rim_grads, bf16[32,128]{1,0:T(8,128)(2,1)S(1)} %collective-permute-done.5.right, bf16[40,128]{1,0:T(8,128)(2,1)S(1)} %collective-permute-done.8.below, ...), custom_call_target="tpu_custom_call" | custom-call | flops 402653184 | bytes 3145728 | tf_op jit(solution)/shard_map/feature/pallas_call | solution.py:36
  29.7 3.5 %collective-permute-done.9.got = bf16[288,128]{1,0:T(8,128)(2,1)S(1)} collective-permute-done((bf16[288,128]{1,0:T(8,128)(2,1)S(1)}, bf16[288,128]{1,0:T(8,128)(2,1)S(1)}, u32[]{:S(2)}, u32[]{:S(2)}) %collective-permute-start.9) | collective-permute-done | bytes 73760 | tf_op jit(solution)/shard_map/ppermute | solution.py:444
  33.3 1.8 %collective-permute-start.13 = (bf16[288,128]{1,0:T(8,128)(2,1)S(1)}, bf16[288,128]{1,0:T(8,128)(2,1)S(1)}, u32[]{:S(2)}, u32[]{:S(2)}) collective-permute-start(bf16[288,128]{1,0:T(8,128)(2,1)S(1)} %get-tuple-element.96.held_a), channel_id=1, source_target_pairs={{0,2},{2,0},{4,6},{6,4},{8,10},{10,8},{12,14},{14,12},{1,3},{3,1},... | collective-permute-start | bytes 221192 | tf_op jit(solution)/shard_map/ppermute | solution.py:444
  35.2 0.5 %collective-permute-start.15 = (bf16[288,128]{1,0:T(8,128)(2,1)S(1)}, bf16[288,128]{1,0:T(8,128)(2,1)S(1)}, u32[]{:S(2)}, u32[]{:S(2)}) collective-permute-start(bf16[288,128]{1,0:T(8,128)(2,1)S(1)} %get-tuple-element.96.held_a), channel_id=1, source_target_pairs={{0,1},{1,0},{2,3},{3,2},{4,5},{5,4},{6,7},{7,6},{8,9},{9,8},{10,11... | collective-permute-start | bytes 221192 | tf_op jit(solution)/shard_map/ppermute | solution.py:429
  35.7 1.9 %collective-permute-done.14.got_b = bf16[288,128]{1,0:T(8,128)(2,1)S(1)} collective-permute-done((bf16[288,128]{1,0:T(8,128)(2,1)S(1)}, bf16[288,128]{1,0:T(8,128)(2,1)S(1)}, u32[]{:S(2)}, u32[]{:S(2)}) %collective-permute-start.14) | collective-permute-done | bytes 73760 | tf_op jit(solution)/shard_map/ppermute | solution.py:444
  38.1 0.7 %collective-permute-done.18.far_got_b = bf16[288,128]{1,0:T(8,128)(2,1)S(1)} collective-permute-done((bf16[288,128]{1,0:T(8,128)(2,1)S(1)}, bf16[288,128]{1,0:T(8,128)(2,1)S(1)}, u32[]{:S(2)}, u32[]{:S(2)}) %collective-permute-start.18) | collective-permute-done | bytes 73760 | tf_op jit(solution)/shard_map/ppermute | solution.py:429
  39.0 1.4 %final.1 = (f32[4,288,128]{2,1,0:T(8,128)}, f32[4,288,128]{2,1,0:T(8,128)}, f32[1,128]{1,0:T(1,128)}) custom-call(bf16[288,128]{1,0:T(8,128)(2,1)S(1)} %get-tuple-element.96.held_a, bf16[288,128]{1,0:T(8,128)(2,1)S(1)} %collective-permute-done.13.got_a, bf16[288,128]{1,0:T(8,128)(2,1)S(1)} %whole.11.held_b, ...), custom_call_target="tpu_custom_call" | custom-call | bytes 1769472 | tf_op jit(solution)/shard_map/final/pallas_call | solution.py:36
  (37 shorter events, 1.2 us)
Async XLA Ops:
  0.6 10.7 %copy-start.1 = (bf16[3,3,128,128]{3,2,1,0:T(8,128)(2,1)S(1)}, bf16[3,3,128,128]{3,2,1,0:T(8,128)(2,1)}, u32[]{:S(2)}) copy-start(bf16[3,3,128,128]{3,2,1,0:T(8,128)(2,1)} %down_weight.3) | copy-start | bytes 884740
  0.6 10.7 %copy-start.2 = (f32[128]{0:T(128)S(1)}, f32[128]{0:T(128)}, u32[]{:S(2)}) copy-start(f32[128]{0:T(128)} %down_bias.1) | copy-start | bytes 1540
  2.2 8.3 %collective-permute-start.1 = (bf16[2,8,128]{2,1,0:T(8,128)(2,1)S(1)}, bf16[2,8,128]{2,1,0:T(8,128)(2,1)S(1)}, u32[]{:S(2)}, u32[]{:S(2)}) collective-permute-start(bf16[2,8,128]{2,1,0:T(8,128)(2,1)S(1)} %get-tuple-element.59), channel_id=1, source_target_pairs={{0,3},{1,2},{2,5},{3,4},{4,7},{5,6},{6,9},{7,8},{8,11},{9,10},{10,... | collective-permute-start | bytes 12296 | tf_op jit(solution)/shard_map/ppermute | solution.py:439
  4.6 6.7 %collective-permute-start = (bf16[2,64,128]{2,1,0:T(8,128)(2,1)S(1)}, bf16[2,64,128]{2,1,0:T(8,128)(2,1)S(1)}, u32[]{:S(2)}, u32[]{:S(2)}) collective-permute-start(bf16[2,64,128]{2,1,0:T(8,128)(2,1)S(1)} %get-tuple-element.58), channel_id=1, source_target_pairs={{0,2},{2,4},{4,6},{6,8},{8,10},{10,12},{12,14},{14,0},{1,3},{3,5},... | collective-permute-start | bytes 98312 | tf_op jit(solution)/shard_map/ppermute | solution.py:429
  6.2 5.1 %collective-permute-start.2 = (bf16[2,64,128]{2,1,0:T(8,128)(2,1)S(1)}, bf16[2,64,128]{2,1,0:T(8,128)(2,1)S(1)}, u32[]{:S(2)}, u32[]{:S(2)}) collective-permute-start(bf16[2,64,128]{2,1,0:T(8,128)(2,1)S(1)} %get-tuple-element.60), channel_id=1, source_target_pairs={{0,1},{1,0},{2,3},{3,2},{4,5},{5,4},{6,7},{7,6},{8,9},{9,8},{10,11... | collective-permute-start | bytes 98312 | tf_op jit(solution)/shard_map/ppermute | solution.py:429
  11.9 2.8 %collective-permute-start.4 = (bf16[576,128]{1,0:T(8,128)(2,1)S(1)}, bf16[576,128]{1,0:T(8,128)(2,1)S(1)}, u32[]{:S(2)}, u32[]{:S(2)}) collective-permute-start(bf16[576,128]{1,0:T(8,128)(2,1)S(1)} %get-tuple-element.78), channel_id=1, source_target_pairs={{0,1},{1,0},{2,3},{3,2},{4,5},{5,4},{6,7},{7,6},{8,9},{9,8},{10,11... | collective-permute-start | bytes 442376 | tf_op jit(solution)/shard_map/ppermute | solution.py:429
  12.0 1.6 %collective-permute-start.3 = (bf16[592,128]{1,0:T(8,128)(2,1)S(1)}, bf16[592,128]{1,0:T(8,128)(2,1)S(1)}, u32[]{:S(2)}, u32[]{:S(2)}) collective-permute-start(bf16[592,128]{1,0:T(8,128)(2,1)S(1)} %get-tuple-element.68), channel_id=1, source_target_pairs={{0,1},{1,0},{2,3},{3,2},{4,5},{5,4},{6,7},{7,6},{8,9},{9,8},{10,11... | collective-permute-start | bytes 454664 | tf_op jit(solution)/shard_map/ppermute | solution.py:429
  12.5 2.2 %collective-permute-start.5 = (bf16[32,128]{1,0:T(8,128)(2,1)S(1)}, bf16[32,128]{1,0:T(8,128)(2,1)S(1)}, u32[]{:S(2)}, u32[]{:S(2)}) collective-permute-start(bf16[32,128]{1,0:T(8,128)(2,1)S(1)} %get-tuple-element.103), channel_id=1, source_target_pairs={{0,1},{1,0},{2,3},{3,2},{4,5},{5,4},{6,7},{7,6},{8,9},{9,8},{10,11... | collective-permute-start | bytes 24584 | tf_op jit(solution)/shard_map/ppermute | solution.py:429
  12.5 15.4 %copy-start = (bf16[64,64,128]{2,1,0:T(8,128)(2,1)S(1)}, bf16[64,64,128]{2,1,0:T(8,128)(2,1)}, u32[]{:S(2)}) copy-start(bf16[64,64,128]{2,1,0:T(8,128)(2,1)} %cot.3) | copy-start | bytes 3145732
  13.6 6.6 %collective-permute-start.10 = (bf16[304,128]{1,0:T(8,128)(2,1)S(1)}, bf16[304,128]{1,0:T(8,128)(2,1)S(1)}, u32[]{:S(2)}, u32[]{:S(2)}) collective-permute-start(bf16[304,128]{1,0:T(8,128)(2,1)S(1)} %get-tuple-element.90), channel_id=1, source_target_pairs={{0,2},{2,0},{4,6},{6,4},{8,10},{10,8},{12,14},{14,12},{1,3},{3,1},... | collective-permute-start | bytes 233480 | tf_op jit(solution)/shard_map/ppermute | solution.py:444
  14.7 4.4 %collective-permute-start.6 = (bf16[288,128]{1,0:T(8,128)(2,1)S(1)}, bf16[288,128]{1,0:T(8,128)(2,1)S(1)}, u32[]{:S(2)}, u32[]{:S(2)}) collective-permute-start(bf16[288,128]{1,0:T(8,128)(2,1)S(1)} %get-tuple-element.82), channel_id=1, source_target_pairs={{0,4},{2,6},{4,0},{6,2},{8,12},{10,14},{12,8},{14,10},{1,5},{3,7},... | collective-permute-start | bytes 221192 | tf_op jit(solution)/shard_map/ppermute | solution.py:444
  19.2 7.8 %collective-permute-start.7 = (bf16[288,128]{1,0:T(8,128)(2,1)S(1)}, bf16[288,128]{1,0:T(8,128)(2,1)S(1)}, u32[]{:S(2)}, u32[]{:S(2)}) collective-permute-start(bf16[288,128]{1,0:T(8,128)(2,1)S(1)} %whole.6.held), channel_id=1, source_target_pairs={{0,2},{2,0},{4,6},{6,4},{8,10},{10,8},{12,14},{14,12},{1,3},{3,1},... | collective-permute-start | bytes 221192 | tf_op jit(solution)/shard_map/ppermute | solution.py:444
  20.2 4.6 %collective-permute-start.11 = (bf16[304,128]{1,0:T(8,128)(2,1)S(1)}, bf16[304,128]{1,0:T(8,128)(2,1)S(1)}, u32[]{:S(2)}, u32[]{:S(2)}) collective-permute-start(bf16[304,128]{1,0:T(8,128)(2,1)S(1)} %get-tuple-element.92.held), channel_id=1, source_target_pairs={{0,4},{2,6},{4,0},{6,2},{8,12},{10,14},{12,8},{14,10},{1,5},{3,7},... | collective-permute-start | bytes 233480 | tf_op jit(solution)/shard_map/ppermute | solution.py:444
  21.4 5.5 %collective-permute-start.8 = (bf16[40,128]{1,0:T(8,128)(2,1)S(1)}, bf16[40,128]{1,0:T(8,128)(2,1)S(1)}, u32[]{:S(2)}, u32[]{:S(2)}) collective-permute-start(bf16[40,128]{1,0:T(8,128)(2,1)S(1)} %pad_maximum_fusion), channel_id=1, source_target_pairs={{0,14},{2,0},{4,2},{6,4},{8,6},{10,8},{12,10},{14,12},{1,15},{3,1}... | collective-permute-start | bytes 30728 | tf_op jit(solution)/shard_map/ppermute | solution.py:429
  24.9 8.4 %collective-permute-start.12 = (bf16[304,128]{1,0:T(8,128)(2,1)S(1)}, bf16[304,128]{1,0:T(8,128)(2,1)S(1)}, u32[]{:S(2)}, u32[]{:S(2)}) collective-permute-start(bf16[304,128]{1,0:T(8,128)(2,1)S(1)} %get-tuple-element.94.held), channel_id=1, source_target_pairs={{0,8},{2,10},{4,12},{6,14},{8,0},{10,2},{12,4},{14,6},{1,9},{3,11}... | collective-permute-start | bytes 233480 | tf_op jit(solution)/shard_map/ppermute | solution.py:444
  27.0 6.2 %collective-permute-start.9 = (bf16[288,128]{1,0:T(8,128)(2,1)S(1)}, bf16[288,128]{1,0:T(8,128)(2,1)S(1)}, u32[]{:S(2)}, u32[]{:S(2)}) collective-permute-start(bf16[288,128]{1,0:T(8,128)(2,1)S(1)} %whole.7.held), channel_id=1, source_target_pairs={{0,8},{2,10},{4,12},{6,14},{8,0},{10,2},{12,4},{14,6},{1,9},{3,11}... | collective-permute-start | bytes 221192 | tf_op jit(solution)/shard_map/ppermute | solution.py:444
  33.2 4.4 %collective-permute-start.14 = (bf16[288,128]{1,0:T(8,128)(2,1)S(1)}, bf16[288,128]{1,0:T(8,128)(2,1)S(1)}, u32[]{:S(2)}, u32[]{:S(2)}) collective-permute-start(bf16[288,128]{1,0:T(8,128)(2,1)S(1)} %whole.11.held_b), channel_id=1, source_target_pairs={{0,4},{2,6},{4,0},{6,2},{8,12},{10,14},{12,8},{14,10},{1,5},{3,7},... | collective-permute-start | bytes 221192 | tf_op jit(solution)/shard_map/ppermute | solution.py:444
  33.3 4.4 %collective-permute-start.13 = (bf16[288,128]{1,0:T(8,128)(2,1)S(1)}, bf16[288,128]{1,0:T(8,128)(2,1)S(1)}, u32[]{:S(2)}, u32[]{:S(2)}) collective-permute-start(bf16[288,128]{1,0:T(8,128)(2,1)S(1)} %get-tuple-element.96.held_a), channel_id=1, source_target_pairs={{0,2},{2,0},{4,6},{6,4},{8,10},{10,8},{12,14},{14,12},{1,3},{3,1},... | collective-permute-start | bytes 221192 | tf_op jit(solution)/shard_map/ppermute | solution.py:444
  35.2 3.0 %collective-permute-start.17 = (bf16[288,128]{1,0:T(8,128)(2,1)S(1)}, bf16[288,128]{1,0:T(8,128)(2,1)S(1)}, u32[]{:S(2)}, u32[]{:S(2)}) collective-permute-start(bf16[288,128]{1,0:T(8,128)(2,1)S(1)} %whole.11.held_b), channel_id=1, source_target_pairs={{0,1},{1,0},{2,3},{3,2},{4,5},{5,4},{6,7},{7,6},{8,9},{9,8},{10,11... | collective-permute-start | bytes 221192 | tf_op jit(solution)/shard_map/ppermute | solution.py:429
  35.2 3.0 %collective-permute-start.15 = (bf16[288,128]{1,0:T(8,128)(2,1)S(1)}, bf16[288,128]{1,0:T(8,128)(2,1)S(1)}, u32[]{:S(2)}, u32[]{:S(2)}) collective-permute-start(bf16[288,128]{1,0:T(8,128)(2,1)S(1)} %get-tuple-element.96.held_a), channel_id=1, source_target_pairs={{0,1},{1,0},{2,3},{3,2},{4,5},{5,4},{6,7},{7,6},{8,9},{9,8},{10,11... | collective-permute-start | bytes 221192 | tf_op jit(solution)/shard_map/ppermute | solution.py:429
  37.6 1.3 %collective-permute-start.18 = (bf16[288,128]{1,0:T(8,128)(2,1)S(1)}, bf16[288,128]{1,0:T(8,128)(2,1)S(1)}, u32[]{:S(2)}, u32[]{:S(2)}) collective-permute-start(bf16[288,128]{1,0:T(8,128)(2,1)S(1)} %collective-permute-done.14.got_b), channel_id=1, source_target_pairs={{0,1},{1,0},{2,3},{3,2},{4,5},{5,4},{6,7},{7,6},{8,9},{9,8},{10,11... | collective-permute-start | bytes 221192 | tf_op jit(solution)/shard_map/ppermute | solution.py:429
  37.7 1.3 %collective-permute-start.16 = (bf16[288,128]{1,0:T(8,128)(2,1)S(1)}, bf16[288,128]{1,0:T(8,128)(2,1)S(1)}, u32[]{:S(2)}, u32[]{:S(2)}) collective-permute-start(bf16[288,128]{1,0:T(8,128)(2,1)S(1)} %collective-permute-done.13.got_a), channel_id=1, source_target_pairs={{0,1},{1,0},{2,3},{3,2},{4,5},{5,4},{6,7},{7,6},{8,9},{9,8},{10,11... | collective-permute-start | bytes 221192 | tf_op jit(solution)/shard_map/ppermute | solution.py:429

commit v7 on v5

--- a/solution.py
+++ b/solution.py
@@ -7,6 +7,7 @@
 from jax.experimental.pallas import tpu as pltpu
 from jax.sharding import PartitionSpec as P
 
+
 F32 = jnp.float32
 BF16 = jnp.bfloat16
 VM = pl.BlockSpec(memory_space=pltpu.VMEM)
@@ -14,14 +15,13 @@
 SIDE = 16
 
 
-def call(body, out_shape, scratch=(), in_specs=None, n_in=0, flops=0, nbytes=0, name=None, near=(), far=(), room=4, out_specs=None):
+def call(body, out_shape, scratch=(), in_specs=None, n_in=0, flops=0, nbytes=0, near=(), far=(), room=4, out_specs=None):
     kernel = pl.pallas_call(
         body,
         out_shape=out_shape,
         in_specs=in_specs if in_specs is not None else [VM] * n_in,
         out_specs=out_specs or jax.tree.map(lambda _: VM, out_shape),
         scratch_shapes=list(scratch),
-        name=name,
         compiler_params=pltpu.CompilerParams(vmem_limit_bytes=room << 20),
         cost_estimate=pl.CostEstimate(flops=flops, transcendentals=0, bytes_accessed=nbytes),
     )
@@ -331,11 +331,12 @@
 
 def final_body(
     positions, held_a, got_a, held_b, got_b, far_held_a, far_got_a, far_held_b, far_got_b, bias_in,
-    down, up, bias_out, mine, far, sems,
+    down, up, bias_out,
 ):
     channels = held_a.shape[1]
     core = lax.axis_index("narrow")
     bit_a, bit_b = bit_of(positions[0]), bit_of(positions[1])
+
     def square(ref):
         block = ref[...].astype(F32).reshape(-1, 8, channels)
         return jnp.sum(block * block, axis=0)
@@ -356,22 +357,18 @@
     for at, (near_ref, far_ref) in enumerate(
         ((held_a, far_held_a), (got_a, far_got_a), (held_b, far_held_b), (got_b, far_got_b))
     ):
-        mine[at] = near_ref[...].astype(F32) * factor
-        far[at] = far_ref[...].astype(F32) * factor
+        near_block = near_ref[...].astype(F32) * factor
+        far_block = far_ref[...].astype(F32) * factor
 
         @pl.when(core == 0)
         def _():
-            pltpu.make_async_copy(mine.at[at], down.at[spots[at]], sems.at[at]).start()
-            pltpu.make_async_copy(far.at[at], up.at[spots[at]], sems.at[4 + at]).start()
+            down[spots[at]] = near_block
+            up[spots[at]] = far_block
 
         @pl.when(core != 0)
         def _():
-            pltpu.make_async_copy(mine.at[at], up.at[spots[at]], sems.at[at]).start()
-            pltpu.make_async_copy(far.at[at], down.at[spots[at]], sems.at[4 + at]).start()
-
-    for at in range(4):
-        pltpu.make_async_copy(mine.at[at], down.at[spots[at]], sems.at[at]).wait()
-        pltpu.make_async_copy(far.at[at], up.at[spots[at]], sems.at[4 + at]).wait()
+            up[spots[at]] = near_block
+            down[spots[at]] = far_block
 
 
 def feature_body(grads, rim_grads, right, below, cot, down_weight, out, wide, pairs, near_mat, low_mat, woven):
@@ -443,7 +440,7 @@
     return lax.ppermute(value, "wide", [(at, at ^ (1 << position)) for at in range(count)])
 
 
-def shards(features, cotangent, down_weight, down_bias, up_weight):
+def program(features, cotangent, down_weight, down_bias, up_weight):
     tile_rows, tile_cols, channels = features.shape
     half_rows, half_cols = tile_rows // 2, tile_cols // 2
     pixels = half_rows * half_cols
@@ -467,7 +464,6 @@
         ],
         in_specs=[ANY] * 5,
         nbytes=1 << 19,
-        name="edges",
         far=(0, 1, 2, 3, 4),
         room=8,
     )(features, cotangent, down_weight, up_weight, down_bias.reshape(1, channels))
@@ -498,7 +494,6 @@
         n_in=5,
         flops=6 * pixels * taps * channels,
         nbytes=6 << 20,
-        name="interior",
         near=(0, 1, 2, 3, 4),
         room=12,
     )(feat_near, cot_near, down_near, bias_near, up_near)
@@ -525,7 +520,6 @@
         n_in=12,
         flops=1 << 26,
         nbytes=3 << 20,
-        name="rim",
         near=tuple(range(12)),
         room=8,
     )(
@@ -540,7 +534,6 @@
         n_in=8,
         flops=2 * pixels * taps * channels,
         nbytes=3 << 20,
-        name="mine",
         near=tuple(range(8)),
         room=12,
     )(feat_patch, cot_patch, act, grads, feat_rim, cot_rim, rim_act, rim_masked)
@@ -564,7 +557,6 @@
             (vm((half, channels), F32), vm((half + SIDE, channels), BF16), vm((8, channels), F32)),
             n_in=3,
             nbytes=half * channels * 12,
-            name="halve",
             near=(0, 1, 2),
         )(held_a, got_a, bias_sum)
         held_b, send_b = call(
@@ -572,7 +564,6 @@
             (vm((half, channels), F32), vm((half, channels), BF16)),
             n_in=2,
             nbytes=half * channels * 12,
-            name="halve",
             near=(0, 1),
         )(held_b, got_b)
         got_a = traded(send_a, order_a[step])
@@ -590,7 +581,6 @@
         n_in=6,
         flops=2 * pixels * 6 * 2 * channels * channels,
         nbytes=3 << 20,
-        name="feature",
         near=(0, 1, 2, 3, 4, 5),
         room=16,
     )(grads, rim_grads, from_right, from_below, cot_near, down_near)
@@ -601,7 +591,6 @@
             (vm((half + side, channels), BF16), vm((8, channels), F32)),
             n_in=3,
             nbytes=half * channels * 8,
-            name="whole",
             near=(0, 1, 2),
         )(held_a, got_a, bias_sum)
         held_b = call(
@@ -609,7 +598,6 @@
             vm((half, channels), BF16),
             n_in=2,
             nbytes=half * channels * 8,
-            name="whole",
             near=(0, 1),
         )(held_b, got_b)
         if step < bits:
@@ -628,18 +616,18 @@
                 functools.partial(place_body, order_a[step]),
                 vm((half, channels), BF16),
                 n_in=2,
-                name="place",
                 near=(0, 1),
             )(held_a, got_a)
             held_b = call(
                 functools.partial(place_body, order_b[step]),
                 vm((half, channels), BF16),
                 n_in=2,
-                name="place",
                 near=(0, 1),
             )(held_b, got_b)
     blocks = (held_a, got_a, held_b, got_b)
-    far_blocks = [turned(block, "narrow", 1) for block in blocks]
+    far_blocks = []
+    for block in blocks:
+        far_blocks.append(turned(block, "narrow", 1))
     size = taps // 4
     down, up, bias_grad = call(
         functools.partial(final_body, (order_a[0], order_b[0])),
@@ -648,17 +636,10 @@
             sds((4, size, channels), F32),
             sds((1, channels), F32),
         ),
-        scratch=[
-            pltpu.VMEM((4, size, channels), F32),
-            pltpu.VMEM((4, size, channels), F32),
-            pltpu.SemaphoreType.DMA((8,)),
-        ],
         n_in=9,
         nbytes=12 * taps * channels,
-        name="final",
         near=tuple(range(9)),
         room=8,
-        out_specs=(ANY, ANY, VM),
     )(*blocks, *far_blocks, bias_sum)
     shape = (3, 3, channels, channels)
     return (feature_grad, down.reshape(shape), up.reshape(shape), bias_grad.reshape(channels))
@@ -666,7 +647,7 @@
 
 def solution(mesh):
     return jax.shard_map(
-        shards,
+        program,
         mesh=mesh,
         in_specs=(
             P(("groups", "wide"), "narrow", None),

time: 41.1 us -> 40.7 us (level)
  Pallas kernels: 9.95 us -> 9.51 us
    pallas_call x14, Pallas kernels: 9.95 us -> 9.51 us  [run(): return kernel(*placed)]
where the time goes in v7:
time: 40.7 us; the launch traced here: 40.5 us
  starting transfers between devices  16.9 us (42%)
  waiting for transfers between devices  13.3 us (33%)
  Pallas kernels  9.51 us (23%)
  between operations  0.74 us (2%)
    ppermute x8, waiting for transfers between devices, traded(): lax.ppermute(value, 'wide', [(at, at ^ 1 << position) for at in range(cou...  9.93 us
    pallas_call x14, Pallas kernels, run(): return kernel(*placed)  9.51 us
    ppermute x8, starting transfers between devices, traded(): lax.ppermute(value, 'wide', [(at, at ^ 1 << position) for at in range(cou...  8.13 us
    ppermute x10, starting transfers between devices, turned(): lax.ppermute(value, axis, [(at, (at + steps) % count) for at in range(cou...  6.31 us
    ppermute x10, waiting for transfers between devices, turned(): lax.ppermute(value, axis, [(at, (at + steps) % count) for at in range(cou...  3.36 us
    ppermute x1, starting transfers between devices, turned_both(): return lax.ppermute(value, ('wide', 'narrow'), pairs)  2.46 us
  transfers between devices with their start and end apart: 19, of which 9 were waited for; matrix products, arithmetic and copies ran while one was open for 0% of the time, Pallas kernels for 14%

profile of v7, /device:TPU:0, one launch (start us, length us, event | category | flops | bytes accessed | tf_op | source)
XLA Modules:
  0.0 40.5 jit_solution(8091338798233730291)
XLA Ops:
  0.6 2.0 %shard_map.84 = (bf16[64,64,128]{2,1,0:T(8,128)(2,1)S(1)}, bf16[64,64,128]{2,1,0:T(8,128)(2,1)S(1)}, bf16[3,3,128,128]{3,2,1,0:T(8,128)(2,1)S(1)}, bf16[3,3,128,...) custom-call(bf16[64,64,128]{2,1,0:T(8,128)(2,1)} %feat.1, ...), custom_call_target="tpu_custom_call" | custom-call | bytes 524288 | tf_op jit(solution)/shard_map/pallas_call | solution.py:36
  2.6 2.5 %collective-permute-start.1 = (bf16[2,8,128]{2,1,0:T(8,128)(2,1)S(1)}, bf16[2,8,128]{2,1,0:T(8,128)(2,1)S(1)}, u32[]{:S(2)}, u32[]{:S(2)}) collective-permute-start(bf16[2,8,128]{2,1,0:T(8,128)(2,1)S(1)} %get-tuple-element.67), channel_id=1, source_target_pairs={{0,3},{1,2},{2,5},{3,4},{4,7},{5,6},{6,9},{7,8},{8,11},{9,10},{10,... | collective-permute-start | bytes 12296 | tf_op jit(solution)/shard_map/ppermute | solution.py:435
  5.1 1.5 %collective-permute-start = (bf16[2,64,128]{2,1,0:T(8,128)(2,1)S(1)}, bf16[2,64,128]{2,1,0:T(8,128)(2,1)S(1)}, u32[]{:S(2)}, u32[]{:S(2)}) collective-permute-start(bf16[2,64,128]{2,1,0:T(8,128)(2,1)S(1)} %get-tuple-element.66), channel_id=1, source_target_pairs={{0,2},{2,4},{4,6},{6,8},{8,10},{10,12},{12,14},{14,0},{1,3},{3,5},... | collective-permute-start | bytes 98312 | tf_op jit(solution)/shard_map/ppermute | solution.py:425
  7.0 2.7 %shard_map.85 = (bf16[32,32,1152]{2,1,0:T(8,128)(2,1)S(1)}, bf16[32,32,1152]{2,1,0:T(8,128)(2,1)S(1)}, bf16[1024,128]{1,0:T(8,128)(2,1)S(1)}, bf16[1024,128]{1,0...) custom-call(bf16[64,64,128]{2,1,0:T(8,128)(2,1)S(1)} %get-tuple-elem, ...), custom_call_target="tpu_custom_call" | custom-call | flops 905969664 | bytes 6291456 | tf_op jit(solution)/shard_map/pallas_call | solution.py:36
  9.7 2.0 %collective-permute-done.top = bf16[2,64,128]{2,1,0:T(8,128)(2,1)S(1)} collective-permute-done((bf16[2,64,128]{2,1,0:T(8,128)(2,1)S(1)}, bf16[2,64,128]{2,1,0:T(8,128)(2,1)S(1)}, u32[]{:S(2)}, u32[]{:S(2)}) %collective-permute-start) | collective-permute-done | bytes 32800 | tf_op jit(solution)/shard_map/ppermute | solution.py:425
  11.7 0.5 %shard_map.86 = (bf16[64,128]{1,0:T(8,128)(2,1)S(1)}, bf16[64,1152]{1,0:T(8,128)(2,1)S(1)}, bf16[64,1152]{1,0:T(8,128)(2,1)S(1)}, bf16[64,128]{1,0:T(8,128)(2,1)...) custom-call(bf16[32,32,1152]{2,1,0:T(8,128)(2,1)S(1)} %get-tuple-ele, ...), custom_call_target="tpu_custom_call" | custom-call | flops 67108864 | bytes 3145728 | tf_op jit(solution)/shard_map/pallas_call | solution.py:36
  12.9 0.9 %shard_map.87 = (f32[576,128]{1,0:T(8,128)S(1)}, f32[576,128]{1,0:T(8,128)S(1)}) custom-call(bf16[32,32,1152]{2,1,0:T(8,128)(2,1)S(1)} %get-tuple-element.62.feat_patch, bf16[32,32,1152]{2,1,0:T(8,128)(2,1)S(1)} %get-tuple-element.63.cot_patch, bf16[1024,128]{1,0:T(8,128)(2,1)S(1)} %get-tuple-element.77.act, bf16[1024,128]{1,0:T(8,128)(2,1)S(1)} %get-tuple-element.78.grads, ...), custom_call_target="tpu_custom_call" | custom-call | flops 301989888 | bytes 3145728 | tf_op jit(solution)/shard_map/pallas_call | solution.py:36
  14.1 1.4 %collective-permute-start.6 = (bf16[288,128]{1,0:T(8,128)(2,1)S(1)}, bf16[288,128]{1,0:T(8,128)(2,1)S(1)}, u32[]{:S(2)}, u32[]{:S(2)}) collective-permute-start(bf16[288,128]{1,0:T(8,128)(2,1)S(1)} %get-tuple-element.90), channel_id=1, source_target_pairs={{0,4},{2,6},{4,0},{6,2},{8,12},{10,14},{12,8},{14,10},{1,5},{3,7},... | collective-permute-start | bytes 221192 | tf_op jit(solution)/shard_map/ppermute | solution.py:440
  15.6 3.1 %collective-permute-done.6.got = bf16[288,128]{1,0:T(8,128)(2,1)S(1)} collective-permute-done((bf16[288,128]{1,0:T(8,128)(2,1)S(1)}, bf16[288,128]{1,0:T(8,128)(2,1)S(1)}, u32[]{:S(2)}, u32[]{:S(2)}) %collective-permute-start.6) | collective-permute-done | bytes 73760 | tf_op jit(solution)/shard_map/ppermute | solution.py:440
  18.7 1.9 %collective-permute-start.7 = (bf16[288,128]{1,0:T(8,128)(2,1)S(1)}, bf16[288,128]{1,0:T(8,128)(2,1)S(1)}, u32[]{:S(2)}, u32[]{:S(2)}) collective-permute-start(bf16[288,128]{1,0:T(8,128)(2,1)S(1)} %shard_map.89.held), channel_id=1, source_target_pairs={{0,2},{2,0},{4,6},{6,4},{8,10},{10,8},{12,14},{14,12},{1,3},{3,1},... | collective-permute-start | bytes 221192 | tf_op jit(solution)/shard_map/ppermute | solution.py:440
  20.9 3.2 %collective-permute-start.8 = (bf16[40,128]{1,0:T(8,128)(2,1)S(1)}, bf16[40,128]{1,0:T(8,128)(2,1)S(1)}, u32[]{:S(2)}, u32[]{:S(2)}) collective-permute-start(bf16[40,128]{1,0:T(8,128)(2,1)S(1)} %pad_maximum_fusion), channel_id=1, source_target_pairs={{0,14},{2,0},{4,2},{6,4},{8,6},{10,8},{12,10},{14,12},{1,15},{3,1}... | collective-permute-start | bytes 30728 | tf_op jit(solution)/shard_map/ppermute | solution.py:425
  24.1 1.1 %collective-permute-done.11.got = bf16[304,128]{1,0:T(8,128)(2,1)S(1)} collective-permute-done((bf16[304,128]{1,0:T(8,128)(2,1)S(1)}, bf16[304,128]{1,0:T(8,128)(2,1)S(1)}, u32[]{:S(2)}, u32[]{:S(2)}) %collective-permute-start.11) | collective-permute-done | bytes 77856 | tf_op jit(solution)/shard_map/ppermute | solution.py:440
  25.2 1.0 %collective-permute-start.12 = (bf16[304,128]{1,0:T(8,128)(2,1)S(1)}, bf16[304,128]{1,0:T(8,128)(2,1)S(1)}, u32[]{:S(2)}, u32[]{:S(2)}) collective-permute-start(bf16[304,128]{1,0:T(8,128)(2,1)S(1)} %get-tuple-element.102.held), channel_id=1, source_target_pairs={{0,8},{2,10},{4,12},{6,14},{8,0},{10,2},{12,4},{14,6},{1,9},{3,11}... | collective-permute-start | bytes 233480 | tf_op jit(solution)/shard_map/ppermute | solution.py:440
  26.2 2.0 %collective-permute-start.9 = (bf16[288,128]{1,0:T(8,128)(2,1)S(1)}, bf16[288,128]{1,0:T(8,128)(2,1)S(1)}, u32[]{:S(2)}, u32[]{:S(2)}) collective-permute-start(bf16[288,128]{1,0:T(8,128)(2,1)S(1)} %shard_map.90.held), channel_id=1, source_target_pairs={{0,8},{2,10},{4,12},{6,14},{8,0},{10,2},{12,4},{14,6},{1,9},{3,11}... | collective-permute-start | bytes 221192 | tf_op jit(solution)/shard_map/ppermute | solution.py:440
  28.2 1.8 %shard_map.91 = bf16[64,64,128]{2,1,0:T(8,128)(2,1)} custom-call(bf16[1024,128]{1,0:T(8,128)(2,1)S(1)} %get-tuple-element.78.grads, bf16[64,128]{1,0:T(8,128)(2,1)S(1)} %get-tuple-element.87.rim_grads, bf16[32,128]{1,0:T(8,128)(2,1)S(1)} %collective-permute-done.5.right, bf16[40,128]{1,0:T(8,128)(2,1)S(1)} %collective-permute-done.8.below, ...), custom_call_target="tpu_custom_call" | custom-call | flops 402653184 | bytes 3145728 | tf_op jit(solution)/shard_map/pallas_call | solution.py:36
  30.0 2.8 %collective-permute-done.9.got = bf16[288,128]{1,0:T(8,128)(2,1)S(1)} collective-permute-done((bf16[288,128]{1,0:T(8,128)(2,1)S(1)}, bf16[288,128]{1,0:T(8,128)(2,1)S(1)}, u32[]{:S(2)}, u32[]{:S(2)}) %collective-permute-start.9) | collective-permute-done | bytes 73760 | tf_op jit(solution)/shard_map/ppermute | solution.py:440
  32.8 0.6 %collective-permute-start.14 = (bf16[288,128]{1,0:T(8,128)(2,1)S(1)}, bf16[288,128]{1,0:T(8,128)(2,1)S(1)}, u32[]{:S(2)}, u32[]{:S(2)}) collective-permute-start(bf16[288,128]{1,0:T(8,128)(2,1)S(1)} %shard_map.96.held_b), channel_id=1, source_target_pairs={{0,4},{2,6},{4,0},{6,2},{8,12},{10,14},{12,8},{14,10},{1,5},{3,7},... | collective-permute-start | bytes 221192 | tf_op jit(solution)/shard_map/ppermute | solution.py:440
  33.4 0.9 %collective-permute-start.13 = (bf16[288,128]{1,0:T(8,128)(2,1)S(1)}, bf16[288,128]{1,0:T(8,128)(2,1)S(1)}, u32[]{:S(2)}, u32[]{:S(2)}) collective-permute-start(bf16[288,128]{1,0:T(8,128)(2,1)S(1)} %get-tuple-element.104.held_a), channel_id=1, source_target_pairs={{0,2},{2,0},{4,6},{6,4},{8,10},{10,8},{12,14},{14,12},{1,3},{3,1},... | collective-permute-start | bytes 221192 | tf_op jit(solution)/shard_map/ppermute | solution.py:440
  34.3 0.5 %collective-permute-start.15 = (bf16[288,128]{1,0:T(8,128)(2,1)S(1)}, bf16[288,128]{1,0:T(8,128)(2,1)S(1)}, u32[]{:S(2)}, u32[]{:S(2)}) collective-permute-start(bf16[288,128]{1,0:T(8,128)(2,1)S(1)} %get-tuple-element.104.held_a), channel_id=1, source_target_pairs={{0,1},{1,0},{2,3},{3,2},{4,5},{5,4},{6,7},{7,6},{8,9},{9,8},{10,11... | collective-permute-start | bytes 221192 | tf_op jit(solution)/shard_map/ppermute | solution.py:425
  34.8 2.4 %collective-permute-done.14.got_b = bf16[288,128]{1,0:T(8,128)(2,1)S(1)} collective-permute-done((bf16[288,128]{1,0:T(8,128)(2,1)S(1)}, bf16[288,128]{1,0:T(8,128)(2,1)S(1)}, u32[]{:S(2)}, u32[]{:S(2)}) %collective-permute-start.14) | collective-permute-done | bytes 73760 | tf_op jit(solution)/shard_map/ppermute | solution.py:440
  37.2 0.6 %collective-permute-done.13.got_a = bf16[288,128]{1,0:T(8,128)(2,1)S(1)} collective-permute-done((bf16[288,128]{1,0:T(8,128)(2,1)S(1)}, bf16[288,128]{1,0:T(8,128)(2,1)S(1)}, u32[]{:S(2)}, u32[]{:S(2)}) %collective-permute-start.13) | collective-permute-done | bytes 73760 | tf_op jit(solution)/shard_map/ppermute | solution.py:440
  37.8 0.7 %collective-permute-done.18.far_got_b = bf16[288,128]{1,0:T(8,128)(2,1)S(1)} collective-permute-done((bf16[288,128]{1,0:T(8,128)(2,1)S(1)}, bf16[288,128]{1,0:T(8,128)(2,1)S(1)}, u32[]{:S(2)}, u32[]{:S(2)}) %collective-permute-start.18) | collective-permute-done | bytes 73760 | tf_op jit(solution)/shard_map/ppermute | solution.py:425
  38.5 0.6 %collective-permute-done.16.far_got_a = bf16[288,128]{1,0:T(8,128)(2,1)S(1)} collective-permute-done((bf16[288,128]{1,0:T(8,128)(2,1)S(1)}, bf16[288,128]{1,0:T(8,128)(2,1)S(1)}, u32[]{:S(2)}, u32[]{:S(2)}) %collective-permute-start.16) | collective-permute-done | bytes 73760 | tf_op jit(solution)/shard_map/ppermute | solution.py:425
  39.1 1.4 %shard_map.97 = (f32[4,288,128]{2,1,0:T(8,128)}, f32[4,288,128]{2,1,0:T(8,128)}, f32[1,128]{1,0:T(1,128)}) custom-call(bf16[288,128]{1,0:T(8,128)(2,1)S(1)} %get-tuple-element.104.held_a, bf16[288,128]{1,0:T(8,128)(2,1)S(1)} %collective-permute-done.13.got_a, bf16[288,128]{1,0:T(8,128)(2,1)S(1)} %shard_map.96.held_b, ...), custom_call_target="tpu_custom_call" | custom-call | bytes 1769472 | tf_op jit(solution)/shard_map/pallas_call | solution.py:36
  (31 shorter events, 1.7 us)
Async XLA Ops:
  2.6 7.1 %collective-permute-start.1 = (bf16[2,8,128]{2,1,0:T(8,128)(2,1)S(1)}, bf16[2,8,128]{2,1,0:T(8,128)(2,1)S(1)}, u32[]{:S(2)}, u32[]{:S(2)}) collective-permute-start(bf16[2,8,128]{2,1,0:T(8,128)(2,1)S(1)} %get-tuple-element.67), channel_id=1, source_target_pairs={{0,3},{1,2},{2,5},{3,4},{4,7},{5,6},{6,9},{7,8},{8,11},{9,10},{10,... | collective-permute-start | bytes 12296 | tf_op jit(solution)/shard_map/ppermute | solution.py:435
  5.1 6.7 %collective-permute-start = (bf16[2,64,128]{2,1,0:T(8,128)(2,1)S(1)}, bf16[2,64,128]{2,1,0:T(8,128)(2,1)S(1)}, u32[]{:S(2)}, u32[]{:S(2)}) collective-permute-start(bf16[2,64,128]{2,1,0:T(8,128)(2,1)S(1)} %get-tuple-element.66), channel_id=1, source_target_pairs={{0,2},{2,4},{4,6},{6,8},{8,10},{10,12},{12,14},{14,0},{1,3},{3,5},... | collective-permute-start | bytes 98312 | tf_op jit(solution)/shard_map/ppermute | solution.py:425
  6.6 5.1 %collective-permute-start.2 = (bf16[2,64,128]{2,1,0:T(8,128)(2,1)S(1)}, bf16[2,64,128]{2,1,0:T(8,128)(2,1)S(1)}, u32[]{:S(2)}, u32[]{:S(2)}) collective-permute-start(bf16[2,64,128]{2,1,0:T(8,128)(2,1)S(1)} %get-tuple-element.68), channel_id=1, source_target_pairs={{0,1},{1,0},{2,3},{3,2},{4,5},{5,4},{6,7},{7,6},{8,9},{9,8},{10,11... | collective-permute-start | bytes 98312 | tf_op jit(solution)/shard_map/ppermute | solution.py:425
  12.3 1.8 %collective-permute-start.4 = (bf16[576,128]{1,0:T(8,128)(2,1)S(1)}, bf16[576,128]{1,0:T(8,128)(2,1)S(1)}, u32[]{:S(2)}, u32[]{:S(2)}) collective-permute-start(bf16[576,128]{1,0:T(8,128)(2,1)S(1)} %get-tuple-element.86), channel_id=1, source_target_pairs={{0,1},{1,0},{2,3},{3,2},{4,5},{5,4},{6,7},{7,6},{8,9},{9,8},{10,11... | collective-permute-start | bytes 442376 | tf_op jit(solution)/shard_map/ppermute | solution.py:425
  12.4 1.6 %collective-permute-start.3 = (bf16[592,128]{1,0:T(8,128)(2,1)S(1)}, bf16[592,128]{1,0:T(8,128)(2,1)S(1)}, u32[]{:S(2)}, u32[]{:S(2)}) collective-permute-start(bf16[592,128]{1,0:T(8,128)(2,1)S(1)} %get-tuple-element.76), channel_id=1, source_target_pairs={{0,1},{1,0},{2,3},{3,2},{4,5},{5,4},{6,7},{7,6},{8,9},{9,8},{10,11... | collective-permute-start | bytes 454664 | tf_op jit(solution)/shard_map/ppermute | solution.py:425
  12.9 1.2 %collective-permute-start.5 = (bf16[32,128]{1,0:T(8,128)(2,1)S(1)}, bf16[32,128]{1,0:T(8,128)(2,1)S(1)}, u32[]{:S(2)}, u32[]{:S(2)}) collective-permute-start(bf16[32,128]{1,0:T(8,128)(2,1)S(1)} %get-tuple-element.111), channel_id=1, source_target_pairs={{0,1},{1,0},{2,3},{3,2},{4,5},{5,4},{6,7},{7,6},{8,9},{9,8},{10,11... | collective-permute-start | bytes 24584 | tf_op jit(solution)/shard_map/ppermute | solution.py:425
  14.0 6.6 %collective-permute-start.10 = (bf16[304,128]{1,0:T(8,128)(2,1)S(1)}, bf16[304,128]{1,0:T(8,128)(2,1)S(1)}, u32[]{:S(2)}, u32[]{:S(2)}) collective-permute-start(bf16[304,128]{1,0:T(8,128)(2,1)S(1)} %get-tuple-element.98), channel_id=1, source_target_pairs={{0,2},{2,0},{4,6},{6,4},{8,10},{10,8},{12,14},{14,12},{1,3},{3,1},... | collective-permute-start | bytes 233480 | tf_op jit(solution)/shard_map/ppermute | solution.py:440
  14.1 4.5 %collective-permute-start.6 = (bf16[288,128]{1,0:T(8,128)(2,1)S(1)}, bf16[288,128]{1,0:T(8,128)(2,1)S(1)}, u32[]{:S(2)}, u32[]{:S(2)}) collective-permute-start(bf16[288,128]{1,0:T(8,128)(2,1)S(1)} %get-tuple-element.90), channel_id=1, source_target_pairs={{0,4},{2,6},{4,0},{6,2},{8,12},{10,14},{12,8},{14,10},{1,5},{3,7},... | collective-permute-start | bytes 221192 | tf_op jit(solution)/shard_map/ppermute | solution.py:440
  18.7 7.5 %collective-permute-start.7 = (bf16[288,128]{1,0:T(8,128)(2,1)S(1)}, bf16[288,128]{1,0:T(8,128)(2,1)S(1)}, u32[]{:S(2)}, u32[]{:S(2)}) collective-permute-start(bf16[288,128]{1,0:T(8,128)(2,1)S(1)} %shard_map.89.held), channel_id=1, source_target_pairs={{0,2},{2,0},{4,6},{6,4},{8,10},{10,8},{12,14},{14,12},{1,3},{3,1},... | collective-permute-start | bytes 221192 | tf_op jit(solution)/shard_map/ppermute | solution.py:440
  20.7 4.5 %collective-permute-start.11 = (bf16[304,128]{1,0:T(8,128)(2,1)S(1)}, bf16[304,128]{1,0:T(8,128)(2,1)S(1)}, u32[]{:S(2)}, u32[]{:S(2)}) collective-permute-start(bf16[304,128]{1,0:T(8,128)(2,1)S(1)} %get-tuple-element.100.held), channel_id=1, source_target_pairs={{0,4},{2,6},{4,0},{6,2},{8,12},{10,14},{12,8},{14,10},{1,5},{3,7},... | collective-permute-start | bytes 233480 | tf_op jit(solution)/shard_map/ppermute | solution.py:440
  20.9 5.3 %collective-permute-start.8 = (bf16[40,128]{1,0:T(8,128)(2,1)S(1)}, bf16[40,128]{1,0:T(8,128)(2,1)S(1)}, u32[]{:S(2)}, u32[]{:S(2)}) collective-permute-start(bf16[40,128]{1,0:T(8,128)(2,1)S(1)} %pad_maximum_fusion), channel_id=1, source_target_pairs={{0,14},{2,0},{4,2},{6,4},{8,6},{10,8},{12,10},{14,12},{1,15},{3,1}... | collective-permute-start | bytes 30728 | tf_op jit(solution)/shard_map/ppermute | solution.py:425
  25.2 8.2 %collective-permute-start.12 = (bf16[304,128]{1,0:T(8,128)(2,1)S(1)}, bf16[304,128]{1,0:T(8,128)(2,1)S(1)}, u32[]{:S(2)}, u32[]{:S(2)}) collective-permute-start(bf16[304,128]{1,0:T(8,128)(2,1)S(1)} %get-tuple-element.102.held), channel_id=1, source_target_pairs={{0,8},{2,10},{4,12},{6,14},{8,0},{10,2},{12,4},{14,6},{1,9},{3,11}... | collective-permute-start | bytes 233480 | tf_op jit(solution)/shard_map/ppermute | solution.py:440
  26.2 6.6 %collective-permute-start.9 = (bf16[288,128]{1,0:T(8,128)(2,1)S(1)}, bf16[288,128]{1,0:T(8,128)(2,1)S(1)}, u32[]{:S(2)}, u32[]{:S(2)}) collective-permute-start(bf16[288,128]{1,0:T(8,128)(2,1)S(1)} %shard_map.90.held), channel_id=1, source_target_pairs={{0,8},{2,10},{4,12},{6,14},{8,0},{10,2},{12,4},{14,6},{1,9},{3,11}... | collective-permute-start | bytes 221192 | tf_op jit(solution)/shard_map/ppermute | solution.py:440
  32.8 4.4 %collective-permute-start.14 = (bf16[288,128]{1,0:T(8,128)(2,1)S(1)}, bf16[288,128]{1,0:T(8,128)(2,1)S(1)}, u32[]{:S(2)}, u32[]{:S(2)}) collective-permute-start(bf16[288,128]{1,0:T(8,128)(2,1)S(1)} %shard_map.96.held_b), channel_id=1, source_target_pairs={{0,4},{2,6},{4,0},{6,2},{8,12},{10,14},{12,8},{14,10},{1,5},{3,7},... | collective-permute-start | bytes 221192 | tf_op jit(solution)/shard_map/ppermute | solution.py:440
  33.4 4.4 %collective-permute-start.13 = (bf16[288,128]{1,0:T(8,128)(2,1)S(1)}, bf16[288,128]{1,0:T(8,128)(2,1)S(1)}, u32[]{:S(2)}, u32[]{:S(2)}) collective-permute-start(bf16[288,128]{1,0:T(8,128)(2,1)S(1)} %get-tuple-element.104.held_a), channel_id=1, source_target_pairs={{0,2},{2,0},{4,6},{6,4},{8,10},{10,8},{12,14},{14,12},{1,3},{3,1},... | collective-permute-start | bytes 221192 | tf_op jit(solution)/shard_map/ppermute | solution.py:440
  34.3 3.5 %collective-permute-start.17 = (bf16[288,128]{1,0:T(8,128)(2,1)S(1)}, bf16[288,128]{1,0:T(8,128)(2,1)S(1)}, u32[]{:S(2)}, u32[]{:S(2)}) collective-permute-start(bf16[288,128]{1,0:T(8,128)(2,1)S(1)} %shard_map.96.held_b), channel_id=1, source_target_pairs={{0,1},{1,0},{2,3},{3,2},{4,5},{5,4},{6,7},{7,6},{8,9},{9,8},{10,11... | collective-permute-start | bytes 221192 | tf_op jit(solution)/shard_map/ppermute | solution.py:425
  34.3 3.5 %collective-permute-start.15 = (bf16[288,128]{1,0:T(8,128)(2,1)S(1)}, bf16[288,128]{1,0:T(8,128)(2,1)S(1)}, u32[]{:S(2)}, u32[]{:S(2)}) collective-permute-start(bf16[288,128]{1,0:T(8,128)(2,1)S(1)} %get-tuple-element.104.held_a), channel_id=1, source_target_pairs={{0,1},{1,0},{2,3},{3,2},{4,5},{5,4},{6,7},{7,6},{8,9},{9,8},{10,11... | collective-permute-start | bytes 221192 | tf_op jit(solution)/shard_map/ppermute | solution.py:425
  37.2 1.3 %collective-permute-start.18 = (bf16[288,128]{1,0:T(8,128)(2,1)S(1)}, bf16[288,128]{1,0:T(8,128)(2,1)S(1)}, u32[]{:S(2)}, u32[]{:S(2)}) collective-permute-start(bf16[288,128]{1,0:T(8,128)(2,1)S(1)} %collective-permute-done.14.got_b), channel_id=1, source_target_pairs={{0,1},{1,0},{2,3},{3,2},{4,5},{5,4},{6,7},{7,6},{8,9},{9,8},{10,11... | collective-permute-start | bytes 221192 | tf_op jit(solution)/shard_map/ppermute | solution.py:425
  37.8 1.3 %collective-permute-start.16 = (bf16[288,128]{1,0:T(8,128)(2,1)S(1)}, bf16[288,128]{1,0:T(8,128)(2,1)S(1)}, u32[]{:S(2)}, u32[]{:S(2)}) collective-permute-start(bf16[288,128]{1,0:T(8,128)(2,1)S(1)} %collective-permute-done.13.got_a), channel_id=1, source_target_pairs={{0,1},{1,0},{2,3},{3,2},{4,5},{5,4},{6,7},{7,6},{8,9},{9,8},{10,11... | collective-permute-start | bytes 221192 | tf_op jit(solution)/shard_map/ppermute | solution.py:425

commit v8 on v7

--- a/solution.py
+++ b/solution.py
@@ -539,14 +539,12 @@
     )(feat_patch, cot_patch, act, grads, feat_rim, cot_rim, rim_act, rim_masked)
     from_right = turned(rim_grads[half_cols:], "narrow", -1)
     got_a, mine_a, mine_b = lax.optimization_barrier((got_a, mine_a, mine_b))
-    got_b, from_right = lax.optimization_barrier((got_b, from_right))
-    from_below = turned(
-        jnp.concatenate([rim_grads[:half_cols], from_right[:8]], axis=0), "wide", -1
-    )
+    low = jnp.concatenate([rim_grads[:half_cols], from_right[:8]], axis=0)
+    from_below = turned(low, "wide", -1)
 
     bits = lax.axis_size("wide").bit_length() - 1
-    order_a = list(range(bits))
-    order_b = order_a[1::-1] + order_a[2:]
+    order_a = [1, 0, *range(2, bits)] if bits > 1 else list(range(bits))
+    order_b = [0, 2, 1, *range(3, bits)] if bits > 2 else list(range(bits))
     halvings = 1 if bits <= 3 else 2
     half = taps // 2
     held_a, held_b = mine_a, mine_b
@@ -603,8 +601,6 @@
         if step < bits:
             got_a = traded(held_a, order_a[step])
             got_b = traded(held_b, order_b[step])
-            if step == halvings:
-                got_b, from_below = lax.optimization_barrier((got_b, from_below))
             if step == bits - 1:
                 got_b, feature_grad = lax.optimization_barrier((got_b, feature_grad))
     for step in reversed(range(halvings)):

time: 40.7 us -> 42.5 us (1.044)
  starting transfers between devices: 16.9 us -> 17.8 us
  waiting for transfers between devices: 13.3 us -> 14.2 us
    ppermute x10, waiting for transfers between devices: 3.36 us -> 5.83 us  [turned(): lax.ppermute(value, axis, [(at, (at + steps) % count) for at in range(cou...]
    ppermute x8, waiting for transfers between devices: 9.93 us -> 8.34 us  [traded(): lax.ppermute(value, 'wide', [(at, at ^ 1 << position) for at in range(cou...]
    ppermute x8, starting transfers between devices: 8.13 us -> 9.31 us  [traded(): lax.ppermute(value, 'wide', [(at, at ^ 1 << position) for at in range(cou...]
  transfers between devices with their start and end apart: 19 -> 19, of which waited for: 9 -> 8; matrix products, arithmetic and copies ran while one was open for 0% -> 0% of each run, Pallas kernels for 14% -> 13%
where the time goes in v8:
time: 42.5 us; the launch traced here: 42.2 us
  starting transfers between devices  17.8 us (42%)
  waiting for transfers between devices  14.2 us (33%)
  Pallas kernels  9.52 us (22%)
  between operations  0.75 us (2%)
    pallas_call x14, Pallas kernels, run(): return kernel(*placed)  9.52 us
    ppermute x8, starting transfers between devices, traded(): lax.ppermute(value, 'wide', [(at, at ^ 1 << position) for at in range(cou...  9.31 us
    ppermute x8, waiting for transfers between devices, traded(): lax.ppermute(value, 'wide', [(at, at ^ 1 << position) for at in range(cou...  8.34 us
    ppermute x10, starting transfers between devices, turned(): lax.ppermute(value, axis, [(at, (at + steps) % count) for at in range(cou...  5.99 us
    ppermute x10, waiting for transfers between devices, turned(): lax.ppermute(value, axis, [(at, (at + steps) % count) for at in range(cou...  5.83 us
    ppermute x1, starting transfers between devices, turned_both(): return lax.ppermute(value, ('wide', 'narrow'), pairs)  2.46 us
  transfers between devices with their start and end apart: 19, of which 8 were waited for; matrix products, arithmetic and copies ran while one was open for 0% of the time, Pallas kernels for 13%

profile of v8, /device:TPU:0, one launch (start us, length us, event | category | flops | bytes accessed | tf_op | source)
XLA Modules:
  0.0 42.2 jit_solution(16426471625172490140)
XLA Ops:
  0.6 2.0 %shard_map.84 = (bf16[64,64,128]{2,1,0:T(8,128)(2,1)S(1)}, bf16[64,64,128]{2,1,0:T(8,128)(2,1)S(1)}, bf16[3,3,128,128]{3,2,1,0:T(8,128)(2,1)S(1)}, bf16[3,3,128,...) custom-call(bf16[64,64,128]{2,1,0:T(8,128)(2,1)} %feat.1, ...), custom_call_target="tpu_custom_call" | custom-call | bytes 524288 | tf_op jit(solution)/shard_map/pallas_call | solution.py:36
  2.6 2.5 %collective-permute-start.1 = (bf16[2,8,128]{2,1,0:T(8,128)(2,1)S(1)}, bf16[2,8,128]{2,1,0:T(8,128)(2,1)S(1)}, u32[]{:S(2)}, u32[]{:S(2)}) collective-permute-start(bf16[2,8,128]{2,1,0:T(8,128)(2,1)S(1)} %get-tuple-element.64), channel_id=1, source_target_pairs={{0,3},{1,2},{2,5},{3,4},{4,7},{5,6},{6,9},{7,8},{8,11},{9,10},{10,... | collective-permute-start | bytes 12296 | tf_op jit(solution)/shard_map/ppermute | solution.py:435
  5.1 1.5 %collective-permute-start = (bf16[2,64,128]{2,1,0:T(8,128)(2,1)S(1)}, bf16[2,64,128]{2,1,0:T(8,128)(2,1)S(1)}, u32[]{:S(2)}, u32[]{:S(2)}) collective-permute-start(bf16[2,64,128]{2,1,0:T(8,128)(2,1)S(1)} %get-tuple-element.63), channel_id=1, source_target_pairs={{0,2},{2,4},{4,6},{6,8},{8,10},{10,12},{12,14},{14,0},{1,3},{3,5},... | collective-permute-start | bytes 98312 | tf_op jit(solution)/shard_map/ppermute | solution.py:425
  7.0 2.7 %shard_map.85 = (bf16[32,32,1152]{2,1,0:T(8,128)(2,1)S(1)}, bf16[32,32,1152]{2,1,0:T(8,128)(2,1)S(1)}, bf16[1024,128]{1,0:T(8,128)(2,1)S(1)}, bf16[1024,128]{1,0...) custom-call(bf16[64,64,128]{2,1,0:T(8,128)(2,1)S(1)} %get-tuple-elem, ...), custom_call_target="tpu_custom_call" | custom-call | flops 905969664 | bytes 6291456 | tf_op jit(solution)/shard_map/pallas_call | solution.py:36
  9.7 2.0 %collective-permute-done.top = bf16[2,64,128]{2,1,0:T(8,128)(2,1)S(1)} collective-permute-done((bf16[2,64,128]{2,1,0:T(8,128)(2,1)S(1)}, bf16[2,64,128]{2,1,0:T(8,128)(2,1)S(1)}, u32[]{:S(2)}, u32[]{:S(2)}) %collective-permute-start) | collective-permute-done | bytes 32800 | tf_op jit(solution)/shard_map/ppermute | solution.py:425
  11.7 0.5 %shard_map.86 = (bf16[64,128]{1,0:T(8,128)(2,1)S(1)}, bf16[64,1152]{1,0:T(8,128)(2,1)S(1)}, bf16[64,1152]{1,0:T(8,128)(2,1)S(1)}, bf16[64,128]{1,0:T(8,128)(2,1)...) custom-call(bf16[32,32,1152]{2,1,0:T(8,128)(2,1)S(1)} %get-tuple-ele, ...), custom_call_target="tpu_custom_call" | custom-call | flops 67108864 | bytes 3145728 | tf_op jit(solution)/shard_map/pallas_call | solution.py:36
  12.9 0.9 %shard_map.87 = (f32[576,128]{1,0:T(8,128)S(1)}, f32[576,128]{1,0:T(8,128)S(1)}) custom-call(bf16[32,32,1152]{2,1,0:T(8,128)(2,1)S(1)} %get-tuple-element.59.feat_patch, bf16[32,32,1152]{2,1,0:T(8,128)(2,1)S(1)} %get-tuple-element.60.cot_patch, bf16[1024,128]{1,0:T(8,128)(2,1)S(1)} %get-tuple-element.74.act, bf16[1024,128]{1,0:T(8,128)(2,1)S(1)} %get-tuple-element.75.grads, ...), custom_call_target="tpu_custom_call" | custom-call | flops 301989888 | bytes 3145728 | tf_op jit(solution)/shard_map/pallas_call | solution.py:36
  14.0 1.2 %collective-permute-start.5 = (bf16[288,128]{1,0:T(8,128)(2,1)S(1)}, bf16[288,128]{1,0:T(8,128)(2,1)S(1)}, u32[]{:S(2)}, u32[]{:S(2)}) collective-permute-start(bf16[288,128]{1,0:T(8,128)(2,1)S(1)} %get-tuple-element.85), channel_id=1, source_target_pairs={{0,2},{2,0},{4,6},{6,4},{8,10},{10,8},{12,14},{14,12},{1,3},{3,1},... | collective-permute-start | bytes 221192 | tf_op jit(solution)/shard_map/ppermute | solution.py:440
  15.1 3.4 %collective-permute-done.5.got = bf16[288,128]{1,0:T(8,128)(2,1)S(1)} collective-permute-done((bf16[288,128]{1,0:T(8,128)(2,1)S(1)}, bf16[288,128]{1,0:T(8,128)(2,1)S(1)}, u32[]{:S(2)}, u32[]{:S(2)}) %collective-permute-start.5) | collective-permute-done | bytes 73760 | tf_op jit(solution)/shard_map/ppermute | solution.py:440
  18.5 2.3 %collective-permute-start.6 = (bf16[288,128]{1,0:T(8,128)(2,1)S(1)}, bf16[288,128]{1,0:T(8,128)(2,1)S(1)}, u32[]{:S(2)}, u32[]{:S(2)}) collective-permute-start(bf16[288,128]{1,0:T(8,128)(2,1)S(1)} %shard_map.89.held), channel_id=1, source_target_pairs={{0,8},{2,10},{4,12},{6,14},{8,0},{10,2},{12,4},{14,6},{1,9},{3,11}... | collective-permute-start | bytes 221192 | tf_op jit(solution)/shard_map/ppermute | solution.py:440
  21.0 1.2 %collective-permute-done.8.right = bf16[32,128]{1,0:T(8,128)(2,1)S(1)} collective-permute-done((bf16[32,128]{1,0:T(8,128)(2,1)S(1)}, bf16[32,128]{1,0:T(8,128)(2,1)S(1)}, u32[]{:S(2)}, u32[]{:S(2)}) %collective-permute-start.8) | collective-permute-done | bytes 8224 | tf_op jit(solution)/shard_map/ppermute | solution.py:425
  22.2 1.7 %collective-permute-done.6.got = bf16[288,128]{1,0:T(8,128)(2,1)S(1)} collective-permute-done((bf16[288,128]{1,0:T(8,128)(2,1)S(1)}, bf16[288,128]{1,0:T(8,128)(2,1)S(1)}, u32[]{:S(2)}, u32[]{:S(2)}) %collective-permute-start.6) | collective-permute-done | bytes 73760 | tf_op jit(solution)/shard_map/ppermute | solution.py:440
  23.9 1.9 %collective-permute-start.7 = (bf16[288,128]{1,0:T(8,128)(2,1)S(1)}, bf16[288,128]{1,0:T(8,128)(2,1)S(1)}, u32[]{:S(2)}, u32[]{:S(2)}) collective-permute-start(bf16[288,128]{1,0:T(8,128)(2,1)S(1)} %shard_map.90.held), channel_id=1, source_target_pairs={{0,4},{2,6},{4,0},{6,2},{8,12},{10,14},{12,8},{14,10},{1,5},{3,7},... | collective-permute-start | bytes 221192 | tf_op jit(solution)/shard_map/ppermute | solution.py:440
  25.9 0.9 %collective-permute-start.12 = (bf16[304,128]{1,0:T(8,128)(2,1)S(1)}, bf16[304,128]{1,0:T(8,128)(2,1)S(1)}, u32[]{:S(2)}, u32[]{:S(2)}) collective-permute-start(bf16[304,128]{1,0:T(8,128)(2,1)S(1)} %get-tuple-element.96.held), channel_id=1, source_target_pairs={{0,8},{2,10},{4,12},{6,14},{8,0},{10,2},{12,4},{14,6},{1,9},{3,11}... | collective-permute-start | bytes 233480 | tf_op jit(solution)/shard_map/ppermute | solution.py:440
  26.7 2.9 %collective-permute-start.9 = (bf16[40,128]{1,0:T(8,128)(2,1)S(1)}, bf16[40,128]{1,0:T(8,128)(2,1)S(1)}, u32[]{:S(2)}, u32[]{:S(2)}) collective-permute-start(bf16[40,128]{1,0:T(8,128)(2,1)S(1)} %pad_maximum_fusion), channel_id=1, source_target_pairs={{0,14},{2,0},{4,2},{6,4},{8,6},{10,8},{12,10},{14,12},{1,15},{3,1}... | collective-permute-start | bytes 30728 | tf_op jit(solution)/shard_map/ppermute | solution.py:425
  29.6 1.4 %collective-permute-done.9.below = bf16[40,128]{1,0:T(8,128)(2,1)S(1)} collective-permute-done((bf16[40,128]{1,0:T(8,128)(2,1)S(1)}, bf16[40,128]{1,0:T(8,128)(2,1)S(1)}, u32[]{:S(2)}, u32[]{:S(2)}) %collective-permute-start.9) | collective-permute-done | bytes 10272 | tf_op jit(solution)/shard_map/ppermute | solution.py:425
  31.0 1.8 %shard_map.91 = bf16[64,64,128]{2,1,0:T(8,128)(2,1)} custom-call(bf16[1024,128]{1,0:T(8,128)(2,1)S(1)} %get-tuple-element.75.grads, bf16[64,128]{1,0:T(8,128)(2,1)S(1)} %get-tuple-element.86.rim_grads, bf16[32,128]{1,0:T(8,128)(2,1)S(1)} %collective-permute-done.8.right, bf16[40,128]{1,0:T(8,128)(2,1)S(1)} %collective-permute-done.9.below, ...), custom_call_target="tpu_custom_call" | custom-call | flops 402653184 | bytes 3145728 | tf_op jit(solution)/shard_map/pallas_call | solution.py:36
  32.8 2.3 %collective-permute-start.14 = (bf16[288,128]{1,0:T(8,128)(2,1)S(1)}, bf16[288,128]{1,0:T(8,128)(2,1)S(1)}, u32[]{:S(2)}, u32[]{:S(2)}) collective-permute-start(bf16[288,128]{1,0:T(8,128)(2,1)S(1)} %shard_map.96.held_b), channel_id=1, source_target_pairs={{0,2},{2,0},{4,6},{6,4},{8,10},{10,8},{12,14},{14,12},{1,3},{3,1},... | collective-permute-start | bytes 221192 | tf_op jit(solution)/shard_map/ppermute | solution.py:440
  35.1 0.6 %collective-permute-start.13 = (bf16[288,128]{1,0:T(8,128)(2,1)S(1)}, bf16[288,128]{1,0:T(8,128)(2,1)S(1)}, u32[]{:S(2)}, u32[]{:S(2)}) collective-permute-start(bf16[288,128]{1,0:T(8,128)(2,1)S(1)} %get-tuple-element.98.held_a), channel_id=1, source_target_pairs={{0,4},{2,6},{4,0},{6,2},{8,12},{10,14},{12,8},{14,10},{1,5},{3,7},... | collective-permute-start | bytes 221192 | tf_op jit(solution)/shard_map/ppermute | solution.py:440
  35.8 0.5 %collective-permute-start.15 = (bf16[288,128]{1,0:T(8,128)(2,1)S(1)}, bf16[288,128]{1,0:T(8,128)(2,1)S(1)}, u32[]{:S(2)}, u32[]{:S(2)}) collective-permute-start(bf16[288,128]{1,0:T(8,128)(2,1)S(1)} %get-tuple-element.98.held_a), channel_id=1, source_target_pairs={{0,1},{1,0},{2,3},{3,2},{4,5},{5,4},{6,7},{7,6},{8,9},{9,8},{10,11... | collective-permute-start | bytes 221192 | tf_op jit(solution)/shard_map/ppermute | solution.py:425
  36.3 1.2 %collective-permute-done.14.got_b = bf16[288,128]{1,0:T(8,128)(2,1)S(1)} collective-permute-done((bf16[288,128]{1,0:T(8,128)(2,1)S(1)}, bf16[288,128]{1,0:T(8,128)(2,1)S(1)}, u32[]{:S(2)}, u32[]{:S(2)}) %collective-permute-start.14) | collective-permute-done | bytes 73760 | tf_op jit(solution)/shard_map/ppermute | solution.py:440
  37.5 2.1 %collective-permute-done.13.got_a = bf16[288,128]{1,0:T(8,128)(2,1)S(1)} collective-permute-done((bf16[288,128]{1,0:T(8,128)(2,1)S(1)}, bf16[288,128]{1,0:T(8,128)(2,1)S(1)}, u32[]{:S(2)}, u32[]{:S(2)}) %collective-permute-start.13) | collective-permute-done | bytes 73760 | tf_op jit(solution)/shard_map/ppermute | solution.py:440
  39.6 1.2 %collective-permute-done.16.far_got_a = bf16[288,128]{1,0:T(8,128)(2,1)S(1)} collective-permute-done((bf16[288,128]{1,0:T(8,128)(2,1)S(1)}, bf16[288,128]{1,0:T(8,128)(2,1)S(1)}, u32[]{:S(2)}, u32[]{:S(2)}) %collective-permute-start.16) | collective-permute-done | bytes 73760 | tf_op jit(solution)/shard_map/ppermute | solution.py:425
  40.8 1.4 %shard_map.97 = (f32[4,288,128]{2,1,0:T(8,128)}, f32[4,288,128]{2,1,0:T(8,128)}, f32[1,128]{1,0:T(1,128)}) custom-call(bf16[288,128]{1,0:T(8,128)(2,1)S(1)} %get-tuple-element.98.held_a, bf16[288,128]{1,0:T(8,128)(2,1)S(1)} %collective-permute-done.13.got_a, bf16[288,128]{1,0:T(8,128)(2,1)S(1)} %shard_map.96.held_b, ...), custom_call_target="tpu_custom_call" | custom-call | bytes 1769472 | tf_op jit(solution)/shard_map/pallas_call | solution.py:36
  (31 shorter events, 1.5 us)
Async XLA Ops:
  2.6 7.1 %collective-permute-start.1 = (bf16[2,8,128]{2,1,0:T(8,128)(2,1)S(1)}, bf16[2,8,128]{2,1,0:T(8,128)(2,1)S(1)}, u32[]{:S(2)}, u32[]{:S(2)}) collective-permute-start(bf16[2,8,128]{2,1,0:T(8,128)(2,1)S(1)} %get-tuple-element.64), channel_id=1, source_target_pairs={{0,3},{1,2},{2,5},{3,4},{4,7},{5,6},{6,9},{7,8},{8,11},{9,10},{10,... | collective-permute-start | bytes 12296 | tf_op jit(solution)/shard_map/ppermute | solution.py:435
  5.1 6.7 %collective-permute-start = (bf16[2,64,128]{2,1,0:T(8,128)(2,1)S(1)}, bf16[2,64,128]{2,1,0:T(8,128)(2,1)S(1)}, u32[]{:S(2)}, u32[]{:S(2)}) collective-permute-start(bf16[2,64,128]{2,1,0:T(8,128)(2,1)S(1)} %get-tuple-element.63), channel_id=1, source_target_pairs={{0,2},{2,4},{4,6},{6,8},{8,10},{10,12},{12,14},{14,0},{1,3},{3,5},... | collective-permute-start | bytes 98312 | tf_op jit(solution)/shard_map/ppermute | solution.py:425
  6.6 5.1 %collective-permute-start.2 = (bf16[2,64,128]{2,1,0:T(8,128)(2,1)S(1)}, bf16[2,64,128]{2,1,0:T(8,128)(2,1)S(1)}, u32[]{:S(2)}, u32[]{:S(2)}) collective-permute-start(bf16[2,64,128]{2,1,0:T(8,128)(2,1)S(1)} %get-tuple-element.65), channel_id=1, source_target_pairs={{0,1},{1,0},{2,3},{3,2},{4,5},{5,4},{6,7},{7,6},{8,9},{9,8},{10,11... | collective-permute-start | bytes 98312 | tf_op jit(solution)/shard_map/ppermute | solution.py:425
  12.3 1.5 %collective-permute-start.3 = (bf16[592,128]{1,0:T(8,128)(2,1)S(1)}, bf16[592,128]{1,0:T(8,128)(2,1)S(1)}, u32[]{:S(2)}, u32[]{:S(2)}) collective-permute-start(bf16[592,128]{1,0:T(8,128)(2,1)S(1)} %get-tuple-element.73), channel_id=1, source_target_pairs={{0,1},{1,0},{2,3},{3,2},{4,5},{5,4},{6,7},{7,6},{8,9},{9,8},{10,11... | collective-permute-start | bytes 454664 | tf_op jit(solution)/shard_map/ppermute | solution.py:425
  12.4 1.6 %collective-permute-start.4 = (bf16[576,128]{1,0:T(8,128)(2,1)S(1)}, bf16[576,128]{1,0:T(8,128)(2,1)S(1)}, u32[]{:S(2)}, u32[]{:S(2)}) collective-permute-start(bf16[576,128]{1,0:T(8,128)(2,1)S(1)} %get-tuple-element.83), channel_id=1, source_target_pairs={{0,1},{1,0},{2,3},{3,2},{4,5},{5,4},{6,7},{7,6},{8,9},{9,8},{10,11... | collective-permute-start | bytes 442376 | tf_op jit(solution)/shard_map/ppermute | solution.py:425
  13.9 7.0 %collective-permute-start.10 = (bf16[304,128]{1,0:T(8,128)(2,1)S(1)}, bf16[304,128]{1,0:T(8,128)(2,1)S(1)}, u32[]{:S(2)}, u32[]{:S(2)}) collective-permute-start(bf16[304,128]{1,0:T(8,128)(2,1)S(1)} %get-tuple-element.92), channel_id=1, source_target_pairs={{0,4},{2,6},{4,0},{6,2},{8,12},{10,14},{12,8},{14,10},{1,5},{3,7},... | collective-permute-start | bytes 233480 | tf_op jit(solution)/shard_map/ppermute | solution.py:440
  14.0 4.5 %collective-permute-start.5 = (bf16[288,128]{1,0:T(8,128)(2,1)S(1)}, bf16[288,128]{1,0:T(8,128)(2,1)S(1)}, u32[]{:S(2)}, u32[]{:S(2)}) collective-permute-start(bf16[288,128]{1,0:T(8,128)(2,1)S(1)} %get-tuple-element.85), channel_id=1, source_target_pairs={{0,2},{2,0},{4,6},{6,4},{8,10},{10,8},{12,14},{14,12},{1,3},{3,1},... | collective-permute-start | bytes 221192 | tf_op jit(solution)/shard_map/ppermute | solution.py:440
  18.5 5.4 %collective-permute-start.6 = (bf16[288,128]{1,0:T(8,128)(2,1)S(1)}, bf16[288,128]{1,0:T(8,128)(2,1)S(1)}, u32[]{:S(2)}, u32[]{:S(2)}) collective-permute-start(bf16[288,128]{1,0:T(8,128)(2,1)S(1)} %shard_map.89.held), channel_id=1, source_target_pairs={{0,8},{2,10},{4,12},{6,14},{8,0},{10,2},{12,4},{14,6},{1,9},{3,11}... | collective-permute-start | bytes 221192 | tf_op jit(solution)/shard_map/ppermute | solution.py:440
  20.9 5.0 %collective-permute-start.11 = (bf16[304,128]{1,0:T(8,128)(2,1)S(1)}, bf16[304,128]{1,0:T(8,128)(2,1)S(1)}, u32[]{:S(2)}, u32[]{:S(2)}) collective-permute-start(bf16[304,128]{1,0:T(8,128)(2,1)S(1)} %get-tuple-element.94.held), channel_id=1, source_target_pairs={{0,2},{2,0},{4,6},{6,4},{8,10},{10,8},{12,14},{14,12},{1,3},{3,1},... | collective-permute-start | bytes 233480 | tf_op jit(solution)/shard_map/ppermute | solution.py:440
  21.0 1.2 %collective-permute-start.8 = (bf16[32,128]{1,0:T(8,128)(2,1)S(1)}, bf16[32,128]{1,0:T(8,128)(2,1)S(1)}, u32[]{:S(2)}, u32[]{:S(2)}) collective-permute-start(bf16[32,128]{1,0:T(8,128)(2,1)S(1)} %get-tuple-element.105), channel_id=1, source_target_pairs={{0,1},{1,0},{2,3},{3,2},{4,5},{5,4},{6,7},{7,6},{8,9},{9,8},{10,11... | collective-permute-start | bytes 24584 | tf_op jit(solution)/shard_map/ppermute | solution.py:425
  23.9 8.9 %collective-permute-start.7 = (bf16[288,128]{1,0:T(8,128)(2,1)S(1)}, bf16[288,128]{1,0:T(8,128)(2,1)S(1)}, u32[]{:S(2)}, u32[]{:S(2)}) collective-permute-start(bf16[288,128]{1,0:T(8,128)(2,1)S(1)} %shard_map.90.held), channel_id=1, source_target_pairs={{0,4},{2,6},{4,0},{6,2},{8,12},{10,14},{12,8},{14,10},{1,5},{3,7},... | collective-permute-start | bytes 221192 | tf_op jit(solution)/shard_map/ppermute | solution.py:440
  25.9 9.3 %collective-permute-start.12 = (bf16[304,128]{1,0:T(8,128)(2,1)S(1)}, bf16[304,128]{1,0:T(8,128)(2,1)S(1)}, u32[]{:S(2)}, u32[]{:S(2)}) collective-permute-start(bf16[304,128]{1,0:T(8,128)(2,1)S(1)} %get-tuple-element.96.held), channel_id=1, source_target_pairs={{0,8},{2,10},{4,12},{6,14},{8,0},{10,2},{12,4},{14,6},{1,9},{3,11}... | collective-permute-start | bytes 233480 | tf_op jit(solution)/shard_map/ppermute | solution.py:440
  26.7 4.3 %collective-permute-start.9 = (bf16[40,128]{1,0:T(8,128)(2,1)S(1)}, bf16[40,128]{1,0:T(8,128)(2,1)S(1)}, u32[]{:S(2)}, u32[]{:S(2)}) collective-permute-start(bf16[40,128]{1,0:T(8,128)(2,1)S(1)} %pad_maximum_fusion), channel_id=1, source_target_pairs={{0,14},{2,0},{4,2},{6,4},{8,6},{10,8},{12,10},{14,12},{1,15},{3,1}... | collective-permute-start | bytes 30728 | tf_op jit(solution)/shard_map/ppermute | solution.py:425
  32.8 4.6 %collective-permute-start.14 = (bf16[288,128]{1,0:T(8,128)(2,1)S(1)}, bf16[288,128]{1,0:T(8,128)(2,1)S(1)}, u32[]{:S(2)}, u32[]{:S(2)}) collective-permute-start(bf16[288,128]{1,0:T(8,128)(2,1)S(1)} %shard_map.96.held_b), channel_id=1, source_target_pairs={{0,2},{2,0},{4,6},{6,4},{8,10},{10,8},{12,14},{14,12},{1,3},{3,1},... | collective-permute-start | bytes 221192 | tf_op jit(solution)/shard_map/ppermute | solution.py:440
  35.1 4.4 %collective-permute-start.13 = (bf16[288,128]{1,0:T(8,128)(2,1)S(1)}, bf16[288,128]{1,0:T(8,128)(2,1)S(1)}, u32[]{:S(2)}, u32[]{:S(2)}) collective-permute-start(bf16[288,128]{1,0:T(8,128)(2,1)S(1)} %get-tuple-element.98.held_a), channel_id=1, source_target_pairs={{0,4},{2,6},{4,0},{6,2},{8,12},{10,14},{12,8},{14,10},{1,5},{3,7},... | collective-permute-start | bytes 221192 | tf_op jit(solution)/shard_map/ppermute | solution.py:440
  35.8 3.8 %collective-permute-start.17 = (bf16[288,128]{1,0:T(8,128)(2,1)S(1)}, bf16[288,128]{1,0:T(8,128)(2,1)S(1)}, u32[]{:S(2)}, u32[]{:S(2)}) collective-permute-start(bf16[288,128]{1,0:T(8,128)(2,1)S(1)} %shard_map.96.held_b), channel_id=1, source_target_pairs={{0,1},{1,0},{2,3},{3,2},{4,5},{5,4},{6,7},{7,6},{8,9},{9,8},{10,11... | collective-permute-start | bytes 221192 | tf_op jit(solution)/shard_map/ppermute | solution.py:425
  35.8 3.8 %collective-permute-start.15 = (bf16[288,128]{1,0:T(8,128)(2,1)S(1)}, bf16[288,128]{1,0:T(8,128)(2,1)S(1)}, u32[]{:S(2)}, u32[]{:S(2)}) collective-permute-start(bf16[288,128]{1,0:T(8,128)(2,1)S(1)} %get-tuple-element.98.held_a), channel_id=1, source_target_pairs={{0,1},{1,0},{2,3},{3,2},{4,5},{5,4},{6,7},{7,6},{8,9},{9,8},{10,11... | collective-permute-start | bytes 221192 | tf_op jit(solution)/shard_map/ppermute | solution.py:425
  37.4 2.1 %collective-permute-start.18 = (bf16[288,128]{1,0:T(8,128)(2,1)S(1)}, bf16[288,128]{1,0:T(8,128)(2,1)S(1)}, u32[]{:S(2)}, u32[]{:S(2)}) collective-permute-start(bf16[288,128]{1,0:T(8,128)(2,1)S(1)} %collective-permute-done.14.got_b), channel_id=1, source_target_pairs={{0,1},{1,0},{2,3},{3,2},{4,5},{5,4},{6,7},{7,6},{8,9},{9,8},{10,11... | collective-permute-start | bytes 221192 | tf_op jit(solution)/shard_map/ppermute | solution.py:425
  39.6 1.3 %collective-permute-start.16 = (bf16[288,128]{1,0:T(8,128)(2,1)S(1)}, bf16[288,128]{1,0:T(8,128)(2,1)S(1)}, u32[]{:S(2)}, u32[]{:S(2)}) collective-permute-start(bf16[288,128]{1,0:T(8,128)(2,1)S(1)} %collective-permute-done.13.got_a), channel_id=1, source_target_pairs={{0,1},{1,0},{2,3},{3,2},{4,5},{5,4},{6,7},{7,6},{8,9},{9,8},{10,11... | collective-permute-start | bytes 221192 | tf_op jit(solution)/shard_map/ppermute | solution.py:425

commit v9 on v8

--- a/solution.py
+++ b/solution.py
@@ -48,35 +48,24 @@
 
 def edge_body(
     feat, cot, down, up, bias, feat_near, cot_near, down_near, up_near, bias_near,
-    rows, cols, corner, strip, wide_strip, sems,
+    rows, cols, wide_strip, sems,
 ):
     tile_rows, tile_cols, _ = feat.shape
-    copies = []
-    for which, ref in enumerate((feat, cot)):
-        copies.append(
-            pltpu.make_async_copy(ref.at[tile_rows - 1], rows.at[which], sems.at[2 * which])
-        )
-        copies.append(
-            pltpu.make_async_copy(
-                ref.at[:, pl.ds(tile_cols - 16, 16), :], strip.at[which], sems.at[2 * which + 1]
-            )
-        )
     bulk = [
-        pltpu.make_async_copy(feat, feat_near, sems.at[4]),
-        pltpu.make_async_copy(cot, cot_near, sems.at[5]),
-        pltpu.make_async_copy(down, down_near, sems.at[6]),
-        pltpu.make_async_copy(up, up_near, sems.at[7]),
-        pltpu.make_async_copy(bias, bias_near, sems.at[8]),
+        pltpu.make_async_copy(feat, feat_near, sems.at[0]),
+        pltpu.make_async_copy(cot, cot_near, sems.at[1]),
+        pltpu.make_async_copy(down, down_near, sems.at[2]),
+        pltpu.make_async_copy(up, up_near, sems.at[3]),
+        pltpu.make_async_copy(bias, bias_near, sems.at[4]),
     ]
-    for copy in copies + bulk:
+    for copy in bulk:
         copy.start()
-    for copy in copies:
-        copy.wait()
-    for which in range(2):
-        wide_strip[...] = strip[which].astype(F32).reshape(wide_strip.shape)
+    for which, near in enumerate((feat_near, cot_near)):
+        bulk[which].wait()
+        rows[which] = near[tile_rows - 1]
+        wide_strip[...] = near[:, tile_cols - 16 :, :].astype(F32).reshape(wide_strip.shape)
         cols[which] = wide_strip[pl.ds(15, tile_rows, stride=16), :].astype(BF16)
-        corner[which] = wide_strip[tile_rows * 16 - 8 :, :].astype(BF16)
-    for copy in bulk:
+    for copy in bulk[2:]:
         copy.wait()
 
 
@@ -166,12 +155,12 @@
         raw_other[...] = taps_of(True, feat_patch[...].reshape(pixels, taps), grads[...])
 
 
-def rim_patches(patch, firsts, top, left, corner, out, line, column):
+def rim_patches(patch, firsts, top, left, out, line, column):
     half_rows, half_cols, taps = patch.shape
     channels = taps // 9
     above = lax.axis_index("wide") > 0
     aside = lax.axis_index("narrow") > 0
-    line[0:8, :] = if_any(above & aside, corner[...].astype(F32))
+    line[0:8, :] = jnp.zeros((8, channels), F32)
     line[8:, :] = if_any(above, top[...].astype(F32))
     column[0, 0:8, :] = line[0:8, :]
     column[0, 8:, :] = if_any(aside, left[...].astype(F32))
@@ -197,7 +186,7 @@
 
 
 def rim_body(
-    feat_patch, cot_patch, feat_firsts, cot_firsts, top, left, corner, raw_other, raw_bias,
+    feat_patch, cot_patch, feat_firsts, cot_firsts, top, left, raw_other, raw_bias,
     up_mat, down_weight, down_bias,
     rim_grads, feat_rim, cot_rim, rim_act, rim_masked, other_a, other_b, bias_part,
     line, column,
@@ -206,9 +195,9 @@
     channels = taps // 9
     half = taps // 2
     rim_patches(
-        feat_patch, feat_firsts, top.at[0], left.at[0], corner.at[0], feat_rim, line, column
-    )
-    rim_patches(cot_patch, cot_firsts, top.at[1], left.at[1], corner.at[1], cot_rim, line, column)
+        feat_patch, feat_firsts, top.at[0], left.at[0], feat_rim, line, column
+    )
+    rim_patches(cot_patch, cot_firsts, top.at[1], left.at[1], cot_rim, line, column)
     pre = jnp.dot(
         feat_rim[...], down_weight[...].reshape(taps, channels), preferred_element_type=F32
     ) + down_bias[...].reshape(1, channels)
@@ -216,9 +205,12 @@
         cot_rim[...], up_mat[...], (((1,), (1,)), ((), ())), preferred_element_type=F32
     )
     value, grad = pointwise(pre, act_grad)
-    once = lax.broadcasted_iota(jnp.int32, value.shape, 0) != half_cols
-    act = if_any(once, value).astype(BF16)
-    masked = if_any(once, grad).astype(BF16)
+    at = lax.broadcasted_iota(jnp.int32, value.shape, 0)
+    once = at != half_cols
+    core = lax.axis_index("narrow")
+    counted = once & ((at > 0) | (core == 0))
+    act = if_any(counted, value).astype(BF16)
+    masked = if_any(counted, grad).astype(BF16)
     rim_act[...] = act
     rim_masked[...] = masked
     full = grad.astype(BF16).astype(F32)
@@ -228,7 +220,7 @@
     fine = (total - coarse.astype(F32)).astype(BF16)
     bias_part[...] = jnp.broadcast_to(coarse.astype(F32) + fine.astype(F32), bias_part.shape)
     put_side(other_a, half, coarse, fine)
-    core = lax.axis_index("narrow")
+    put_pixel(other_a, half + SIDE, top, feat_rim, cot_rim)
 
     def give(more):
         other_a[0:half, :] = (raw_other[0:half, :] + more[0:half]).astype(BF16)
@@ -241,6 +233,70 @@
     @pl.when(core != 0)
     def _():
         give(taps_of(True, feat_rim[...], masked))
+
+
+def put_pixel(out, at, top, feat_rim, cot_rim):
+    _, cols, channels = top.shape
+    core = lax.axis_index("narrow")
+    above = lax.axis_index("wide") > 0
+    row = lax.broadcasted_iota(jnp.int32, (2 * SIDE, channels), 0)
+    block = jnp.zeros((2 * SIDE, channels), F32)
+    for which, rim in enumerate((feat_rim, cot_rim)):
+        corner = top[which, cols - 16 :, :].astype(F32)[15:16]
+        corner = if_any(above & (core == 0), corner)
+        block = jnp.where(row == which * SIDE, corner, block)
+        for tap in range(1, 9):
+            value = rim[0:16, tap * channels : (tap + 1) * channels].astype(F32)[0:1]
+            value = if_any(core > 0, value)
+            block = jnp.where(row == which * SIDE + tap, value, block)
+    out[at : at + 2 * SIDE, :] = block.astype(BF16)
+
+
+def late_body(
+    own, got, mine_a, mine_b, rim_grads, down_weight, down_bias, up_mat,
+    out_a, out_b, grads_out, late, feat_row, cot_row,
+):
+    half, channels = mine_a.shape
+    taps = 2 * half
+    core = lax.axis_index("narrow")
+    span = slice(half + SIDE, half + 3 * SIDE)
+    pixel = own[span, :].astype(F32) + got[span, :].astype(F32)
+    first = lax.broadcasted_iota(jnp.int32, (SIDE, channels), 0) == 0
+    for which, row in enumerate((feat_row, cot_row)):
+        for tap in range(9):
+            at = which * SIDE + tap
+            row[:, tap * channels : (tap + 1) * channels] = if_any(
+                first, jnp.broadcast_to(pixel[at : at + 1], (SIDE, channels))
+            ).astype(BF16)
+    pre = jnp.dot(
+        feat_row[...], down_weight[...].reshape(taps, channels), preferred_element_type=F32
+    ) + down_bias[...].reshape(1, channels)
+    act_grad = lax.dot_general(
+        cot_row[...], up_mat[...], (((1,), (1,)), ((), ())), preferred_element_type=F32
+    )
+    value, grad = pointwise(pre, act_grad)
+    act = if_any(first, value).astype(BF16)
+    grad = if_any(first, grad).astype(BF16)
+    only = grad.astype(F32)[0:1]
+    late[...] = jnp.broadcast_to(only, late.shape)
+    half_cols = rim_grads.shape[0] // 2
+    row = lax.broadcasted_iota(jnp.int32, rim_grads.shape, 0)
+    ours = ((row == 0) | (row == half_cols)) & (core > 0)
+    grads_out[...] = jnp.where(
+        ours, jnp.broadcast_to(only, rim_grads.shape), rim_grads[...].astype(F32)
+    ).astype(BF16)
+
+    def add(more):
+        out_a[...] = mine_a[...] + more[0:half]
+        out_b[...] = mine_b[...] + more[half:]
+
+    @pl.when(core == 0)
+    def _():
+        add(taps_of(True, feat_row[...], grad))
+
+    @pl.when(core != 0)
+    def _():
+        add(taps_of(False, cot_row[...], act))
 
 
 def mine_body(
@@ -282,8 +338,10 @@
     return lax.rem(lax.shift_right_logical(lax.axis_index("wide"), jnp.int32(position)), 2)
 
 
-def joined_bias(bias_in, got, size, out, sent, at):
+def joined_bias(bias_in, got, size, out, sent, at, late=None):
     total = bias_in[0:1, :] + take_side(got, size)
+    if late is not None:
+        total = total + late[0:1, :]
     coarse = total.astype(BF16)
     fine = (total - coarse.astype(F32)).astype(BF16)
     out[...] = jnp.broadcast_to(coarse.astype(F32) + fine.astype(F32), out.shape)
@@ -302,9 +360,9 @@
 
 def halve_body(position, held, got, *rest):
     size = held.shape[0]
-    if len(rest) == 4:
-        bias_in, keep, send, bias_out = rest
-        joined_bias(bias_in, got, size, bias_out, send, size // 2)
+    if len(rest) > 3:
+        bias_in, *late, keep, send, bias_out = rest
+        joined_bias(bias_in, got, size, bias_out, send, size // 2, *late)
     else:
         keep, send = rest
     split(position, held, got, 0, size, keep, send)
@@ -425,16 +483,6 @@
     return lax.ppermute(value, axis, [(at, (at + steps) % count) for at in range(count)])
 
 
-def turned_both(value):
-    count, cores = lax.axis_size("wide"), lax.axis_size("narrow")
-    pairs = [
-        (at * cores + core, (at + 1) % count * cores + (core + 1) % cores)
-        for at in range(count)
-        for core in range(cores)
-    ]
-    return lax.ppermute(value, ("wide", "narrow"), pairs)
-
-
 def traded(value, position):
     count = lax.axis_size("wide")
     return lax.ppermute(value, "wide", [(at, at ^ (1 << position)) for at in range(count)])
@@ -445,7 +493,7 @@
     half_rows, half_cols = tile_rows // 2, tile_cols // 2
     pixels = half_rows * half_cols
     taps = 9 * channels
-    feat_near, cot_near, down_near, up_near, bias_near, rows, cols, corner = call(
+    feat_near, cot_near, down_near, up_near, bias_near, rows, cols = call(
         edge_body,
         (
             vm(features.shape, BF16),
@@ -455,12 +503,10 @@
             vm((1, channels), F32),
             vm((2, tile_cols, channels), BF16),
             vm((2, tile_rows, channels), BF16),
-            vm((2, 8, channels), BF16),
         ),
         scratch=[
-            pltpu.VMEM((2, tile_rows, 16, channels), BF16),
             pltpu.VMEM((tile_rows * 16, channels), F32),
-            pltpu.SemaphoreType.DMA((9,)),
+            pltpu.SemaphoreType.DMA((5,)),
         ],
         in_specs=[ANY] * 5,
         nbytes=1 << 19,
@@ -468,7 +514,6 @@
         room=8,
     )(features, cotangent, down_weight, up_weight, down_bias.reshape(1, channels))
     from_above = turned(rows, "wide", 1)
-    from_corner = turned_both(corner)
     from_left = turned(cols, "narrow", 1)
     patches = vm((half_rows, half_cols, taps), BF16)
     firsts = vm((2, tile_rows, channels), BF16)
@@ -497,8 +542,8 @@
         near=(0, 1, 2, 3, 4),
         room=12,
     )(feat_near, cot_near, down_near, bias_near, up_near)
-    from_above, from_corner, from_left, raw_other = lax.optimization_barrier(
-        (from_above, from_corner, from_left, raw_other)
+    from_above, from_left, raw_other = lax.optimization_barrier(
+        (from_above, from_left, raw_other)
     )
     pieces = half_cols + half_rows
     rim_grads, feat_rim, cot_rim, rim_act, rim_masked, other_a, other_b, bias_sum = call(
@@ -509,7 +554,7 @@
             vm((pieces, taps), BF16),
             vm((pieces, channels), BF16),
             vm((pieces, channels), BF16),
-            vm((taps // 2 + SIDE, channels), BF16),
+            vm((taps // 2 + 3 * SIDE, channels), BF16),
             vm((taps // 2, channels), BF16),
             vm((8, channels), F32),
         ),
@@ -517,13 +562,13 @@
             pltpu.VMEM((tile_cols + 8, channels), F32),
             pltpu.VMEM((3, tile_rows + 8, channels), F32),
         ],
-        n_in=12,
+        n_in=11,
         flops=1 << 26,
         nbytes=3 << 20,
-        near=tuple(range(12)),
+        near=tuple(range(11)),
         room=8,
     )(
-        feat_patch, cot_patch, feat_firsts, cot_firsts, from_above, from_left, from_corner,
+        feat_patch, cot_patch, feat_firsts, cot_firsts, from_above, from_left,
         raw_other, raw_bias, up_mat, down_near, bias_near,
     )
     got_a = turned(other_a, "narrow", 1)
@@ -537,8 +582,23 @@
         near=tuple(range(8)),
         room=12,
     )(feat_patch, cot_patch, act, grads, feat_rim, cot_rim, rim_act, rim_masked)
+    got_a, mine_a, mine_b = lax.optimization_barrier((got_a, mine_a, mine_b))
+    mine_a, mine_b, rim_grads, late = call(
+        late_body,
+        (
+            vm((taps // 2, channels), F32),
+            vm((taps // 2, channels), F32),
+            vm((pieces, channels), BF16),
+            vm((8, channels), F32),
+        ),
+        scratch=[pltpu.VMEM((SIDE, taps), BF16), pltpu.VMEM((SIDE, taps), BF16)],
+        n_in=8,
+        flops=1 << 24,
+        nbytes=1 << 20,
+        near=tuple(range(8)),
+        room=8,
+    )(other_a, got_a, mine_a, mine_b, rim_grads, down_near, bias_near, up_mat)
     from_right = turned(rim_grads[half_cols:], "narrow", -1)
-    got_a, mine_a, mine_b = lax.optimization_barrier((got_a, mine_a, mine_b))
     low = jnp.concatenate([rim_grads[:half_cols], from_right[:8]], axis=0)
     from_below = turned(low, "wide", -1)
 
@@ -553,10 +613,10 @@
         held_a, send_a, bias_sum = call(
             functools.partial(halve_body, order_a[step]),
             (vm((half, channels), F32), vm((half + SIDE, channels), BF16), vm((8, channels), F32)),
-            n_in=3,
+            n_in=3 if step else 4,
             nbytes=half * channels * 12,
-            near=(0, 1, 2),
-        )(held_a, got_a, bias_sum)
+            near=(0, 1, 2) if step else (0, 1, 2, 3),
+        )(held_a, got_a, bias_sum, *(() if step else (late,)))
         held_b, send_b = call(
             functools.partial(halve_body, order_b[step]),
             (vm((half, channels), F32), vm((half, channels), BF16)),

time: 42.5 us -> 41.9 us (0.986)
  waiting for transfers between devices: 14.2 us -> 13.5 us
    ppermute x1 -> x0, starting transfers between devices: 2.46 us -> none  [turned_both(): return lax.ppermute(value, ('wide', 'narrow'), pairs)]
    ppermute x8, starting transfers between devices: 9.31 us -> 10.6 us  [traded(): lax.ppermute(value, 'wide', [(at, at ^ 1 << position) for at in range(cou...]
    ppermute x10, starting transfers between devices: 5.99 us -> 7.08 us  [turned(): lax.ppermute(value, axis, [(at, (at + steps) % count) for at in range(cou...]
    ppermute x8, waiting for transfers between devices: 8.34 us -> 7.46 us  [traded(): lax.ppermute(value, 'wide', [(at, at ^ 1 << position) for at in range(cou...]
    pallas_call x14 -> x15, Pallas kernels: 9.52 us -> 9.75 us  [run(): return kernel(*placed)]
  transfers between devices with their start and end apart: 19 -> 18, of which waited for: 8 -> 8; matrix products, arithmetic and copies ran while one was open for 0% -> 0% of each run, Pallas kernels for 13% -> 15%
where the time goes in v9:
time: 41.9 us; the launch traced here: 41.7 us
  starting transfers between devices  17.7 us (42%)
  waiting for transfers between devices  13.5 us (32%)
  Pallas kernels  9.75 us (23%)
  between operations  0.75 us (2%)
    ppermute x8, starting transfers between devices, traded(): lax.ppermute(value, 'wide', [(at, at ^ 1 << position) for at in range(cou...  10.6 us
    pallas_call x15, Pallas kernels, run(): return kernel(*placed)  9.75 us
    ppermute x8, waiting for transfers between devices, traded(): lax.ppermute(value, 'wide', [(at, at ^ 1 << position) for at in range(cou...  7.46 us
    ppermute x10, starting transfers between devices, turned(): lax.ppermute(value, axis, [(at, (at + steps) % count) for at in range(cou...  7.08 us
    ppermute x10, waiting for transfers between devices, turned(): lax.ppermute(value, axis, [(at, (at + steps) % count) for at in range(cou...  6.05 us
  transfers between devices with their start and end apart: 18, of which 8 were waited for; matrix products, arithmetic and copies ran while one was open for 0% of the time, Pallas kernels for 15%

profile of v9, /device:TPU:0, one launch (start us, length us, event | category | flops | bytes accessed | tf_op | source)
XLA Modules:
  0.0 41.7 jit_solution(13384721066542746211)
XLA Ops:
  0.6 1.7 %shard_map.84 = (bf16[64,64,128]{2,1,0:T(8,128)(2,1)S(1)}, bf16[64,64,128]{2,1,0:T(8,128)(2,1)S(1)}, bf16[3,3,128,128]{3,2,1,0:T(8,128)(2,1)S(1)}, bf16[3,3,128,...) custom-call(bf16[64,64,128]{2,1,0:T(8,128)(2,1)} %feat.1, ...), custom_call_target="tpu_custom_call" | custom-call | bytes 524288 | tf_op jit(solution)/shard_map/pallas_call | solution.py:36
  2.4 3.0 %collective-permute-start = (bf16[2,64,128]{2,1,0:T(8,128)(2,1)S(1)}, bf16[2,64,128]{2,1,0:T(8,128)(2,1)S(1)}, u32[]{:S(2)}, u32[]{:S(2)}) collective-permute-start(bf16[2,64,128]{2,1,0:T(8,128)(2,1)S(1)} %get-tuple-element.65), channel_id=1, source_target_pairs={{0,2},{2,4},{4,6},{6,8},{8,10},{10,12},{12,14},{14,0},{1,3},{3,5},... | collective-permute-start | bytes 98312 | tf_op jit(solution)/shard_map/ppermute | solution.py:483
  5.4 2.7 %shard_map.85 = (bf16[32,32,1152]{2,1,0:T(8,128)(2,1)S(1)}, bf16[32,32,1152]{2,1,0:T(8,128)(2,1)S(1)}, bf16[1024,128]{1,0:T(8,128)(2,1)S(1)}, bf16[1024,128]{1,0...) custom-call(bf16[64,64,128]{2,1,0:T(8,128)(2,1)S(1)} %get-tuple-elem, ...), custom_call_target="tpu_custom_call" | custom-call | flops 905969664 | bytes 6291456 | tf_op jit(solution)/shard_map/pallas_call | solution.py:36
  8.1 2.2 %collective-permute-done.top = bf16[2,64,128]{2,1,0:T(8,128)(2,1)S(1)} collective-permute-done((bf16[2,64,128]{2,1,0:T(8,128)(2,1)S(1)}, bf16[2,64,128]{2,1,0:T(8,128)(2,1)S(1)}, u32[]{:S(2)}, u32[]{:S(2)}) %collective-permute-start) | collective-permute-done | bytes 32800 | tf_op jit(solution)/shard_map/ppermute | solution.py:483
  10.3 0.5 %shard_map.86 = (bf16[64,128]{1,0:T(8,128)(2,1)S(1)}, bf16[64,1152]{1,0:T(8,128)(2,1)S(1)}, bf16[64,1152]{1,0:T(8,128)(2,1)S(1)}, bf16[64,128]{1,0:T(8,128)(2,1)...) custom-call(bf16[32,32,1152]{2,1,0:T(8,128)(2,1)S(1)} %get-tuple-ele, ...), custom_call_target="tpu_custom_call" | custom-call | flops 67108864 | bytes 3145728 | tf_op jit(solution)/shard_map/pallas_call | solution.py:36
  11.0 0.5 %collective-permute-start.3 = (bf16[576,128]{1,0:T(8,128)(2,1)S(1)}, bf16[576,128]{1,0:T(8,128)(2,1)S(1)}, u32[]{:S(2)}, u32[]{:S(2)}) collective-permute-start(bf16[576,128]{1,0:T(8,128)(2,1)S(1)} %get-tuple-element.87), channel_id=1, source_target_pairs={{0,1},{1,0},{2,3},{3,2},{4,5},{5,4},{6,7},{7,6},{8,9},{9,8},{10,11... | collective-permute-start | bytes 442376 | tf_op jit(solution)/shard_map/ppermute | solution.py:483
  11.4 0.9 %shard_map.87 = (f32[576,128]{1,0:T(8,128)S(1)}, f32[576,128]{1,0:T(8,128)S(1)}) custom-call(bf16[32,32,1152]{2,1,0:T(8,128)(2,1)S(1)} %get-tuple-element.61.feat_patch, bf16[32,32,1152]{2,1,0:T(8,128)(2,1)S(1)} %get-tuple-element.62.cot_patch, bf16[1024,128]{1,0:T(8,128)(2,1)S(1)} %get-tuple-element.74.act, bf16[1024,128]{1,0:T(8,128)(2,1)S(1)} %get-tuple-element.75.grads, ...), custom_call_target="tpu_custom_call" | custom-call | flops 301989888 | bytes 3145728 | tf_op jit(solution)/shard_map/pallas_call | solution.py:36
  13.1 1.4 %collective-permute-start.4 = (bf16[288,128]{1,0:T(8,128)(2,1)S(1)}, bf16[288,128]{1,0:T(8,128)(2,1)S(1)}, u32[]{:S(2)}, u32[]{:S(2)}) collective-permute-start(bf16[288,128]{1,0:T(8,128)(2,1)S(1)} %get-tuple-element.89), channel_id=1, source_target_pairs={{0,2},{2,0},{4,6},{6,4},{8,10},{10,8},{12,14},{14,12},{1,3},{3,1},... | collective-permute-start | bytes 221192 | tf_op jit(solution)/shard_map/ppermute | solution.py:488
  14.4 3.0 %collective-permute-done.4.got = bf16[288,128]{1,0:T(8,128)(2,1)S(1)} collective-permute-done((bf16[288,128]{1,0:T(8,128)(2,1)S(1)}, bf16[288,128]{1,0:T(8,128)(2,1)S(1)}, u32[]{:S(2)}, u32[]{:S(2)}) %collective-permute-start.4) | collective-permute-done | bytes 73760 | tf_op jit(solution)/shard_map/ppermute | solution.py:488
  17.5 2.6 %collective-permute-start.5 = (bf16[288,128]{1,0:T(8,128)(2,1)S(1)}, bf16[288,128]{1,0:T(8,128)(2,1)S(1)}, u32[]{:S(2)}, u32[]{:S(2)}) collective-permute-start(bf16[288,128]{1,0:T(8,128)(2,1)S(1)} %shard_map.90.held), channel_id=1, source_target_pairs={{0,8},{2,10},{4,12},{6,14},{8,0},{10,2},{12,4},{14,6},{1,9},{3,11}... | collective-permute-start | bytes 221192 | tf_op jit(solution)/shard_map/ppermute | solution.py:488
  20.1 0.7 %collective-permute-start.10 = (bf16[304,128]{1,0:T(8,128)(2,1)S(1)}, bf16[304,128]{1,0:T(8,128)(2,1)S(1)}, u32[]{:S(2)}, u32[]{:S(2)}) collective-permute-start(bf16[304,128]{1,0:T(8,128)(2,1)S(1)} %get-tuple-element.98.held), channel_id=1, source_target_pairs={{0,2},{2,0},{4,6},{6,4},{8,10},{10,8},{12,14},{14,12},{1,3},{3,1},... | collective-permute-start | bytes 233480 | tf_op jit(solution)/shard_map/ppermute | solution.py:488
  20.8 1.2 %collective-permute-done.7.right = bf16[32,128]{1,0:T(8,128)(2,1)S(1)} collective-permute-done((bf16[32,128]{1,0:T(8,128)(2,1)S(1)}, bf16[32,128]{1,0:T(8,128)(2,1)S(1)}, u32[]{:S(2)}, u32[]{:S(2)}) %collective-permute-start.7) | collective-permute-done | bytes 8224 | tf_op jit(solution)/shard_map/ppermute | solution.py:483
  21.9 0.9 %collective-permute-done.5.got = bf16[288,128]{1,0:T(8,128)(2,1)S(1)} collective-permute-done((bf16[288,128]{1,0:T(8,128)(2,1)S(1)}, bf16[288,128]{1,0:T(8,128)(2,1)S(1)}, u32[]{:S(2)}, u32[]{:S(2)}) %collective-permute-start.5) | collective-permute-done | bytes 73760 | tf_op jit(solution)/shard_map/ppermute | solution.py:488
  22.8 2.1 %collective-permute-start.6 = (bf16[288,128]{1,0:T(8,128)(2,1)S(1)}, bf16[288,128]{1,0:T(8,128)(2,1)S(1)}, u32[]{:S(2)}, u32[]{:S(2)}) collective-permute-start(bf16[288,128]{1,0:T(8,128)(2,1)S(1)} %shard_map.91.held), channel_id=1, source_target_pairs={{0,4},{2,6},{4,0},{6,2},{8,12},{10,14},{12,8},{14,10},{1,5},{3,7},... | collective-permute-start | bytes 221192 | tf_op jit(solution)/shard_map/ppermute | solution.py:488
  24.9 1.0 %collective-permute-start.11 = (bf16[304,128]{1,0:T(8,128)(2,1)S(1)}, bf16[304,128]{1,0:T(8,128)(2,1)S(1)}, u32[]{:S(2)}, u32[]{:S(2)}) collective-permute-start(bf16[304,128]{1,0:T(8,128)(2,1)S(1)} %get-tuple-element.100.held), channel_id=1, source_target_pairs={{0,8},{2,10},{4,12},{6,14},{8,0},{10,2},{12,4},{14,6},{1,9},{3,11}... | collective-permute-start | bytes 233480 | tf_op jit(solution)/shard_map/ppermute | solution.py:488
  26.0 3.0 %collective-permute-start.8 = (bf16[40,128]{1,0:T(8,128)(2,1)S(1)}, bf16[40,128]{1,0:T(8,128)(2,1)S(1)}, u32[]{:S(2)}, u32[]{:S(2)}) collective-permute-start(bf16[40,128]{1,0:T(8,128)(2,1)S(1)} %pad_maximum_fusion), channel_id=1, source_target_pairs={{0,14},{2,0},{4,2},{6,4},{8,6},{10,8},{12,10},{14,12},{1,15},{3,1}... | collective-permute-start | bytes 30728 | tf_op jit(solution)/shard_map/ppermute | solution.py:483
  28.9 1.4 %collective-permute-done.8.below = bf16[40,128]{1,0:T(8,128)(2,1)S(1)} collective-permute-done((bf16[40,128]{1,0:T(8,128)(2,1)S(1)}, bf16[40,128]{1,0:T(8,128)(2,1)S(1)}, u32[]{:S(2)}, u32[]{:S(2)}) %collective-permute-start.8) | collective-permute-done | bytes 10272 | tf_op jit(solution)/shard_map/ppermute | solution.py:483
  30.3 1.8 %shard_map.92 = bf16[64,64,128]{2,1,0:T(8,128)(2,1)} custom-call(bf16[1024,128]{1,0:T(8,128)(2,1)S(1)} %get-tuple-element.75.grads, bf16[64,128]{1,0:T(8,128)(2,1)S(1)} %get-tuple-element.90.rim_grads, bf16[32,128]{1,0:T(8,128)(2,1)S(1)} %collective-permute-done.7.right, bf16[40,128]{1,0:T(8,128)(2,1)S(1)} %collective-permute-done.8.below, ...), custom_call_target="tpu_custom_call" | custom-call | flops 402653184 | bytes 3145728 | tf_op jit(solution)/shard_map/pallas_call | solution.py:36
  32.1 2.5 %collective-permute-start.13 = (bf16[288,128]{1,0:T(8,128)(2,1)S(1)}, bf16[288,128]{1,0:T(8,128)(2,1)S(1)}, u32[]{:S(2)}, u32[]{:S(2)}) collective-permute-start(bf16[288,128]{1,0:T(8,128)(2,1)S(1)} %shard_map.97.held_b), channel_id=1, source_target_pairs={{0,2},{2,0},{4,6},{6,4},{8,10},{10,8},{12,14},{14,12},{1,3},{3,1},... | collective-permute-start | bytes 221192 | tf_op jit(solution)/shard_map/ppermute | solution.py:488
  35.0 0.5 %collective-permute-start.14 = (bf16[288,128]{1,0:T(8,128)(2,1)S(1)}, bf16[288,128]{1,0:T(8,128)(2,1)S(1)}, u32[]{:S(2)}, u32[]{:S(2)}) collective-permute-start(bf16[288,128]{1,0:T(8,128)(2,1)S(1)} %get-tuple-element.102.held_a), channel_id=1, source_target_pairs={{0,1},{1,0},{2,3},{3,2},{4,5},{5,4},{6,7},{7,6},{8,9},{9,8},{10,11... | collective-permute-start | bytes 221192 | tf_op jit(solution)/shard_map/ppermute | solution.py:483
  35.5 1.4 %collective-permute-done.13.got_b = bf16[288,128]{1,0:T(8,128)(2,1)S(1)} collective-permute-done((bf16[288,128]{1,0:T(8,128)(2,1)S(1)}, bf16[288,128]{1,0:T(8,128)(2,1)S(1)}, u32[]{:S(2)}, u32[]{:S(2)}) %collective-permute-start.13) | collective-permute-done | bytes 73760 | tf_op jit(solution)/shard_map/ppermute | solution.py:488
  36.9 2.1 %collective-permute-done.12.got_a = bf16[288,128]{1,0:T(8,128)(2,1)S(1)} collective-permute-done((bf16[288,128]{1,0:T(8,128)(2,1)S(1)}, bf16[288,128]{1,0:T(8,128)(2,1)S(1)}, u32[]{:S(2)}, u32[]{:S(2)}) %collective-permute-start.12) | collective-permute-done | bytes 73760 | tf_op jit(solution)/shard_map/ppermute | solution.py:488
  39.1 1.2 %collective-permute-done.15.far_got_a = bf16[288,128]{1,0:T(8,128)(2,1)S(1)} collective-permute-done((bf16[288,128]{1,0:T(8,128)(2,1)S(1)}, bf16[288,128]{1,0:T(8,128)(2,1)S(1)}, u32[]{:S(2)}, u32[]{:S(2)}) %collective-permute-start.15) | collective-permute-done | bytes 73760 | tf_op jit(solution)/shard_map/ppermute | solution.py:483
  40.3 1.4 %shard_map.98 = (f32[4,288,128]{2,1,0:T(8,128)}, f32[4,288,128]{2,1,0:T(8,128)}, f32[1,128]{1,0:T(1,128)}) custom-call(bf16[288,128]{1,0:T(8,128)(2,1)S(1)} %get-tuple-element.102.held_a, bf16[288,128]{1,0:T(8,128)(2,1)S(1)} %collective-permute-done.12.got_a, bf16[288,128]{1,0:T(8,128)(2,1)S(1)} %shard_map.97.held_b, ...), custom_call_target="tpu_custom_call" | custom-call | bytes 1769472 | tf_op jit(solution)/shard_map/pallas_call | solution.py:36
  (30 shorter events, 1.2 us)
Async XLA Ops:
  2.4 8.0 %collective-permute-start = (bf16[2,64,128]{2,1,0:T(8,128)(2,1)S(1)}, bf16[2,64,128]{2,1,0:T(8,128)(2,1)S(1)}, u32[]{:S(2)}, u32[]{:S(2)}) collective-permute-start(bf16[2,64,128]{2,1,0:T(8,128)(2,1)S(1)} %get-tuple-element.65), channel_id=1, source_target_pairs={{0,2},{2,4},{4,6},{6,8},{8,10},{10,12},{12,14},{14,0},{1,3},{3,5},... | collective-permute-start | bytes 98312 | tf_op jit(solution)/shard_map/ppermute | solution.py:483
  5.4 4.9 %collective-permute-start.1 = (bf16[2,64,128]{2,1,0:T(8,128)(2,1)S(1)}, bf16[2,64,128]{2,1,0:T(8,128)(2,1)S(1)}, u32[]{:S(2)}, u32[]{:S(2)}) collective-permute-start(bf16[2,64,128]{2,1,0:T(8,128)(2,1)S(1)} %get-tuple-element.66), channel_id=1, source_target_pairs={{0,1},{1,0},{2,3},{3,2},{4,5},{5,4},{6,7},{7,6},{8,9},{9,8},{10,11... | collective-permute-start | bytes 98312 | tf_op jit(solution)/shard_map/ppermute | solution.py:483
  10.9 1.5 %collective-permute-start.2 = (bf16[624,128]{1,0:T(8,128)(2,1)S(1)}, bf16[624,128]{1,0:T(8,128)(2,1)S(1)}, u32[]{:S(2)}, u32[]{:S(2)}) collective-permute-start(bf16[624,128]{1,0:T(8,128)(2,1)S(1)} %get-tuple-element.73.own), channel_id=1, source_target_pairs={{0,1},{1,0},{2,3},{3,2},{4,5},{5,4},{6,7},{7,6},{8,9},{9,8},{10,11... | collective-permute-start | bytes 479240 | tf_op jit(solution)/shard_map/ppermute | solution.py:483
  11.0 2.0 %collective-permute-start.3 = (bf16[576,128]{1,0:T(8,128)(2,1)S(1)}, bf16[576,128]{1,0:T(8,128)(2,1)S(1)}, u32[]{:S(2)}, u32[]{:S(2)}) collective-permute-start(bf16[576,128]{1,0:T(8,128)(2,1)S(1)} %get-tuple-element.87), channel_id=1, source_target_pairs={{0,1},{1,0},{2,3},{3,2},{4,5},{5,4},{6,7},{7,6},{8,9},{9,8},{10,11... | collective-permute-start | bytes 442376 | tf_op jit(solution)/shard_map/ppermute | solution.py:483
  12.9 7.2 %collective-permute-start.9 = (bf16[304,128]{1,0:T(8,128)(2,1)S(1)}, bf16[304,128]{1,0:T(8,128)(2,1)S(1)}, u32[]{:S(2)}, u32[]{:S(2)}) collective-permute-start(bf16[304,128]{1,0:T(8,128)(2,1)S(1)} %get-tuple-element.96), channel_id=1, source_target_pairs={{0,4},{2,6},{4,0},{6,2},{8,12},{10,14},{12,8},{14,10},{1,5},{3,7},... | collective-permute-start | bytes 233480 | tf_op jit(solution)/shard_map/ppermute | solution.py:488
  13.1 4.4 %collective-permute-start.4 = (bf16[288,128]{1,0:T(8,128)(2,1)S(1)}, bf16[288,128]{1,0:T(8,128)(2,1)S(1)}, u32[]{:S(2)}, u32[]{:S(2)}) collective-permute-start(bf16[288,128]{1,0:T(8,128)(2,1)S(1)} %get-tuple-element.89), channel_id=1, source_target_pairs={{0,2},{2,0},{4,6},{6,4},{8,10},{10,8},{12,14},{14,12},{1,3},{3,1},... | collective-permute-start | bytes 221192 | tf_op jit(solution)/shard_map/ppermute | solution.py:488
  17.5 5.3 %collective-permute-start.5 = (bf16[288,128]{1,0:T(8,128)(2,1)S(1)}, bf16[288,128]{1,0:T(8,128)(2,1)S(1)}, u32[]{:S(2)}, u32[]{:S(2)}) collective-permute-start(bf16[288,128]{1,0:T(8,128)(2,1)S(1)} %shard_map.90.held), channel_id=1, source_target_pairs={{0,8},{2,10},{4,12},{6,14},{8,0},{10,2},{12,4},{14,6},{1,9},{3,11}... | collective-permute-start | bytes 221192 | tf_op jit(solution)/shard_map/ppermute | solution.py:488
  20.1 4.8 %collective-permute-start.10 = (bf16[304,128]{1,0:T(8,128)(2,1)S(1)}, bf16[304,128]{1,0:T(8,128)(2,1)S(1)}, u32[]{:S(2)}, u32[]{:S(2)}) collective-permute-start(bf16[304,128]{1,0:T(8,128)(2,1)S(1)} %get-tuple-element.98.held), channel_id=1, source_target_pairs={{0,2},{2,0},{4,6},{6,4},{8,10},{10,8},{12,14},{14,12},{1,3},{3,1},... | collective-permute-start | bytes 233480 | tf_op jit(solution)/shard_map/ppermute | solution.py:488
  20.8 1.2 %collective-permute-start.7 = (bf16[32,128]{1,0:T(8,128)(2,1)S(1)}, bf16[32,128]{1,0:T(8,128)(2,1)S(1)}, u32[]{:S(2)}, u32[]{:S(2)}) collective-permute-start(bf16[32,128]{1,0:T(8,128)(2,1)S(1)} %get-tuple-element.109), channel_id=1, source_target_pairs={{0,1},{1,0},{2,3},{3,2},{4,5},{5,4},{6,7},{7,6},{8,9},{9,8},{10,11... | collective-permute-start | bytes 24584 | tf_op jit(solution)/shard_map/ppermute | solution.py:483
  22.8 9.3 %collective-permute-start.6 = (bf16[288,128]{1,0:T(8,128)(2,1)S(1)}, bf16[288,128]{1,0:T(8,128)(2,1)S(1)}, u32[]{:S(2)}, u32[]{:S(2)}) collective-permute-start(bf16[288,128]{1,0:T(8,128)(2,1)S(1)} %shard_map.91.held), channel_id=1, source_target_pairs={{0,4},{2,6},{4,0},{6,2},{8,12},{10,14},{12,8},{14,10},{1,5},{3,7},... | collective-permute-start | bytes 221192 | tf_op jit(solution)/shard_map/ppermute | solution.py:488
  24.9 9.7 %collective-permute-start.11 = (bf16[304,128]{1,0:T(8,128)(2,1)S(1)}, bf16[304,128]{1,0:T(8,128)(2,1)S(1)}, u32[]{:S(2)}, u32[]{:S(2)}) collective-permute-start(bf16[304,128]{1,0:T(8,128)(2,1)S(1)} %get-tuple-element.100.held), channel_id=1, source_target_pairs={{0,8},{2,10},{4,12},{6,14},{8,0},{10,2},{12,4},{14,6},{1,9},{3,11}... | collective-permute-start | bytes 233480 | tf_op jit(solution)/shard_map/ppermute | solution.py:488
  26.0 4.4 %collective-permute-start.8 = (bf16[40,128]{1,0:T(8,128)(2,1)S(1)}, bf16[40,128]{1,0:T(8,128)(2,1)S(1)}, u32[]{:S(2)}, u32[]{:S(2)}) collective-permute-start(bf16[40,128]{1,0:T(8,128)(2,1)S(1)} %pad_maximum_fusion), channel_id=1, source_target_pairs={{0,14},{2,0},{4,2},{6,4},{8,6},{10,8},{12,10},{14,12},{1,15},{3,1}... | collective-permute-start | bytes 30728 | tf_op jit(solution)/shard_map/ppermute | solution.py:483
  32.1 4.8 %collective-permute-start.13 = (bf16[288,128]{1,0:T(8,128)(2,1)S(1)}, bf16[288,128]{1,0:T(8,128)(2,1)S(1)}, u32[]{:S(2)}, u32[]{:S(2)}) collective-permute-start(bf16[288,128]{1,0:T(8,128)(2,1)S(1)} %shard_map.97.held_b), channel_id=1, source_target_pairs={{0,2},{2,0},{4,6},{6,4},{8,10},{10,8},{12,14},{14,12},{1,3},{3,1},... | collective-permute-start | bytes 221192 | tf_op jit(solution)/shard_map/ppermute | solution.py:488
  34.6 4.4 %collective-permute-start.12 = (bf16[288,128]{1,0:T(8,128)(2,1)S(1)}, bf16[288,128]{1,0:T(8,128)(2,1)S(1)}, u32[]{:S(2)}, u32[]{:S(2)}) collective-permute-start(bf16[288,128]{1,0:T(8,128)(2,1)S(1)} %get-tuple-element.102.held_a), channel_id=1, source_target_pairs={{0,4},{2,6},{4,0},{6,2},{8,12},{10,14},{12,8},{14,10},{1,5},{3,7},... | collective-permute-start | bytes 221192 | tf_op jit(solution)/shard_map/ppermute | solution.py:488
  35.0 4.1 %collective-permute-start.16 = (bf16[288,128]{1,0:T(8,128)(2,1)S(1)}, bf16[288,128]{1,0:T(8,128)(2,1)S(1)}, u32[]{:S(2)}, u32[]{:S(2)}) collective-permute-start(bf16[288,128]{1,0:T(8,128)(2,1)S(1)} %shard_map.97.held_b), channel_id=1, source_target_pairs={{0,1},{1,0},{2,3},{3,2},{4,5},{5,4},{6,7},{7,6},{8,9},{9,8},{10,11... | collective-permute-start | bytes 221192 | tf_op jit(solution)/shard_map/ppermute | solution.py:483
  35.0 4.1 %collective-permute-start.14 = (bf16[288,128]{1,0:T(8,128)(2,1)S(1)}, bf16[288,128]{1,0:T(8,128)(2,1)S(1)}, u32[]{:S(2)}, u32[]{:S(2)}) collective-permute-start(bf16[288,128]{1,0:T(8,128)(2,1)S(1)} %get-tuple-element.102.held_a), channel_id=1, source_target_pairs={{0,1},{1,0},{2,3},{3,2},{4,5},{5,4},{6,7},{7,6},{8,9},{9,8},{10,11... | collective-permute-start | bytes 221192 | tf_op jit(solution)/shard_map/ppermute | solution.py:483
  36.9 2.1 %collective-permute-start.17 = (bf16[288,128]{1,0:T(8,128)(2,1)S(1)}, bf16[288,128]{1,0:T(8,128)(2,1)S(1)}, u32[]{:S(2)}, u32[]{:S(2)}) collective-permute-start(bf16[288,128]{1,0:T(8,128)(2,1)S(1)} %collective-permute-done.13.got_b), channel_id=1, source_target_pairs={{0,1},{1,0},{2,3},{3,2},{4,5},{5,4},{6,7},{7,6},{8,9},{9,8},{10,11... | collective-permute-start | bytes 221192 | tf_op jit(solution)/shard_map/ppermute | solution.py:483
  39.1 1.3 %collective-permute-start.15 = (bf16[288,128]{1,0:T(8,128)(2,1)S(1)}, bf16[288,128]{1,0:T(8,128)(2,1)S(1)}, u32[]{:S(2)}, u32[]{:S(2)}) collective-permute-start(bf16[288,128]{1,0:T(8,128)(2,1)S(1)} %collective-permute-done.12.got_a), channel_id=1, source_target_pairs={{0,1},{1,0},{2,3},{3,2},{4,5},{5,4},{6,7},{7,6},{8,9},{9,8},{10,11... | collective-permute-start | bytes 221192 | tf_op jit(solution)/shard_map/ppermute | solution.py:483

commit v10 on v9

--- a/solution.py
+++ b/solution.py
@@ -396,8 +396,11 @@
     bit_a, bit_b = bit_of(positions[0]), bit_of(positions[1])
 
     def square(ref):
-        block = ref[...].astype(F32).reshape(-1, 8, channels)
-        return jnp.sum(block * block, axis=0)
+        total = jnp.zeros((32, channels), F32)
+        for at in range(0, ref.shape[0], 32):
+            block = ref[at : at + 32, :].astype(F32)
+            total = total + block * block
+        return total
 
     def pair(one, two, three, four):
         return (square(one) + square(two)) + (square(three) + square(four))
@@ -412,21 +415,22 @@
     factor = jnp.broadcast_to(factor, (1, channels))
     bias_out[...] = bias * factor
     spots = (bit_a, 1 - bit_a, 2 + bit_b, 3 - bit_b)
-    for at, (near_ref, far_ref) in enumerate(
-        ((held_a, far_held_a), (got_a, far_got_a), (held_b, far_held_b), (got_b, far_got_b))
-    ):
-        near_block = near_ref[...].astype(F32) * factor
-        far_block = far_ref[...].astype(F32) * factor
-
-        @pl.when(core == 0)
-        def _():
-            down[spots[at]] = near_block
-            up[spots[at]] = far_block
-
-        @pl.when(core != 0)
-        def _():
-            up[spots[at]] = near_block
-            down[spots[at]] = far_block
+
+    def write(near_out, far_out):
+        near = (held_a, got_a, held_b, got_b)
+        far = (far_held_a, far_got_a, far_held_b, far_got_b)
+        for out, refs in ((near_out, near), (far_out, far)):
+            for spot, ref in zip(spots, refs):
+                for at in range(0, ref.shape[0], 32):
+                    out[spot, at : at + 32, :] = ref[at : at + 32, :].astype(F32) * factor
+
+    @pl.when(core == 0)
+    def _():
+        write(down, up)
+
+    @pl.when(core != 0)
+    def _():
+        write(up, down)
 
 
 def feature_body(grads, rim_grads, right, below, cot, down_weight, out, wide, pairs, near_mat, low_mat, woven):

time: 41.9 us -> 41.7 us (level)
  no operation moved by 1% of the time
where the time goes in v10:
time: 41.7 us; the launch traced here: 41.6 us
  starting transfers between devices  17.7 us (42%)
  waiting for transfers between devices  13.5 us (32%)
  Pallas kernels  9.61 us (23%)
  between operations  0.75 us (2%)
    ppermute x8, starting transfers between devices, traded(): lax.ppermute(value, 'wide', [(at, at ^ 1 << position) for at in range(cou...  10.6 us
    pallas_call x15, Pallas kernels, run(): return kernel(*placed)  9.61 us
    ppermute x8, waiting for transfers between devices, traded(): lax.ppermute(value, 'wide', [(at, at ^ 1 << position) for at in range(cou...  7.46 us
    ppermute x10, starting transfers between devices, turned(): lax.ppermute(value, axis, [(at, (at + steps) % count) for at in range(cou...  7.08 us
    ppermute x10, waiting for transfers between devices, turned(): lax.ppermute(value, axis, [(at, (at + steps) % count) for at in range(cou...  6.05 us
  transfers between devices with their start and end apart: 18, of which 8 were waited for; matrix products, arithmetic and copies ran while one was open for 0% of the time, Pallas kernels for 15%

profile of v10, /device:TPU:0, one launch (start us, length us, event | category | flops | bytes accessed | tf_op | source)
XLA Modules:
  0.0 41.6 jit_solution(7141391443065617745)
XLA Ops:
  0.6 1.7 %shard_map.84 = (bf16[64,64,128]{2,1,0:T(8,128)(2,1)S(1)}, bf16[64,64,128]{2,1,0:T(8,128)(2,1)S(1)}, bf16[3,3,128,128]{3,2,1,0:T(8,128)(2,1)S(1)}, bf16[3,3,128,...) custom-call(bf16[64,64,128]{2,1,0:T(8,128)(2,1)} %feat.1, ...), custom_call_target="tpu_custom_call" | custom-call | bytes 524288 | tf_op jit(solution)/shard_map/pallas_call | solution.py:36
  2.4 3.0 %collective-permute-start = (bf16[2,64,128]{2,1,0:T(8,128)(2,1)S(1)}, bf16[2,64,128]{2,1,0:T(8,128)(2,1)S(1)}, u32[]{:S(2)}, u32[]{:S(2)}) collective-permute-start(bf16[2,64,128]{2,1,0:T(8,128)(2,1)S(1)} %get-tuple-element.65), channel_id=1, source_target_pairs={{0,2},{2,4},{4,6},{6,8},{8,10},{10,12},{12,14},{14,0},{1,3},{3,5},... | collective-permute-start | bytes 98312 | tf_op jit(solution)/shard_map/ppermute | solution.py:487
  5.4 2.7 %shard_map.85 = (bf16[32,32,1152]{2,1,0:T(8,128)(2,1)S(1)}, bf16[32,32,1152]{2,1,0:T(8,128)(2,1)S(1)}, bf16[1024,128]{1,0:T(8,128)(2,1)S(1)}, bf16[1024,128]{1,0...) custom-call(bf16[64,64,128]{2,1,0:T(8,128)(2,1)S(1)} %get-tuple-elem, ...), custom_call_target="tpu_custom_call" | custom-call | flops 905969664 | bytes 6291456 | tf_op jit(solution)/shard_map/pallas_call | solution.py:36
  8.1 2.2 %collective-permute-done.top = bf16[2,64,128]{2,1,0:T(8,128)(2,1)S(1)} collective-permute-done((bf16[2,64,128]{2,1,0:T(8,128)(2,1)S(1)}, bf16[2,64,128]{2,1,0:T(8,128)(2,1)S(1)}, u32[]{:S(2)}, u32[]{:S(2)}) %collective-permute-start) | collective-permute-done | bytes 32800 | tf_op jit(solution)/shard_map/ppermute | solution.py:487
  10.3 0.5 %shard_map.86 = (bf16[64,128]{1,0:T(8,128)(2,1)S(1)}, bf16[64,1152]{1,0:T(8,128)(2,1)S(1)}, bf16[64,1152]{1,0:T(8,128)(2,1)S(1)}, bf16[64,128]{1,0:T(8,128)(2,1)...) custom-call(bf16[32,32,1152]{2,1,0:T(8,128)(2,1)S(1)} %get-tuple-ele, ...), custom_call_target="tpu_custom_call" | custom-call | flops 67108864 | bytes 3145728 | tf_op jit(solution)/shard_map/pallas_call | solution.py:36
  11.0 0.5 %collective-permute-start.3 = (bf16[576,128]{1,0:T(8,128)(2,1)S(1)}, bf16[576,128]{1,0:T(8,128)(2,1)S(1)}, u32[]{:S(2)}, u32[]{:S(2)}) collective-permute-start(bf16[576,128]{1,0:T(8,128)(2,1)S(1)} %get-tuple-element.87), channel_id=1, source_target_pairs={{0,1},{1,0},{2,3},{3,2},{4,5},{5,4},{6,7},{7,6},{8,9},{9,8},{10,11... | collective-permute-start | bytes 442376 | tf_op jit(solution)/shard_map/ppermute | solution.py:487
  11.4 0.9 %shard_map.87 = (f32[576,128]{1,0:T(8,128)S(1)}, f32[576,128]{1,0:T(8,128)S(1)}) custom-call(bf16[32,32,1152]{2,1,0:T(8,128)(2,1)S(1)} %get-tuple-element.61.feat_patch, bf16[32,32,1152]{2,1,0:T(8,128)(2,1)S(1)} %get-tuple-element.62.cot_patch, bf16[1024,128]{1,0:T(8,128)(2,1)S(1)} %get-tuple-element.74.act, bf16[1024,128]{1,0:T(8,128)(2,1)S(1)} %get-tuple-element.75.grads, ...), custom_call_target="tpu_custom_call" | custom-call | flops 301989888 | bytes 3145728 | tf_op jit(solution)/shard_map/pallas_call | solution.py:36
  13.1 1.4 %collective-permute-start.4 = (bf16[288,128]{1,0:T(8,128)(2,1)S(1)}, bf16[288,128]{1,0:T(8,128)(2,1)S(1)}, u32[]{:S(2)}, u32[]{:S(2)}) collective-permute-start(bf16[288,128]{1,0:T(8,128)(2,1)S(1)} %get-tuple-element.89), channel_id=1, source_target_pairs={{0,2},{2,0},{4,6},{6,4},{8,10},{10,8},{12,14},{14,12},{1,3},{3,1},... | collective-permute-start | bytes 221192 | tf_op jit(solution)/shard_map/ppermute | solution.py:492
  14.4 3.0 %collective-permute-done.4.got = bf16[288,128]{1,0:T(8,128)(2,1)S(1)} collective-permute-done((bf16[288,128]{1,0:T(8,128)(2,1)S(1)}, bf16[288,128]{1,0:T(8,128)(2,1)S(1)}, u32[]{:S(2)}, u32[]{:S(2)}) %collective-permute-start.4) | collective-permute-done | bytes 73760 | tf_op jit(solution)/shard_map/ppermute | solution.py:492
  17.5 2.6 %collective-permute-start.5 = (bf16[288,128]{1,0:T(8,128)(2,1)S(1)}, bf16[288,128]{1,0:T(8,128)(2,1)S(1)}, u32[]{:S(2)}, u32[]{:S(2)}) collective-permute-start(bf16[288,128]{1,0:T(8,128)(2,1)S(1)} %shard_map.90.held), channel_id=1, source_target_pairs={{0,8},{2,10},{4,12},{6,14},{8,0},{10,2},{12,4},{14,6},{1,9},{3,11}... | collective-permute-start | bytes 221192 | tf_op jit(solution)/shard_map/ppermute | solution.py:492
  20.1 0.7 %collective-permute-start.10 = (bf16[304,128]{1,0:T(8,128)(2,1)S(1)}, bf16[304,128]{1,0:T(8,128)(2,1)S(1)}, u32[]{:S(2)}, u32[]{:S(2)}) collective-permute-start(bf16[304,128]{1,0:T(8,128)(2,1)S(1)} %get-tuple-element.98.held), channel_id=1, source_target_pairs={{0,2},{2,0},{4,6},{6,4},{8,10},{10,8},{12,14},{14,12},{1,3},{3,1},... | collective-permute-start | bytes 233480 | tf_op jit(solution)/shard_map/ppermute | solution.py:492
  20.8 1.2 %collective-permute-done.7.right = bf16[32,128]{1,0:T(8,128)(2,1)S(1)} collective-permute-done((bf16[32,128]{1,0:T(8,128)(2,1)S(1)}, bf16[32,128]{1,0:T(8,128)(2,1)S(1)}, u32[]{:S(2)}, u32[]{:S(2)}) %collective-permute-start.7) | collective-permute-done | bytes 8224 | tf_op jit(solution)/shard_map/ppermute | solution.py:487
  21.9 0.9 %collective-permute-done.5.got = bf16[288,128]{1,0:T(8,128)(2,1)S(1)} collective-permute-done((bf16[288,128]{1,0:T(8,128)(2,1)S(1)}, bf16[288,128]{1,0:T(8,128)(2,1)S(1)}, u32[]{:S(2)}, u32[]{:S(2)}) %collective-permute-start.5) | collective-permute-done | bytes 73760 | tf_op jit(solution)/shard_map/ppermute | solution.py:492
  22.8 2.1 %collective-permute-start.6 = (bf16[288,128]{1,0:T(8,128)(2,1)S(1)}, bf16[288,128]{1,0:T(8,128)(2,1)S(1)}, u32[]{:S(2)}, u32[]{:S(2)}) collective-permute-start(bf16[288,128]{1,0:T(8,128)(2,1)S(1)} %shard_map.91.held), channel_id=1, source_target_pairs={{0,4},{2,6},{4,0},{6,2},{8,12},{10,14},{12,8},{14,10},{1,5},{3,7},... | collective-permute-start | bytes 221192 | tf_op jit(solution)/shard_map/ppermute | solution.py:492
  24.9 1.0 %collective-permute-start.11 = (bf16[304,128]{1,0:T(8,128)(2,1)S(1)}, bf16[304,128]{1,0:T(8,128)(2,1)S(1)}, u32[]{:S(2)}, u32[]{:S(2)}) collective-permute-start(bf16[304,128]{1,0:T(8,128)(2,1)S(1)} %get-tuple-element.100.held), channel_id=1, source_target_pairs={{0,8},{2,10},{4,12},{6,14},{8,0},{10,2},{12,4},{14,6},{1,9},{3,11}... | collective-permute-start | bytes 233480 | tf_op jit(solution)/shard_map/ppermute | solution.py:492
  26.0 3.0 %collective-permute-start.8 = (bf16[40,128]{1,0:T(8,128)(2,1)S(1)}, bf16[40,128]{1,0:T(8,128)(2,1)S(1)}, u32[]{:S(2)}, u32[]{:S(2)}) collective-permute-start(bf16[40,128]{1,0:T(8,128)(2,1)S(1)} %pad_maximum_fusion), channel_id=1, source_target_pairs={{0,14},{2,0},{4,2},{6,4},{8,6},{10,8},{12,10},{14,12},{1,15},{3,1}... | collective-permute-start | bytes 30728 | tf_op jit(solution)/shard_map/ppermute | solution.py:487
  28.9 1.4 %collective-permute-done.8.below = bf16[40,128]{1,0:T(8,128)(2,1)S(1)} collective-permute-done((bf16[40,128]{1,0:T(8,128)(2,1)S(1)}, bf16[40,128]{1,0:T(8,128)(2,1)S(1)}, u32[]{:S(2)}, u32[]{:S(2)}) %collective-permute-start.8) | collective-permute-done | bytes 10272 | tf_op jit(solution)/shard_map/ppermute | solution.py:487
  30.3 1.8 %shard_map.92 = bf16[64,64,128]{2,1,0:T(8,128)(2,1)} custom-call(bf16[1024,128]{1,0:T(8,128)(2,1)S(1)} %get-tuple-element.75.grads, bf16[64,128]{1,0:T(8,128)(2,1)S(1)} %get-tuple-element.90.rim_grads, bf16[32,128]{1,0:T(8,128)(2,1)S(1)} %collective-permute-done.7.right, bf16[40,128]{1,0:T(8,128)(2,1)S(1)} %collective-permute-done.8.below, ...), custom_call_target="tpu_custom_call" | custom-call | flops 402653184 | bytes 3145728 | tf_op jit(solution)/shard_map/pallas_call | solution.py:36
  32.1 2.5 %collective-permute-start.13 = (bf16[288,128]{1,0:T(8,128)(2,1)S(1)}, bf16[288,128]{1,0:T(8,128)(2,1)S(1)}, u32[]{:S(2)}, u32[]{:S(2)}) collective-permute-start(bf16[288,128]{1,0:T(8,128)(2,1)S(1)} %shard_map.97.held_b), channel_id=1, source_target_pairs={{0,2},{2,0},{4,6},{6,4},{8,10},{10,8},{12,14},{14,12},{1,3},{3,1},... | collective-permute-start | bytes 221192 | tf_op jit(solution)/shard_map/ppermute | solution.py:492
  35.0 0.5 %collective-permute-start.14 = (bf16[288,128]{1,0:T(8,128)(2,1)S(1)}, bf16[288,128]{1,0:T(8,128)(2,1)S(1)}, u32[]{:S(2)}, u32[]{:S(2)}) collective-permute-start(bf16[288,128]{1,0:T(8,128)(2,1)S(1)} %get-tuple-element.102.held_a), channel_id=1, source_target_pairs={{0,1},{1,0},{2,3},{3,2},{4,5},{5,4},{6,7},{7,6},{8,9},{9,8},{10,11... | collective-permute-start | bytes 221192 | tf_op jit(solution)/shard_map/ppermute | solution.py:487
  35.5 1.4 %collective-permute-done.13.got_b = bf16[288,128]{1,0:T(8,128)(2,1)S(1)} collective-permute-done((bf16[288,128]{1,0:T(8,128)(2,1)S(1)}, bf16[288,128]{1,0:T(8,128)(2,1)S(1)}, u32[]{:S(2)}, u32[]{:S(2)}) %collective-permute-start.13) | collective-permute-done | bytes 73760 | tf_op jit(solution)/shard_map/ppermute | solution.py:492
  36.9 2.1 %collective-permute-done.12.got_a = bf16[288,128]{1,0:T(8,128)(2,1)S(1)} collective-permute-done((bf16[288,128]{1,0:T(8,128)(2,1)S(1)}, bf16[288,128]{1,0:T(8,128)(2,1)S(1)}, u32[]{:S(2)}, u32[]{:S(2)}) %collective-permute-start.12) | collective-permute-done | bytes 73760 | tf_op jit(solution)/shard_map/ppermute | solution.py:492
  39.1 1.2 %collective-permute-done.15.far_got_a = bf16[288,128]{1,0:T(8,128)(2,1)S(1)} collective-permute-done((bf16[288,128]{1,0:T(8,128)(2,1)S(1)}, bf16[288,128]{1,0:T(8,128)(2,1)S(1)}, u32[]{:S(2)}, u32[]{:S(2)}) %collective-permute-start.15) | collective-permute-done | bytes 73760 | tf_op jit(solution)/shard_map/ppermute | solution.py:487
  40.3 1.2 %shard_map.98 = (f32[4,288,128]{2,1,0:T(8,128)}, f32[4,288,128]{2,1,0:T(8,128)}, f32[1,128]{1,0:T(1,128)}) custom-call(bf16[288,128]{1,0:T(8,128)(2,1)S(1)} %get-tuple-element.102.held_a, bf16[288,128]{1,0:T(8,128)(2,1)S(1)} %collective-permute-done.12.got_a, bf16[288,128]{1,0:T(8,128)(2,1)S(1)} %shard_map.97.held_b, ...), custom_call_target="tpu_custom_call" | custom-call | bytes 1769472 | tf_op jit(solution)/shard_map/pallas_call | solution.py:36
  (30 shorter events, 1.2 us)
Async XLA Ops:
  2.4 8.0 %collective-permute-start = (bf16[2,64,128]{2,1,0:T(8,128)(2,1)S(1)}, bf16[2,64,128]{2,1,0:T(8,128)(2,1)S(1)}, u32[]{:S(2)}, u32[]{:S(2)}) collective-permute-start(bf16[2,64,128]{2,1,0:T(8,128)(2,1)S(1)} %get-tuple-element.65), channel_id=1, source_target_pairs={{0,2},{2,4},{4,6},{6,8},{8,10},{10,12},{12,14},{14,0},{1,3},{3,5},... | collective-permute-start | bytes 98312 | tf_op jit(solution)/shard_map/ppermute | solution.py:487
  5.4 4.9 %collective-permute-start.1 = (bf16[2,64,128]{2,1,0:T(8,128)(2,1)S(1)}, bf16[2,64,128]{2,1,0:T(8,128)(2,1)S(1)}, u32[]{:S(2)}, u32[]{:S(2)}) collective-permute-start(bf16[2,64,128]{2,1,0:T(8,128)(2,1)S(1)} %get-tuple-element.66), channel_id=1, source_target_pairs={{0,1},{1,0},{2,3},{3,2},{4,5},{5,4},{6,7},{7,6},{8,9},{9,8},{10,11... | collective-permute-start | bytes 98312 | tf_op jit(solution)/shard_map/ppermute | solution.py:487
  10.9 1.5 %collective-permute-start.2 = (bf16[624,128]{1,0:T(8,128)(2,1)S(1)}, bf16[624,128]{1,0:T(8,128)(2,1)S(1)}, u32[]{:S(2)}, u32[]{:S(2)}) collective-permute-start(bf16[624,128]{1,0:T(8,128)(2,1)S(1)} %get-tuple-element.73.own), channel_id=1, source_target_pairs={{0,1},{1,0},{2,3},{3,2},{4,5},{5,4},{6,7},{7,6},{8,9},{9,8},{10,11... | collective-permute-start | bytes 479240 | tf_op jit(solution)/shard_map/ppermute | solution.py:487
  11.0 2.0 %collective-permute-start.3 = (bf16[576,128]{1,0:T(8,128)(2,1)S(1)}, bf16[576,128]{1,0:T(8,128)(2,1)S(1)}, u32[]{:S(2)}, u32[]{:S(2)}) collective-permute-start(bf16[576,128]{1,0:T(8,128)(2,1)S(1)} %get-tuple-element.87), channel_id=1, source_target_pairs={{0,1},{1,0},{2,3},{3,2},{4,5},{5,4},{6,7},{7,6},{8,9},{9,8},{10,11... | collective-permute-start | bytes 442376 | tf_op jit(solution)/shard_map/ppermute | solution.py:487
  12.9 7.2 %collective-permute-start.9 = (bf16[304,128]{1,0:T(8,128)(2,1)S(1)}, bf16[304,128]{1,0:T(8,128)(2,1)S(1)}, u32[]{:S(2)}, u32[]{:S(2)}) collective-permute-start(bf16[304,128]{1,0:T(8,128)(2,1)S(1)} %get-tuple-element.96), channel_id=1, source_target_pairs={{0,4},{2,6},{4,0},{6,2},{8,12},{10,14},{12,8},{14,10},{1,5},{3,7},... | collective-permute-start | bytes 233480 | tf_op jit(solution)/shard_map/ppermute | solution.py:492
  13.1 4.4 %collective-permute-start.4 = (bf16[288,128]{1,0:T(8,128)(2,1)S(1)}, bf16[288,128]{1,0:T(8,128)(2,1)S(1)}, u32[]{:S(2)}, u32[]{:S(2)}) collective-permute-start(bf16[288,128]{1,0:T(8,128)(2,1)S(1)} %get-tuple-element.89), channel_id=1, source_target_pairs={{0,2},{2,0},{4,6},{6,4},{8,10},{10,8},{12,14},{14,12},{1,3},{3,1},... | collective-permute-start | bytes 221192 | tf_op jit(solution)/shard_map/ppermute | solution.py:492
  17.5 5.3 %collective-permute-start.5 = (bf16[288,128]{1,0:T(8,128)(2,1)S(1)}, bf16[288,128]{1,0:T(8,128)(2,1)S(1)}, u32[]{:S(2)}, u32[]{:S(2)}) collective-permute-start(bf16[288,128]{1,0:T(8,128)(2,1)S(1)} %shard_map.90.held), channel_id=1, source_target_pairs={{0,8},{2,10},{4,12},{6,14},{8,0},{10,2},{12,4},{14,6},{1,9},{3,11}... | collective-permute-start | bytes 221192 | tf_op jit(solution)/shard_map/ppermute | solution.py:492
  20.1 4.8 %collective-permute-start.10 = (bf16[304,128]{1,0:T(8,128)(2,1)S(1)}, bf16[304,128]{1,0:T(8,128)(2,1)S(1)}, u32[]{:S(2)}, u32[]{:S(2)}) collective-permute-start(bf16[304,128]{1,0:T(8,128)(2,1)S(1)} %get-tuple-element.98.held), channel_id=1, source_target_pairs={{0,2},{2,0},{4,6},{6,4},{8,10},{10,8},{12,14},{14,12},{1,3},{3,1},... | collective-permute-start | bytes 233480 | tf_op jit(solution)/shard_map/ppermute | solution.py:492
  20.8 1.2 %collective-permute-start.7 = (bf16[32,128]{1,0:T(8,128)(2,1)S(1)}, bf16[32,128]{1,0:T(8,128)(2,1)S(1)}, u32[]{:S(2)}, u32[]{:S(2)}) collective-permute-start(bf16[32,128]{1,0:T(8,128)(2,1)S(1)} %get-tuple-element.109), channel_id=1, source_target_pairs={{0,1},{1,0},{2,3},{3,2},{4,5},{5,4},{6,7},{7,6},{8,9},{9,8},{10,11... | collective-permute-start | bytes 24584 | tf_op jit(solution)/shard_map/ppermute | solution.py:487
  22.8 9.3 %collective-permute-start.6 = (bf16[288,128]{1,0:T(8,128)(2,1)S(1)}, bf16[288,128]{1,0:T(8,128)(2,1)S(1)}, u32[]{:S(2)}, u32[]{:S(2)}) collective-permute-start(bf16[288,128]{1,0:T(8,128)(2,1)S(1)} %shard_map.91.held), channel_id=1, source_target_pairs={{0,4},{2,6},{4,0},{6,2},{8,12},{10,14},{12,8},{14,10},{1,5},{3,7},... | collective-permute-start | bytes 221192 | tf_op jit(solution)/shard_map/ppermute | solution.py:492
  24.9 9.7 %collective-permute-start.11 = (bf16[304,128]{1,0:T(8,128)(2,1)S(1)}, bf16[304,128]{1,0:T(8,128)(2,1)S(1)}, u32[]{:S(2)}, u32[]{:S(2)}) collective-permute-start(bf16[304,128]{1,0:T(8,128)(2,1)S(1)} %get-tuple-element.100.held), channel_id=1, source_target_pairs={{0,8},{2,10},{4,12},{6,14},{8,0},{10,2},{12,4},{14,6},{1,9},{3,11}... | collective-permute-start | bytes 233480 | tf_op jit(solution)/shard_map/ppermute | solution.py:492
  26.0 4.4 %collective-permute-start.8 = (bf16[40,128]{1,0:T(8,128)(2,1)S(1)}, bf16[40,128]{1,0:T(8,128)(2,1)S(1)}, u32[]{:S(2)}, u32[]{:S(2)}) collective-permute-start(bf16[40,128]{1,0:T(8,128)(2,1)S(1)} %pad_maximum_fusion), channel_id=1, source_target_pairs={{0,14},{2,0},{4,2},{6,4},{8,6},{10,8},{12,10},{14,12},{1,15},{3,1}... | collective-permute-start | bytes 30728 | tf_op jit(solution)/shard_map/ppermute | solution.py:487
  32.1 4.8 %collective-permute-start.13 = (bf16[288,128]{1,0:T(8,128)(2,1)S(1)}, bf16[288,128]{1,0:T(8,128)(2,1)S(1)}, u32[]{:S(2)}, u32[]{:S(2)}) collective-permute-start(bf16[288,128]{1,0:T(8,128)(2,1)S(1)} %shard_map.97.held_b), channel_id=1, source_target_pairs={{0,2},{2,0},{4,6},{6,4},{8,10},{10,8},{12,14},{14,12},{1,3},{3,1},... | collective-permute-start | bytes 221192 | tf_op jit(solution)/shard_map/ppermute | solution.py:492
  34.6 4.4 %collective-permute-start.12 = (bf16[288,128]{1,0:T(8,128)(2,1)S(1)}, bf16[288,128]{1,0:T(8,128)(2,1)S(1)}, u32[]{:S(2)}, u32[]{:S(2)}) collective-permute-start(bf16[288,128]{1,0:T(8,128)(2,1)S(1)} %get-tuple-element.102.held_a), channel_id=1, source_target_pairs={{0,4},{2,6},{4,0},{6,2},{8,12},{10,14},{12,8},{14,10},{1,5},{3,7},... | collective-permute-start | bytes 221192 | tf_op jit(solution)/shard_map/ppermute | solution.py:492
  35.0 4.1 %collective-permute-start.16 = (bf16[288,128]{1,0:T(8,128)(2,1)S(1)}, bf16[288,128]{1,0:T(8,128)(2,1)S(1)}, u32[]{:S(2)}, u32[]{:S(2)}) collective-permute-start(bf16[288,128]{1,0:T(8,128)(2,1)S(1)} %shard_map.97.held_b), channel_id=1, source_target_pairs={{0,1},{1,0},{2,3},{3,2},{4,5},{5,4},{6,7},{7,6},{8,9},{9,8},{10,11... | collective-permute-start | bytes 221192 | tf_op jit(solution)/shard_map/ppermute | solution.py:487
  35.0 4.1 %collective-permute-start.14 = (bf16[288,128]{1,0:T(8,128)(2,1)S(1)}, bf16[288,128]{1,0:T(8,128)(2,1)S(1)}, u32[]{:S(2)}, u32[]{:S(2)}) collective-permute-start(bf16[288,128]{1,0:T(8,128)(2,1)S(1)} %get-tuple-element.102.held_a), channel_id=1, source_target_pairs={{0,1},{1,0},{2,3},{3,2},{4,5},{5,4},{6,7},{7,6},{8,9},{9,8},{10,11... | collective-permute-start | bytes 221192 | tf_op jit(solution)/shard_map/ppermute | solution.py:487
  36.9 2.1 %collective-permute-start.17 = (bf16[288,128]{1,0:T(8,128)(2,1)S(1)}, bf16[288,128]{1,0:T(8,128)(2,1)S(1)}, u32[]{:S(2)}, u32[]{:S(2)}) collective-permute-start(bf16[288,128]{1,0:T(8,128)(2,1)S(1)} %collective-permute-done.13.got_b), channel_id=1, source_target_pairs={{0,1},{1,0},{2,3},{3,2},{4,5},{5,4},{6,7},{7,6},{8,9},{9,8},{10,11... | collective-permute-start | bytes 221192 | tf_op jit(solution)/shard_map/ppermute | solution.py:487
  39.1 1.3 %collective-permute-start.15 = (bf16[288,128]{1,0:T(8,128)(2,1)S(1)}, bf16[288,128]{1,0:T(8,128)(2,1)S(1)}, u32[]{:S(2)}, u32[]{:S(2)}) collective-permute-start(bf16[288,128]{1,0:T(8,128)(2,1)S(1)} %collective-permute-done.12.got_a), channel_id=1, source_target_pairs={{0,1},{1,0},{2,3},{3,2},{4,5},{5,4},{6,7},{7,6},{8,9},{9,8},{10,11... | collective-permute-start | bytes 221192 | tf_op jit(solution)/shard_map/ppermute | solution.py:487

commit v11 on v10

--- a/solution.py
+++ b/solution.py
@@ -253,8 +253,8 @@
 
 
 def late_body(
-    own, got, mine_a, mine_b, rim_grads, down_weight, down_bias, up_mat,
-    out_a, out_b, grads_out, late, feat_row, cot_row,
+    position, own, got, mine_a, mine_b, rim_grads, down_weight, down_bias, up_mat, bias_in,
+    keep, send, out_b, grads_out, bias_out, feat_row, cot_row, held,
 ):
     half, channels = mine_a.shape
     taps = 2 * half
@@ -278,7 +278,7 @@
     act = if_any(first, value).astype(BF16)
     grad = if_any(first, grad).astype(BF16)
     only = grad.astype(F32)[0:1]
-    late[...] = jnp.broadcast_to(only, late.shape)
+    joined_bias(bias_in, got, half, bias_out, send, half // 2, only)
     half_cols = rim_grads.shape[0] // 2
     row = lax.broadcasted_iota(jnp.int32, rim_grads.shape, 0)
     ours = ((row == 0) | (row == half_cols)) & (core > 0)
@@ -287,7 +287,7 @@
     ).astype(BF16)
 
     def add(more):
-        out_a[...] = mine_a[...] + more[0:half]
+        held[...] = mine_a[...] + more[0:half]
         out_b[...] = mine_b[...] + more[half:]
 
     @pl.when(core == 0)
@@ -297,6 +297,8 @@
     @pl.when(core != 0)
     def _():
         add(taps_of(False, cot_row[...], act))
+
+    split(position, held, got, 0, half, keep, send)
 
 
 def mine_body(
@@ -361,8 +363,8 @@
 def halve_body(position, held, got, *rest):
     size = held.shape[0]
     if len(rest) > 3:
-        bias_in, *late, keep, send, bias_out = rest
-        joined_bias(bias_in, got, size, bias_out, send, size // 2, *late)
+        bias_in, keep, send, bias_out = rest
+        joined_bias(bias_in, got, size, bias_out, send, size // 2)
     else:
         keep, send = rest
     split(position, held, got, 0, size, keep, send)
@@ -587,40 +589,51 @@
         room=12,
     )(feat_patch, cot_patch, act, grads, feat_rim, cot_rim, rim_act, rim_masked)
     got_a, mine_a, mine_b = lax.optimization_barrier((got_a, mine_a, mine_b))
-    mine_a, mine_b, rim_grads, late = call(
-        late_body,
+    bits = lax.axis_size("wide").bit_length() - 1
+    order_a = [1, 0, *range(2, bits)] if bits > 1 else list(range(bits))
+    order_b = [0, 2, 1, *range(3, bits)] if bits > 2 else list(range(bits))
+    half = taps // 4
+    held_a, send_a, mine_b, rim_grads, bias_sum = call(
+        functools.partial(late_body, order_a[0]),
         (
-            vm((taps // 2, channels), F32),
+            vm((half, channels), F32),
+            vm((half + SIDE, channels), BF16),
             vm((taps // 2, channels), F32),
             vm((pieces, channels), BF16),
             vm((8, channels), F32),
         ),
-        scratch=[pltpu.VMEM((SIDE, taps), BF16), pltpu.VMEM((SIDE, taps), BF16)],
-        n_in=8,
+        scratch=[
+            pltpu.VMEM((SIDE, taps), BF16),
+            pltpu.VMEM((SIDE, taps), BF16),
+            pltpu.VMEM((taps // 2, channels), F32),
+        ],
+        n_in=9,
         flops=1 << 24,
         nbytes=1 << 20,
-        near=tuple(range(8)),
+        near=tuple(range(9)),
         room=8,
-    )(other_a, got_a, mine_a, mine_b, rim_grads, down_near, bias_near, up_mat)
+    )(other_a, got_a, mine_a, mine_b, rim_grads, down_near, bias_near, up_mat, bias_sum)
     from_right = turned(rim_grads[half_cols:], "narrow", -1)
     low = jnp.concatenate([rim_grads[:half_cols], from_right[:8]], axis=0)
     from_below = turned(low, "wide", -1)
 
-    bits = lax.axis_size("wide").bit_length() - 1
-    order_a = [1, 0, *range(2, bits)] if bits > 1 else list(range(bits))
-    order_b = [0, 2, 1, *range(3, bits)] if bits > 2 else list(range(bits))
     halvings = 1 if bits <= 3 else 2
     half = taps // 2
-    held_a, held_b = mine_a, mine_b
+    held_b = mine_b
     for step in range(halvings):
         half //= 2
-        held_a, send_a, bias_sum = call(
-            functools.partial(halve_body, order_a[step]),
-            (vm((half, channels), F32), vm((half + SIDE, channels), BF16), vm((8, channels), F32)),
-            n_in=3 if step else 4,
-            nbytes=half * channels * 12,
-            near=(0, 1, 2) if step else (0, 1, 2, 3),
-        )(held_a, got_a, bias_sum, *(() if step else (late,)))
+        if step:
+            held_a, send_a, bias_sum = call(
+                functools.partial(halve_body, order_a[step]),
+                (
+                    vm((half, channels), F32),
+                    vm((half + SIDE, channels), BF16),
+                    vm((8, channels), F32),
+                ),
+                n_in=3,
+                nbytes=half * channels * 12,
+                near=(0, 1, 2),
+            )(held_a, got_a, bias_sum)
         held_b, send_b = call(
             functools.partial(halve_body, order_b[step]),
             (vm((half, channels), F32), vm((half, channels), BF16)),

time: 41.7 us -> 41.8 us (level)
    pallas_call x15 -> x14, Pallas kernels: 9.61 us -> 9.69 us  [run(): return kernel(*placed)]
where the time goes in v11:
time: 41.8 us; the launch traced here: 41.6 us
  starting transfers between devices  17.7 us (42%)
  waiting for transfers between devices  13.5 us (32%)
  Pallas kernels  9.69 us (23%)
  between operations  0.74 us (2%)
    ppermute x8, starting transfers between devices, traded(): lax.ppermute(value, 'wide', [(at, at ^ 1 << position) for at in range(cou...  10.6 us
    pallas_call x14, Pallas kernels, run(): return kernel(*placed)  9.69 us
    ppermute x8, waiting for transfers between devices, traded(): lax.ppermute(value, 'wide', [(at, at ^ 1 << position) for at in range(cou...  7.46 us
    ppermute x10, starting transfers between devices, turned(): lax.ppermute(value, axis, [(at, (at + steps) % count) for at in range(cou...  7.08 us
    ppermute x10, waiting for transfers between devices, turned(): lax.ppermute(value, axis, [(at, (at + steps) % count) for at in range(cou...  6.04 us
  transfers between devices with their start and end apart: 18, of which 8 were waited for; matrix products, arithmetic and copies ran while one was open for 0% of the time, Pallas kernels for 15%

profile of v11, /device:TPU:0, one launch (start us, length us, event | category | flops | bytes accessed | tf_op | source)
XLA Modules:
  0.0 41.6 jit_solution(302596868311699378)
XLA Ops:
  0.6 1.7 %shard_map.84 = (bf16[64,64,128]{2,1,0:T(8,128)(2,1)S(1)}, bf16[64,64,128]{2,1,0:T(8,128)(2,1)S(1)}, bf16[3,3,128,128]{3,2,1,0:T(8,128)(2,1)S(1)}, bf16[3,3,128,...) custom-call(bf16[64,64,128]{2,1,0:T(8,128)(2,1)} %feat.1, ...), custom_call_target="tpu_custom_call" | custom-call | bytes 524288 | tf_op jit(solution)/shard_map/pallas_call | solution.py:36
  2.4 3.0 %collective-permute-start = (bf16[2,64,128]{2,1,0:T(8,128)(2,1)S(1)}, bf16[2,64,128]{2,1,0:T(8,128)(2,1)S(1)}, u32[]{:S(2)}, u32[]{:S(2)}) collective-permute-start(bf16[2,64,128]{2,1,0:T(8,128)(2,1)S(1)} %get-tuple-element.63), channel_id=1, source_target_pairs={{0,2},{2,4},{4,6},{6,8},{8,10},{10,12},{12,14},{14,0},{1,3},{3,5},... | collective-permute-start | bytes 98312 | tf_op jit(solution)/shard_map/ppermute | solution.py:489
  5.4 2.7 %shard_map.85 = (bf16[32,32,1152]{2,1,0:T(8,128)(2,1)S(1)}, bf16[32,32,1152]{2,1,0:T(8,128)(2,1)S(1)}, bf16[1024,128]{1,0:T(8,128)(2,1)S(1)}, bf16[1024,128]{1,0...) custom-call(bf16[64,64,128]{2,1,0:T(8,128)(2,1)S(1)} %get-tuple-elem, ...), custom_call_target="tpu_custom_call" | custom-call | flops 905969664 | bytes 6291456 | tf_op jit(solution)/shard_map/pallas_call | solution.py:36
  8.1 2.2 %collective-permute-done.top = bf16[2,64,128]{2,1,0:T(8,128)(2,1)S(1)} collective-permute-done((bf16[2,64,128]{2,1,0:T(8,128)(2,1)S(1)}, bf16[2,64,128]{2,1,0:T(8,128)(2,1)S(1)}, u32[]{:S(2)}, u32[]{:S(2)}) %collective-permute-start) | collective-permute-done | bytes 32800 | tf_op jit(solution)/shard_map/ppermute | solution.py:489
  10.3 0.5 %shard_map.86 = (bf16[64,128]{1,0:T(8,128)(2,1)S(1)}, bf16[64,1152]{1,0:T(8,128)(2,1)S(1)}, bf16[64,1152]{1,0:T(8,128)(2,1)S(1)}, bf16[64,128]{1,0:T(8,128)(2,1)...) custom-call(bf16[32,32,1152]{2,1,0:T(8,128)(2,1)S(1)} %get-tuple-ele, ...), custom_call_target="tpu_custom_call" | custom-call | flops 67108864 | bytes 3145728 | tf_op jit(solution)/shard_map/pallas_call | solution.py:36
  11.5 0.9 %shard_map.87 = (f32[576,128]{1,0:T(8,128)S(1)}, f32[576,128]{1,0:T(8,128)S(1)}) custom-call(bf16[32,32,1152]{2,1,0:T(8,128)(2,1)S(1)} %get-tuple-element.59.feat_patch, bf16[32,32,1152]{2,1,0:T(8,128)(2,1)S(1)} %get-tuple-element.60.cot_patch, bf16[1024,128]{1,0:T(8,128)(2,1)S(1)} %get-tuple-element.72.act, bf16[1024,128]{1,0:T(8,128)(2,1)S(1)} %get-tuple-element.73.grads, ...), custom_call_target="tpu_custom_call" | custom-call | flops 301989888 | bytes 3145728 | tf_op jit(solution)/shard_map/pallas_call | solution.py:36
  12.4 0.6 %shard_map.88 = (f32[288,128]{1,0:T(8,128)S(1)}, bf16[304,128]{1,0:T(8,128)(2,1)S(1)}, f32[576,128]{1,0:T(8,128)S(1)}, bf16[64,128]{1,0:T(8,128)(2,1)S(1)}, f32[8,128]{1,0:T(8,128)S(1)}) custom-call(bf16[624,128]{1,0:T(8,128)(2,1)S(1)} %get-tuple-element.71.own, bf16[624,128]{1,0:T(8,128)(2,1)S(1)} %collective-permute-done.2.got, ...), custom_call_target="tpu_custom_call" | custom-call | flops 16777216 | bytes 1048576 | tf_op jit(solution)/shard_map/pallas_call | solution.py:36
  13.1 1.4 %collective-permute-start.4 = (bf16[288,128]{1,0:T(8,128)(2,1)S(1)}, bf16[288,128]{1,0:T(8,128)(2,1)S(1)}, u32[]{:S(2)}, u32[]{:S(2)}) collective-permute-start(bf16[288,128]{1,0:T(8,128)(2,1)S(1)} %get-tuple-element.88), channel_id=1, source_target_pairs={{0,2},{2,0},{4,6},{6,4},{8,10},{10,8},{12,14},{14,12},{1,3},{3,1},... | collective-permute-start | bytes 221192 | tf_op jit(solution)/shard_map/ppermute | solution.py:494
  14.5 3.0 %collective-permute-done.4.got = bf16[288,128]{1,0:T(8,128)(2,1)S(1)} collective-permute-done((bf16[288,128]{1,0:T(8,128)(2,1)S(1)}, bf16[288,128]{1,0:T(8,128)(2,1)S(1)}, u32[]{:S(2)}, u32[]{:S(2)}) %collective-permute-start.4) | collective-permute-done | bytes 73760 | tf_op jit(solution)/shard_map/ppermute | solution.py:494
  17.5 2.6 %collective-permute-start.5 = (bf16[288,128]{1,0:T(8,128)(2,1)S(1)}, bf16[288,128]{1,0:T(8,128)(2,1)S(1)}, u32[]{:S(2)}, u32[]{:S(2)}) collective-permute-start(bf16[288,128]{1,0:T(8,128)(2,1)S(1)} %shard_map.90.held), channel_id=1, source_target_pairs={{0,8},{2,10},{4,12},{6,14},{8,0},{10,2},{12,4},{14,6},{1,9},{3,11}... | collective-permute-start | bytes 221192 | tf_op jit(solution)/shard_map/ppermute | solution.py:494
  20.2 0.7 %collective-permute-start.10 = (bf16[304,128]{1,0:T(8,128)(2,1)S(1)}, bf16[304,128]{1,0:T(8,128)(2,1)S(1)}, u32[]{:S(2)}, u32[]{:S(2)}) collective-permute-start(bf16[304,128]{1,0:T(8,128)(2,1)S(1)} %get-tuple-element.94.held), channel_id=1, source_target_pairs={{0,2},{2,0},{4,6},{6,4},{8,10},{10,8},{12,14},{14,12},{1,3},{3,1},... | collective-permute-start | bytes 233480 | tf_op jit(solution)/shard_map/ppermute | solution.py:494
  20.8 1.2 %collective-permute-done.7.right = bf16[32,128]{1,0:T(8,128)(2,1)S(1)} collective-permute-done((bf16[32,128]{1,0:T(8,128)(2,1)S(1)}, bf16[32,128]{1,0:T(8,128)(2,1)S(1)}, u32[]{:S(2)}, u32[]{:S(2)}) %collective-permute-start.7) | collective-permute-done | bytes 8224 | tf_op jit(solution)/shard_map/ppermute | solution.py:489
  22.0 0.9 %collective-permute-done.5.got = bf16[288,128]{1,0:T(8,128)(2,1)S(1)} collective-permute-done((bf16[288,128]{1,0:T(8,128)(2,1)S(1)}, bf16[288,128]{1,0:T(8,128)(2,1)S(1)}, u32[]{:S(2)}, u32[]{:S(2)}) %collective-permute-start.5) | collective-permute-done | bytes 73760 | tf_op jit(solution)/shard_map/ppermute | solution.py:494
  22.9 2.1 %collective-permute-start.6 = (bf16[288,128]{1,0:T(8,128)(2,1)S(1)}, bf16[288,128]{1,0:T(8,128)(2,1)S(1)}, u32[]{:S(2)}, u32[]{:S(2)}) collective-permute-start(bf16[288,128]{1,0:T(8,128)(2,1)S(1)} %shard_map.91.held), channel_id=1, source_target_pairs={{0,4},{2,6},{4,0},{6,2},{8,12},{10,14},{12,8},{14,10},{1,5},{3,7},... | collective-permute-start | bytes 221192 | tf_op jit(solution)/shard_map/ppermute | solution.py:494
  25.0 1.0 %collective-permute-start.11 = (bf16[304,128]{1,0:T(8,128)(2,1)S(1)}, bf16[304,128]{1,0:T(8,128)(2,1)S(1)}, u32[]{:S(2)}, u32[]{:S(2)}) collective-permute-start(bf16[304,128]{1,0:T(8,128)(2,1)S(1)} %get-tuple-element.96.held), channel_id=1, source_target_pairs={{0,8},{2,10},{4,12},{6,14},{8,0},{10,2},{12,4},{14,6},{1,9},{3,11}... | collective-permute-start | bytes 233480 | tf_op jit(solution)/shard_map/ppermute | solution.py:494
  26.0 3.0 %collective-permute-start.8 = (bf16[40,128]{1,0:T(8,128)(2,1)S(1)}, bf16[40,128]{1,0:T(8,128)(2,1)S(1)}, u32[]{:S(2)}, u32[]{:S(2)}) collective-permute-start(bf16[40,128]{1,0:T(8,128)(2,1)S(1)} %pad_maximum_fusion), channel_id=1, source_target_pairs={{0,14},{2,0},{4,2},{6,4},{8,6},{10,8},{12,10},{14,12},{1,15},{3,1}... | collective-permute-start | bytes 30728 | tf_op jit(solution)/shard_map/ppermute | solution.py:489
  29.0 1.4 %collective-permute-done.8.below = bf16[40,128]{1,0:T(8,128)(2,1)S(1)} collective-permute-done((bf16[40,128]{1,0:T(8,128)(2,1)S(1)}, bf16[40,128]{1,0:T(8,128)(2,1)S(1)}, u32[]{:S(2)}, u32[]{:S(2)}) %collective-permute-start.8) | collective-permute-done | bytes 10272 | tf_op jit(solution)/shard_map/ppermute | solution.py:489
  30.4 1.8 %shard_map.92 = bf16[64,64,128]{2,1,0:T(8,128)(2,1)} custom-call(bf16[1024,128]{1,0:T(8,128)(2,1)S(1)} %get-tuple-element.73.grads, bf16[64,128]{1,0:T(8,128)(2,1)S(1)} %get-tuple-element.89.rim_grads, bf16[32,128]{1,0:T(8,128)(2,1)S(1)} %collective-permute-done.7.right, bf16[40,128]{1,0:T(8,128)(2,1)S(1)} %collective-permute-done.8.below, ...), custom_call_target="tpu_custom_call" | custom-call | flops 402653184 | bytes 3145728 | tf_op jit(solution)/shard_map/pallas_call | solution.py:36
  32.2 2.5 %collective-permute-start.13 = (bf16[288,128]{1,0:T(8,128)(2,1)S(1)}, bf16[288,128]{1,0:T(8,128)(2,1)S(1)}, u32[]{:S(2)}, u32[]{:S(2)}) collective-permute-start(bf16[288,128]{1,0:T(8,128)(2,1)S(1)} %shard_map.96.held_b), channel_id=1, source_target_pairs={{0,2},{2,0},{4,6},{6,4},{8,10},{10,8},{12,14},{14,12},{1,3},{3,1},... | collective-permute-start | bytes 221192 | tf_op jit(solution)/shard_map/ppermute | solution.py:494
  35.0 0.5 %collective-permute-start.14 = (bf16[288,128]{1,0:T(8,128)(2,1)S(1)}, bf16[288,128]{1,0:T(8,128)(2,1)S(1)}, u32[]{:S(2)}, u32[]{:S(2)}) collective-permute-start(bf16[288,128]{1,0:T(8,128)(2,1)S(1)} %get-tuple-element.98.held_a), channel_id=1, source_target_pairs={{0,1},{1,0},{2,3},{3,2},{4,5},{5,4},{6,7},{7,6},{8,9},{9,8},{10,11... | collective-permute-start | bytes 221192 | tf_op jit(solution)/shard_map/ppermute | solution.py:489
  35.6 1.4 %collective-permute-done.13.got_b = bf16[288,128]{1,0:T(8,128)(2,1)S(1)} collective-permute-done((bf16[288,128]{1,0:T(8,128)(2,1)S(1)}, bf16[288,128]{1,0:T(8,128)(2,1)S(1)}, u32[]{:S(2)}, u32[]{:S(2)}) %collective-permute-start.13) | collective-permute-done | bytes 73760 | tf_op jit(solution)/shard_map/ppermute | solution.py:494
  37.0 2.1 %collective-permute-done.12.got_a = bf16[288,128]{1,0:T(8,128)(2,1)S(1)} collective-permute-done((bf16[288,128]{1,0:T(8,128)(2,1)S(1)}, bf16[288,128]{1,0:T(8,128)(2,1)S(1)}, u32[]{:S(2)}, u32[]{:S(2)}) %collective-permute-start.12) | collective-permute-done | bytes 73760 | tf_op jit(solution)/shard_map/ppermute | solution.py:494
  39.1 1.2 %collective-permute-done.15.far_got_a = bf16[288,128]{1,0:T(8,128)(2,1)S(1)} collective-permute-done((bf16[288,128]{1,0:T(8,128)(2,1)S(1)}, bf16[288,128]{1,0:T(8,128)(2,1)S(1)}, u32[]{:S(2)}, u32[]{:S(2)}) %collective-permute-start.15) | collective-permute-done | bytes 73760 | tf_op jit(solution)/shard_map/ppermute | solution.py:489
  40.4 1.2 %shard_map.97 = (f32[4,288,128]{2,1,0:T(8,128)}, f32[4,288,128]{2,1,0:T(8,128)}, f32[1,128]{1,0:T(1,128)}) custom-call(bf16[288,128]{1,0:T(8,128)(2,1)S(1)} %get-tuple-element.98.held_a, bf16[288,128]{1,0:T(8,128)(2,1)S(1)} %collective-permute-done.12.got_a, bf16[288,128]{1,0:T(8,128)(2,1)S(1)} %shard_map.96.held_b, ...), custom_call_target="tpu_custom_call" | custom-call | bytes 1769472 | tf_op jit(solution)/shard_map/pallas_call | solution.py:36
  (29 shorter events, 1.2 us)
Async XLA Ops:
  2.4 8.0 %collective-permute-start = (bf16[2,64,128]{2,1,0:T(8,128)(2,1)S(1)}, bf16[2,64,128]{2,1,0:T(8,128)(2,1)S(1)}, u32[]{:S(2)}, u32[]{:S(2)}) collective-permute-start(bf16[2,64,128]{2,1,0:T(8,128)(2,1)S(1)} %get-tuple-element.63), channel_id=1, source_target_pairs={{0,2},{2,4},{4,6},{6,8},{8,10},{10,12},{12,14},{14,0},{1,3},{3,5},... | collective-permute-start | bytes 98312 | tf_op jit(solution)/shard_map/ppermute | solution.py:489
  5.4 4.9 %collective-permute-start.1 = (bf16[2,64,128]{2,1,0:T(8,128)(2,1)S(1)}, bf16[2,64,128]{2,1,0:T(8,128)(2,1)S(1)}, u32[]{:S(2)}, u32[]{:S(2)}) collective-permute-start(bf16[2,64,128]{2,1,0:T(8,128)(2,1)S(1)} %get-tuple-element.64), channel_id=1, source_target_pairs={{0,1},{1,0},{2,3},{3,2},{4,5},{5,4},{6,7},{7,6},{8,9},{9,8},{10,11... | collective-permute-start | bytes 98312 | tf_op jit(solution)/shard_map/ppermute | solution.py:489
  10.9 1.5 %collective-permute-start.2 = (bf16[624,128]{1,0:T(8,128)(2,1)S(1)}, bf16[624,128]{1,0:T(8,128)(2,1)S(1)}, u32[]{:S(2)}, u32[]{:S(2)}) collective-permute-start(bf16[624,128]{1,0:T(8,128)(2,1)S(1)} %get-tuple-element.71.own), channel_id=1, source_target_pairs={{0,1},{1,0},{2,3},{3,2},{4,5},{5,4},{6,7},{7,6},{8,9},{9,8},{10,11... | collective-permute-start | bytes 479240 | tf_op jit(solution)/shard_map/ppermute | solution.py:489
  11.0 2.1 %collective-permute-start.3 = (bf16[576,128]{1,0:T(8,128)(2,1)S(1)}, bf16[576,128]{1,0:T(8,128)(2,1)S(1)}, u32[]{:S(2)}, u32[]{:S(2)}) collective-permute-start(bf16[576,128]{1,0:T(8,128)(2,1)S(1)} %get-tuple-element.86), channel_id=1, source_target_pairs={{0,1},{1,0},{2,3},{3,2},{4,5},{5,4},{6,7},{7,6},{8,9},{9,8},{10,11... | collective-permute-start | bytes 442376 | tf_op jit(solution)/shard_map/ppermute | solution.py:489
  13.0 7.2 %collective-permute-start.9 = (bf16[304,128]{1,0:T(8,128)(2,1)S(1)}, bf16[304,128]{1,0:T(8,128)(2,1)S(1)}, u32[]{:S(2)}, u32[]{:S(2)}) collective-permute-start(bf16[304,128]{1,0:T(8,128)(2,1)S(1)} %get-tuple-element.92), channel_id=1, source_target_pairs={{0,4},{2,6},{4,0},{6,2},{8,12},{10,14},{12,8},{14,10},{1,5},{3,7},... | collective-permute-start | bytes 233480 | tf_op jit(solution)/shard_map/ppermute | solution.py:494
  13.1 4.4 %collective-permute-start.4 = (bf16[288,128]{1,0:T(8,128)(2,1)S(1)}, bf16[288,128]{1,0:T(8,128)(2,1)S(1)}, u32[]{:S(2)}, u32[]{:S(2)}) collective-permute-start(bf16[288,128]{1,0:T(8,128)(2,1)S(1)} %get-tuple-element.88), channel_id=1, source_target_pairs={{0,2},{2,0},{4,6},{6,4},{8,10},{10,8},{12,14},{14,12},{1,3},{3,1},... | collective-permute-start | bytes 221192 | tf_op jit(solution)/shard_map/ppermute | solution.py:494
  17.5 5.3 %collective-permute-start.5 = (bf16[288,128]{1,0:T(8,128)(2,1)S(1)}, bf16[288,128]{1,0:T(8,128)(2,1)S(1)}, u32[]{:S(2)}, u32[]{:S(2)}) collective-permute-start(bf16[288,128]{1,0:T(8,128)(2,1)S(1)} %shard_map.90.held), channel_id=1, source_target_pairs={{0,8},{2,10},{4,12},{6,14},{8,0},{10,2},{12,4},{14,6},{1,9},{3,11}... | collective-permute-start | bytes 221192 | tf_op jit(solution)/shard_map/ppermute | solution.py:494
  20.2 4.8 %collective-permute-start.10 = (bf16[304,128]{1,0:T(8,128)(2,1)S(1)}, bf16[304,128]{1,0:T(8,128)(2,1)S(1)}, u32[]{:S(2)}, u32[]{:S(2)}) collective-permute-start(bf16[304,128]{1,0:T(8,128)(2,1)S(1)} %get-tuple-element.94.held), channel_id=1, source_target_pairs={{0,2},{2,0},{4,6},{6,4},{8,10},{10,8},{12,14},{14,12},{1,3},{3,1},... | collective-permute-start | bytes 233480 | tf_op jit(solution)/shard_map/ppermute | solution.py:494
  20.8 1.2 %collective-permute-start.7 = (bf16[32,128]{1,0:T(8,128)(2,1)S(1)}, bf16[32,128]{1,0:T(8,128)(2,1)S(1)}, u32[]{:S(2)}, u32[]{:S(2)}) collective-permute-start(bf16[32,128]{1,0:T(8,128)(2,1)S(1)} %get-tuple-element.105), channel_id=1, source_target_pairs={{0,1},{1,0},{2,3},{3,2},{4,5},{5,4},{6,7},{7,6},{8,9},{9,8},{10,11... | collective-permute-start | bytes 24584 | tf_op jit(solution)/shard_map/ppermute | solution.py:489
  22.9 9.3 %collective-permute-start.6 = (bf16[288,128]{1,0:T(8,128)(2,1)S(1)}, bf16[288,128]{1,0:T(8,128)(2,1)S(1)}, u32[]{:S(2)}, u32[]{:S(2)}) collective-permute-start(bf16[288,128]{1,0:T(8,128)(2,1)S(1)} %shard_map.91.held), channel_id=1, source_target_pairs={{0,4},{2,6},{4,0},{6,2},{8,12},{10,14},{12,8},{14,10},{1,5},{3,7},... | collective-permute-start | bytes 221192 | tf_op jit(solution)/shard_map/ppermute | solution.py:494
  25.0 9.7 %collective-permute-start.11 = (bf16[304,128]{1,0:T(8,128)(2,1)S(1)}, bf16[304,128]{1,0:T(8,128)(2,1)S(1)}, u32[]{:S(2)}, u32[]{:S(2)}) collective-permute-start(bf16[304,128]{1,0:T(8,128)(2,1)S(1)} %get-tuple-element.96.held), channel_id=1, source_target_pairs={{0,8},{2,10},{4,12},{6,14},{8,0},{10,2},{12,4},{14,6},{1,9},{3,11}... | collective-permute-start | bytes 233480 | tf_op jit(solution)/shard_map/ppermute | solution.py:494
  26.0 4.4 %collective-permute-start.8 = (bf16[40,128]{1,0:T(8,128)(2,1)S(1)}, bf16[40,128]{1,0:T(8,128)(2,1)S(1)}, u32[]{:S(2)}, u32[]{:S(2)}) collective-permute-start(bf16[40,128]{1,0:T(8,128)(2,1)S(1)} %pad_maximum_fusion), channel_id=1, source_target_pairs={{0,14},{2,0},{4,2},{6,4},{8,6},{10,8},{12,10},{14,12},{1,15},{3,1}... | collective-permute-start | bytes 30728 | tf_op jit(solution)/shard_map/ppermute | solution.py:489
  32.2 4.8 %collective-permute-start.13 = (bf16[288,128]{1,0:T(8,128)(2,1)S(1)}, bf16[288,128]{1,0:T(8,128)(2,1)S(1)}, u32[]{:S(2)}, u32[]{:S(2)}) collective-permute-start(bf16[288,128]{1,0:T(8,128)(2,1)S(1)} %shard_map.96.held_b), channel_id=1, source_target_pairs={{0,2},{2,0},{4,6},{6,4},{8,10},{10,8},{12,14},{14,12},{1,3},{3,1},... | collective-permute-start | bytes 221192 | tf_op jit(solution)/shard_map/ppermute | solution.py:494
  34.7 4.4 %collective-permute-start.12 = (bf16[288,128]{1,0:T(8,128)(2,1)S(1)}, bf16[288,128]{1,0:T(8,128)(2,1)S(1)}, u32[]{:S(2)}, u32[]{:S(2)}) collective-permute-start(bf16[288,128]{1,0:T(8,128)(2,1)S(1)} %get-tuple-element.98.held_a), channel_id=1, source_target_pairs={{0,4},{2,6},{4,0},{6,2},{8,12},{10,14},{12,8},{14,10},{1,5},{3,7},... | collective-permute-start | bytes 221192 | tf_op jit(solution)/shard_map/ppermute | solution.py:494
  35.0 4.1 %collective-permute-start.16 = (bf16[288,128]{1,0:T(8,128)(2,1)S(1)}, bf16[288,128]{1,0:T(8,128)(2,1)S(1)}, u32[]{:S(2)}, u32[]{:S(2)}) collective-permute-start(bf16[288,128]{1,0:T(8,128)(2,1)S(1)} %shard_map.96.held_b), channel_id=1, source_target_pairs={{0,1},{1,0},{2,3},{3,2},{4,5},{5,4},{6,7},{7,6},{8,9},{9,8},{10,11... | collective-permute-start | bytes 221192 | tf_op jit(solution)/shard_map/ppermute | solution.py:489
  35.0 4.1 %collective-permute-start.14 = (bf16[288,128]{1,0:T(8,128)(2,1)S(1)}, bf16[288,128]{1,0:T(8,128)(2,1)S(1)}, u32[]{:S(2)}, u32[]{:S(2)}) collective-permute-start(bf16[288,128]{1,0:T(8,128)(2,1)S(1)} %get-tuple-element.98.held_a), channel_id=1, source_target_pairs={{0,1},{1,0},{2,3},{3,2},{4,5},{5,4},{6,7},{7,6},{8,9},{9,8},{10,11... | collective-permute-start | bytes 221192 | tf_op jit(solution)/shard_map/ppermute | solution.py:489
  37.0 2.1 %collective-permute-start.17 = (bf16[288,128]{1,0:T(8,128)(2,1)S(1)}, bf16[288,128]{1,0:T(8,128)(2,1)S(1)}, u32[]{:S(2)}, u32[]{:S(2)}) collective-permute-start(bf16[288,128]{1,0:T(8,128)(2,1)S(1)} %collective-permute-done.13.got_b), channel_id=1, source_target_pairs={{0,1},{1,0},{2,3},{3,2},{4,5},{5,4},{6,7},{7,6},{8,9},{9,8},{10,11... | collective-permute-start | bytes 221192 | tf_op jit(solution)/shard_map/ppermute | solution.py:489
  39.1 1.3 %collective-permute-start.15 = (bf16[288,128]{1,0:T(8,128)(2,1)S(1)}, bf16[288,128]{1,0:T(8,128)(2,1)S(1)}, u32[]{:S(2)}, u32[]{:S(2)}) collective-permute-start(bf16[288,128]{1,0:T(8,128)(2,1)S(1)} %collective-permute-done.12.got_a), channel_id=1, source_target_pairs={{0,1},{1,0},{2,3},{3,2},{4,5},{5,4},{6,7},{7,6},{8,9},{9,8},{10,11... | collective-permute-start | bytes 221192 | tf_op jit(solution)/shard_map/ppermute | solution.py:489

commit v12 on v10

--- a/solution.py
+++ b/solution.py
@@ -63,8 +63,8 @@
     for which, near in enumerate((feat_near, cot_near)):
         bulk[which].wait()
         rows[which] = near[tile_rows - 1]
-        wide_strip[...] = near[:, tile_cols - 16 :, :].astype(F32).reshape(wide_strip.shape)
-        cols[which] = wide_strip[pl.ds(15, tile_rows, stride=16), :].astype(BF16)
+        wide_strip[...] = near[:, tile_cols - 16 :, :].astype(F32)[:, 8:, :].reshape(wide_strip.shape)
+        cols[which] = wide_strip[pl.ds(7, tile_rows, stride=8), :].astype(BF16)
     for copy in bulk[2:]:
         copy.wait()
 
@@ -509,7 +509,7 @@
             vm((2, tile_rows, channels), BF16),
         ),
         scratch=[
-            pltpu.VMEM((tile_rows * 16, channels), F32),
+            pltpu.VMEM((tile_rows * 8, channels), F32),
             pltpu.SemaphoreType.DMA((5,)),
         ],
         in_specs=[ANY] * 5,
@@ -576,7 +576,6 @@
         raw_other, raw_bias, up_mat, down_near, bias_near,
     )
     got_a = turned(other_a, "narrow", 1)
-    got_b = turned(other_b, "narrow", 1)
     mine_a, mine_b = call(
         mine_body,
         (vm((taps // 2, channels), F32), vm((taps // 2, channels), F32)),
@@ -586,6 +585,8 @@
         near=tuple(range(8)),
         room=12,
     )(feat_patch, cot_patch, act, grads, feat_rim, cot_rim, rim_act, rim_masked)
+    other_b, mine_a = lax.optimization_barrier((other_b, mine_a))
+    got_b = turned(other_b, "narrow", 1)
     got_a, mine_a, mine_b = lax.optimization_barrier((got_a, mine_a, mine_b))
     mine_a, mine_b, rim_grads, late = call(
         late_body,

time: 41.7 us -> 41.8 us (level)
  waiting for transfers between devices: 13.5 us -> 14.8 us
  starting transfers between devices: 17.7 us -> 16.5 us
    ppermute x8, starting transfers between devices: 10.6 us -> 9.77 us  [traded(): lax.ppermute(value, 'wide', [(at, at ^ 1 << position) for at in range(cou...]
    ppermute x8, waiting for transfers between devices: 7.46 us -> 8.15 us  [traded(): lax.ppermute(value, 'wide', [(at, at ^ 1 << position) for at in range(cou...]
    ppermute x10, waiting for transfers between devices: 6.05 us -> 6.62 us  [turned(): lax.ppermute(value, axis, [(at, (at + steps) % count) for at in range(cou...]
  transfers between devices with their start and end apart: 18 -> 18, of which waited for: 8 -> 10; matrix products, arithmetic and copies ran while one was open for 0% -> 0% of each run, Pallas kernels for 15% -> 15%
where the time goes in v12:
time: 41.8 us; the launch traced here: 41.6 us
  starting transfers between devices  16.5 us (39%)
  waiting for transfers between devices  14.8 us (35%)
  Pallas kernels  9.6 us (23%)
  between operations  0.74 us (2%)
    ppermute x8, starting transfers between devices, traded(): lax.ppermute(value, 'wide', [(at, at ^ 1 << position) for at in range(cou...  9.77 us
    pallas_call x15, Pallas kernels, run(): return kernel(*placed)  9.6 us
    ppermute x8, waiting for transfers between devices, traded(): lax.ppermute(value, 'wide', [(at, at ^ 1 << position) for at in range(cou...  8.15 us
    ppermute x10, starting transfers between devices, turned(): lax.ppermute(value, axis, [(at, (at + steps) % count) for at in range(cou...  6.76 us
    ppermute x10, waiting for transfers between devices, turned(): lax.ppermute(value, axis, [(at, (at + steps) % count) for at in range(cou...  6.62 us
  transfers between devices with their start and end apart: 18, of which 10 were waited for; matrix products, arithmetic and copies ran while one was open for 0% of the time, Pallas kernels for 15%

profile of v12, /device:TPU:0, one launch (start us, length us, event | category | flops | bytes accessed | tf_op | source)
XLA Modules:
  0.0 41.6 jit_solution(13923633855109058871)
XLA Ops:
  0.6 1.7 %shard_map.84 = (bf16[64,64,128]{2,1,0:T(8,128)(2,1)S(1)}, bf16[64,64,128]{2,1,0:T(8,128)(2,1)S(1)}, bf16[3,3,128,128]{3,2,1,0:T(8,128)(2,1)S(1)}, bf16[3,3,128,...) custom-call(bf16[64,64,128]{2,1,0:T(8,128)(2,1)} %feat.1, ...), custom_call_target="tpu_custom_call" | custom-call | bytes 524288 | tf_op jit(solution)/shard_map/pallas_call | solution.py:36
  2.4 3.0 %collective-permute-start = (bf16[2,64,128]{2,1,0:T(8,128)(2,1)S(1)}, bf16[2,64,128]{2,1,0:T(8,128)(2,1)S(1)}, u32[]{:S(2)}, u32[]{:S(2)}) collective-permute-start(bf16[2,64,128]{2,1,0:T(8,128)(2,1)S(1)} %get-tuple-element.67), channel_id=1, source_target_pairs={{0,2},{2,4},{4,6},{6,8},{8,10},{10,12},{12,14},{14,0},{1,3},{3,5},... | collective-permute-start | bytes 98312 | tf_op jit(solution)/shard_map/ppermute | solution.py:487
  5.4 2.7 %shard_map.85 = (bf16[32,32,1152]{2,1,0:T(8,128)(2,1)S(1)}, bf16[32,32,1152]{2,1,0:T(8,128)(2,1)S(1)}, bf16[1024,128]{1,0:T(8,128)(2,1)S(1)}, bf16[1024,128]{1,0...) custom-call(bf16[64,64,128]{2,1,0:T(8,128)(2,1)S(1)} %get-tuple-elem, ...), custom_call_target="tpu_custom_call" | custom-call | flops 905969664 | bytes 6291456 | tf_op jit(solution)/shard_map/pallas_call | solution.py:36
  8.1 2.2 %collective-permute-done.top = bf16[2,64,128]{2,1,0:T(8,128)(2,1)S(1)} collective-permute-done((bf16[2,64,128]{2,1,0:T(8,128)(2,1)S(1)}, bf16[2,64,128]{2,1,0:T(8,128)(2,1)S(1)}, u32[]{:S(2)}, u32[]{:S(2)}) %collective-permute-start) | collective-permute-done | bytes 32800 | tf_op jit(solution)/shard_map/ppermute | solution.py:487
  10.3 0.5 %shard_map.86 = (bf16[64,128]{1,0:T(8,128)(2,1)S(1)}, bf16[64,1152]{1,0:T(8,128)(2,1)S(1)}, bf16[64,1152]{1,0:T(8,128)(2,1)S(1)}, bf16[64,128]{1,0:T(8,128)(2,1)...) custom-call(bf16[32,32,1152]{2,1,0:T(8,128)(2,1)S(1)} %get-tuple-ele, ...), custom_call_target="tpu_custom_call" | custom-call | flops 67108864 | bytes 3145728 | tf_op jit(solution)/shard_map/pallas_call | solution.py:36
  11.0 0.9 %shard_map.87 = (f32[576,128]{1,0:T(8,128)S(1)}, f32[576,128]{1,0:T(8,128)S(1)}) custom-call(bf16[32,32,1152]{2,1,0:T(8,128)(2,1)S(1)} %get-tuple-element.63.feat_patch, bf16[32,32,1152]{2,1,0:T(8,128)(2,1)S(1)} %get-tuple-element.64.cot_patch, bf16[1024,128]{1,0:T(8,128)(2,1)S(1)} %get-tuple-element.77.act, bf16[1024,128]{1,0:T(8,128)(2,1)S(1)} %get-tuple-element.78.grads, ...), custom_call_target="tpu_custom_call" | custom-call | flops 301989888 | bytes 3145728 | tf_op jit(solution)/shard_map/pallas_call | solution.py:36
  12.3 0.5 %shard_map.88 = (f32[576,128]{1,0:T(8,128)S(1)}, f32[576,128]{1,0:T(8,128)S(1)}, bf16[64,128]{1,0:T(8,128)(2,1)S(1)}, f32[8,128]{1,0:T(8,128)S(1)}) custom-call(bf16[624,128]{1,0:T(8,128)(2,1)S(1)} %get-tuple-element.75.own, bf16[624,128]{1,0:T(8,128)(2,1)S(1)} %collective-permute-done.2.got, f32[576,128]{1,0:T(8,128)S(1)} %get-tuple-element.87.mine_a, ...), custom_call_target="tpu_custom_call" | custom-call | flops 16777216 | bytes 1048576 | tf_op jit(solution)/shard_map/pallas_call | solution.py:36
  13.4 1.1 %collective-permute-start.4 = (bf16[288,128]{1,0:T(8,128)(2,1)S(1)}, bf16[288,128]{1,0:T(8,128)(2,1)S(1)}, u32[]{:S(2)}, u32[]{:S(2)}) collective-permute-start(bf16[288,128]{1,0:T(8,128)(2,1)S(1)} %get-tuple-element.93), channel_id=1, source_target_pairs={{0,2},{2,0},{4,6},{6,4},{8,10},{10,8},{12,14},{14,12},{1,3},{3,1},... | collective-permute-start | bytes 221192 | tf_op jit(solution)/shard_map/ppermute | solution.py:492
  14.4 3.3 %collective-permute-done.4.got = bf16[288,128]{1,0:T(8,128)(2,1)S(1)} collective-permute-done((bf16[288,128]{1,0:T(8,128)(2,1)S(1)}, bf16[288,128]{1,0:T(8,128)(2,1)S(1)}, u32[]{:S(2)}, u32[]{:S(2)}) %collective-permute-start.4) | collective-permute-done | bytes 73760 | tf_op jit(solution)/shard_map/ppermute | solution.py:492
  17.8 2.2 %collective-permute-start.5 = (bf16[288,128]{1,0:T(8,128)(2,1)S(1)}, bf16[288,128]{1,0:T(8,128)(2,1)S(1)}, u32[]{:S(2)}, u32[]{:S(2)}) collective-permute-start(bf16[288,128]{1,0:T(8,128)(2,1)S(1)} %shard_map.90.held), channel_id=1, source_target_pairs={{0,8},{2,10},{4,12},{6,14},{8,0},{10,2},{12,4},{14,6},{1,9},{3,11}... | collective-permute-start | bytes 221192 | tf_op jit(solution)/shard_map/ppermute | solution.py:492
  20.1 0.7 %collective-permute-start.10 = (bf16[304,128]{1,0:T(8,128)(2,1)S(1)}, bf16[304,128]{1,0:T(8,128)(2,1)S(1)}, u32[]{:S(2)}, u32[]{:S(2)}) collective-permute-start(bf16[304,128]{1,0:T(8,128)(2,1)S(1)} %get-tuple-element.102.held), channel_id=1, source_target_pairs={{0,2},{2,0},{4,6},{6,4},{8,10},{10,8},{12,14},{14,12},{1,3},{3,1},... | collective-permute-start | bytes 233480 | tf_op jit(solution)/shard_map/ppermute | solution.py:492
  20.7 1.2 %collective-permute-done.7.right = bf16[32,128]{1,0:T(8,128)(2,1)S(1)} collective-permute-done((bf16[32,128]{1,0:T(8,128)(2,1)S(1)}, bf16[32,128]{1,0:T(8,128)(2,1)S(1)}, u32[]{:S(2)}, u32[]{:S(2)}) %collective-permute-start.7) | collective-permute-done | bytes 8224 | tf_op jit(solution)/shard_map/ppermute | solution.py:487
  21.9 1.2 %collective-permute-done.5.got = bf16[288,128]{1,0:T(8,128)(2,1)S(1)} collective-permute-done((bf16[288,128]{1,0:T(8,128)(2,1)S(1)}, bf16[288,128]{1,0:T(8,128)(2,1)S(1)}, u32[]{:S(2)}, u32[]{:S(2)}) %collective-permute-start.5) | collective-permute-done | bytes 73760 | tf_op jit(solution)/shard_map/ppermute | solution.py:492
  23.1 1.7 %collective-permute-start.6 = (bf16[288,128]{1,0:T(8,128)(2,1)S(1)}, bf16[288,128]{1,0:T(8,128)(2,1)S(1)}, u32[]{:S(2)}, u32[]{:S(2)}) collective-permute-start(bf16[288,128]{1,0:T(8,128)(2,1)S(1)} %shard_map.91.held), channel_id=1, source_target_pairs={{0,4},{2,6},{4,0},{6,2},{8,12},{10,14},{12,8},{14,10},{1,5},{3,7},... | collective-permute-start | bytes 221192 | tf_op jit(solution)/shard_map/ppermute | solution.py:492
  24.9 1.2 %collective-permute-start.11 = (bf16[304,128]{1,0:T(8,128)(2,1)S(1)}, bf16[304,128]{1,0:T(8,128)(2,1)S(1)}, u32[]{:S(2)}, u32[]{:S(2)}) collective-permute-start(bf16[304,128]{1,0:T(8,128)(2,1)S(1)} %get-tuple-element.104.held), channel_id=1, source_target_pairs={{0,8},{2,10},{4,12},{6,14},{8,0},{10,2},{12,4},{14,6},{1,9},{3,11}... | collective-permute-start | bytes 233480 | tf_op jit(solution)/shard_map/ppermute | solution.py:492
  26.1 2.9 %collective-permute-start.8 = (bf16[40,128]{1,0:T(8,128)(2,1)S(1)}, bf16[40,128]{1,0:T(8,128)(2,1)S(1)}, u32[]{:S(2)}, u32[]{:S(2)}) collective-permute-start(bf16[40,128]{1,0:T(8,128)(2,1)S(1)} %pad_maximum_fusion), channel_id=1, source_target_pairs={{0,14},{2,0},{4,2},{6,4},{8,6},{10,8},{12,10},{14,12},{1,15},{3,1}... | collective-permute-start | bytes 30728 | tf_op jit(solution)/shard_map/ppermute | solution.py:487
  29.0 1.4 %collective-permute-done.8.below = bf16[40,128]{1,0:T(8,128)(2,1)S(1)} collective-permute-done((bf16[40,128]{1,0:T(8,128)(2,1)S(1)}, bf16[40,128]{1,0:T(8,128)(2,1)S(1)}, u32[]{:S(2)}, u32[]{:S(2)}) %collective-permute-start.8) | collective-permute-done | bytes 10272 | tf_op jit(solution)/shard_map/ppermute | solution.py:487
  30.4 1.8 %shard_map.92 = bf16[64,64,128]{2,1,0:T(8,128)(2,1)} custom-call(bf16[1024,128]{1,0:T(8,128)(2,1)S(1)} %get-tuple-element.78.grads, bf16[64,128]{1,0:T(8,128)(2,1)S(1)} %get-tuple-element.94.rim_grads, bf16[32,128]{1,0:T(8,128)(2,1)S(1)} %collective-permute-done.7.right, bf16[40,128]{1,0:T(8,128)(2,1)S(1)} %collective-permute-done.8.below, ...), custom_call_target="tpu_custom_call" | custom-call | flops 402653184 | bytes 3145728 | tf_op jit(solution)/shard_map/pallas_call | solution.py:36
  32.2 2.5 %collective-permute-start.13 = (bf16[288,128]{1,0:T(8,128)(2,1)S(1)}, bf16[288,128]{1,0:T(8,128)(2,1)S(1)}, u32[]{:S(2)}, u32[]{:S(2)}) collective-permute-start(bf16[288,128]{1,0:T(8,128)(2,1)S(1)} %shard_map.97.held_b), channel_id=1, source_target_pairs={{0,2},{2,0},{4,6},{6,4},{8,10},{10,8},{12,14},{14,12},{1,3},{3,1},... | collective-permute-start | bytes 221192 | tf_op jit(solution)/shard_map/ppermute | solution.py:492
  35.0 0.5 %collective-permute-start.14 = (bf16[288,128]{1,0:T(8,128)(2,1)S(1)}, bf16[288,128]{1,0:T(8,128)(2,1)S(1)}, u32[]{:S(2)}, u32[]{:S(2)}) collective-permute-start(bf16[288,128]{1,0:T(8,128)(2,1)S(1)} %get-tuple-element.106.held_a), channel_id=1, source_target_pairs={{0,1},{1,0},{2,3},{3,2},{4,5},{5,4},{6,7},{7,6},{8,9},{9,8},{10,11... | collective-permute-start | bytes 221192 | tf_op jit(solution)/shard_map/ppermute | solution.py:487
  35.5 1.5 %collective-permute-done.13.got_b = bf16[288,128]{1,0:T(8,128)(2,1)S(1)} collective-permute-done((bf16[288,128]{1,0:T(8,128)(2,1)S(1)}, bf16[288,128]{1,0:T(8,128)(2,1)S(1)}, u32[]{:S(2)}, u32[]{:S(2)}) %collective-permute-start.13) | collective-permute-done | bytes 73760 | tf_op jit(solution)/shard_map/ppermute | solution.py:492
  37.0 2.1 %collective-permute-done.12.got_a = bf16[288,128]{1,0:T(8,128)(2,1)S(1)} collective-permute-done((bf16[288,128]{1,0:T(8,128)(2,1)S(1)}, bf16[288,128]{1,0:T(8,128)(2,1)S(1)}, u32[]{:S(2)}, u32[]{:S(2)}) %collective-permute-start.12) | collective-permute-done | bytes 73760 | tf_op jit(solution)/shard_map/ppermute | solution.py:492
  39.2 1.2 %collective-permute-done.15.far_got_a = bf16[288,128]{1,0:T(8,128)(2,1)S(1)} collective-permute-done((bf16[288,128]{1,0:T(8,128)(2,1)S(1)}, bf16[288,128]{1,0:T(8,128)(2,1)S(1)}, u32[]{:S(2)}, u32[]{:S(2)}) %collective-permute-start.15) | collective-permute-done | bytes 73760 | tf_op jit(solution)/shard_map/ppermute | solution.py:487
  40.4 1.2 %shard_map.98 = (f32[4,288,128]{2,1,0:T(8,128)}, f32[4,288,128]{2,1,0:T(8,128)}, f32[1,128]{1,0:T(1,128)}) custom-call(bf16[288,128]{1,0:T(8,128)(2,1)S(1)} %get-tuple-element.106.held_a, bf16[288,128]{1,0:T(8,128)(2,1)S(1)} %collective-permute-done.12.got_a, bf16[288,128]{1,0:T(8,128)(2,1)S(1)} %shard_map.97.held_b, ...), custom_call_target="tpu_custom_call" | custom-call | bytes 1769472 | tf_op jit(solution)/shard_map/pallas_call | solution.py:36
  (30 shorter events, 1.5 us)
Async XLA Ops:
  2.4 8.0 %collective-permute-start = (bf16[2,64,128]{2,1,0:T(8,128)(2,1)S(1)}, bf16[2,64,128]{2,1,0:T(8,128)(2,1)S(1)}, u32[]{:S(2)}, u32[]{:S(2)}) collective-permute-start(bf16[2,64,128]{2,1,0:T(8,128)(2,1)S(1)} %get-tuple-element.67), channel_id=1, source_target_pairs={{0,2},{2,4},{4,6},{6,8},{8,10},{10,12},{12,14},{14,0},{1,3},{3,5},... | collective-permute-start | bytes 98312 | tf_op jit(solution)/shard_map/ppermute | solution.py:487
  5.4 4.9 %collective-permute-start.1 = (bf16[2,64,128]{2,1,0:T(8,128)(2,1)S(1)}, bf16[2,64,128]{2,1,0:T(8,128)(2,1)S(1)}, u32[]{:S(2)}, u32[]{:S(2)}) collective-permute-start(bf16[2,64,128]{2,1,0:T(8,128)(2,1)S(1)} %get-tuple-element.68), channel_id=1, source_target_pairs={{0,1},{1,0},{2,3},{3,2},{4,5},{5,4},{6,7},{7,6},{8,9},{9,8},{10,11... | collective-permute-start | bytes 98312 | tf_op jit(solution)/shard_map/ppermute | solution.py:487
  10.9 1.5 %collective-permute-start.2 = (bf16[624,128]{1,0:T(8,128)(2,1)S(1)}, bf16[624,128]{1,0:T(8,128)(2,1)S(1)}, u32[]{:S(2)}, u32[]{:S(2)}) collective-permute-start(bf16[624,128]{1,0:T(8,128)(2,1)S(1)} %get-tuple-element.75.own), channel_id=1, source_target_pairs={{0,1},{1,0},{2,3},{3,2},{4,5},{5,4},{6,7},{7,6},{8,9},{9,8},{10,11... | collective-permute-start | bytes 479240 | tf_op jit(solution)/shard_map/ppermute | solution.py:487
  11.9 1.4 %collective-permute-start.3 = (bf16[576,128]{1,0:T(8,128)(2,1)S(1)}, bf16[576,128]{1,0:T(8,128)(2,1)S(1)}, u32[]{:S(2)}, u32[]{:S(2)}) collective-permute-start(bf16[576,128]{1,0:T(8,128)(2,1)S(1)} %get-tuple-element.91), channel_id=1, source_target_pairs={{0,1},{1,0},{2,3},{3,2},{4,5},{5,4},{6,7},{7,6},{8,9},{9,8},{10,11... | collective-permute-start | bytes 442376 | tf_op jit(solution)/shard_map/ppermute | solution.py:487
  12.9 7.2 %collective-permute-start.9 = (bf16[304,128]{1,0:T(8,128)(2,1)S(1)}, bf16[304,128]{1,0:T(8,128)(2,1)S(1)}, u32[]{:S(2)}, u32[]{:S(2)}) collective-permute-start(bf16[304,128]{1,0:T(8,128)(2,1)S(1)} %get-tuple-element.100), channel_id=1, source_target_pairs={{0,4},{2,6},{4,0},{6,2},{8,12},{10,14},{12,8},{14,10},{1,5},{3,7},... | collective-permute-start | bytes 233480 | tf_op jit(solution)/shard_map/ppermute | solution.py:492
  13.4 4.4 %collective-permute-start.4 = (bf16[288,128]{1,0:T(8,128)(2,1)S(1)}, bf16[288,128]{1,0:T(8,128)(2,1)S(1)}, u32[]{:S(2)}, u32[]{:S(2)}) collective-permute-start(bf16[288,128]{1,0:T(8,128)(2,1)S(1)} %get-tuple-element.93), channel_id=1, source_target_pairs={{0,2},{2,0},{4,6},{6,4},{8,10},{10,8},{12,14},{14,12},{1,3},{3,1},... | collective-permute-start | bytes 221192 | tf_op jit(solution)/shard_map/ppermute | solution.py:492
  17.8 5.3 %collective-permute-start.5 = (bf16[288,128]{1,0:T(8,128)(2,1)S(1)}, bf16[288,128]{1,0:T(8,128)(2,1)S(1)}, u32[]{:S(2)}, u32[]{:S(2)}) collective-permute-start(bf16[288,128]{1,0:T(8,128)(2,1)S(1)} %shard_map.90.held), channel_id=1, source_target_pairs={{0,8},{2,10},{4,12},{6,14},{8,0},{10,2},{12,4},{14,6},{1,9},{3,11}... | collective-permute-start | bytes 221192 | tf_op jit(solution)/shard_map/ppermute | solution.py:492
  20.1 4.8 %collective-permute-start.10 = (bf16[304,128]{1,0:T(8,128)(2,1)S(1)}, bf16[304,128]{1,0:T(8,128)(2,1)S(1)}, u32[]{:S(2)}, u32[]{:S(2)}) collective-permute-start(bf16[304,128]{1,0:T(8,128)(2,1)S(1)} %get-tuple-element.102.held), channel_id=1, source_target_pairs={{0,2},{2,0},{4,6},{6,4},{8,10},{10,8},{12,14},{14,12},{1,3},{3,1},... | collective-permute-start | bytes 233480 | tf_op jit(solution)/shard_map/ppermute | solution.py:492
  20.7 1.2 %collective-permute-start.7 = (bf16[32,128]{1,0:T(8,128)(2,1)S(1)}, bf16[32,128]{1,0:T(8,128)(2,1)S(1)}, u32[]{:S(2)}, u32[]{:S(2)}) collective-permute-start(bf16[32,128]{1,0:T(8,128)(2,1)S(1)} %get-tuple-element.113), channel_id=1, source_target_pairs={{0,1},{1,0},{2,3},{3,2},{4,5},{5,4},{6,7},{7,6},{8,9},{9,8},{10,11... | collective-permute-start | bytes 24584 | tf_op jit(solution)/shard_map/ppermute | solution.py:487
  23.1 9.0 %collective-permute-start.6 = (bf16[288,128]{1,0:T(8,128)(2,1)S(1)}, bf16[288,128]{1,0:T(8,128)(2,1)S(1)}, u32[]{:S(2)}, u32[]{:S(2)}) collective-permute-start(bf16[288,128]{1,0:T(8,128)(2,1)S(1)} %shard_map.91.held), channel_id=1, source_target_pairs={{0,4},{2,6},{4,0},{6,2},{8,12},{10,14},{12,8},{14,10},{1,5},{3,7},... | collective-permute-start | bytes 221192 | tf_op jit(solution)/shard_map/ppermute | solution.py:492
  24.9 9.8 %collective-permute-start.11 = (bf16[304,128]{1,0:T(8,128)(2,1)S(1)}, bf16[304,128]{1,0:T(8,128)(2,1)S(1)}, u32[]{:S(2)}, u32[]{:S(2)}) collective-permute-start(bf16[304,128]{1,0:T(8,128)(2,1)S(1)} %get-tuple-element.104.held), channel_id=1, source_target_pairs={{0,8},{2,10},{4,12},{6,14},{8,0},{10,2},{12,4},{14,6},{1,9},{3,11}... | collective-permute-start | bytes 233480 | tf_op jit(solution)/shard_map/ppermute | solution.py:492
  26.1 4.3 %collective-permute-start.8 = (bf16[40,128]{1,0:T(8,128)(2,1)S(1)}, bf16[40,128]{1,0:T(8,128)(2,1)S(1)}, u32[]{:S(2)}, u32[]{:S(2)}) collective-permute-start(bf16[40,128]{1,0:T(8,128)(2,1)S(1)} %pad_maximum_fusion), channel_id=1, source_target_pairs={{0,14},{2,0},{4,2},{6,4},{8,6},{10,8},{12,10},{14,12},{1,15},{3,1}... | collective-permute-start | bytes 30728 | tf_op jit(solution)/shard_map/ppermute | solution.py:487
  32.2 4.8 %collective-permute-start.13 = (bf16[288,128]{1,0:T(8,128)(2,1)S(1)}, bf16[288,128]{1,0:T(8,128)(2,1)S(1)}, u32[]{:S(2)}, u32[]{:S(2)}) collective-permute-start(bf16[288,128]{1,0:T(8,128)(2,1)S(1)} %shard_map.97.held_b), channel_id=1, source_target_pairs={{0,2},{2,0},{4,6},{6,4},{8,10},{10,8},{12,14},{14,12},{1,3},{3,1},... | collective-permute-start | bytes 221192 | tf_op jit(solution)/shard_map/ppermute | solution.py:492
  34.7 4.4 %collective-permute-start.12 = (bf16[288,128]{1,0:T(8,128)(2,1)S(1)}, bf16[288,128]{1,0:T(8,128)(2,1)S(1)}, u32[]{:S(2)}, u32[]{:S(2)}) collective-permute-start(bf16[288,128]{1,0:T(8,128)(2,1)S(1)} %get-tuple-element.106.held_a), channel_id=1, source_target_pairs={{0,4},{2,6},{4,0},{6,2},{8,12},{10,14},{12,8},{14,10},{1,5},{3,7},... | collective-permute-start | bytes 221192 | tf_op jit(solution)/shard_map/ppermute | solution.py:492
  35.0 4.1 %collective-permute-start.16 = (bf16[288,128]{1,0:T(8,128)(2,1)S(1)}, bf16[288,128]{1,0:T(8,128)(2,1)S(1)}, u32[]{:S(2)}, u32[]{:S(2)}) collective-permute-start(bf16[288,128]{1,0:T(8,128)(2,1)S(1)} %shard_map.97.held_b), channel_id=1, source_target_pairs={{0,1},{1,0},{2,3},{3,2},{4,5},{5,4},{6,7},{7,6},{8,9},{9,8},{10,11... | collective-permute-start | bytes 221192 | tf_op jit(solution)/shard_map/ppermute | solution.py:487
  35.0 4.1 %collective-permute-start.14 = (bf16[288,128]{1,0:T(8,128)(2,1)S(1)}, bf16[288,128]{1,0:T(8,128)(2,1)S(1)}, u32[]{:S(2)}, u32[]{:S(2)}) collective-permute-start(bf16[288,128]{1,0:T(8,128)(2,1)S(1)} %get-tuple-element.106.held_a), channel_id=1, source_target_pairs={{0,1},{1,0},{2,3},{3,2},{4,5},{5,4},{6,7},{7,6},{8,9},{9,8},{10,11... | collective-permute-start | bytes 221192 | tf_op jit(solution)/shard_map/ppermute | solution.py:487
  37.0 2.1 %collective-permute-start.17 = (bf16[288,128]{1,0:T(8,128)(2,1)S(1)}, bf16[288,128]{1,0:T(8,128)(2,1)S(1)}, u32[]{:S(2)}, u32[]{:S(2)}) collective-permute-start(bf16[288,128]{1,0:T(8,128)(2,1)S(1)} %collective-permute-done.13.got_b), channel_id=1, source_target_pairs={{0,1},{1,0},{2,3},{3,2},{4,5},{5,4},{6,7},{7,6},{8,9},{9,8},{10,11... | collective-permute-start | bytes 221192 | tf_op jit(solution)/shard_map/ppermute | solution.py:487
  39.1 1.3 %collective-permute-start.15 = (bf16[288,128]{1,0:T(8,128)(2,1)S(1)}, bf16[288,128]{1,0:T(8,128)(2,1)S(1)}, u32[]{:S(2)}, u32[]{:S(2)}) collective-permute-start(bf16[288,128]{1,0:T(8,128)(2,1)S(1)} %collective-permute-done.12.got_a), channel_id=1, source_target_pairs={{0,1},{1,0},{2,3},{3,2},{4,5},{5,4},{6,7},{7,6},{8,9},{9,8},{10,11... | collective-permute-start | bytes 221192 | tf_op jit(solution)/shard_map/ppermute | solution.py:487
